TPU v7x, 256 devices: a whole 4x4x8 slice. The times are simulated.
256 devices in a mesh: ctx: 32 (over z, y_lo, core), head: 8 (over x, y_hi).
Axes of the slice: x: 4, y: 4 (y_hi: 2, y_lo: 2; y = y_hi * 2 + y_lo), z: 8, core: 2. Of those that a mesh axis runs over, the one named last changes fastest.
Arguments:
- hidden: bfloat16 [4096, 8192], P('ctx', 'head'), may hold values from -6 to 6
- query: bfloat16 [4096, 8192], P('ctx', 'head'), may hold values from -60 to 60
- fresh_key_value: bfloat16 [2, 4096, 1024], P(None, 'ctx', 'head'), may hold values from -6 to 6
- cached_key_value: bfloat16 [2, 8192, 1024], P(None, 'ctx', 'head'), may hold values from -6 to 6
- positions: int32 [3, 4096], P(None, 'ctx'), may hold values from 0 to 4095
- out_weight: bfloat16 [8192, 8192], P('head', 'ctx'), may hold values from -0.0625 to 0.0625
- norm_gain: float32 [8192], P('head'), may hold values from 0.25 to 1.75
- layer3_key_value_weight: bfloat16 [8192, 2048], P(None, 'head'), may hold values from -0.0625 to 0.0625
- layer3_key_value_bias: float32 [2048], P('head'), may hold values from -3 to 3
- keep_index: int32 [4096], P('ctx'), may hold values from 0 to 127, as said below
- keep_count: int32 [32], P('ctx'), may hold values from 64 to 128, as said below
Outputs:
- layer2_out: bfloat16 [4096, 8192], P('ctx', 'head')
- layer3_packed_key_value: bfloat16 [4096, 2048], P('ctx', 'head')
Inputs may be any that keep to these rules, and one draw needn't show every extreme that they name: `keep_index`: within each block of 128 entries, the first keep_count entries are the kept rows in rising order (all text rows and every second visual row), the rest the dropped rows in rising order. `keep_count`: some block keeps all 128 rows in every draw.
All inputs are finite; a program needn't handle non-finite values.
Results may differ from a plain program's by a relative error of at most 0.012.
Values may be sent and summed in bfloat16 or wider, within the bound.
No kernel may reach another device: no remote copies, remote signals or barrier semaphores. Data moves between devices by JAX's collectives and lax.ppermute only.
A program may use at most 192 MiB of HBM per device.

v0:
```python
import jax
import jax.numpy as jnp
from jax import lax
from jax.sharding import PartitionSpec as P

MODEL_WIDTH = 8192
HEAD_DIMENSION = 128


def copy_for_each(shard, axis):
    size = lax.axis_size(axis)
    return lax.all_to_all(
        jnp.broadcast_to(shard[None], (size, *shard.shape)), axis, 0, 0, tiled=True
    )


def taken_together(shard, axis):
    everything = copy_for_each(shard, axis)
    return jnp.sum(everything, axis=0)


def joined_along(pieces, dim):
    shape = list(pieces.shape[1:])
    shape[dim] *= pieces.shape[0]
    return jnp.moveaxis(pieces, 0, dim).reshape(shape)


def gather_directly(shard, axis, dim):
    pieces = copy_for_each(shard, axis)
    return joined_along(pieces, dim)


def tables(positions, head_size):
    half = head_size // 2
    column = jnp.arange(half)
    frequency = jnp.power(jnp.float32(1000000.0), -(2.0 * column.astype(jnp.float32)) / head_size)
    section = (column >= head_size // 8).astype(jnp.int32) + (
        column >= head_size // 8 + 3 * head_size // 16
    ).astype(jnp.int32)
    places = positions.astype(jnp.float32)
    chosen = jnp.where(
        section[None, :] == 0,
        places[0][:, None],
        jnp.where(section[None, :] == 1, places[1][:, None], places[2][:, None]),
    )
    angles = chosen * frequency[None, :]
    return (jnp.cos(angles), jnp.sin(angles))


def apply_rotary(x, cosine_table, sine_table):
    half = x.shape[-1] // 2
    first_half = x[..., :half]
    second_half = x[..., half:]
    cosine_table = cosine_table[:, None, :]
    sine_table = sine_table[:, None, :]
    return jnp.concatenate(
        [
            first_half * cosine_table - second_half * sine_table,
            second_half * cosine_table + first_half * sine_table,
        ],
        axis=-1,
    )


def empty_state(rows, kv_local, query_group_width, head_size):
    return (
        jnp.full((rows, kv_local, query_group_width), -1e30, jnp.float32),
        jnp.zeros((rows, kv_local, query_group_width), jnp.float32),
        jnp.zeros((rows, kv_local, query_group_width, head_size), jnp.float32),
    )


def attend(grouped_rows, running, key_matrix_rows, value_matrix_rows, visible):
    head_size = grouped_rows.shape[-1]
    kv_local = grouped_rows.shape[1]
    key_heads = key_matrix_rows.reshape(key_matrix_rows.shape[0], kv_local, head_size)
    value_heads = value_matrix_rows.reshape(value_matrix_rows.shape[0], kv_local, head_size)
    scores = jnp.einsum(
        "nkgd,rkd->nkgr", grouped_rows, key_heads, preferred_element_type=jnp.float32
    ) * head_size ** (-0.5)
    if visible is not None:
        scores = jnp.where(visible[:, None, None, :], scores, -1e30)
    maxima, totals, weighted = running
    raised = jnp.maximum(maxima, jnp.max(scores, axis=-1))
    expos = jnp.exp(scores - raised[..., None])
    if visible is not None:
        expos = jnp.where(visible[:, None, None, :], expos, 0.0)
    factor = jnp.exp(maxima - raised)
    totals = totals * factor + jnp.sum(expos, axis=-1)
    weighted = weighted * factor[..., None] + jnp.einsum(
        "nkgr,rkd->nkgd",
        expos.astype(jnp.bfloat16),
        value_heads,
        preferred_element_type=jnp.float32,
    )
    return (raised, totals, weighted)


def local(
    hidden,
    query,
    fresh_key_value,
    cached_key_value,
    positions,
    out_weight,
    norm_gain,
    layer3_key_value_weight,
    layer3_key_value_bias,
    keep_index,
    keep_count,
):
    new_rows = hidden.shape[0]
    head_size = HEAD_DIMENSION
    kv_local = fresh_key_value.shape[2] // head_size
    q_local = query.shape[1] // head_size
    query_group_width = q_local // kv_local
    cosine_table, sine_table = tables(positions, head_size)
    rotary_query_rows = apply_rotary(
        query.astype(jnp.float32).reshape(new_rows, q_local, head_size), cosine_table, sine_table
    ).astype(jnp.bfloat16)
    grouped_rows = rotary_query_rows.reshape(new_rows, kv_local, query_group_width, head_size)
    rotary_key_rows = apply_rotary(
        fresh_key_value[0].astype(jnp.float32).reshape(new_rows, kv_local, head_size),
        cosine_table,
        sine_table,
    ).astype(jnp.bfloat16)
    recent = jnp.stack(
        [rotary_key_rows.reshape(new_rows, kv_local * head_size), fresh_key_value[1]]
    )
    first_row = lax.axis_index("ctx") * new_rows
    shard_piece = lax.all_gather(cached_key_value, "ctx", axis=1, tiled=True)
    running = attend(
        grouped_rows,
        empty_state(new_rows, kv_local, query_group_width, head_size),
        shard_piece[0],
        shard_piece[1],
        None,
    )
    query_pos = first_row + jnp.arange(new_rows)
    shard_piece = lax.all_gather(recent, "ctx", axis=1, tiled=True)
    key_pos = jnp.arange(shard_piece.shape[1])
    visible = key_pos[None, :] <= query_pos[:, None]
    maxima, totals, weighted = attend(
        grouped_rows, running, shard_piece[0], shard_piece[1], visible
    )
    attn = (
        (weighted / totals[..., None]).reshape(new_rows, q_local * head_size).astype(jnp.bfloat16)
    )
    partial_sum = jnp.dot(
        attn,
        lax.all_gather(out_weight, "ctx", axis=1, tiled=True),
        preferred_element_type=jnp.float32,
    )
    head_summed = lax.psum_scatter(
        partial_sum.astype(jnp.bfloat16), "head", scatter_dimension=1, tiled=True
    ).astype(jnp.float32)
    layer2_out = (hidden.astype(jnp.float32) + head_summed).astype(jnp.bfloat16)
    widened = layer2_out.astype(jnp.float32)
    squares = taken_together(jnp.sum(widened * widened, axis=1), "head")
    normalized_rows = (
        widened * lax.rsqrt(squares / MODEL_WIDTH + 1e-06)[:, None] * norm_gain
    ).astype(jnp.bfloat16)
    full_rows = gather_directly(normalized_rows, "head", 1)
    layer_three_key_value = (
        jnp.dot(full_rows, layer3_key_value_weight, preferred_element_type=jnp.float32)
        + layer3_key_value_bias
    ).reshape(new_rows, kv_local, 2, head_size)
    layer_three_keys = apply_rotary(layer_three_key_value[:, :, 0], cosine_table, sine_table)
    layer_three_key_value = (
        jnp.stack([layer_three_keys, layer_three_key_value[:, :, 1]], axis=2)
        .reshape(new_rows, 2 * kv_local * head_size)
        .astype(jnp.bfloat16)
    )
    selected_rows = jnp.take(layer_three_key_value, keep_index, axis=0)
    block_occupied = jnp.arange(new_rows) < keep_count[0]
    layer3_packed_key_value = jnp.where(
        block_occupied[:, None], selected_rows, jnp.zeros_like(selected_rows)
    )
    return (layer2_out, layer3_packed_key_value)


def solution(mesh):
    placed = (
        P("ctx", "head"),
        P("ctx", "head"),
        P(None, "ctx", "head"),
        P(None, "ctx", "head"),
        P(None, "ctx"),
        P("head", "ctx"),
        P("head"),
        P(None, "head"),
        P("head"),
        P("ctx"),
        P("ctx"),
    )
    return jax.shard_map(
        local,
        mesh=mesh,
        in_specs=placed,
        out_specs=(P("ctx", "head"), P("ctx", "head")),
        check_vma=False,
    )
```

profile of v0, /device:TPU:1, one launch (start us, length us, event | category | flops | bytes accessed | tf_op | source)
XLA Modules:
  0.0 416.7 jit_solution(4495611728508093874)
XLA Ops:
  7.2 0.0 all-gather.6.cloned.1.call-start
  7.3 0.7 convert_element_type.107
  8.0 0.8 bitcast_convert_fusion
  8.8 0.4 fusion.43
  9.1 0.7 pad_maximum_fusion.1
  9.8 0.0 all-gather.6.cloned.1.call-update
  9.9 0.0 all-gather.4.cloned.1.call-start
  9.9 0.7 all-gather.4.cloned.1.call-update
  10.6 0.0 all-gather.8.cloned.1.call-start
  10.7 0.7 all-gather.8.cloned.1.call-update
  11.3 0.0 reduce-scatter.2.cloned.1.call-start
  11.4 1.1 copy.40
  12.6 0.2 copy.58
  12.8 0.2 copy.59
  13.0 0.3 fusion.42
  13.4 0.1 subtract_convert_fusion
  13.5 0.3 iota_compare_fusion
  13.9 65.6 %all-gather.6.cloned.1.call-done = bf16[2,4096,128]{2,1,0:T(8,128)(2,1)} async-done(((bf16[2,128,128]{2,1,0:T(8,128)(2,1)}), bf16[2,4096,128]{2,1,0:T(8,128)(2,1)}) %all-gather.6.cloned.1.call-update) | async-done | bytes 2097168 | tf_op jit(solution)/shard_map/all_gather | solution.py:140
  79.4 8.3 %fusion.6 = (f32[128,8]{0,1:T(8,128)S(1)}, f32[4096,128,8]{1,0,2:T(8,128)}) fusion(pred[128,4096]{0,1:T(8,128)(4,1)S(1)} %iota_compare_fusion, bf16[128,8,64]{2,0,1:T(8,128)(2,1)S(1)} %get-tuple-element.7, bf16[128,8,64]{2,0,1:T(8,128)(2,1)S(1)} %get-tuple-element.6, bf16[2,4096,128]{2,1,0:T(8,128)(2,1)} %all-gather.6.cloned.1.call-done), kind=kOutput, calls=%fused_computation.10 | convolution fusion | flops 1086848000 | bytes 18616320 | tf_op jit(solution)/shard_map/nkgd,rkd->nkgr/dot_general | solution.py:78
  87.7 60.1 %all-gather.4.cloned.1.call-done = bf16[2,8192,128]{2,1,0:T(8,128)(2,1)} async-done(((bf16[2,256,128]{2,1,0:T(8,128)(2,1)}), bf16[2,8192,128]{2,1,0:T(8,128)(2,1)}) %all-gather.4.cloned.1.call-update) | async-done | bytes 4194320 | tf_op jit(solution)/shard_map/all_gather | solution.py:131
  147.8 16.6 %bitcast_reduce_fusion = (f32[128,8]{0,1:T(8,128)S(1)}, f32[128,8,8192]{2,0,1:T(8,128)}) fusion(bf16[2,8192,128]{2,1,0:T(8,128)(2,1)} %all-gather.4.cloned.1.call-done, bf16[128,8,64]{2,0,1:T(8,128)(2,1)S(1)} %get-tuple-element.7, bf16[128,8,64]{2,0,1:T(8,128)(2,1)S(1)} %get-tuple-element.6), kind=kOutput, calls=%fused_computation.2 | convolution fusion | flops 2164784128 | bytes 35917824 | tf_op jit(solution)/shard_map/nkgd,rkd->nkgr/dot_general | solution.py:78
  164.4 4.0 fusion.7
  168.5 14.6 %fusion.1 = f32[128,8]{0,1:T(8,128)S(1)} fusion(f32[128,8,8192]{2,0,1:T(8,128)} %get-tuple-element.25, f32[128,8]{0,1:T(8,128)S(1)} %get-tuple-element.18), kind=kLoop, calls=%fused_computation.4 | loop fusion | flops 25164800 | bytes 33562624 | tf_op jit(solution)/shard_map/reduce_sum | solution.py:89
  183.1 15.4 %fusion.26 = f32[1,128,128,8]{2,1,3,0:T(8,128)S(1)} fusion(bf16[2,8192,128]{2,1,0:T(8,128)(2,1)} %all-gather.4.cloned.1.call-done, f32[128,8,8192]{2,0,1:T(8,128)} %get-tuple-element.25, f32[128,8]{0,1:T(8,128)S(1)} %get-tuple-element.18, f32[128,8]{0,1:T(8,128)S(1)} %get-tuple-element.5, f32[128,8]{0,1:T(8,128)S(1)} %get-tuple-element.16), kind=kOutput, calls=%fused_computation.25 | convolution fusion | flops 2172911616 | bytes 36188160 | tf_op jit(solution)/shard_map/nkgr,rkd->nkgd/dot_general | solution.py:90
  198.5 10.6 %fusion.33 = bf16[1,128,128,8]{2,1,3,0:T(8,128)(2,1)S(1)} fusion(f32[1,128,128,8]{2,1,3,0:T(8,128)S(1)} %fusion.26, f32[4096,128,8]{1,0,2:T(8,128)} %get-tuple-element.27, f32[128,8]{0,1:T(8,128)S(1)} %get-tuple-element.17, pred[128,4096]{0,1:T(8,128)(4,1)S(1)} %iota_compare_fusion, bf16[2,4096,128]{2,1,0:T(8,128)(2,1)} %all-gather.6.cloned.1.call-done, ...), kind=kOutput, calls=%fused_computation.31 | convolution fusion | flops 1095106560 | bytes 19144704 | tf_op jit(solution)/shard_map/nkgr,rkd->nkgd/dot_general | solution.py:90
  209.1 0.0 copy-start.2
  209.1 0.0 copy-start.13
  209.2 64.7 %all-gather.8.cloned.1.call-done = bf16[1024,8192]{1,0:T(8,128)(2,1)} async-done(((bf16[1024,256]{1,0:T(8,128)(2,1)}), bf16[1024,8192]{1,0:T(8,128)(2,1)}) %all-gather.8.cloned.1.call-update) | async-done | bytes 16777232 | tf_op jit(solution)/shard_map/all_gather | solution.py:151
  273.9 9.6 %convolution_convert_fusion = bf16[128,8192]{1,0:T(8,128)(2,1)} fusion(bf16[128,1024]{0,1:T(8,128)(2,1)S(1)} %bitcast.151, bf16[1024,8192]{1,0:T(8,128)(2,1)} %all-gather.8.cloned.1.call-done), kind=kOutput, calls=%fused_computation.13 | convolution fusion | flops 2148532224 | bytes 19136512 | tf_op jit(solution)/shard_map/dot_general | solution.py:149
  283.5 0.0 reduce-scatter.2.cloned.1.call-update
  283.5 76.2 %reduce-scatter.2.cloned.1.call-done = bf16[128,1024]{1,0:T(8,128)(2,1)} async-done(((bf16[128,8192]{1,0:T(8,128)(2,1)}), bf16[128,1024]{1,0:T(8,128)(2,1)}) %reduce-scatter.2.cloned.1.call-update) | async-done | bytes 262160 | tf_op jit(solution)/shard_map/reduce_scatter | solution.py:154
  359.7 1.1 fusion.36
  360.8 10.1 %all_to_all.11 = f32[8,1,128]{2,1,0:T(1,128)S(1)} all-to-all(f32[8,1,128]{2,1,0:T(1,128)S(1)} %broadcast_in_dim.158), channel_id=1, replica_groups=mesh['ctx'=32,'head'=8] {'head'}, dimensions={0} | all-to-all | bytes 8192 | tf_op jit(solution)/shard_map/all_to_all | solution.py:12
  371.0 0.1 fusion.38
  371.1 0.2 copy.47
  371.3 1.6 broadcast_in_dim.159
  372.9 3.6 all-to-all-start.1
  377.2 27.2 %all-to-all-done.1 = bf16[8,128,1024]{1,2,0:T(8,128)(2,1)S(1)} async-done(((bf16[8,128,1024]{1,2,0:T(8,128)(2,1)}), bf16[8,128,1024]{1,2,0:T(8,128)(2,1)S(1)}, u32[]{:S(2)}, u32[]{:S(2)}) %all-to-all-start.1) | async-done | bytes 2097184 | tf_op jit(solution)/shard_map/all_to_all | solution.py:12
  404.4 3.0 convolution_add_fusion
  407.4 0.1 copy.48
  407.5 0.1 copy.60
  407.7 0.4 subtract_convert_fusion.1
  408.1 0.1 copy.61
  408.2 0.1 maximum_bitcast_fusion
  408.3 0.1 copy.51
  408.4 0.1 copy.52
  408.5 0.8 gather_fusion
  409.4 0.7 select_select_fusion
  (46 shorter events, 0.2 us)
Async XLA Ops:
  7.2 72.3 %all-gather.6.cloned.1.call-start = ((), (), s32[]{:S(2)}) async-start(), calls=%async_computation.4 | async-start | bytes 2162688 | tf_op jit(solution)/shard_map/all_gather | solution.py:140
  7.2 80.5 %copy-start.7 = (pred[64]{0:T(512)(128)(4,1)}, pred[64]{0:T(512)(128)(4,1)S(1)}, u32[]{:S(2)}) copy-start(pred[64]{0:T(512)(128)(4,1)S(1)} %get-tuple-element.28) | copy-start | bytes 196
  7.2 80.5 %copy-start.9 = (pred[64]{0:T(512)(128)(4,1)}, pred[64]{0:T(512)(128)(4,1)S(1)}, u32[]{:S(2)}) copy-start(pred[64]{0:T(512)(128)(4,1)S(1)} %get-tuple-element.29) | copy-start | bytes 196
  7.3 80.4 %copy-start.11 = (f32[64]{0:T(128)}, f32[64]{0:T(128)S(1)}, u32[]{:S(2)}) copy-start(f32[64]{0:T(128)S(1)} %multiply_power_fusion) | copy-start | bytes 772
  8.0 79.8 %copy-start.3 = (f32[128]{0:T(128)}, f32[128]{0:T(128)S(1)}, u32[]{:S(2)}) copy-start(f32[128]{0:T(128)S(1)} %get-tuple-element.22) | copy-start | bytes 1540
  8.0 79.8 %copy-start.5 = (f32[128]{0:T(128)}, f32[128]{0:T(128)S(1)}, u32[]{:S(2)}) copy-start(f32[128]{0:T(128)S(1)} %get-tuple-element.23) | copy-start | bytes 1540
  9.9 138.0 %all-gather.4.cloned.1.call-start = ((), (), s32[]{:S(2)}) async-start(), calls=%async_computation.3 | async-start | bytes 4325376 | tf_op jit(solution)/shard_map/all_gather | solution.py:131
  10.6 263.3 %all-gather.8.cloned.1.call-start = ((), (), s32[]{:S(2)}) async-start(), calls=%async_computation.5 | async-start | bytes 17301504 | tf_op jit(solution)/shard_map/all_gather | solution.py:151
  11.3 348.3 %reduce-scatter.2.cloned.1.call-start = ((), (), s32[]{:S(2)}) async-start(), calls=%async_computation.6 | async-start | bytes 2359296 | tf_op jit(solution)/shard_map/reduce_scatter | solution.py:154
  147.8 16.6 %copy-start = (f32[4096,128,8]{1,0,2:T(8,128)S(1)}, f32[4096,128,8]{1,0,2:T(8,128)}, u32[]{:S(2)}) copy-start(f32[4096,128,8]{1,0,2:T(8,128)} %get-tuple-element.27) | copy-start | bytes 50331652
  209.1 150.5 %copy-start.2 = (bf16[128,1024]{1,0:T(8,128)(2,1)S(1)}, bf16[128,1024]{1,0:T(8,128)(2,1)}, u32[]{:S(2)}) copy-start(bf16[128,1024]{1,0:T(8,128)(2,1)} %param.11) | copy-start | bytes 786436
  209.1 161.8 %copy-start.13 = (f32[1024]{0:T(1024)S(1)}, f32[1024]{0:T(1024)}, u32[]{:S(2)}) copy-start(f32[1024]{0:T(1024)} %param.17) | copy-start | bytes 12292
  209.2 168.0 %copy-start.15 = (s32[128]{0:T(128)S(1)}, s32[128]{0:T(128)}, u32[]{:S(2)}) copy-start(s32[128]{0:T(128)} %param.20) | copy-start | bytes 1540
  209.2 195.2 %copy-start.14 = (f32[256]{0:T(256)S(1)}, f32[256]{0:T(256)}, u32[]{:S(2)}) copy-start(f32[256]{0:T(256)} %param.19) | copy-start | bytes 3076
  273.9 133.8 %copy-start.4 = (f32[128]{0:T(128)S(1)}, f32[128]{0:T(128)}, u32[]{:S(2)}) copy-start(f32[128]{0:T(128)} %copy-done.3) | copy-start | bytes 1540
  273.9 133.8 %copy-start.6 = (f32[128]{0:T(128)S(1)}, f32[128]{0:T(128)}, u32[]{:S(2)}) copy-start(f32[128]{0:T(128)} %copy-done.5) | copy-start | bytes 1540
  273.9 133.8 %copy-start.8 = (pred[64]{0:T(512)(128)(4,1)S(1)}, pred[64]{0:T(512)(128)(4,1)}, u32[]{:S(2)}) copy-start(pred[64]{0:T(512)(128)(4,1)} %copy-done.7) | copy-start | bytes 196
  273.9 133.8 %copy-start.10 = (pred[64]{0:T(512)(128)(4,1)S(1)}, pred[64]{0:T(512)(128)(4,1)}, u32[]{:S(2)}) copy-start(pred[64]{0:T(512)(128)(4,1)} %copy-done.9) | copy-start | bytes 196
  273.9 133.8 %copy-start.12 = (f32[64]{0:T(128)S(1)}, f32[64]{0:T(128)}, u32[]{:S(2)}) copy-start(f32[64]{0:T(128)} %copy-done.11) | copy-start | bytes 772
  360.8 49.3 %copy-start.1 = (bf16[128,1024]{1,0:T(8,128)(2,1)}, bf16[128,1024]{1,0:T(8,128)(2,1)S(1)}, u32[]{:S(2)}) copy-start(bf16[128,1024]{1,0:T(8,128)(2,1)S(1)} %get-tuple-element.3) | copy-start | bytes 786436
  372.9 31.5 %all-to-all-start.1 = ((bf16[8,128,1024]{1,2,0:T(8,128)(2,1)}), bf16[8,128,1024]{1,2,0:T(8,128)(2,1)S(1)}, u32[]{:S(2)}, u32[]{:S(2)}) async-start(bf16[8,128,1024]{1,2,0:T(8,128)(2,1)} %broadcast_in_dim.159), calls=%async_computation.2 | async-start | bytes 4194304 | tf_op jit(solution)/shard_map/all_to_all | solution.py:12
Sparse Core Ops, SparseCore 0:
  10.4 68.9 all-gather.5
  81.3 66.5 all-gather.3
  149.6 124.2 all-gather.7
  283.6 76.0 reduce-scatter.1
where the time goes:
time: 418 us; the launch traced here: 417 us
  waiting for transfers between devices  295 us (71%)
  matrix products  63.5 us (15%)
  other arithmetic  24.5 us (6%)
  between operations  14.8 us (4%)
  blocking collectives  10.1 us (2%)
  local copies, waits for them, and re-layouts  4.8 us (1%)
    reduce_scatter x1, waiting for transfers between devices, local(): lax.psum_scatter(partial_sum.astype(jnp.bfloat16), 'head', scatter_dimens...  76.2 us
    all_gather x1, waiting for transfers between devices, local(): shard_piece = lax.all_gather(recent, 'ctx', axis=1, tiled=True)  65.6 us
    all_gather x1, waiting for transfers between devices, local(): lax.all_gather(out_weight, 'ctx', axis=1, tiled=True)  64.7 us
    all_gather x1, waiting for transfers between devices, local(): shard_piece = lax.all_gather(cached_key_value, 'ctx', axis=1, tiled=True)  60.1 us
    all_to_all x1, waiting for transfers between devices, copy_for_each(): lax.all_to_all(jnp.broadcast_to(shard[None], (size, *shard.shape)), axis,...  27.2 us
    dot_general x2, matrix products, attend(): jnp.einsum('nkgr,rkd->nkgd', expos.astype(jnp.bfloat16), value_heads, pre...  26 us
    dot_general x2, matrix products, attend(): jnp.einsum('nkgd,rkd->nkgr', grouped_rows, key_heads, preferred_element_t...  24.9 us
    reduce_sum x2, other arithmetic, attend(): totals = totals * factor + jnp.sum(expos, axis=-1)  18.6 us
  transfers between devices with their start and end apart: 5, of which 5 were waited for; matrix products, arithmetic and copies ran while one was open for 17% of the time, Pallas kernels for 0%

commit v1 on v0

v1 whole, which is shorter than its diff:
```python
import functools

import jax
import jax.numpy as jnp
from jax import lax
from jax.experimental import pallas as pl
from jax.experimental.pallas import tpu as pltpu
from jax.sharding import Mesh
from jax.sharding import PartitionSpec as P

MODEL_WIDTH = 8192
HEAD = 128
ROWS = 128
CACHED = 256
GROUP = 8
Z = 8
LOG2E = 1.4426950408889634
SCALE = HEAD ** (-0.5) * LOG2E
CTX_AXES = ("z", "yl", "c")
HEAD_AXES = ("x", "yh")
VMEM = 56 * 1024 * 1024
CHUNK = 256
KEY_STEP = 1024


def params(**more):
    return pltpu.CompilerParams(vmem_limit_bytes=VMEM, **more)


def tables(positions, head_size):
    half = head_size // 2
    column = jnp.arange(half)
    frequency = jnp.power(jnp.float32(1000000.0), -(2.0 * column.astype(jnp.float32)) / head_size)
    section = (column >= head_size // 8).astype(jnp.int32) + (
        column >= head_size // 8 + 3 * head_size // 16
    ).astype(jnp.int32)
    places = positions.astype(jnp.float32)
    chosen = jnp.where(
        section[None, :] == 0,
        places[0][:, None],
        jnp.where(section[None, :] == 1, places[1][:, None], places[2][:, None]),
    )
    angles = chosen * frequency[None, :]
    cosine, sine = jnp.cos(angles), jnp.sin(angles)
    return (
        jnp.concatenate([cosine, cosine], axis=1),
        jnp.concatenate([-sine, sine], axis=1),
    )


def rotated(x, cosine, sine):
    return x * cosine + pltpu.roll(x, HEAD // 2, 1) * sine


def prepare_kernel(query, fresh, cached, cosine, sine, query_out, kv_out):
    cos, sin = cosine[...], sine[...]
    for g in range(GROUP):
        piece = query[:, g * HEAD : (g + 1) * HEAD].astype(jnp.float32)
        query_out[g] = rotated(piece, cos, sin).astype(jnp.bfloat16)
    kv_out[:, :CACHED, :] = cached[...]
    kv_out[0, CACHED:, :] = rotated(fresh[0].astype(jnp.float32), cos, sin).astype(jnp.bfloat16)
    kv_out[1, CACHED:, :] = fresh[1]


def prepare(query, fresh, cached, cosine, sine):
    return pl.pallas_call(
        prepare_kernel,
        out_shape=(
            jax.ShapeDtypeStruct((GROUP, ROWS, HEAD), jnp.bfloat16),
            jax.ShapeDtypeStruct((2, CACHED + ROWS, HEAD), jnp.bfloat16),
        ),
        compiler_params=params(),
        name="prepare",
        cost_estimate=pl.CostEstimate(flops=2_000_000, bytes_accessed=1_500_000, transcendentals=0),
    )(query, fresh, cached, cosine, sine)


def column_of(row):
    return jnp.transpose(jnp.broadcast_to(row, (ROWS, ROWS)))


def row_of(column):
    return jnp.transpose(column)[0:1, :]


def attend_kernel(place, query, *refs):
    kv = refs[:Z]
    out, lse_out, keys, values, key_token = refs[Z:]
    step = pl.program_id(0)
    z, yl, c, rc = place[0], place[1], place[2], place[3]

    @pl.when(step == 0)
    def _():
        lane = lax.broadcasted_iota(jnp.int32, (8, ROWS), 1)
        for d in range(Z):
            block = kv[d]
            keys[:, d * CACHED : (d + 1) * CACHED] = jnp.transpose(block[0, :CACHED, :])
            at = Z * CACHED + d * ROWS
            keys[:, at : at + ROWS] = jnp.transpose(block[0, CACHED:, :])
            values[d * CACHED : (d + 1) * CACHED, :HEAD] = block[1, :CACHED, :]
            values[at : at + ROWS, :HEAD] = block[1, CACHED:, :]
            source = lax.rem(z - d + Z, Z)
            key_token[:, d * ROWS : (d + 1) * ROWS] = (
                source * 4 + yl * 2 + c
            ) * ROWS + lane
        values[:, HEAD:] = jnp.ones((Z * (CACHED + ROWS), HEAD), jnp.bfloat16)

    per_block = GROUP * ROWS // CHUNK
    ryl = step // per_block
    block = z * 4 + (yl ^ ryl) * 2 + (c ^ rc)
    inside = lax.broadcasted_iota(jnp.int32, (CHUNK, 1), 0) & (ROWS - 1)
    query_token = block * ROWS + inside
    q = query[...]
    m = jnp.full((CHUNK, 1), -1e30, jnp.float32)
    acc = jnp.zeros((CHUNK, 2 * HEAD), jnp.float32)
    for at in range(0, Z * (CACHED + ROWS), KEY_STEP):
        scores = jnp.dot(q, keys[:, at : at + KEY_STEP], preferred_element_type=jnp.float32)
        if at >= Z * CACHED:
            first = at - Z * CACHED
            visible = key_token[0:1, first : first + KEY_STEP] <= query_token
            scores = jnp.where(visible, scores, -1e30)
        raised = jnp.maximum(m, jnp.max(scores, axis=1, keepdims=True))
        weights = jnp.exp2((scores - raised) * SCALE).astype(jnp.bfloat16)
        factor = jnp.exp2((m - raised) * SCALE)
        acc = acc * factor + jnp.dot(
            weights, values[at : at + KEY_STEP, :], preferred_element_type=jnp.float32
        )
        m = raised
    totals = acc[:, HEAD:]
    out[...] = (acc[:, :HEAD] / totals).astype(jnp.bfloat16)
    lse = m * SCALE + jnp.log2(totals)
    for k in range(CHUNK // ROWS):
        lse_out[step * (CHUNK // ROWS) + k] = row_of(lse[k * ROWS : (k + 1) * ROWS, :])


def attend(place, query, kv):
    rows = query.shape[0]
    total = Z * (CACHED + ROWS)
    whole = pl.BlockSpec((2, CACHED + ROWS, HEAD), lambda i, s: (0, 0, 0))
    return pl.pallas_call(
        attend_kernel,
        grid_spec=pltpu.PrefetchScalarGridSpec(
            num_scalar_prefetch=1,
            grid=(rows // CHUNK,),
            in_specs=[pl.BlockSpec((CHUNK, HEAD), lambda i, s: (i, 0))] + [whole] * Z,
            out_specs=[
                pl.BlockSpec((CHUNK, HEAD), lambda i, s: (i, 0)),
                pl.BlockSpec((rows // ROWS, 1, ROWS), lambda i, s: (0, 0, 0)),
            ],
            scratch_shapes=[
                pltpu.VMEM((HEAD, total), jnp.bfloat16),
                pltpu.VMEM((total, 2 * HEAD), jnp.bfloat16),
                pltpu.VMEM((8, Z * ROWS), jnp.int32),
            ],
        ),
        out_shape=(
            jax.ShapeDtypeStruct((rows, HEAD), jnp.bfloat16),
            jax.ShapeDtypeStruct((rows // ROWS, 1, ROWS), jnp.float32),
        ),
        compiler_params=params(),
        name="attend",
        cost_estimate=pl.CostEstimate(
            flops=4 * rows * total * HEAD,
            bytes_accessed=4 * rows * HEAD + 4 * total * HEAD,
            transcendentals=rows * total,
        ),
    )(place, query, *kv)


def merged(first, second, first_lse, second_lse):
    a, b = column_of(first_lse), column_of(second_lse)
    top = jnp.maximum(a, b)
    wa, wb = jnp.exp2(a - top), jnp.exp2(b - top)
    total = wa + wb
    value = (first.astype(jnp.float32) * wa + second.astype(jnp.float32) * wb) / total
    return value.astype(jnp.bfloat16), top + jnp.log2(total)


def merge_kernel(own, own_lse, other, other_lse, out, lse_out):
    for k in range(own.shape[0] // ROWS):
        at = slice(k * ROWS, (k + 1) * ROWS)
        value, lse = merged(own[at, :], other[at, :], own_lse[k], other_lse[k])
        out[at, :] = value
        lse_out[k] = row_of(lse)


def merge_last_kernel(own, own_lse, other, other_lse, out):
    for y in range(2):
        for g in range(GROUP):
            k, j = y * GROUP + g, (1 - y) * GROUP + g
            value, _ = merged(
                own[k * ROWS : (k + 1) * ROWS, :],
                other[j * ROWS : (j + 1) * ROWS, :],
                own_lse[k],
                other_lse[j],
            )
            out[y, :, g * HEAD : (g + 1) * HEAD] = value


def merge(own, own_lse, other, other_lse):
    return pl.pallas_call(
        merge_kernel,
        out_shape=(
            jax.ShapeDtypeStruct(own.shape, own.dtype),
            jax.ShapeDtypeStruct(own_lse.shape, own_lse.dtype),
        ),
        compiler_params=params(),
        name="merge",
    )(own, own_lse, other, other_lse)


def merge_last(own, own_lse, other, other_lse):
    return pl.pallas_call(
        merge_last_kernel,
        out_shape=jax.ShapeDtypeStruct((2, ROWS, GROUP * HEAD), jnp.bfloat16),
        compiler_params=params(),
        name="merge_last",
    )(own, own_lse, other, other_lse)


def project_kernel(place, near, far, weight, out):
    yl, c = place[1], place[2]
    for rc, rows in ((0, near), (1, far)):
        for ryl in range(2):
            q = (yl ^ ryl) * 2 + (c ^ rc)
            out[q, 0] = jnp.dot(
                rows[ryl], weight[0], preferred_element_type=jnp.float32
            ).astype(jnp.bfloat16)


def project(place, near, far, weight):
    width = GROUP * HEAD
    columns = weight.shape[2]
    return pl.pallas_call(
        project_kernel,
        grid_spec=pltpu.PrefetchScalarGridSpec(
            num_scalar_prefetch=1,
            grid=(Z,),
            in_specs=[
                pl.BlockSpec((2, ROWS, width), lambda i, s: (0, 0, 0)),
                pl.BlockSpec((2, ROWS, width), lambda i, s: (0, 0, 0)),
                pl.BlockSpec((1, width, columns), lambda i, s: (i, 0, 0)),
            ],
            out_specs=pl.BlockSpec((4, 1, ROWS, columns), lambda i, s: (0, i, 0, 0)),
        ),
        out_shape=jax.ShapeDtypeStruct((4, Z, ROWS, columns), jnp.bfloat16),
        compiler_params=params(),
        name="project",
    )(place, near, far, weight)


PAD = 16


def third_kernel(place, received, hidden, gain, near, far, out, partial, scaled):
    c = place[2]
    columns = received.shape[3]
    squares = jnp.zeros((ROWS, 1), jnp.float32)
    for q in range(4):
        at = slice(q * columns, (q + 1) * columns)
        total = received[q, 0].astype(jnp.float32)
        for h in range(1, Z):
            total = total + received[q, h].astype(jnp.float32)
        result = (hidden[:, at].astype(jnp.float32) + total).astype(jnp.bfloat16)
        out[:, at] = result
        wide = result.astype(jnp.float32)
        squares = squares + jnp.sum(wide * wide, axis=1, keepdims=True)
        scaled[q // 2, :, (q % 2) * columns : (q % 2 + 1) * columns] = (
            wide * gain[:, at]
        ).astype(jnp.bfloat16)
    row = row_of(jnp.broadcast_to(squares, (ROWS, ROWS)))
    high = row.astype(jnp.bfloat16)
    low = (row - high.astype(jnp.float32)).astype(jnp.bfloat16)
    tail = jnp.broadcast_to(
        jnp.concatenate([high, low], axis=1).astype(jnp.float32), (PAD, 2 * ROWS)
    ).astype(jnp.bfloat16)
    near_rows, far_rows = scaled[c], scaled[1 - c]
    for h in range(Z):
        product = jnp.dot(near_rows, near[h], preferred_element_type=jnp.float32) + jnp.dot(
            far_rows, far[h], preferred_element_type=jnp.float32
        )
        partial[h, :ROWS, :] = product.astype(jnp.bfloat16)
        partial[h, ROWS:, :] = tail


def third_partials(place, received, hidden, gain, near, far):
    vmem = pl.BlockSpec(memory_space=pltpu.VMEM)
    width = hidden.shape[1]
    return pl.pallas_call(
        third_kernel,
        in_specs=[pl.BlockSpec(memory_space=pltpu.SMEM)] + [vmem] * 5,
        out_specs=(vmem, vmem),
        out_shape=(
            jax.ShapeDtypeStruct(hidden.shape, jnp.bfloat16),
            jax.ShapeDtypeStruct((Z, ROWS + PAD, 2 * HEAD), jnp.bfloat16),
        ),
        scratch_shapes=[pltpu.VMEM((2, ROWS, width // 2), jnp.bfloat16)],
        compiler_params=params(),
        name="third",
    )(place, received, hidden, gain, near, far)


def final_kernel(count, partial, bias, cosine, sine, index, out):
    total = partial[0, :ROWS, :].astype(jnp.float32)
    tail = partial[0, ROWS:, :].astype(jnp.float32)
    for h in range(1, Z):
        total = total + partial[h, :ROWS, :].astype(jnp.float32)
        tail = tail + partial[h, ROWS:, :].astype(jnp.float32)
    squares = tail[0:1, :ROWS] + tail[0:1, ROWS:]
    factor = lax.rsqrt(column_of(squares) / MODEL_WIDTH + 1e-06)
    keys = total[:, :HEAD] * factor + bias[:, :HEAD]
    values = total[:, HEAD:] * factor + bias[:, HEAD:]
    keys = rotated(keys, cosine[...], sine[...])
    rows = jnp.concatenate([keys, values], axis=1).astype(jnp.bfloat16)
    slot = lax.broadcasted_iota(jnp.int32, (ROWS, ROWS), 1)
    token = lax.broadcasted_iota(jnp.int32, (ROWS, ROWS), 0)
    chosen = (token == index[...]) & (slot < count[0])
    pick = jnp.where(chosen, 1.0, 0.0).astype(jnp.bfloat16)
    out[...] = lax.dot_general(
        pick, rows, (((0,), (0,)), ((), ())), preferred_element_type=jnp.float32
    ).astype(jnp.bfloat16)


def final(count, partial, bias, cosine, sine, index):
    vmem = pl.BlockSpec(memory_space=pltpu.VMEM)
    return pl.pallas_call(
        final_kernel,
        in_specs=[pl.BlockSpec(memory_space=pltpu.SMEM)] + [vmem] * 5,
        out_specs=vmem,
        out_shape=jax.ShapeDtypeStruct((ROWS, 2 * HEAD), jnp.bfloat16),
        compiler_params=params(),
        name="final",
    )(count, partial, bias, cosine, sine, index)


def swap(x, axis):
    return lax.ppermute(x, axis, [(0, 1), (1, 0)])


def along_z(x, distance):
    return lax.ppermute(x, "z", [(i, (i + distance) % Z) for i in range(Z)])


def local(
    hidden,
    query,
    fresh_key_value,
    cached_key_value,
    positions,
    out_weight,
    norm_gain,
    layer3_key_value_weight,
    layer3_key_value_bias,
    keep_index,
    keep_count,
):
    z, yl, c = lax.axis_index("z"), lax.axis_index("yl"), lax.axis_index("c")
    place = jnp.stack([z, yl, c, jnp.zeros_like(c)]).astype(jnp.int32)
    far_place = jnp.stack([z, yl, c, jnp.ones_like(c)]).astype(jnp.int32)

    cosine, sine = tables(positions, HEAD)
    rotated_query, kv = prepare(query, fresh_key_value, cached_key_value, cosine, sine)
    pieces = [kv] + [along_z(kv, d) for d in range(1, Z)]
    rotated_query = rotated_query.reshape(GROUP * ROWS, HEAD)
    near_query = jnp.concatenate([rotated_query, swap(rotated_query, "yl")], axis=0)
    far_query = swap(near_query, "c")
    weight = lax.all_gather(out_weight, "z")

    third_rows = layer3_key_value_weight.reshape(Z, 2, MODEL_WIDTH // Z // 2, 2 * HEAD)
    third_rows = lax.dynamic_index_in_dim(third_rows, c, axis=1, keepdims=False)
    third_near = lax.all_to_all(third_rows, HEAD_AXES, 0, 0, tiled=True)
    third_far = swap(third_near, "c")

    send, send_lse = attend(far_place, far_query, pieces)
    got, got_lse = swap(send, "c"), swap(send_lse, "c")
    own, own_lse = attend(place, near_query, pieces)
    own, own_lse = merge(own, own_lse, got, got_lse)
    got, got_lse = swap(own, "yl"), swap(own_lse, "yl")
    near = merge_last(own, own_lse, got, got_lse)
    far = swap(near, "c")

    products = project(place, near, far, weight)
    products = products.reshape(4 * Z, *products.shape[2:])
    received = lax.all_to_all(products, ("yl", "c", "x", "yh"), 0, 0, tiled=True)
    received = received.reshape(4, Z, *received.shape[1:])

    layer2_out, partial = third_partials(
        place, received, hidden, norm_gain.reshape(1, -1), third_near, third_far
    )
    partial = lax.all_to_all(partial, HEAD_AXES, 0, 0, tiled=True)
    packed = final(
        keep_count,
        partial,
        layer3_key_value_bias.reshape(1, -1),
        cosine,
        sine,
        keep_index.reshape(1, -1),
    )
    return (layer2_out, packed)


def solution(mesh):
    split = Mesh(mesh.devices.reshape(Z, 2, 2, 4, 2), CTX_AXES + HEAD_AXES)
    placed = (
        P(CTX_AXES, HEAD_AXES),
        P(CTX_AXES, HEAD_AXES),
        P(None, CTX_AXES, HEAD_AXES),
        P(None, CTX_AXES, HEAD_AXES),
        P(None, CTX_AXES),
        P(HEAD_AXES, CTX_AXES),
        P(HEAD_AXES),
        P(None, HEAD_AXES),
        P(HEAD_AXES),
        P(CTX_AXES),
        P(CTX_AXES),
    )
    return jax.shard_map(
        local,
        mesh=split,
        in_specs=placed,
        out_specs=(P(CTX_AXES, HEAD_AXES), P(CTX_AXES, HEAD_AXES)),
        check_vma=False,
    )
```

time: 418 us -> 221 us (0.53)
  waiting for transfers between devices: 295 us -> 97.9 us
  matrix products: 63.5 us -> 0 us
  Pallas kernels: 0 us -> 56.7 us
  starting transfers between devices: 3.76 us -> 39.5 us
  other arithmetic: 24.5 us -> 4.03 us
  blocking collectives: 10.1 us -> 0 us
    all_gather x3 -> x1, waiting for transfers between devices: 190 us -> 0.01 us  [local(): weight = lax.all_gather(out_weight, 'z')]
    reduce_scatter x1 -> x0, waiting for transfers between devices: 76.2 us -> none  [local(): lax.psum_scatter(partial_sum.astype(jnp.bfloat16), 'head', scatter_dimens...]
    dot_general x6 -> x0, matrix products: 63.5 us -> none  [the longest x2 26 us: attend(): jnp.einsum('nkgr,rkd->nkgd', expos.astype(jnp.bfloat16), value_heads, pre...]
    ppermute x0 -> x15, waiting for transfers between devices: none -> 57.1 us  [the longest x7 38.4 us: along_z(): return lax.ppermute(x, 'z', [(i, (i + distance) % Z) for i in range(Z)])]
    pallas_call x0 -> x8, Pallas kernels: none -> 56.7 us  [the longest x2 32.6 us: attend(): pl.pallas_call(attend_kernel, grid_spec=pltpu.PrefetchScalarGridSpec(num_...]
    ppermute x0 -> x15, starting transfers between devices: none -> 21.4 us  [the longest x7 11.4 us: along_z(): return lax.ppermute(x, 'z', [(i, (i + distance) % Z) for i in range(Z)])]
    reduce_sum x4 -> x0, other arithmetic: 19.8 us -> none  [the longest x2 18.6 us: attend(): totals = totals * factor + jnp.sum(expos, axis=-1)]
    all_to_all x1 -> x3, starting transfers between devices: 3.6 us -> 18 us  [the longest x1 7.66 us: local(): lax.all_to_all(products, ('yl', 'c', 'x', 'yh'), 0, 0, tiled=True)]
  transfers between devices with their start and end apart: 5 -> 19, of which waited for: 5 -> 10; matrix products, arithmetic and copies ran while one was open for 17% -> 3% of each run, Pallas kernels for 0% -> 23%
where the time goes in v1:
time: 221 us
  waiting for transfers between devices  97.9 us (44%)
  Pallas kernels  56.7 us (26%)
  starting transfers between devices  39.5 us (18%)
  between operations  14.8 us (7%)
  local copies, waits for them, and re-layouts  7.87 us (4%)
  other arithmetic  4.03 us (2%)
    ppermute x7, waiting for transfers between devices, along_z(): return lax.ppermute(x, 'z', [(i, (i + distance) % Z) for i in range(Z)])  38.4 us
    pallas_call x2, Pallas kernels, attend(): pl.pallas_call(attend_kernel, grid_spec=pltpu.PrefetchScalarGridSpec(num_...  32.6 us
    all_to_all x1, waiting for transfers between devices, local(): lax.all_to_all(products, ('yl', 'c', 'x', 'yh'), 0, 0, tiled=True)  29.8 us
    ppermute x8, waiting for transfers between devices, swap(): return lax.ppermute(x, axis, [(0, 1), (1, 0)])  18.7 us
    ppermute x7, starting transfers between devices, along_z(): return lax.ppermute(x, 'z', [(i, (i + distance) % Z) for i in range(Z)])  11.4 us
    all_to_all x1, waiting for transfers between devices, local(): partial = lax.all_to_all(partial, HEAD_AXES, 0, 0, tiled=True)  10.3 us
    ppermute x8, starting transfers between devices, swap(): return lax.ppermute(x, axis, [(0, 1), (1, 0)])  9.96 us
    pallas_call x1, Pallas kernels, project(): pl.pallas_call(project_kernel, grid_spec=pltpu.PrefetchScalarGridSpec(num...  8.77 us
  transfers between devices with their start and end apart: 19, of which 10 were waited for; matrix products, arithmetic and copies ran while one was open for 3% of the time, Pallas kernels for 23%

profile of v1, /device:TPU:1, one launch (start us, length us, event | category | flops | bytes accessed | tf_op | source)
XLA Modules:
  0.0 220.7 jit_solution(7782313216549245025)
XLA Ops:
  7.2 0.7 all-gather.3.cloned.1.call-update
  7.9 0.7 convert_element_type.36
  8.6 0.3 fusion.2
  9.0 0.8 pad_maximum_fusion.1
  9.7 2.0 prepare.1
  11.7 2.1 collective-permute-start
  13.9 5.1 %collective-permute-done = bf16[1024,128]{1,0:T(8,128)(2,1)S(1)} collective-permute-done((bf16[1024,128]{1,0:T(8,128)(2,1)}, bf16[1024,128]{1,0:T(8,128)(2,1)S(1)}, u32[]{:S(2)}, u32[]{:S(2)}) %collective-permute-start) | collective-permute-done | bytes 262176 | tf_op jit(solution)/shard_map/ppermute | solution.py:337
  19.0 1.0 pad_maximum_fusion.query
  20.0 2.7 %collective-permute-start.8 = (bf16[2048,128]{1,0:T(8,128)(2,1)S(1)}, bf16[2048,128]{1,0:T(8,128)(2,1)S(1)}, u32[]{:S(2)}, u32[]{:S(2)}) collective-permute-start(bf16[2048,128]{1,0:T(8,128)(2,1)S(1)} %pad_maximum_fusion.query), channel_id=1, source_target_pairs={{0,8},{8,0},{1,9},{9,1},{2,10},{10,2},{3,11},{11,3},{4,12},{12,4},... | collective-permute-start | bytes 1572872 | tf_op jit(solution)/shard_map/ppermute | solution.py:337
  22.6 1.6 collective-permute-start.1
  24.2 3.0 %collective-permute-start.2 = (bf16[2,384,128]{2,1,0:T(8,128)(2,1)}, bf16[2,384,128]{2,1,0:T(8,128)(2,1)S(1)}, u32[]{:S(2)}, u32[]{:S(2)}) collective-permute-start(bf16[2,384,128]{2,1,0:T(8,128)(2,1)} %get-tuple-element.13.refs_0_), channel_id=1, source_target_pairs={{0,64},{32,96},{64,128},{96,160},{128,192},{160,224},{192,0},{224,... | collective-permute-start | bytes 589832 | tf_op jit(solution)/shard_map/ppermute | solution.py:341
  27.2 3.8 %collective-permute-start.3 = (bf16[2,384,128]{2,1,0:T(8,128)(2,1)}, bf16[2,384,128]{2,1,0:T(8,128)(2,1)S(1)}, u32[]{:S(2)}, u32[]{:S(2)}) collective-permute-start(bf16[2,384,128]{2,1,0:T(8,128)(2,1)} %get-tuple-element.13.refs_0_), channel_id=1, source_target_pairs={{0,96},{32,128},{64,160},{96,192},{128,224},{160,0},{192,32},{224,... | collective-permute-start | bytes 589832 | tf_op jit(solution)/shard_map/ppermute | solution.py:341
  31.0 0.5 collective-permute-start.4
  31.4 6.3 %collective-permute-done.1.refs_1_ = bf16[2,384,128]{2,1,0:T(8,128)(2,1)S(1)} collective-permute-done((bf16[2,384,128]{2,1,0:T(8,128)(2,1)}, bf16[2,384,128]{2,1,0:T(8,128)(2,1)S(1)}, u32[]{:S(2)}, u32[]{:S(2)}) %collective-permute-start.1) | collective-permute-done | bytes 196640 | tf_op jit(solution)/shard_map/ppermute | solution.py:341
  37.7 2.4 %collective-permute-start.5 = (bf16[2,384,128]{2,1,0:T(8,128)(2,1)}, bf16[2,384,128]{2,1,0:T(8,128)(2,1)}, u32[]{:S(2)}, u32[]{:S(2)}) collective-permute-start(bf16[2,384,128]{2,1,0:T(8,128)(2,1)} %get-tuple-element.13.refs_0_), channel_id=1, source_target_pairs={{0,160},{32,192},{64,224},{96,0},{128,32},{160,64},{192,96},{224,1... | collective-permute-start | bytes 589832 | tf_op jit(solution)/shard_map/ppermute | solution.py:341
  40.1 10.7 %collective-permute-done.2.refs_2_ = bf16[2,384,128]{2,1,0:T(8,128)(2,1)S(1)} collective-permute-done((bf16[2,384,128]{2,1,0:T(8,128)(2,1)}, bf16[2,384,128]{2,1,0:T(8,128)(2,1)S(1)}, u32[]{:S(2)}, u32[]{:S(2)}) %collective-permute-start.2) | collective-permute-done | bytes 196640 | tf_op jit(solution)/shard_map/ppermute | solution.py:341
  50.8 0.2 collective-permute-start.6
  51.0 16.3 %collective-permute-done.3.refs_3_ = bf16[2,384,128]{2,1,0:T(8,128)(2,1)S(1)} collective-permute-done((bf16[2,384,128]{2,1,0:T(8,128)(2,1)}, bf16[2,384,128]{2,1,0:T(8,128)(2,1)S(1)}, u32[]{:S(2)}, u32[]{:S(2)}) %collective-permute-start.3) | collective-permute-done | bytes 196640 | tf_op jit(solution)/shard_map/ppermute | solution.py:341
  67.4 3.2 %dynamic-slice_bitcast_fusion = bf16[8,512,256]{2,1,0:T(8,128)(2,1)} fusion(bf16[8,2,512,256]{3,2,1,0:T(8,128)(2,1)} %bitcast.23, s32[]{:T(128)S(6)} %select_n.14), kind=kLoop, calls=%fused_computation | loop fusion | bytes 4194308 | tf_op jit(solution)/shard_map/jit(dynamic_index_in_dim)/squeeze | solution.py:370
  70.6 6.8 %all-to-all-start.1 = ((bf16[8,512,256]{2,1,0:T(8,128)(2,1)}), bf16[8,512,256]{2,1,0:T(8,128)(2,1)S(1)}, u32[]{:S(2)}, u32[]{:S(2)}) async-start(bf16[8,512,256]{2,1,0:T(8,128)(2,1)} %dynamic-slice_bitcast_fusion), calls=%async_computation.1 | async-start | bytes 4194304 | tf_op jit(solution)/shard_map/all_to_all | solution.py:371
  77.4 0.7 pad_add_fusion.2
  78.1 3.7 %collective-permute-done.4.refs_4_ = bf16[2,384,128]{2,1,0:T(8,128)(2,1)} collective-permute-done((bf16[2,384,128]{2,1,0:T(8,128)(2,1)}, bf16[2,384,128]{2,1,0:T(8,128)(2,1)}, u32[]{:S(2)}, u32[]{:S(2)}) %collective-permute-start.4) | collective-permute-done | bytes 196640 | tf_op jit(solution)/shard_map/ppermute | solution.py:341
  81.8 1.5 collective-permute-done.7.refs_7_
  83.2 0.8 copy-done.8
  84.0 16.3 %attend.3 = (bf16[2048,128]{1,0:T(8,128)(2,1)}, f32[16,1,128]{2,1,0:T(1,128)}) custom-call(s32[4]{0:T(128)} %get-tuple-element.22.place, bf16[2048,128]{1,0:T(8,128)(2,1)} %copy-done.8, bf16[2,384,128]{2,1,0:T(8,128)(2,1)} %get-tuple-element.13.refs_0_, bf16[2,384,128]{2,1,0:T(8,128)(2,1)} %copy-done.9, bf16[2,384,128]{2,1,0:T(8,128)(2,1)} %copy-done.10, ...), custom_call_target="tpu_custom_call" | custom-call | flops 3221225472 | bytes 2621440 | tf_op jit(solution)/shard_map/attend/pallas_call | solution.py:140
  100.3 2.2 %collective-permute-start.9 = (bf16[2048,128]{1,0:T(8,128)(2,1)}, bf16[2048,128]{1,0:T(8,128)(2,1)S(1)}, u32[]{:S(2)}, u32[]{:S(2)}) collective-permute-start(bf16[2048,128]{1,0:T(8,128)(2,1)} %get-tuple-element.16), channel_id=1, source_target_pairs={{0,8},{8,0},{1,9},{9,1},{2,10},{10,2},{3,11},{11,3},{4,12},{12,4},... | collective-permute-start | bytes 1572872 | tf_op jit(solution)/shard_map/ppermute | solution.py:337
  102.5 0.6 pad_add_fusion.place
  103.1 16.3 %attend.2 = (bf16[2048,128]{1,0:T(8,128)(2,1)}, f32[16,1,128]{2,1,0:T(1,128)}) custom-call(s32[4]{0:T(128)} %pad_add_fusion.place, bf16[2048,128]{1,0:T(8,128)(2,1)} %copy-done.3, bf16[2,384,128]{2,1,0:T(8,128)(2,1)} %get-tuple-element.13.refs_0_, bf16[2,384,128]{2,1,0:T(8,128)(2,1)} %copy-done.9, bf16[2,384,128]{2,1,0:T(8,128)(2,1)} %copy-done.10, ...), custom_call_target="tpu_custom_call" | custom-call | flops 3221225472 | bytes 2621440 | tf_op jit(solution)/shard_map/attend/pallas_call | solution.py:140
  119.4 0.6 copy-done.6
  120.0 0.3 copy-done.4
  120.3 3.7 %merge.1 = (bf16[2048,128]{1,0:T(8,128)(2,1)}, f32[16,1,128]{2,1,0:T(1,128)}) custom-call(bf16[2048,128]{1,0:T(8,128)(2,1)} %get-tuple-element.14.own, f32[16,1,128]{2,1,0:T(1,128)} %get-tuple-element.15.own_lse, bf16[2048,128]{1,0:T(8,128)(2,1)} %copy-done.4, f32[16,1,128]{2,1,0:T(1,128)} %copy-done.6), custom_call_target="tpu_custom_call" | custom-call | tf_op jit(solution)/shard_map/merge/pallas_call | solution.py:201
  124.0 1.5 collective-permute-start.11
  125.5 11.9 %collective-permute-done.12.other_lse = f32[16,1,128]{2,1,0:T(1,128)S(1)} collective-permute-done((f32[16,1,128]{2,1,0:T(1,128)}, f32[16,1,128]{2,1,0:T(1,128)S(1)}, u32[]{:S(2)}, u32[]{:S(2)}) %collective-permute-start.12) | collective-permute-done | bytes 8224 | tf_op jit(solution)/shard_map/ppermute | solution.py:337
  137.4 0.6 copy-done.7
  138.0 0.8 copy-done.2
  138.8 2.6 %merge_last.1.near = bf16[2,128,1024]{2,1,0:T(8,128)(2,1)} custom-call(bf16[2048,128]{1,0:T(8,128)(2,1)} %get-tuple-element.18.own, f32[16,1,128]{2,1,0:T(1,128)} %get-tuple-element.19.own_lse, bf16[2048,128]{1,0:T(8,128)(2,1)} %copy-done.2, f32[16,1,128]{2,1,0:T(1,128)} %copy-done.7), custom_call_target="tpu_custom_call" | custom-call | tf_op jit(solution)/shard_map/merge_last/pallas_call | solution.py:213
  141.4 1.3 collective-permute-start.13
  142.8 0.1 collective-permute-start.14
  142.9 1.6 collective-permute-done.13.far
  144.5 0.8 copy-done.5
  145.3 8.8 %project.1 = bf16[4,8,128,256]{3,2,1,0:T(8,128)(2,1)} custom-call(s32[4]{0:T(128)} %pad_add_fusion.place, bf16[2,128,1024]{2,1,0:T(8,128)(2,1)} %merge_last.1.near, bf16[2,128,1024]{2,1,0:T(8,128)(2,1)} %copy-done.5, bf16[8,1024,256]{2,1,0:T(8,128)(2,1)} %bitcast.22), custom_call_target="tpu_custom_call" | custom-call | tf_op jit(solution)/shard_map/project/pallas_call | solution.py:234
  154.1 7.7 %all-to-all-start = ((bf16[32,128,256]{2,1,0:T(8,128)(2,1)}), bf16[32,128,256]{2,1,0:T(8,128)(2,1)}, u32[]{:S(2)}, u32[]{:S(2)}) async-start(bf16[32,128,256]{2,1,0:T(8,128)(2,1)} %bitcast.21), calls=%async_computation | async-start | bytes 4194304 | tf_op jit(solution)/shard_map/all_to_all | solution.py:384
  161.8 29.8 %all-to-all-done = bf16[32,128,256]{2,1,0:T(8,128)(2,1)} async-done(((bf16[32,128,256]{2,1,0:T(8,128)(2,1)}), bf16[32,128,256]{2,1,0:T(8,128)(2,1)}, u32[]{:S(2)}, u32[]{:S(2)}) %all-to-all-start) | async-done | bytes 2097184 | tf_op jit(solution)/shard_map/all_to_all | solution.py:384
  191.5 4.9 %third.1 = (bf16[128,1024]{1,0:T(8,128)(2,1)}, bf16[8,144,256]{2,1,0:T(8,128)(2,1)}) custom-call(s32[4]{0:T(128)} %pad_add_fusion.place, bf16[4,8,128,256]{3,2,1,0:T(8,128)(2,1)} %bitcast.9.received, bf16[128,1024]{1,0:T(8,128)(2,1)} %hidden.1, f32[1,1024]{1,0:T(1,128)} %bitcast.26, bf16[8,512,256]{2,1,0:T(8,128)(2,1)} %copy-done, ...), custom_call_target="tpu_custom_call" | custom-call | tf_op jit(solution)/shard_map/third/pallas_call | solution.py:289
  196.5 3.5 %all-to-all-start.2 = ((bf16[8,144,256]{2,1,0:T(8,128)(2,1)}), bf16[8,144,256]{2,1,0:T(8,128)(2,1)S(1)}, u32[]{:S(2)}, u32[]{:S(2)}) async-start(bf16[8,144,256]{2,1,0:T(8,128)(2,1)} %get-tuple-element.21), calls=%async_computation.2 | async-start | bytes 1179648 | tf_op jit(solution)/shard_map/all_to_all | solution.py:390
  200.7 10.3 %all-to-all-done.2.partial = bf16[8,144,256]{2,1,0:T(8,128)(2,1)S(1)} async-done(((bf16[8,144,256]{2,1,0:T(8,128)(2,1)}), bf16[8,144,256]{2,1,0:T(8,128)(2,1)S(1)}, u32[]{:S(2)}, u32[]{:S(2)}) %all-to-all-start.2) | async-done | bytes 589856 | tf_op jit(solution)/shard_map/all_to_all | solution.py:390
  211.0 0.8 copy-done.1
  211.8 2.1 final.1
  (34 shorter events, 0.2 us)
Async XLA Ops:
  7.2 137.4 %all-gather.3.cloned.1.call-start = ((), (), s32[]{:S(2)}) async-start(), calls=%async_computation.3 | async-start | bytes 4718592 | tf_op jit(solution)/shard_map/all_gather | solution.py:367
  11.7 7.2 %collective-permute-start = (bf16[1024,128]{1,0:T(8,128)(2,1)}, bf16[1024,128]{1,0:T(8,128)(2,1)S(1)}, u32[]{:S(2)}, u32[]{:S(2)}) collective-permute-start(bf16[1024,128]{1,0:T(8,128)(2,1)} %bitcast.24), channel_id=1, source_target_pairs={{0,16},{16,0},{1,17},{17,1},{2,18},{18,2},{3,19},{19,3},{4,20},{20... | collective-permute-start | bytes 786440 | tf_op jit(solution)/shard_map/ppermute | solution.py:337
  19.9 50.6 %copy-start.3 = (bf16[2048,128]{1,0:T(8,128)(2,1)}, bf16[2048,128]{1,0:T(8,128)(2,1)S(1)}, u32[]{:S(2)}) copy-start(bf16[2048,128]{1,0:T(8,128)(2,1)S(1)} %pad_maximum_fusion.query) | copy-start | bytes 1572868
  20.0 63.3 %collective-permute-start.8 = (bf16[2048,128]{1,0:T(8,128)(2,1)S(1)}, bf16[2048,128]{1,0:T(8,128)(2,1)S(1)}, u32[]{:S(2)}, u32[]{:S(2)}) collective-permute-start(bf16[2048,128]{1,0:T(8,128)(2,1)S(1)} %pad_maximum_fusion.query), channel_id=1, source_target_pairs={{0,8},{8,0},{1,9},{9,1},{2,10},{10,2},{3,11},{11,3},{4,12},{12,4},... | collective-permute-start | bytes 1572872 | tf_op jit(solution)/shard_map/ppermute | solution.py:337
  22.6 15.1 %collective-permute-start.1 = (bf16[2,384,128]{2,1,0:T(8,128)(2,1)}, bf16[2,384,128]{2,1,0:T(8,128)(2,1)S(1)}, u32[]{:S(2)}, u32[]{:S(2)}) collective-permute-start(bf16[2,384,128]{2,1,0:T(8,128)(2,1)} %get-tuple-element.13.refs_0_), channel_id=1, source_target_pairs={{0,32},{32,64},{64,96},{96,128},{128,160},{160,192},{192,224},{224... | collective-permute-start | bytes 589832 | tf_op jit(solution)/shard_map/ppermute | solution.py:341
  24.2 26.5 %collective-permute-start.2 = (bf16[2,384,128]{2,1,0:T(8,128)(2,1)}, bf16[2,384,128]{2,1,0:T(8,128)(2,1)S(1)}, u32[]{:S(2)}, u32[]{:S(2)}) collective-permute-start(bf16[2,384,128]{2,1,0:T(8,128)(2,1)} %get-tuple-element.13.refs_0_), channel_id=1, source_target_pairs={{0,64},{32,96},{64,128},{96,160},{128,192},{160,224},{192,0},{224,... | collective-permute-start | bytes 589832 | tf_op jit(solution)/shard_map/ppermute | solution.py:341
  27.2 40.1 %collective-permute-start.3 = (bf16[2,384,128]{2,1,0:T(8,128)(2,1)}, bf16[2,384,128]{2,1,0:T(8,128)(2,1)S(1)}, u32[]{:S(2)}, u32[]{:S(2)}) collective-permute-start(bf16[2,384,128]{2,1,0:T(8,128)(2,1)} %get-tuple-element.13.refs_0_), channel_id=1, source_target_pairs={{0,96},{32,128},{64,160},{96,192},{128,224},{160,0},{192,32},{224,... | collective-permute-start | bytes 589832 | tf_op jit(solution)/shard_map/ppermute | solution.py:341
  31.0 50.8 %collective-permute-start.4 = (bf16[2,384,128]{2,1,0:T(8,128)(2,1)}, bf16[2,384,128]{2,1,0:T(8,128)(2,1)}, u32[]{:S(2)}, u32[]{:S(2)}) collective-permute-start(bf16[2,384,128]{2,1,0:T(8,128)(2,1)} %get-tuple-element.13.refs_0_), channel_id=1, source_target_pairs={{0,128},{32,160},{64,192},{96,224},{128,0},{160,32},{192,64},{224,... | collective-permute-start | bytes 589832 | tf_op jit(solution)/shard_map/ppermute | solution.py:341
  37.7 32.9 %copy-start.9 = (bf16[2,384,128]{2,1,0:T(8,128)(2,1)}, bf16[2,384,128]{2,1,0:T(8,128)(2,1)S(1)}, u32[]{:S(2)}) copy-start(bf16[2,384,128]{2,1,0:T(8,128)(2,1)S(1)} %collective-permute-done.1.refs_1_) | copy-start | bytes 589828
  37.7 44.1 %collective-permute-start.5 = (bf16[2,384,128]{2,1,0:T(8,128)(2,1)}, bf16[2,384,128]{2,1,0:T(8,128)(2,1)}, u32[]{:S(2)}, u32[]{:S(2)}) collective-permute-start(bf16[2,384,128]{2,1,0:T(8,128)(2,1)} %get-tuple-element.13.refs_0_), channel_id=1, source_target_pairs={{0,160},{32,192},{64,224},{96,0},{128,32},{160,64},{192,96},{224,1... | collective-permute-start | bytes 589832 | tf_op jit(solution)/shard_map/ppermute | solution.py:341
  50.8 19.8 %copy-start.10 = (bf16[2,384,128]{2,1,0:T(8,128)(2,1)}, bf16[2,384,128]{2,1,0:T(8,128)(2,1)S(1)}, u32[]{:S(2)}) copy-start(bf16[2,384,128]{2,1,0:T(8,128)(2,1)S(1)} %collective-permute-done.2.refs_2_) | copy-start | bytes 589828
  50.8 31.0 %collective-permute-start.6 = (bf16[2,384,128]{2,1,0:T(8,128)(2,1)}, bf16[2,384,128]{2,1,0:T(8,128)(2,1)}, u32[]{:S(2)}, u32[]{:S(2)}) collective-permute-start(bf16[2,384,128]{2,1,0:T(8,128)(2,1)} %get-tuple-element.13.refs_0_), channel_id=1, source_target_pairs={{0,192},{32,224},{64,0},{96,32},{128,64},{160,96},{192,128},{224,1... | collective-permute-start | bytes 589832 | tf_op jit(solution)/shard_map/ppermute | solution.py:341
  67.3 3.2 %copy-start.11 = (bf16[2,384,128]{2,1,0:T(8,128)(2,1)}, bf16[2,384,128]{2,1,0:T(8,128)(2,1)S(1)}, u32[]{:S(2)}) copy-start(bf16[2,384,128]{2,1,0:T(8,128)(2,1)S(1)} %collective-permute-done.3.refs_3_) | copy-start | bytes 589828
  67.3 15.9 %collective-permute-start.7 = (bf16[2,384,128]{2,1,0:T(8,128)(2,1)}, bf16[2,384,128]{2,1,0:T(8,128)(2,1)}, u32[]{:S(2)}, u32[]{:S(2)}) collective-permute-start(bf16[2,384,128]{2,1,0:T(8,128)(2,1)} %get-tuple-element.13.refs_0_), channel_id=1, source_target_pairs={{0,224},{32,0},{64,32},{96,64},{128,96},{160,128},{192,160},{224,1... | collective-permute-start | bytes 589832 | tf_op jit(solution)/shard_map/ppermute | solution.py:341
  70.6 72.2 %all-to-all-start.1 = ((bf16[8,512,256]{2,1,0:T(8,128)(2,1)}), bf16[8,512,256]{2,1,0:T(8,128)(2,1)S(1)}, u32[]{:S(2)}, u32[]{:S(2)}) async-start(bf16[8,512,256]{2,1,0:T(8,128)(2,1)} %dynamic-slice_bitcast_fusion), calls=%async_computation.1 | async-start | bytes 4194304 | tf_op jit(solution)/shard_map/all_to_all | solution.py:371
  83.2 0.8 copy-start.8
  100.3 19.1 %collective-permute-start.9 = (bf16[2048,128]{1,0:T(8,128)(2,1)}, bf16[2048,128]{1,0:T(8,128)(2,1)S(1)}, u32[]{:S(2)}, u32[]{:S(2)}) collective-permute-start(bf16[2048,128]{1,0:T(8,128)(2,1)} %get-tuple-element.16), channel_id=1, source_target_pairs={{0,8},{8,0},{1,9},{9,1},{2,10},{10,2},{3,11},{11,3},{4,12},{12,4},... | collective-permute-start | bytes 1572872 | tf_op jit(solution)/shard_map/ppermute | solution.py:337
  103.1 16.3 %collective-permute-start.10 = (f32[16,1,128]{2,1,0:T(1,128)}, f32[16,1,128]{2,1,0:T(1,128)S(1)}, u32[]{:S(2)}, u32[]{:S(2)}) collective-permute-start(f32[16,1,128]{2,1,0:T(1,128)} %get-tuple-element.17), channel_id=1, source_target_pairs={{0,8},{8,0},{1,9},{9,1},{2,10},{10,2},{3,11},{11,3},{4,12},{12,4},... | collective-permute-start | bytes 24584 | tf_op jit(solution)/shard_map/ppermute | solution.py:337
  119.4 0.6 copy-start.6
  119.4 0.8 copy-start.4
  124.0 13.4 %collective-permute-start.11 = (bf16[2048,128]{1,0:T(8,128)(2,1)}, bf16[2048,128]{1,0:T(8,128)(2,1)S(1)}, u32[]{:S(2)}, u32[]{:S(2)}) collective-permute-start(bf16[2048,128]{1,0:T(8,128)(2,1)} %get-tuple-element.18.own), channel_id=1, source_target_pairs={{0,16},{16,0},{1,17},{17,1},{2,18},{18,2},{3,19},{19,3},{4,20},{20... | collective-permute-start | bytes 1572872 | tf_op jit(solution)/shard_map/ppermute | solution.py:337
  125.5 11.9 %collective-permute-start.12 = (f32[16,1,128]{2,1,0:T(1,128)}, f32[16,1,128]{2,1,0:T(1,128)S(1)}, u32[]{:S(2)}, u32[]{:S(2)}) collective-permute-start(f32[16,1,128]{2,1,0:T(1,128)} %get-tuple-element.19.own_lse), channel_id=1, source_target_pairs={{0,16},{16,0},{1,17},{17,1},{2,18},{18,2},{3,19},{19,3},{4,20},{20... | collective-permute-start | bytes 24584 | tf_op jit(solution)/shard_map/ppermute | solution.py:337
  137.4 0.6 copy-start.7
  138.0 0.8 copy-start.2
  141.4 3.1 %collective-permute-start.13 = (bf16[2,128,1024]{2,1,0:T(8,128)(2,1)}, bf16[2,128,1024]{2,1,0:T(8,128)(2,1)S(1)}, u32[]{:S(2)}, u32[]{:S(2)}) collective-permute-start(bf16[2,128,1024]{2,1,0:T(8,128)(2,1)} %merge_last.1.near), channel_id=1, source_target_pairs={{0,8},{8,0},{1,9},{9,1},{2,10},{10,2},{3,11},{11,3},{4,12},{12,4},... | collective-permute-start | bytes 1572872 | tf_op jit(solution)/shard_map/ppermute | solution.py:337
  142.8 11.3 %copy-start = (bf16[8,512,256]{2,1,0:T(8,128)(2,1)}, bf16[8,512,256]{2,1,0:T(8,128)(2,1)S(1)}, u32[]{:S(2)}) copy-start(bf16[8,512,256]{2,1,0:T(8,128)(2,1)S(1)} %all-to-all-done.1.near) | copy-start | bytes 6291460
  142.8 19.0 %collective-permute-start.14 = (bf16[8,512,256]{2,1,0:T(8,128)(2,1)S(1)}, bf16[8,512,256]{2,1,0:T(8,128)(2,1)}, u32[]{:S(2)}, u32[]{:S(2)}) collective-permute-start(bf16[8,512,256]{2,1,0:T(8,128)(2,1)S(1)} %all-to-all-done.1.near), channel_id=1, source_target_pairs={{0,8},{8,0},{1,9},{9,1},{2,10},{10,2},{3,11},{11,3},{4,12},{12,4},... | collective-permute-start | bytes 6291464 | tf_op jit(solution)/shard_map/ppermute | solution.py:337
  144.5 0.8 copy-start.5
  154.1 37.5 %all-to-all-start = ((bf16[32,128,256]{2,1,0:T(8,128)(2,1)}), bf16[32,128,256]{2,1,0:T(8,128)(2,1)}, u32[]{:S(2)}, u32[]{:S(2)}) async-start(bf16[32,128,256]{2,1,0:T(8,128)(2,1)} %bitcast.21), calls=%async_computation | async-start | bytes 4194304 | tf_op jit(solution)/shard_map/all_to_all | solution.py:384
  196.5 14.5 %all-to-all-start.2 = ((bf16[8,144,256]{2,1,0:T(8,128)(2,1)}), bf16[8,144,256]{2,1,0:T(8,128)(2,1)S(1)}, u32[]{:S(2)}, u32[]{:S(2)}) async-start(bf16[8,144,256]{2,1,0:T(8,128)(2,1)} %get-tuple-element.21), calls=%async_computation.2 | async-start | bytes 1179648 | tf_op jit(solution)/shard_map/all_to_all | solution.py:390
  211.0 0.8 copy-start.1
Sparse Core Ops, SparseCore 0:
  9.8 92.3 all-gather.2

commit v2 on v1

--- a/solution.py
+++ b/solution.py
@@ -19,8 +19,9 @@
 CTX_AXES = ("z", "yl", "c")
 HEAD_AXES = ("x", "yh")
 VMEM = 56 * 1024 * 1024
-CHUNK = 256
-KEY_STEP = 1024
+CHUNK = 512
+BLOCKS = 3
+DISTANCES = (0, -1, 1, -2, 2, -3, 3, 4)
 
 
 def params(**more):
@@ -57,9 +58,12 @@
     for g in range(GROUP):
         piece = query[:, g * HEAD : (g + 1) * HEAD].astype(jnp.float32)
         query_out[g] = rotated(piece, cos, sin).astype(jnp.bfloat16)
-    kv_out[:, :CACHED, :] = cached[...]
-    kv_out[0, CACHED:, :] = rotated(fresh[0].astype(jnp.float32), cos, sin).astype(jnp.bfloat16)
-    kv_out[1, CACHED:, :] = fresh[1]
+    for k in range(CACHED // ROWS):
+        kv_out[k] = jnp.transpose(cached[0, k * ROWS : (k + 1) * ROWS, :])
+        kv_out[BLOCKS + k] = cached[1, k * ROWS : (k + 1) * ROWS, :]
+    new_key = rotated(fresh[0].astype(jnp.float32), cos, sin).astype(jnp.bfloat16)
+    kv_out[BLOCKS - 1] = jnp.transpose(new_key)
+    kv_out[2 * BLOCKS - 1] = fresh[1]
 
 
 def prepare(query, fresh, cached, cosine, sine):
@@ -67,7 +71,7 @@
         prepare_kernel,
         out_shape=(
             jax.ShapeDtypeStruct((GROUP, ROWS, HEAD), jnp.bfloat16),
-            jax.ShapeDtypeStruct((2, CACHED + ROWS, HEAD), jnp.bfloat16),
+            jax.ShapeDtypeStruct((2 * BLOCKS, ROWS, HEAD), jnp.bfloat16),
         ),
         compiler_params=params(),
         name="prepare",
@@ -83,49 +87,70 @@
     return jnp.transpose(column)[0:1, :]
 
 
-def attend_kernel(place, query, *refs):
-    kv = refs[:Z]
-    out, lse_out, keys, values, key_token = refs[Z:]
+def attend_kernel(cached, fresh, first, last, rc, place, query, *refs):
+    n_in = 1 + max([max(k, v) for k, v in cached] + [max(p[0], p[1]) for pair in fresh for p in pair])
+    pieces, rest = refs[:n_in], list(refs[n_in:])
+    if not first:
+        acc_in, m_in = rest[:2]
+        rest = rest[2:]
+    if last:
+        out, lse_out = rest[:2]
+    else:
+        acc_out, m_out = rest[:2]
+    keys, values = rest[2:]
     step = pl.program_id(0)
-    z, yl, c, rc = place[0], place[1], place[2], place[3]
+    z, yl, c = place[0], place[1], place[2]
+    steps = len(cached) + len(fresh)
+
+    def value_block(ref, k):
+        return ref[BLOCKS + k] if ref.shape[0] == 2 * BLOCKS else ref[k]
 
     @pl.when(step == 0)
     def _():
-        lane = lax.broadcasted_iota(jnp.int32, (8, ROWS), 1)
-        for d in range(Z):
-            block = kv[d]
-            keys[:, d * CACHED : (d + 1) * CACHED] = jnp.transpose(block[0, :CACHED, :])
-            at = Z * CACHED + d * ROWS
-            keys[:, at : at + ROWS] = jnp.transpose(block[0, CACHED:, :])
-            values[d * CACHED : (d + 1) * CACHED, :HEAD] = block[1, :CACHED, :]
-            values[at : at + ROWS, :HEAD] = block[1, CACHED:, :]
-            source = lax.rem(z - d + Z, Z)
-            key_token[:, d * ROWS : (d + 1) * ROWS] = (
-                source * 4 + yl * 2 + c
-            ) * ROWS + lane
-        values[:, HEAD:] = jnp.ones((Z * (CACHED + ROWS), HEAD), jnp.bfloat16)
+        at = 0
+        for kp, vp in cached:
+            for k in range(2):
+                keys[:, at : at + ROWS] = pieces[kp][k]
+                values[at : at + ROWS, :HEAD] = value_block(pieces[vp], k)
+                at += ROWS
+        for pair in fresh:
+            for kp, vp, _ in pair:
+                keys[:, at : at + ROWS] = pieces[kp][BLOCKS - 1]
+                values[at : at + ROWS, :HEAD] = value_block(pieces[vp], BLOCKS - 1)
+                at += ROWS
+        values[:, HEAD:] = jnp.ones((steps * 2 * ROWS, HEAD), jnp.bfloat16)
 
     per_block = GROUP * ROWS // CHUNK
     ryl = step // per_block
     block = z * 4 + (yl ^ ryl) * 2 + (c ^ rc)
     inside = lax.broadcasted_iota(jnp.int32, (CHUNK, 1), 0) & (ROWS - 1)
     query_token = block * ROWS + inside
+    lane = lax.broadcasted_iota(jnp.int32, (1, 2 * ROWS), 1)
     q = query[...]
-    m = jnp.full((CHUNK, 1), -1e30, jnp.float32)
-    acc = jnp.zeros((CHUNK, 2 * HEAD), jnp.float32)
-    for at in range(0, Z * (CACHED + ROWS), KEY_STEP):
-        scores = jnp.dot(q, keys[:, at : at + KEY_STEP], preferred_element_type=jnp.float32)
-        if at >= Z * CACHED:
-            first = at - Z * CACHED
-            visible = key_token[0:1, first : first + KEY_STEP] <= query_token
-            scores = jnp.where(visible, scores, -1e30)
+    if first:
+        m = jnp.full((CHUNK, 1), -1e30, jnp.float32)
+        acc = jnp.zeros((CHUNK, 2 * HEAD), jnp.float32)
+    else:
+        m = m_in[:, 0:1]
+        acc = acc_in[...]
+    for i in range(steps):
+        at = slice(i * 2 * ROWS, (i + 1) * 2 * ROWS)
+        scores = jnp.dot(q, keys[:, at], preferred_element_type=jnp.float32)
+        if i >= len(cached):
+            one, two = (
+                (lax.rem(z + p[2] + Z, Z) * 4 + yl * 2 + c) * ROWS for p in fresh[i - len(cached)]
+            )
+            key_token = jnp.where(lane < ROWS, one + lane, two + lane - ROWS)
+            scores = jnp.where(key_token <= query_token, scores, -1e30)
         raised = jnp.maximum(m, jnp.max(scores, axis=1, keepdims=True))
         weights = jnp.exp2((scores - raised) * SCALE).astype(jnp.bfloat16)
         factor = jnp.exp2((m - raised) * SCALE)
-        acc = acc * factor + jnp.dot(
-            weights, values[at : at + KEY_STEP, :], preferred_element_type=jnp.float32
-        )
+        acc = acc * factor + jnp.dot(weights, values[at, :], preferred_element_type=jnp.float32)
         m = raised
+    if not last:
+        acc_out[...] = acc
+        m_out[...] = jnp.broadcast_to(m, (CHUNK, HEAD))
+        return
     totals = acc[:, HEAD:]
     out[...] = (acc[:, :HEAD] / totals).astype(jnp.bfloat16)
     lse = m * SCALE + jnp.log2(totals)
@@ -133,68 +158,82 @@
         lse_out[step * (CHUNK // ROWS) + k] = row_of(lse[k * ROWS : (k + 1) * ROWS, :])
 
 
-def attend(place, query, kv):
+def attend(place, rc, query, pieces, cached, fresh, state=None, last=False):
     rows = query.shape[0]
-    total = Z * (CACHED + ROWS)
-    whole = pl.BlockSpec((2, CACHED + ROWS, HEAD), lambda i, s: (0, 0, 0))
-    return pl.pallas_call(
-        attend_kernel,
+    total = 2 * ROWS * (len(cached) + len(fresh))
+    row_spec = pl.BlockSpec((CHUNK, HEAD), lambda i, s: (i, 0))
+    wide_spec = pl.BlockSpec((CHUNK, 2 * HEAD), lambda i, s: (i, 0))
+    in_specs = [row_spec] + [pl.BlockSpec(p.shape, lambda i, s: (0, 0, 0)) for p in pieces]
+    args = [query, *pieces]
+    if state is not None:
+        in_specs += [wide_spec, row_spec]
+        args += list(state)
+    if last:
+        out_specs = [row_spec, pl.BlockSpec((rows // ROWS, 1, ROWS), lambda i, s: (0, 0, 0))]
+        out_shape = (
+            jax.ShapeDtypeStruct((rows, HEAD), jnp.bfloat16),
+            jax.ShapeDtypeStruct((rows // ROWS, 1, ROWS), jnp.float32),
+        )
+    else:
+        out_specs = [wide_spec, row_spec]
+        out_shape = (
+            jax.ShapeDtypeStruct((rows, 2 * HEAD), jnp.float32),
+            jax.ShapeDtypeStruct((rows, HEAD), jnp.float32),
+        )
+    return pl.pallas_call(
+        functools.partial(attend_kernel, cached, fresh, state is None, last, rc),
         grid_spec=pltpu.PrefetchScalarGridSpec(
             num_scalar_prefetch=1,
             grid=(rows // CHUNK,),
-            in_specs=[pl.BlockSpec((CHUNK, HEAD), lambda i, s: (i, 0))] + [whole] * Z,
-            out_specs=[
-                pl.BlockSpec((CHUNK, HEAD), lambda i, s: (i, 0)),
-                pl.BlockSpec((rows // ROWS, 1, ROWS), lambda i, s: (0, 0, 0)),
-            ],
+            in_specs=in_specs,
+            out_specs=out_specs,
             scratch_shapes=[
                 pltpu.VMEM((HEAD, total), jnp.bfloat16),
                 pltpu.VMEM((total, 2 * HEAD), jnp.bfloat16),
-                pltpu.VMEM((8, Z * ROWS), jnp.int32),
             ],
         ),
-        out_shape=(
-            jax.ShapeDtypeStruct((rows, HEAD), jnp.bfloat16),
-            jax.ShapeDtypeStruct((rows // ROWS, 1, ROWS), jnp.float32),
-        ),
+        out_shape=out_shape,
         compiler_params=params(),
         name="attend",
         cost_estimate=pl.CostEstimate(
             flops=4 * rows * total * HEAD,
-            bytes_accessed=4 * rows * HEAD + 4 * total * HEAD,
+            bytes_accessed=8 * rows * HEAD + 4 * total * HEAD,
             transcendentals=rows * total,
         ),
-    )(place, query, *kv)
-
-
-def merged(first, second, first_lse, second_lse):
-    a, b = column_of(first_lse), column_of(second_lse)
-    top = jnp.maximum(a, b)
-    wa, wb = jnp.exp2(a - top), jnp.exp2(b - top)
-    total = wa + wb
-    value = (first.astype(jnp.float32) * wa + second.astype(jnp.float32) * wb) / total
-    return value.astype(jnp.bfloat16), top + jnp.log2(total)
+    )(place, *args)
+
+
+def merge_weight(first_lse, second_lse):
+    top = jnp.maximum(first_lse, second_lse)
+    a, b = jnp.exp2(first_lse - top), jnp.exp2(second_lse - top)
+    return a / (a + b), top + jnp.log2(a + b)
+
+
+def merged(first, second, weight):
+    a, b = first.astype(jnp.float32), second.astype(jnp.float32)
+    share = column_of(weight)
+    return (a * share + b * (1.0 - share)).astype(jnp.bfloat16)
 
 
 def merge_kernel(own, own_lse, other, other_lse, out, lse_out):
     for k in range(own.shape[0] // ROWS):
         at = slice(k * ROWS, (k + 1) * ROWS)
-        value, lse = merged(own[at, :], other[at, :], own_lse[k], other_lse[k])
-        out[at, :] = value
-        lse_out[k] = row_of(lse)
+        weight, lse = merge_weight(own_lse[k], other_lse[k])
+        out[at, :] = merged(own[at, :], other[at, :], weight)
+        lse_out[k] = lse
 
 
 def merge_last_kernel(own, own_lse, other, other_lse, out):
     for y in range(2):
         for g in range(GROUP):
             k, j = y * GROUP + g, (1 - y) * GROUP + g
-            value, _ = merged(
-                own[k * ROWS : (k + 1) * ROWS, :],
-                other[j * ROWS : (j + 1) * ROWS, :],
-                own_lse[k],
-                other_lse[j],
+            weight, _ = merge_weight(own_lse[k], other_lse[j])
+            out[y, :, g * HEAD : (g + 1) * HEAD] = merged(
+                own[k * ROWS : (k + 1) * ROWS, :], other[j * ROWS : (j + 1) * ROWS, :], weight
             )
-            out[y, :, g * HEAD : (g + 1) * HEAD] = value
+
+
+MERGE_COST = pl.CostEstimate(flops=2_000_000, bytes_accessed=1_600_000, transcendentals=4096)
 
 
 def merge(own, own_lse, other, other_lse):
@@ -206,6 +245,7 @@
         ),
         compiler_params=params(),
         name="merge",
+        cost_estimate=MERGE_COST,
     )(own, own_lse, other, other_lse)
 
 
@@ -215,38 +255,46 @@
         out_shape=jax.ShapeDtypeStruct((2, ROWS, GROUP * HEAD), jnp.bfloat16),
         compiler_params=params(),
         name="merge_last",
+        cost_estimate=MERGE_COST,
     )(own, own_lse, other, other_lse)
 
 
-def project_kernel(place, near, far, weight, out):
-    yl, c = place[1], place[2]
+def project_kernel(place, near, far, *refs):
+    weights, top, bottom, out = refs[:7], refs[7], refs[8], refs[9]
+    z, yl, c = place[0], place[1], place[2]
+    width = GROUP * HEAD
     for rc, rows in ((0, near), (1, far)):
-        for ryl in range(2):
-            q = (yl ^ ryl) * 2 + (c ^ rc)
-            out[q, 0] = jnp.dot(
-                rows[ryl], weight[0], preferred_element_type=jnp.float32
-            ).astype(jnp.bfloat16)
-
-
-def project(place, near, far, weight):
-    width = GROUP * HEAD
-    columns = weight.shape[2]
+        lhs = rows[...].reshape(2 * ROWS, width)
+        for i, distance in enumerate(DISTANCES):
+            if i < 7:
+                product = jnp.dot(lhs, weights[i][...], preferred_element_type=jnp.float32)
+            else:
+                product = jnp.dot(
+                    lhs[:, : width // 2], top[...], preferred_element_type=jnp.float32
+                ) + jnp.dot(lhs[:, width // 2 :], bottom[...], preferred_element_type=jnp.float32)
+            product = product.astype(jnp.bfloat16)
+            target = lax.rem(z + distance + Z, Z)
+            for ryl in range(2):
+                q = (yl ^ ryl) * 2 + (c ^ rc)
+                out[q, target] = product[ryl * ROWS : (ryl + 1) * ROWS, :]
+
+
+def project(place, near, far, pieces):
+    vmem = pl.BlockSpec(memory_space=pltpu.VMEM)
+    columns = pieces[0].shape[1]
     return pl.pallas_call(
         project_kernel,
-        grid_spec=pltpu.PrefetchScalarGridSpec(
-            num_scalar_prefetch=1,
-            grid=(Z,),
-            in_specs=[
-                pl.BlockSpec((2, ROWS, width), lambda i, s: (0, 0, 0)),
-                pl.BlockSpec((2, ROWS, width), lambda i, s: (0, 0, 0)),
-                pl.BlockSpec((1, width, columns), lambda i, s: (i, 0, 0)),
-            ],
-            out_specs=pl.BlockSpec((4, 1, ROWS, columns), lambda i, s: (0, i, 0, 0)),
+        in_specs=[pl.BlockSpec(memory_space=pltpu.SMEM)] + [vmem] * 11,
+        out_specs=vmem,
+        out_shape=jax.ShapeDtypeStruct((4, Z, ROWS, columns), jnp.bfloat16),
+        compiler_params=params(),
+        name="project",
+        cost_estimate=pl.CostEstimate(
+            flops=2 * 4 * ROWS * GROUP * HEAD * Z * columns,
+            bytes_accessed=4_000_000,
+            transcendentals=0,
         ),
-        out_shape=jax.ShapeDtypeStruct((4, Z, ROWS, columns), jnp.bfloat16),
-        compiler_params=params(),
-        name="project",
-    )(place, near, far, weight)
+    )(place, near, far, *pieces)
 
 
 PAD = 16
@@ -255,7 +303,7 @@
 def third_kernel(place, received, hidden, gain, near, far, out, partial, scaled):
     c = place[2]
     columns = received.shape[3]
-    squares = jnp.zeros((ROWS, 1), jnp.float32)
+    squares = jnp.zeros((ROWS, columns), jnp.float32)
     for q in range(4):
         at = slice(q * columns, (q + 1) * columns)
         total = received[q, 0].astype(jnp.float32)
@@ -264,10 +312,11 @@
         result = (hidden[:, at].astype(jnp.float32) + total).astype(jnp.bfloat16)
         out[:, at] = result
         wide = result.astype(jnp.float32)
-        squares = squares + jnp.sum(wide * wide, axis=1, keepdims=True)
+        squares = squares + wide * wide
         scaled[q // 2, :, (q % 2) * columns : (q % 2 + 1) * columns] = (
             wide * gain[:, at]
         ).astype(jnp.bfloat16)
+    squares = jnp.sum(squares, axis=1, keepdims=True)
     row = row_of(jnp.broadcast_to(squares, (ROWS, ROWS)))
     high = row.astype(jnp.bfloat16)
     low = (row - high.astype(jnp.float32)).astype(jnp.bfloat16)
@@ -341,6 +390,19 @@
     return lax.ppermute(x, "z", [(i, (i + distance) % Z) for i in range(Z)])
 
 
+def after(x, *others):
+    return lax.optimization_barrier((x, others))[0]
+
+
+def step(pair):
+    return [along_z(pair[0], 1), along_z(pair[1], -1)]
+
+
+def last_step(pair):
+    half = pair[0].shape[0] // 2
+    return [along_z(pair[0][:half], 1), along_z(pair[1][half:], -1)]
+
+
 def local(
     hidden,
     query,
@@ -355,31 +417,50 @@
     keep_count,
 ):
     z, yl, c = lax.axis_index("z"), lax.axis_index("yl"), lax.axis_index("c")
-    place = jnp.stack([z, yl, c, jnp.zeros_like(c)]).astype(jnp.int32)
-    far_place = jnp.stack([z, yl, c, jnp.ones_like(c)]).astype(jnp.int32)
+    place = jnp.stack([z, yl, c]).astype(jnp.int32)
 
     cosine, sine = tables(positions, HEAD)
     rotated_query, kv = prepare(query, fresh_key_value, cached_key_value, cosine, sine)
-    pieces = [kv] + [along_z(kv, d) for d in range(1, Z)]
+    weights_1 = step([out_weight, out_weight])
+    kv_1 = list(after(step([kv, kv]), *weights_1))
+    kv_2 = step(kv_1)
+    weights_2 = step(weights_1)
+    kv_3 = step(kv_2)
+    weights_3 = step(weights_2)
+    weights_4 = last_step(weights_3)
+    weights = [out_weight, *weights_1, *weights_2, *weights_3, *weights_4]
     rotated_query = rotated_query.reshape(GROUP * ROWS, HEAD)
     near_query = jnp.concatenate([rotated_query, swap(rotated_query, "yl")], axis=0)
     far_query = swap(near_query, "c")
-    weight = lax.all_gather(out_weight, "z")
-
     third_rows = layer3_key_value_weight.reshape(Z, 2, MODEL_WIDTH // Z // 2, 2 * HEAD)
     third_rows = lax.dynamic_index_in_dim(third_rows, c, axis=1, keepdims=False)
+    third_rows = after(third_rows, *kv_2, near_query)
     third_near = lax.all_to_all(third_rows, HEAD_AXES, 0, 0, tiled=True)
     third_far = swap(third_near, "c")
 
-    send, send_lse = attend(far_place, far_query, pieces)
+    early = [kv, *kv_1, *kv_2]
+    early_cached = [(i, i) for i in range(5)]
+    early_fresh = [[(0, 0, 0), (1, 1, -1)], [(2, 2, 1), (3, 3, -2)]]
+    late_cached = [(1, 1), (2, 2), (3, 4)]
+    late_fresh = [[(0, 0, 2), (1, 1, -3)], [(2, 2, 3), (3, 4, 4)]]
+    near_query = after(near_query, *weights_2)
+    near_state = attend(place, 0, near_query, early, early_cached, early_fresh)
+    kv_3 = list(after(kv_3, near_state))
+    late = [kv_2[1], *kv_3, *last_step(kv_3)]
+    far_query = after(far_query, near_state)
+    far_state = attend(place, 1, far_query, early, early_cached, early_fresh)
+    far_state = after(far_state, *weights_3)
+    send, send_lse = attend(place, 1, far_query, late, late_cached, late_fresh, far_state, True)
     got, got_lse = swap(send, "c"), swap(send_lse, "c")
-    own, own_lse = attend(place, near_query, pieces)
+    own, own_lse = attend(place, 0, near_query, late, late_cached, late_fresh, near_state, True)
+    got_lse = after(got_lse, *weights_4)
     own, own_lse = merge(own, own_lse, got, got_lse)
     got, got_lse = swap(own, "yl"), swap(own_lse, "yl")
+    got_lse = after(got_lse, third_near)
     near = merge_last(own, own_lse, got, got_lse)
     far = swap(near, "c")
 
-    products = project(place, near, far, weight)
+    products = project(place, near, far, weights)
     products = products.reshape(4 * Z, *products.shape[2:])
     received = lax.all_to_all(products, ("yl", "c", "x", "yh"), 0, 0, tiled=True)
     received = received.reshape(4, Z, *received.shape[1:])

time: 221 us -> 202 us (0.914)
  waiting for transfers between devices: 97.9 us -> 64.8 us
  starting transfers between devices: 39.5 us -> 54 us
  between operations: 14.8 us -> 1.57 us
  Pallas kernels: 56.7 us -> 67.6 us
  local copies, waits for them, and re-layouts: 7.87 us -> 10.3 us
    ppermute x7 -> x16, waiting for transfers between devices: 38.4 us -> 9.76 us  [along_z(): return lax.ppermute(x, 'z', [(i, (i + distance) % Z) for i in range(Z)])]
    ppermute x7 -> x16, starting transfers between devices: 11.4 us -> 26.1 us  [along_z(): return lax.ppermute(x, 'z', [(i, (i + distance) % Z) for i in range(Z)])]
    pallas_call x3 -> x5, Pallas kernels: 41.3 us -> 53.8 us  [the longest x4 47.7 us: attend(): pl.pallas_call(functools.partial(attend_kernel, cached, fresh, state is N...]
    ppermute x8, waiting for transfers between devices: 18.7 us -> 14.9 us  [swap(): return lax.ppermute(x, axis, [(0, 1), (1, 0)])]
    unnamed x24 -> x40, local copies, waits for them, and re-layouts: 4.65 us -> 6.19 us
  transfers between devices with their start and end apart: 19 -> 27, of which waited for: 10 -> 7; matrix products, arithmetic and copies ran while one was open for 3% -> 4% of each run, Pallas kernels for 23% -> 29%
where the time goes in v2:
time: 202 us
  Pallas kernels  67.6 us (33%)
  waiting for transfers between devices  64.8 us (32%)
  starting transfers between devices  54 us (27%)
  local copies, waits for them, and re-layouts  10.3 us (5%)
  other arithmetic  3.45 us (2%)
    pallas_call x4, Pallas kernels, attend(): pl.pallas_call(functools.partial(attend_kernel, cached, fresh, state is N...  47.7 us
    all_to_all x1, waiting for transfers between devices, local(): lax.all_to_all(products, ('yl', 'c', 'x', 'yh'), 0, 0, tiled=True)  29.8 us
    ppermute x16, starting transfers between devices, along_z(): return lax.ppermute(x, 'z', [(i, (i + distance) % Z) for i in range(Z)])  26.1 us
    ppermute x8, waiting for transfers between devices, swap(): return lax.ppermute(x, axis, [(0, 1), (1, 0)])  14.9 us
    all_to_all x1, waiting for transfers between devices, local(): partial = lax.all_to_all(partial, HEAD_AXES, 0, 0, tiled=True)  10.3 us
    ppermute x8, starting transfers between devices, swap(): return lax.ppermute(x, axis, [(0, 1), (1, 0)])  10.2 us
    ppermute x16, waiting for transfers between devices, along_z(): return lax.ppermute(x, 'z', [(i, (i + distance) % Z) for i in range(Z)])  9.76 us
    all_to_all x1, starting transfers between devices, local(): lax.all_to_all(products, ('yl', 'c', 'x', 'yh'), 0, 0, tiled=True)  7.51 us
  transfers between devices with their start and end apart: 27, of which 7 were waited for; matrix products, arithmetic and copies ran while one was open for 4% of the time, Pallas kernels for 29%

profile of v2, /device:TPU:1, one launch (start us, length us, event | category | flops | bytes accessed | tf_op | source)
XLA Modules:
  0.0 201.7 jit_solution(3429488708339448416)
XLA Ops:
  0.6 2.5 %collective-permute-start.1 = (bf16[1024,256]{1,0:T(8,128)(2,1)}, bf16[1024,256]{1,0:T(8,128)(2,1)S(1)}, u32[]{:S(2)}, u32[]{:S(2)}) collective-permute-start(bf16[1024,256]{1,0:T(8,128)(2,1)} %refs_0_.1), channel_id=1, source_target_pairs={{0,32},{32,64},{64,96},{96,128},{128,160},{160,192},{192,224},{224... | collective-permute-start | bytes 1572872 | tf_op jit(solution)/shard_map/ppermute | solution.py:390
  3.2 4.0 %collective-permute-start.3 = (bf16[1024,256]{1,0:T(8,128)(2,1)}, bf16[1024,256]{1,0:T(8,128)(2,1)}, u32[]{:S(2)}, u32[]{:S(2)}) collective-permute-start(bf16[1024,256]{1,0:T(8,128)(2,1)} %refs_0_.1), channel_id=1, source_target_pairs={{0,224},{32,0},{64,32},{96,64},{128,96},{160,128},{192,160},{224,1... | collective-permute-start | bytes 1572872 | tf_op jit(solution)/shard_map/ppermute | solution.py:390
  7.2 0.7 convert_element_type.36
  8.3 0.7 pad_maximum_fusion.1
  9.0 2.0 prepare.1
  11.0 1.3 collective-permute-start
  12.3 2.7 %collective-permute-start.6 = (bf16[6,128,128]{2,1,0:T(8,128)(2,1)}, bf16[6,128,128]{2,1,0:T(8,128)(2,1)S(1)}, u32[]{:S(2)}, u32[]{:S(2)}) collective-permute-start(bf16[6,128,128]{2,1,0:T(8,128)(2,1)} %get-tuple-element.29.refs_0_), channel_id=1, source_target_pairs={{0,224},{32,0},{64,32},{96,64},{128,96},{160,128},{192,160},{224,1... | collective-permute-start | bytes 589832 | tf_op jit(solution)/shard_map/ppermute | solution.py:390
  15.0 8.2 %collective-permute-done.5.refs_1_ = bf16[6,128,128]{2,1,0:T(8,128)(2,1)S(1)} collective-permute-done((bf16[6,128,128]{2,1,0:T(8,128)(2,1)}, bf16[6,128,128]{2,1,0:T(8,128)(2,1)S(1)}, u32[]{:S(2)}, u32[]{:S(2)}) %collective-permute-start.5) | collective-permute-done | bytes 196640 | tf_op jit(solution)/shard_map/ppermute | solution.py:390
  23.2 2.5 %collective-permute-start.7 = (bf16[6,128,128]{2,1,0:T(8,128)(2,1)S(1)}, bf16[6,128,128]{2,1,0:T(8,128)(2,1)S(1)}, u32[]{:S(2)}, u32[]{:S(2)}) collective-permute-start(bf16[6,128,128]{2,1,0:T(8,128)(2,1)S(1)} %collective-permute-done.6.refs_2_), channel_id=1, source_target_pairs={{0,224},{32,0},{64,32},{96,64},{128,96},{160,128},{192,160},{224,1... | collective-permute-start | bytes 589832 | tf_op jit(solution)/shard_map/ppermute | solution.py:390
  25.7 2.7 %collective-permute-start.4 = (bf16[1024,256]{1,0:T(8,128)(2,1)}, bf16[1024,256]{1,0:T(8,128)(2,1)}, u32[]{:S(2)}, u32[]{:S(2)}) collective-permute-start(bf16[1024,256]{1,0:T(8,128)(2,1)} %collective-permute-done.3.refs_2_), channel_id=1, source_target_pairs={{0,224},{32,0},{64,32},{96,64},{128,96},{160,128},{192,160},{224,1... | collective-permute-start | bytes 1572872 | tf_op jit(solution)/shard_map/ppermute | solution.py:390
  28.4 1.0 pad_maximum_fusion.query
  29.4 2.5 %collective-permute-start.13 = (bf16[2048,128]{1,0:T(8,128)(2,1)S(1)}, bf16[2048,128]{1,0:T(8,128)(2,1)}, u32[]{:S(2)}, u32[]{:S(2)}) collective-permute-start(bf16[2048,128]{1,0:T(8,128)(2,1)S(1)} %pad_maximum_fusion.query), channel_id=1, source_target_pairs={{0,8},{8,0},{1,9},{9,1},{2,10},{10,2},{3,11},{11,3},{4,12},{12,4},... | collective-permute-start | bytes 1572872 | tf_op jit(solution)/shard_map/ppermute | solution.py:386
  31.9 3.1 %dynamic-slice_bitcast_fusion = bf16[8,512,256]{2,1,0:T(8,128)(2,1)} fusion(bf16[8,2,512,256]{3,2,1,0:T(8,128)(2,1)} %bitcast.21, s32[]{:T(128)S(6)} %select_n.14), kind=kLoop, calls=%fused_computation | loop fusion | bytes 4194308 | tf_op jit(solution)/shard_map/jit(dynamic_index_in_dim)/squeeze | solution.py:436
  35.1 0.7 copy-done.17
  35.8 6.7 %all-to-all-start = ((bf16[8,512,256]{2,1,0:T(8,128)(2,1)}), bf16[8,512,256]{2,1,0:T(8,128)(2,1)S(1)}, u32[]{:S(2)}, u32[]{:S(2)}) async-start(bf16[8,512,256]{2,1,0:T(8,128)(2,1)} %dynamic-slice_bitcast_fusion), calls=%async_computation | async-start | bytes 4194304 | tf_op jit(solution)/shard_map/all_to_all | solution.py:438
  42.8 2.7 %collective-permute-start.15 = (bf16[1024,256]{1,0:T(8,128)(2,1)}, bf16[1024,256]{1,0:T(8,128)(2,1)}, u32[]{:S(2)}, u32[]{:S(2)}) collective-permute-start(bf16[1024,256]{1,0:T(8,128)(2,1)} %collective-permute-done.4.refs_4_), channel_id=1, source_target_pairs={{0,224},{32,0},{64,32},{96,64},{128,96},{160,128},{192,160},{224,1... | collective-permute-start | bytes 1572872 | tf_op jit(solution)/shard_map/ppermute | solution.py:390
  45.5 2.7 %collective-permute-start.10 = (bf16[6,128,128]{2,1,0:T(8,128)(2,1)S(1)}, bf16[6,128,128]{2,1,0:T(8,128)(2,1)S(1)}, u32[]{:S(2)}, u32[]{:S(2)}) collective-permute-start(bf16[6,128,128]{2,1,0:T(8,128)(2,1)S(1)} %collective-permute-done.7.refs_4_.refs_0_), channel_id=1, source_target_pairs={{0,224},{32,0},{64,32},{96,64},{128,96},{160,128},{192,160},{224,1... | collective-permute-start | bytes 589832 | tf_op jit(solution)/shard_map/ppermute | solution.py:390
  48.2 0.7 pad_add_fusion.place
  48.9 9.2 %attend.4 = (f32[2048,256]{1,0:T(8,128)}, f32[2048,128]{1,0:T(8,128)}) custom-call(s32[3]{0:T(128)} %pad_add_fusion.place, bf16[2048,128]{1,0:T(8,128)(2,1)} %copy-done.3, bf16[6,128,128]{2,1,0:T(8,128)(2,1)} %get-tuple-element.29.refs_0_, bf16[6,128,128]{2,1,0:T(8,128)(2,1)} %copy-done.15, bf16[6,128,128]{2,1,0:T(8,128)(2,1)} %copy-done.16, ...), custom_call_target="tpu_custom_call" | custom-call | flops 1879048192 | bytes 3014656 | tf_op jit(solution)/shard_map/attend/pallas_call | solution.py:183
  58.0 1.1 collective-permute-done.9.refs_1_
  59.2 3.4 %collective-permute-start.11 = (bf16[3,128,128]{2,1,0:T(8,128)(2,1)S(1)}, bf16[3,128,128]{2,1,0:T(8,128)(2,1)S(1)}, u32[]{:S(2)}, u32[]{:S(2)}) collective-permute-start(bf16[3,128,128]{2,1,0:T(8,128)(2,1)S(1)} %slice.24), channel_id=1, source_target_pairs={{0,32},{32,64},{64,96},{96,128},{128,160},{160,192},{192,224},{224... | collective-permute-start | bytes 294920 | tf_op jit(solution)/shard_map/ppermute | solution.py:390
  62.6 9.2 %attend.6 = (f32[2048,256]{1,0:T(8,128)}, f32[2048,128]{1,0:T(8,128)}) custom-call(s32[3]{0:T(128)} %pad_add_fusion.place, bf16[2048,128]{1,0:T(8,128)(2,1)} %collective-permute-done.13.query, bf16[6,128,128]{2,1,0:T(8,128)(2,1)} %get-tuple-element.29.refs_0_, bf16[6,128,128]{2,1,0:T(8,128)(2,1)} %copy-done.15, bf16[6,128,128]{2,1,0:T(8,128)(2,1)} %copy-done.16, ...), custom_call_target="tpu_custom_call" | custom-call | flops 1879048192 | bytes 3014656 | tf_op jit(solution)/shard_map/attend/pallas_call | solution.py:183
  71.9 0.7 copy-done.18
  72.6 0.6 copy-done.19
  73.2 14.7 %attend.7 = (bf16[2048,128]{1,0:T(8,128)(2,1)}, f32[16,1,128]{2,1,0:T(1,128)}) custom-call(s32[3]{0:T(128)} %pad_add_fusion.place, bf16[2048,128]{1,0:T(8,128)(2,1)} %collective-permute-done.13.query, bf16[6,128,128]{2,1,0:T(8,128)(2,1)} %copy-done.14, bf16[6,128,128]{2,1,0:T(8,128)(2,1)} %copy-done.6, bf16[6,128,128]{2,1,0:T(8,128)(2,1)} %copy-done.7, ...), custom_call_target="tpu_custom_call" | custom-call | flops 1342177280 | bytes 2752512 | tf_op jit(solution)/shard_map/attend/pallas_call | solution.py:183
  87.9 3.6 %collective-permute-start.16 = (bf16[2048,128]{1,0:T(8,128)(2,1)}, bf16[2048,128]{1,0:T(8,128)(2,1)S(1)}, u32[]{:S(2)}, u32[]{:S(2)}) collective-permute-start(bf16[2048,128]{1,0:T(8,128)(2,1)} %get-tuple-element.43), channel_id=1, source_target_pairs={{0,8},{8,0},{1,9},{9,1},{2,10},{10,2},{3,11},{11,3},{4,12},{12,4},... | collective-permute-start | bytes 1572872 | tf_op jit(solution)/shard_map/ppermute | solution.py:386
  91.6 1.0 slice.29
  92.6 2.7 %collective-permute-start.19 = (bf16[512,256]{1,0:T(8,128)(2,1)S(1)}, bf16[512,256]{1,0:T(8,128)(2,1)S(1)}, u32[]{:S(2)}, u32[]{:S(2)}) collective-permute-start(bf16[512,256]{1,0:T(8,128)(2,1)S(1)} %slice.29), channel_id=1, source_target_pairs={{0,224},{32,0},{64,32},{96,64},{128,96},{160,128},{192,160},{224,1... | collective-permute-start | bytes 786440 | tf_op jit(solution)/shard_map/ppermute | solution.py:390
  95.3 0.6 collective-permute-start.17
  95.9 14.7 %attend.5 = (bf16[2048,128]{1,0:T(8,128)(2,1)}, f32[16,1,128]{2,1,0:T(1,128)}) custom-call(s32[3]{0:T(128)} %pad_add_fusion.place, bf16[2048,128]{1,0:T(8,128)(2,1)} %copy-done.3, bf16[6,128,128]{2,1,0:T(8,128)(2,1)} %copy-done.14, bf16[6,128,128]{2,1,0:T(8,128)(2,1)} %copy-done.6, bf16[6,128,128]{2,1,0:T(8,128)(2,1)} %copy-done.7, ...), custom_call_target="tpu_custom_call" | custom-call | flops 1342177280 | bytes 2752512 | tf_op jit(solution)/shard_map/attend/pallas_call | solution.py:183
  110.6 0.5 copy-done.8
  111.5 2.4 %merge.1 = (bf16[2048,128]{1,0:T(8,128)(2,1)}, f32[16,1,128]{2,1,0:T(1,128)}) custom-call(bf16[2048,128]{1,0:T(8,128)(2,1)} %get-tuple-element.36.own, f32[16,1,128]{2,1,0:T(1,128)} %get-tuple-element.37.own_lse, bf16[2048,128]{1,0:T(8,128)(2,1)} %copy-done.4, f32[16,1,128]{2,1,0:T(1,128)} %copy-done.8), custom_call_target="tpu_custom_call" | custom-call | flops 2000000 | bytes 1600000 | tf_op jit(solution)/shard_map/merge/pallas_call | solution.py:240
  113.9 1.3 collective-permute-start.20
  115.4 12.5 %collective-permute-done.21.other_lse = f32[16,1,128]{2,1,0:T(1,128)S(1)} collective-permute-done((f32[16,1,128]{2,1,0:T(1,128)}, f32[16,1,128]{2,1,0:T(1,128)S(1)}, u32[]{:S(2)}, u32[]{:S(2)}) %collective-permute-start.21) | collective-permute-done | bytes 8224 | tf_op jit(solution)/shard_map/ppermute | solution.py:386
  127.9 0.6 copy-done.9
  128.5 0.9 copy-done.2
  129.4 2.4 %merge_last.1.near = bf16[2,128,1024]{2,1,0:T(8,128)(2,1)} custom-call(bf16[2048,128]{1,0:T(8,128)(2,1)} %get-tuple-element.46.own, f32[16,1,128]{2,1,0:T(1,128)} %get-tuple-element.47.own_lse, bf16[2048,128]{1,0:T(8,128)(2,1)} %copy-done.2, f32[16,1,128]{2,1,0:T(1,128)} %copy-done.9), custom_call_target="tpu_custom_call" | custom-call | flops 2000000 | bytes 1600000 | tf_op jit(solution)/shard_map/merge_last/pallas_call | solution.py:253
  131.8 0.8 collective-permute-start.22
  132.6 2.5 %collective-permute-done.22.far = bf16[2,128,1024]{2,1,0:T(8,128)(2,1)S(1)} collective-permute-done((bf16[2,128,1024]{2,1,0:T(8,128)(2,1)}, bf16[2,128,1024]{2,1,0:T(8,128)(2,1)S(1)}, u32[]{:S(2)}, u32[]{:S(2)}) %collective-permute-start.22) | collective-permute-done | bytes 524320 | tf_op jit(solution)/shard_map/ppermute | solution.py:386
  135.0 0.8 copy-done.11
  135.8 6.2 %project.1 = bf16[4,8,128,256]{3,2,1,0:T(8,128)(2,1)} custom-call(s32[3]{0:T(128)} %pad_add_fusion.place, bf16[2,128,1024]{2,1,0:T(8,128)(2,1)} %merge_last.1.near, bf16[2,128,1024]{2,1,0:T(8,128)(2,1)} %copy-done.11, bf16[1024,256]{1,0:T(8,128)(2,1)} %refs_0_.1, bf16[1024,256]{1,0:T(8,128)(2,1)} %copy-done.10, ...), custom_call_target="tpu_custom_call" | custom-call | flops 2147483648 | bytes 4000000 | tf_op jit(solution)/shard_map/project/pallas_call | solution.py:285
  142.0 7.5 %all-to-all-start.1 = ((bf16[32,128,256]{2,1,0:T(8,128)(2,1)}), bf16[32,128,256]{2,1,0:T(8,128)(2,1)}, u32[]{:S(2)}, u32[]{:S(2)}) async-start(bf16[32,128,256]{2,1,0:T(8,128)(2,1)} %bitcast.20), calls=%async_computation.1 | async-start | bytes 4194304 | tf_op jit(solution)/shard_map/all_to_all | solution.py:465
  149.5 29.8 %all-to-all-done.1 = bf16[32,128,256]{2,1,0:T(8,128)(2,1)} async-done(((bf16[32,128,256]{2,1,0:T(8,128)(2,1)}), bf16[32,128,256]{2,1,0:T(8,128)(2,1)}, u32[]{:S(2)}, u32[]{:S(2)}) %all-to-all-start.1) | async-done | bytes 2097184 | tf_op jit(solution)/shard_map/all_to_all | solution.py:465
  179.3 4.9 %third.1 = (bf16[128,1024]{1,0:T(8,128)(2,1)}, bf16[8,144,256]{2,1,0:T(8,128)(2,1)}) custom-call(s32[3]{0:T(128)} %pad_add_fusion.place, bf16[4,8,128,256]{3,2,1,0:T(8,128)(2,1)} %bitcast.10.received, bf16[128,1024]{1,0:T(8,128)(2,1)} %hidden.1, f32[1,1024]{1,0:T(1,128)} %bitcast.24, bf16[8,512,256]{2,1,0:T(8,128)(2,1)} %copy-done, ...), custom_call_target="tpu_custom_call" | custom-call | tf_op jit(solution)/shard_map/third/pallas_call | solution.py:338
  184.2 3.5 %all-to-all-start.2 = ((bf16[8,144,256]{2,1,0:T(8,128)(2,1)}), bf16[8,144,256]{2,1,0:T(8,128)(2,1)S(1)}, u32[]{:S(2)}, u32[]{:S(2)}) async-start(bf16[8,144,256]{2,1,0:T(8,128)(2,1)} %get-tuple-element.51), calls=%async_computation.2 | async-start | bytes 1179648 | tf_op jit(solution)/shard_map/all_to_all | solution.py:471
  188.4 10.3 %all-to-all-done.2.partial = bf16[8,144,256]{2,1,0:T(8,128)(2,1)S(1)} async-done(((bf16[8,144,256]{2,1,0:T(8,128)(2,1)}), bf16[8,144,256]{2,1,0:T(8,128)(2,1)S(1)}, u32[]{:S(2)}, u32[]{:S(2)}) %all-to-all-start.2) | async-done | bytes 589856 | tf_op jit(solution)/shard_map/all_to_all | solution.py:471
  198.7 0.8 copy-done.1
  199.6 2.1 %final.1 = bf16[128,256]{1,0:T(8,128)(2,1)} custom-call(s32[1]{0:T(128)S(6)} %copy.15.count, bf16[8,144,256]{2,1,0:T(8,128)(2,1)} %copy-done.1, f32[1,256]{1,0:T(1,128)} %bitcast.25, f32[128,128]{1,0:T(8,128)} %get-tuple-element.58.cosine, f32[128,128]{1,0:T(8,128)} %get-tuple-element.59.sine, s32[1,128]{1,0:T(1,128)} %bitcast.26), custom_call_target="tpu_custom_call" | custom-call | tf_op jit(solution)/shard_map/final/pallas_call | solution.py:375
  (70 shorter events, 1.7 us)
Async XLA Ops:
  0.6 22.6 %collective-permute-start.1 = (bf16[1024,256]{1,0:T(8,128)(2,1)}, bf16[1024,256]{1,0:T(8,128)(2,1)S(1)}, u32[]{:S(2)}, u32[]{:S(2)}) collective-permute-start(bf16[1024,256]{1,0:T(8,128)(2,1)} %refs_0_.1), channel_id=1, source_target_pairs={{0,32},{32,64},{64,96},{96,128},{128,160},{160,192},{192,224},{224... | collective-permute-start | bytes 1572872 | tf_op jit(solution)/shard_map/ppermute | solution.py:390
  3.2 20.0 %collective-permute-start.3 = (bf16[1024,256]{1,0:T(8,128)(2,1)}, bf16[1024,256]{1,0:T(8,128)(2,1)}, u32[]{:S(2)}, u32[]{:S(2)}) collective-permute-start(bf16[1024,256]{1,0:T(8,128)(2,1)} %refs_0_.1), channel_id=1, source_target_pairs={{0,224},{32,0},{64,32},{96,64},{128,96},{160,128},{192,160},{224,1... | collective-permute-start | bytes 1572872 | tf_op jit(solution)/shard_map/ppermute | solution.py:390
  11.0 17.4 %collective-permute-start = (bf16[1024,128]{1,0:T(8,128)(2,1)}, bf16[1024,128]{1,0:T(8,128)(2,1)S(1)}, u32[]{:S(2)}, u32[]{:S(2)}) collective-permute-start(bf16[1024,128]{1,0:T(8,128)(2,1)} %bitcast.22), channel_id=1, source_target_pairs={{0,16},{16,0},{1,17},{17,1},{2,18},{18,2},{3,19},{19,3},{4,20},{20... | collective-permute-start | bytes 786440 | tf_op jit(solution)/shard_map/ppermute | solution.py:386
  12.3 10.9 %collective-permute-start.5 = (bf16[6,128,128]{2,1,0:T(8,128)(2,1)}, bf16[6,128,128]{2,1,0:T(8,128)(2,1)S(1)}, u32[]{:S(2)}, u32[]{:S(2)}) collective-permute-start(bf16[6,128,128]{2,1,0:T(8,128)(2,1)} %get-tuple-element.29.refs_0_), channel_id=1, source_target_pairs={{0,32},{32,64},{64,96},{96,128},{128,160},{160,192},{192,224},{224... | collective-permute-start | bytes 589832 | tf_op jit(solution)/shard_map/ppermute | solution.py:390
  12.3 10.9 %collective-permute-start.6 = (bf16[6,128,128]{2,1,0:T(8,128)(2,1)}, bf16[6,128,128]{2,1,0:T(8,128)(2,1)S(1)}, u32[]{:S(2)}, u32[]{:S(2)}) collective-permute-start(bf16[6,128,128]{2,1,0:T(8,128)(2,1)} %get-tuple-element.29.refs_0_), channel_id=1, source_target_pairs={{0,224},{32,0},{64,32},{96,64},{128,96},{160,128},{192,160},{224,1... | collective-permute-start | bytes 589832 | tf_op jit(solution)/shard_map/ppermute | solution.py:390
  23.2 11.8 %copy-start.15 = (bf16[6,128,128]{2,1,0:T(8,128)(2,1)}, bf16[6,128,128]{2,1,0:T(8,128)(2,1)S(1)}, u32[]{:S(2)}) copy-start(bf16[6,128,128]{2,1,0:T(8,128)(2,1)S(1)} %collective-permute-done.5.refs_1_) | copy-start | bytes 589828
  23.2 11.8 %copy-start.16 = (bf16[6,128,128]{2,1,0:T(8,128)(2,1)}, bf16[6,128,128]{2,1,0:T(8,128)(2,1)S(1)}, u32[]{:S(2)}) copy-start(bf16[6,128,128]{2,1,0:T(8,128)(2,1)S(1)} %collective-permute-done.6.refs_2_) | copy-start | bytes 589828
  23.2 11.8 %copy-start.10 = (bf16[1024,256]{1,0:T(8,128)(2,1)}, bf16[1024,256]{1,0:T(8,128)(2,1)S(1)}, u32[]{:S(2)}) copy-start(bf16[1024,256]{1,0:T(8,128)(2,1)S(1)} %collective-permute-done.1.refs_1_) | copy-start | bytes 1572868
  23.2 11.8 %collective-permute-start.7 = (bf16[6,128,128]{2,1,0:T(8,128)(2,1)S(1)}, bf16[6,128,128]{2,1,0:T(8,128)(2,1)S(1)}, u32[]{:S(2)}, u32[]{:S(2)}) collective-permute-start(bf16[6,128,128]{2,1,0:T(8,128)(2,1)S(1)} %collective-permute-done.6.refs_2_), channel_id=1, source_target_pairs={{0,224},{32,0},{64,32},{96,64},{128,96},{160,128},{192,160},{224,1... | collective-permute-start | bytes 589832 | tf_op jit(solution)/shard_map/ppermute | solution.py:390
  25.7 9.3 %collective-permute-start.8 = (bf16[6,128,128]{2,1,0:T(8,128)(2,1)S(1)}, bf16[6,128,128]{2,1,0:T(8,128)(2,1)S(1)}, u32[]{:S(2)}, u32[]{:S(2)}) collective-permute-start(bf16[6,128,128]{2,1,0:T(8,128)(2,1)S(1)} %collective-permute-done.5.refs_1_), channel_id=1, source_target_pairs={{0,32},{32,64},{64,96},{96,128},{128,160},{160,192},{192,224},{224... | collective-permute-start | bytes 589832 | tf_op jit(solution)/shard_map/ppermute | solution.py:390
  25.7 17.1 %collective-permute-start.2 = (bf16[1024,256]{1,0:T(8,128)(2,1)S(1)}, bf16[1024,256]{1,0:T(8,128)(2,1)}, u32[]{:S(2)}, u32[]{:S(2)}) collective-permute-start(bf16[1024,256]{1,0:T(8,128)(2,1)S(1)} %collective-permute-done.1.refs_1_), channel_id=1, source_target_pairs={{0,32},{32,64},{64,96},{96,128},{128,160},{160,192},{192,224},{224... | collective-permute-start | bytes 1572872 | tf_op jit(solution)/shard_map/ppermute | solution.py:390
  25.7 17.1 %collective-permute-start.4 = (bf16[1024,256]{1,0:T(8,128)(2,1)}, bf16[1024,256]{1,0:T(8,128)(2,1)}, u32[]{:S(2)}, u32[]{:S(2)}) collective-permute-start(bf16[1024,256]{1,0:T(8,128)(2,1)} %collective-permute-done.3.refs_2_), channel_id=1, source_target_pairs={{0,224},{32,0},{64,32},{96,64},{128,96},{160,128},{192,160},{224,1... | collective-permute-start | bytes 1572872 | tf_op jit(solution)/shard_map/ppermute | solution.py:390
  29.4 5.6 %copy-start.3 = (bf16[2048,128]{1,0:T(8,128)(2,1)}, bf16[2048,128]{1,0:T(8,128)(2,1)S(1)}, u32[]{:S(2)}) copy-start(bf16[2048,128]{1,0:T(8,128)(2,1)S(1)} %pad_maximum_fusion.query) | copy-start | bytes 1572868
  29.4 33.2 %collective-permute-start.13 = (bf16[2048,128]{1,0:T(8,128)(2,1)S(1)}, bf16[2048,128]{1,0:T(8,128)(2,1)}, u32[]{:S(2)}, u32[]{:S(2)}) collective-permute-start(bf16[2048,128]{1,0:T(8,128)(2,1)S(1)} %pad_maximum_fusion.query), channel_id=1, source_target_pairs={{0,8},{8,0},{1,9},{9,1},{2,10},{10,2},{3,11},{11,3},{4,12},{12,4},... | collective-permute-start | bytes 1572872 | tf_op jit(solution)/shard_map/ppermute | solution.py:386
  35.0 10.5 %copy-start.14 = (bf16[6,128,128]{2,1,0:T(8,128)(2,1)}, bf16[6,128,128]{2,1,0:T(8,128)(2,1)S(1)}, u32[]{:S(2)}) copy-start(bf16[6,128,128]{2,1,0:T(8,128)(2,1)S(1)} %collective-permute-done.7.refs_4_.refs_0_) | copy-start | bytes 589828
  35.0 0.7 copy-start.17
  35.8 92.1 %all-to-all-start = ((bf16[8,512,256]{2,1,0:T(8,128)(2,1)}), bf16[8,512,256]{2,1,0:T(8,128)(2,1)S(1)}, u32[]{:S(2)}, u32[]{:S(2)}) async-start(bf16[8,512,256]{2,1,0:T(8,128)(2,1)} %dynamic-slice_bitcast_fusion), calls=%async_computation | async-start | bytes 4194304 | tf_op jit(solution)/shard_map/all_to_all | solution.py:438
  42.8 29.0 %collective-permute-start.14 = (bf16[1024,256]{1,0:T(8,128)(2,1)}, bf16[1024,256]{1,0:T(8,128)(2,1)S(1)}, u32[]{:S(2)}, u32[]{:S(2)}) collective-permute-start(bf16[1024,256]{1,0:T(8,128)(2,1)} %collective-permute-done.2.refs_3_), channel_id=1, source_target_pairs={{0,32},{32,64},{64,96},{96,128},{128,160},{160,192},{192,224},{224... | collective-permute-start | bytes 1572872 | tf_op jit(solution)/shard_map/ppermute | solution.py:390
  42.8 29.0 %collective-permute-start.15 = (bf16[1024,256]{1,0:T(8,128)(2,1)}, bf16[1024,256]{1,0:T(8,128)(2,1)}, u32[]{:S(2)}, u32[]{:S(2)}) collective-permute-start(bf16[1024,256]{1,0:T(8,128)(2,1)} %collective-permute-done.4.refs_4_), channel_id=1, source_target_pairs={{0,224},{32,0},{64,32},{96,64},{128,96},{160,128},{192,160},{224,1... | collective-permute-start | bytes 1572872 | tf_op jit(solution)/shard_map/ppermute | solution.py:390
  45.5 13.6 %collective-permute-start.9 = (bf16[6,128,128]{2,1,0:T(8,128)(2,1)}, bf16[6,128,128]{2,1,0:T(8,128)(2,1)S(1)}, u32[]{:S(2)}, u32[]{:S(2)}) collective-permute-start(bf16[6,128,128]{2,1,0:T(8,128)(2,1)} %copy-done.17), channel_id=1, source_target_pairs={{0,32},{32,64},{64,96},{96,128},{128,160},{160,192},{192,224},{224... | collective-permute-start | bytes 589832 | tf_op jit(solution)/shard_map/ppermute | solution.py:390
  45.5 13.6 %collective-permute-start.10 = (bf16[6,128,128]{2,1,0:T(8,128)(2,1)S(1)}, bf16[6,128,128]{2,1,0:T(8,128)(2,1)S(1)}, u32[]{:S(2)}, u32[]{:S(2)}) collective-permute-start(bf16[6,128,128]{2,1,0:T(8,128)(2,1)S(1)} %collective-permute-done.7.refs_4_.refs_0_), channel_id=1, source_target_pairs={{0,224},{32,0},{64,32},{96,64},{128,96},{160,128},{192,160},{224,1... | collective-permute-start | bytes 589832 | tf_op jit(solution)/shard_map/ppermute | solution.py:390
  59.1 12.7 %copy-start.6 = (bf16[6,128,128]{2,1,0:T(8,128)(2,1)}, bf16[6,128,128]{2,1,0:T(8,128)(2,1)S(1)}, u32[]{:S(2)}) copy-start(bf16[6,128,128]{2,1,0:T(8,128)(2,1)S(1)} %collective-permute-done.9.refs_1_) | copy-start | bytes 589828
  59.1 12.7 %copy-start.7 = (bf16[6,128,128]{2,1,0:T(8,128)(2,1)}, bf16[6,128,128]{2,1,0:T(8,128)(2,1)S(1)}, u32[]{:S(2)}) copy-start(bf16[6,128,128]{2,1,0:T(8,128)(2,1)S(1)} %collective-permute-done.10.refs_2_) | copy-start | bytes 589828
  59.2 12.7 %collective-permute-start.11 = (bf16[3,128,128]{2,1,0:T(8,128)(2,1)S(1)}, bf16[3,128,128]{2,1,0:T(8,128)(2,1)S(1)}, u32[]{:S(2)}, u32[]{:S(2)}) collective-permute-start(bf16[3,128,128]{2,1,0:T(8,128)(2,1)S(1)} %slice.24), channel_id=1, source_target_pairs={{0,32},{32,64},{64,96},{96,128},{128,160},{160,192},{192,224},{224... | collective-permute-start | bytes 294920 | tf_op jit(solution)/shard_map/ppermute | solution.py:390
  62.5 9.3 %collective-permute-start.12 = (bf16[3,128,128]{2,1,0:T(8,128)(2,1)S(1)}, bf16[3,128,128]{2,1,0:T(8,128)(2,1)S(1)}, u32[]{:S(2)}, u32[]{:S(2)}) collective-permute-start(bf16[3,128,128]{2,1,0:T(8,128)(2,1)S(1)} %slice.25), channel_id=1, source_target_pairs={{0,224},{32,0},{64,32},{96,64},{128,96},{160,128},{192,160},{224,1... | collective-permute-start | bytes 294920 | tf_op jit(solution)/shard_map/ppermute | solution.py:390
  71.8 19.6 %copy-start.5 = (bf16[1024,256]{1,0:T(8,128)(2,1)}, bf16[1024,256]{1,0:T(8,128)(2,1)S(1)}, u32[]{:S(2)}) copy-start(bf16[1024,256]{1,0:T(8,128)(2,1)S(1)} %collective-permute-done.14.refs_5_) | copy-start | bytes 1572868
  71.9 0.7 copy-start.18
  72.6 0.6 copy-start.19
  87.9 22.7 %collective-permute-start.16 = (bf16[2048,128]{1,0:T(8,128)(2,1)}, bf16[2048,128]{1,0:T(8,128)(2,1)S(1)}, u32[]{:S(2)}, u32[]{:S(2)}) collective-permute-start(bf16[2048,128]{1,0:T(8,128)(2,1)} %get-tuple-element.43), channel_id=1, source_target_pairs={{0,8},{8,0},{1,9},{9,1},{2,10},{10,2},{3,11},{11,3},{4,12},{12,4},... | collective-permute-start | bytes 1572872 | tf_op jit(solution)/shard_map/ppermute | solution.py:386
  91.5 19.1 %collective-permute-start.18 = (bf16[512,256]{1,0:T(8,128)(2,1)S(1)}, bf16[512,256]{1,0:T(8,128)(2,1)S(1)}, u32[]{:S(2)}, u32[]{:S(2)}) collective-permute-start(bf16[512,256]{1,0:T(8,128)(2,1)S(1)} %slice.28), channel_id=1, source_target_pairs={{0,32},{32,64},{64,96},{96,128},{128,160},{160,192},{192,224},{224... | collective-permute-start | bytes 786440 | tf_op jit(solution)/shard_map/ppermute | solution.py:390
  92.6 18.0 %collective-permute-start.19 = (bf16[512,256]{1,0:T(8,128)(2,1)S(1)}, bf16[512,256]{1,0:T(8,128)(2,1)S(1)}, u32[]{:S(2)}, u32[]{:S(2)}) collective-permute-start(bf16[512,256]{1,0:T(8,128)(2,1)S(1)} %slice.29), channel_id=1, source_target_pairs={{0,224},{32,0},{64,32},{96,64},{128,96},{160,128},{192,160},{224,1... | collective-permute-start | bytes 786440 | tf_op jit(solution)/shard_map/ppermute | solution.py:390
  95.3 15.2 %collective-permute-start.17 = (f32[16,1,128]{2,1,0:T(1,128)}, f32[16,1,128]{2,1,0:T(1,128)S(1)}, u32[]{:S(2)}, u32[]{:S(2)}) collective-permute-start(f32[16,1,128]{2,1,0:T(1,128)} %get-tuple-element.44), channel_id=1, source_target_pairs={{0,8},{8,0},{1,9},{9,1},{2,10},{10,2},{3,11},{11,3},{4,12},{12,4},... | collective-permute-start | bytes 24584 | tf_op jit(solution)/shard_map/ppermute | solution.py:386
  110.5 0.6 copy-start.8
  110.6 24.5 %copy-start.12 = (bf16[512,256]{1,0:T(8,128)(2,1)}, bf16[512,256]{1,0:T(8,128)(2,1)S(1)}, u32[]{:S(2)}) copy-start(bf16[512,256]{1,0:T(8,128)(2,1)S(1)} %collective-permute-done.18.refs_7_) | copy-start | bytes 786436
  110.6 24.4 %copy-start.13 = (bf16[512,256]{1,0:T(8,128)(2,1)}, bf16[512,256]{1,0:T(8,128)(2,1)S(1)}, u32[]{:S(2)}) copy-start(bf16[512,256]{1,0:T(8,128)(2,1)S(1)} %collective-permute-done.19.refs_8_) | copy-start | bytes 786436
  110.6 0.9 copy-start.4
  113.9 13.9 %collective-permute-start.20 = (bf16[2048,128]{1,0:T(8,128)(2,1)}, bf16[2048,128]{1,0:T(8,128)(2,1)S(1)}, u32[]{:S(2)}, u32[]{:S(2)}) collective-permute-start(bf16[2048,128]{1,0:T(8,128)(2,1)} %get-tuple-element.46.own), channel_id=1, source_target_pairs={{0,16},{16,0},{1,17},{17,1},{2,18},{18,2},{3,19},{19,3},{4,20},{20... | collective-permute-start | bytes 1572872 | tf_op jit(solution)/shard_map/ppermute | solution.py:386
  115.2 12.6 %collective-permute-start.21 = (f32[16,1,128]{2,1,0:T(1,128)}, f32[16,1,128]{2,1,0:T(1,128)S(1)}, u32[]{:S(2)}, u32[]{:S(2)}) collective-permute-start(f32[16,1,128]{2,1,0:T(1,128)} %get-tuple-element.47.own_lse), channel_id=1, source_target_pairs={{0,16},{16,0},{1,17},{17,1},{2,18},{18,2},{3,19},{19,3},{4,20},{20... | collective-permute-start | bytes 24584 | tf_op jit(solution)/shard_map/ppermute | solution.py:386
  127.9 0.6 copy-start.9
  127.9 14.1 %copy-start = (bf16[8,512,256]{2,1,0:T(8,128)(2,1)}, bf16[8,512,256]{2,1,0:T(8,128)(2,1)S(1)}, u32[]{:S(2)}) copy-start(bf16[8,512,256]{2,1,0:T(8,128)(2,1)S(1)} %all-to-all-done.near) | copy-start | bytes 6291460
  128.5 0.9 copy-start.2
  131.8 3.3 %collective-permute-start.22 = (bf16[2,128,1024]{2,1,0:T(8,128)(2,1)}, bf16[2,128,1024]{2,1,0:T(8,128)(2,1)S(1)}, u32[]{:S(2)}, u32[]{:S(2)}) collective-permute-start(bf16[2,128,1024]{2,1,0:T(8,128)(2,1)} %merge_last.1.near), channel_id=1, source_target_pairs={{0,8},{8,0},{1,9},{9,1},{2,10},{10,2},{3,11},{11,3},{4,12},{12,4},... | collective-permute-start | bytes 1572872 | tf_op jit(solution)/shard_map/ppermute | solution.py:386
  132.6 16.9 %collective-permute-start.23 = (bf16[8,512,256]{2,1,0:T(8,128)(2,1)S(1)}, bf16[8,512,256]{2,1,0:T(8,128)(2,1)}, u32[]{:S(2)}, u32[]{:S(2)}) collective-permute-start(bf16[8,512,256]{2,1,0:T(8,128)(2,1)S(1)} %all-to-all-done.near), channel_id=1, source_target_pairs={{0,8},{8,0},{1,9},{9,1},{2,10},{10,2},{3,11},{11,3},{4,12},{12,4},... | collective-permute-start | bytes 6291464 | tf_op jit(solution)/shard_map/ppermute | solution.py:386
  135.0 0.8 copy-start.11
  142.0 37.3 %all-to-all-start.1 = ((bf16[32,128,256]{2,1,0:T(8,128)(2,1)}), bf16[32,128,256]{2,1,0:T(8,128)(2,1)}, u32[]{:S(2)}, u32[]{:S(2)}) async-start(bf16[32,128,256]{2,1,0:T(8,128)(2,1)} %bitcast.20), calls=%async_computation.1 | async-start | bytes 4194304 | tf_op jit(solution)/shard_map/all_to_all | solution.py:465
  184.2 14.5 %all-to-all-start.2 = ((bf16[8,144,256]{2,1,0:T(8,128)(2,1)}), bf16[8,144,256]{2,1,0:T(8,128)(2,1)S(1)}, u32[]{:S(2)}, u32[]{:S(2)}) async-start(bf16[8,144,256]{2,1,0:T(8,128)(2,1)} %get-tuple-element.51), calls=%async_computation.2 | async-start | bytes 1179648 | tf_op jit(solution)/shard_map/all_to_all | solution.py:471
  198.7 0.8 copy-start.1

commit v3 on v2

--- a/solution.py
+++ b/solution.py
@@ -53,7 +53,11 @@
     return x * cosine + pltpu.roll(x, HEAD // 2, 1) * sine
 
 
-def prepare_kernel(query, fresh, cached, cosine, sine, query_out, kv_out):
+def prepare_kernel(
+    place, query, fresh, cached, cosine, sine, weight, query_out, kv_out, weight_out, sem
+):
+    copy = pltpu.make_async_copy(weight.at[:, place[2]], weight_out, sem)
+    copy.start()
     cos, sin = cosine[...], sine[...]
     for g in range(GROUP):
         piece = query[:, g * HEAD : (g + 1) * HEAD].astype(jnp.float32)
@@ -64,19 +68,27 @@
     new_key = rotated(fresh[0].astype(jnp.float32), cos, sin).astype(jnp.bfloat16)
     kv_out[BLOCKS - 1] = jnp.transpose(new_key)
     kv_out[2 * BLOCKS - 1] = fresh[1]
-
-
-def prepare(query, fresh, cached, cosine, sine):
+    copy.wait()
+
+
+def prepare(place, query, fresh, cached, cosine, sine, weight):
+    vmem = pl.BlockSpec(memory_space=pltpu.VMEM)
     return pl.pallas_call(
         prepare_kernel,
+        in_specs=[pl.BlockSpec(memory_space=pltpu.SMEM)]
+        + [vmem] * 5
+        + [pl.BlockSpec(memory_space=pl.ANY)],
+        out_specs=(vmem, vmem, pl.BlockSpec(memory_space=pl.ANY)),
         out_shape=(
             jax.ShapeDtypeStruct((GROUP, ROWS, HEAD), jnp.bfloat16),
             jax.ShapeDtypeStruct((2 * BLOCKS, ROWS, HEAD), jnp.bfloat16),
+            jax.ShapeDtypeStruct((Z, *weight.shape[2:]), jnp.bfloat16),
         ),
+        scratch_shapes=[pltpu.SemaphoreType.DMA],
         compiler_params=params(),
         name="prepare",
-        cost_estimate=pl.CostEstimate(flops=2_000_000, bytes_accessed=1_500_000, transcendentals=0),
-    )(query, fresh, cached, cosine, sine)
+        cost_estimate=pl.CostEstimate(flops=2_000_000, bytes_accessed=5_500_000, transcendentals=0),
+    )(place, query, fresh, cached, cosine, sine, weight)
 
 
 def column_of(row):
@@ -131,7 +143,7 @@
         m = jnp.full((CHUNK, 1), -1e30, jnp.float32)
         acc = jnp.zeros((CHUNK, 2 * HEAD), jnp.float32)
     else:
-        m = m_in[:, 0:1]
+        m = jnp.max(m_in[...], axis=1, keepdims=True)
         acc = acc_in[...]
     for i in range(steps):
         at = slice(i * 2 * ROWS, (i + 1) * 2 * ROWS)
@@ -420,34 +432,39 @@
     place = jnp.stack([z, yl, c]).astype(jnp.int32)
 
     cosine, sine = tables(positions, HEAD)
-    rotated_query, kv = prepare(query, fresh_key_value, cached_key_value, cosine, sine)
+    rotated_query, kv, third_rows = prepare(
+        place,
+        query,
+        fresh_key_value,
+        cached_key_value,
+        cosine,
+        sine,
+        layer3_key_value_weight.reshape(Z, 2, MODEL_WIDTH // Z // 2, 2 * HEAD),
+    )
     weights_1 = step([out_weight, out_weight])
     kv_1 = list(after(step([kv, kv]), *weights_1))
     kv_2 = step(kv_1)
     weights_2 = step(weights_1)
     kv_3 = step(kv_2)
+    weights_2 = list(after(weights_2, *kv_3))
     weights_3 = step(weights_2)
     weights_4 = last_step(weights_3)
     weights = [out_weight, *weights_1, *weights_2, *weights_3, *weights_4]
     rotated_query = rotated_query.reshape(GROUP * ROWS, HEAD)
     near_query = jnp.concatenate([rotated_query, swap(rotated_query, "yl")], axis=0)
     far_query = swap(near_query, "c")
-    third_rows = layer3_key_value_weight.reshape(Z, 2, MODEL_WIDTH // Z // 2, 2 * HEAD)
-    third_rows = lax.dynamic_index_in_dim(third_rows, c, axis=1, keepdims=False)
-    third_rows = after(third_rows, *kv_2, near_query)
-    third_near = lax.all_to_all(third_rows, HEAD_AXES, 0, 0, tiled=True)
-    third_far = swap(third_near, "c")
-
     early = [kv, *kv_1, *kv_2]
     early_cached = [(i, i) for i in range(5)]
     early_fresh = [[(0, 0, 0), (1, 1, -1)], [(2, 2, 1), (3, 3, -2)]]
     late_cached = [(1, 1), (2, 2), (3, 4)]
     late_fresh = [[(0, 0, 2), (1, 1, -3)], [(2, 2, 3), (3, 4, 4)]]
-    near_query = after(near_query, *weights_2)
     near_state = attend(place, 0, near_query, early, early_cached, early_fresh)
     kv_3 = list(after(kv_3, near_state))
     late = [kv_2[1], *kv_3, *last_step(kv_3)]
-    far_query = after(far_query, near_state)
+    far_query = after(far_query, near_state, *weights_2)
+    third_rows = after(third_rows, *kv_3)
+    third_near = lax.all_to_all(third_rows, HEAD_AXES, 0, 0, tiled=True)
+    third_far = swap(third_near, "c")
     far_state = attend(place, 1, far_query, early, early_cached, early_fresh)
     far_state = after(far_state, *weights_3)
     send, send_lse = attend(place, 1, far_query, late, late_cached, late_fresh, far_state, True)

time: 202 us -> 245 us (1.21)
  Pallas kernels: 67.6 us -> 119 us
  waiting for transfers between devices: 64.8 us -> 59.6 us
  local copies, waits for them, and re-layouts: 10.3 us -> 5.5 us
    pallas_call x1, Pallas kernels: 1.98 us -> 66.5 us  [prepare(): pl.pallas_call(prepare_kernel, in_specs=[pl.BlockSpec(memory_space=pltpu....]
    pallas_call x4, Pallas kernels: 47.7 us -> 34.3 us  [attend(): pl.pallas_call(functools.partial(attend_kernel, cached, fresh, state is N...]
    ppermute x16, waiting for transfers between devices: 9.76 us -> 4.58 us  [along_z(): return lax.ppermute(x, 'z', [(i, (i + distance) % Z) for i in range(Z)])]
    squeeze x1 -> x0, local copies, waits for them, and re-layouts: 3.08 us -> none  [local(): third_rows = lax.dynamic_index_in_dim(third_rows, c, axis=1, keepdims=False)]
    unnamed x40 -> x42, local copies, waits for them, and re-layouts: 6.19 us -> 5.44 us
  transfers between devices with their start and end apart: 27 -> 27, of which waited for: 7 -> 7; matrix products, arithmetic and copies ran while one was open for 4% -> 1% of each run, Pallas kernels for 29% -> 45%
where the time goes in v3:
time: 245 us; the launch traced here: 244 us
  Pallas kernels  119 us (49%)
  waiting for transfers between devices  59.6 us (24%)
  starting transfers between devices  55.1 us (22%)
  local copies, waits for them, and re-layouts  5.5 us (2%)
  other arithmetic  3.46 us (1%)
    pallas_call x1, Pallas kernels, prepare(): pl.pallas_call(prepare_kernel, in_specs=[pl.BlockSpec(memory_space=pltpu....  66.5 us
    pallas_call x4, Pallas kernels, attend(): pl.pallas_call(functools.partial(attend_kernel, cached, fresh, state is N...  34.3 us
    all_to_all x1, waiting for transfers between devices, local(): lax.all_to_all(products, ('yl', 'c', 'x', 'yh'), 0, 0, tiled=True)  29.8 us
    ppermute x16, starting transfers between devices, along_z(): return lax.ppermute(x, 'z', [(i, (i + distance) % Z) for i in range(Z)])  25.9 us
    ppermute x8, waiting for transfers between devices, swap(): return lax.ppermute(x, axis, [(0, 1), (1, 0)])  14.9 us
    ppermute x8, starting transfers between devices, swap(): return lax.ppermute(x, axis, [(0, 1), (1, 0)])  11.5 us
    all_to_all x1, waiting for transfers between devices, local(): partial = lax.all_to_all(partial, HEAD_AXES, 0, 0, tiled=True)  10.3 us
    all_to_all x1, starting transfers between devices, local(): lax.all_to_all(products, ('yl', 'c', 'x', 'yh'), 0, 0, tiled=True)  7.51 us
  transfers between devices with their start and end apart: 27, of which 7 were waited for; matrix products, arithmetic and copies ran while one was open for 1% of the time, Pallas kernels for 45%

profile of v3, /device:TPU:1, one launch (start us, length us, event | category | flops | bytes accessed | tf_op | source)
XLA Modules:
  0.0 244.1 jit_solution(1835697722209529822)
XLA Ops:
  0.6 2.5 %collective-permute-start.3 = (bf16[1024,256]{1,0:T(8,128)(2,1)}, bf16[1024,256]{1,0:T(8,128)(2,1)S(1)}, u32[]{:S(2)}, u32[]{:S(2)}) collective-permute-start(bf16[1024,256]{1,0:T(8,128)(2,1)} %refs_0_.1), channel_id=1, source_target_pairs={{0,32},{32,64},{64,96},{96,128},{128,160},{160,192},{192,224},{224... | collective-permute-start | bytes 1572872 | tf_op jit(solution)/shard_map/ppermute | solution.py:402
  3.2 4.0 %collective-permute-start.4 = (bf16[1024,256]{1,0:T(8,128)(2,1)}, bf16[1024,256]{1,0:T(8,128)(2,1)}, u32[]{:S(2)}, u32[]{:S(2)}) collective-permute-start(bf16[1024,256]{1,0:T(8,128)(2,1)} %refs_0_.1), channel_id=1, source_target_pairs={{0,224},{32,0},{64,32},{96,64},{128,96},{160,128},{192,160},{224,1... | collective-permute-start | bytes 1572872 | tf_op jit(solution)/shard_map/ppermute | solution.py:402
  7.2 0.7 convert_element_type.36
  7.9 0.7 pad_add_fusion.place
  8.9 0.8 pad_maximum_fusion.1
  9.7 66.5 %prepare.1 = (bf16[8,128,128]{2,1,0:T(8,128)(2,1)}, bf16[6,128,128]{2,1,0:T(8,128)(2,1)}, bf16[8,512,256]{2,1,0:T(8,128)(2,1)}) custom-call(s32[3]{0:T(128)} %pad_add_fusion.place, bf16[128,1024]{1,0:T(8,128)(2,1)} %query.1, bf16[2,128,128]{2,1,0:T(8,128)(2,1)} %fresh.1, bf16[2,256,128]{2,1,0:T(8,128)(2,1)} %cached.1, f32[128,128]{1,0:T(8,128)} %get-tuple-element.62.cosine, ...), custom_call_target="tpu_custom_call" | custom-call | flops 2000000 | bytes 5500000 | tf_op jit(solution)/shard_map/prepare/pallas_call | solution.py:76
  76.3 2.7 %collective-permute-start.2 = (bf16[6,128,128]{2,1,0:T(8,128)(2,1)}, bf16[6,128,128]{2,1,0:T(8,128)(2,1)S(1)}, u32[]{:S(2)}, u32[]{:S(2)}) collective-permute-start(bf16[6,128,128]{2,1,0:T(8,128)(2,1)} %get-tuple-element.30.refs_0_), channel_id=1, source_target_pairs={{0,224},{32,0},{64,32},{96,64},{128,96},{160,128},{192,160},{224,1... | collective-permute-start | bytes 589832 | tf_op jit(solution)/shard_map/ppermute | solution.py:402
  78.9 1.3 collective-permute-start
  80.2 2.9 %collective-permute-done.1.refs_1_ = bf16[6,128,128]{2,1,0:T(8,128)(2,1)S(1)} collective-permute-done((bf16[6,128,128]{2,1,0:T(8,128)(2,1)}, bf16[6,128,128]{2,1,0:T(8,128)(2,1)S(1)}, u32[]{:S(2)}, u32[]{:S(2)}) %collective-permute-start.1) | collective-permute-done | bytes 196640 | tf_op jit(solution)/shard_map/ppermute | solution.py:402
  83.3 2.7 %collective-permute-start.5 = (bf16[6,128,128]{2,1,0:T(8,128)(2,1)S(1)}, bf16[6,128,128]{2,1,0:T(8,128)(2,1)S(1)}, u32[]{:S(2)}, u32[]{:S(2)}) collective-permute-start(bf16[6,128,128]{2,1,0:T(8,128)(2,1)S(1)} %collective-permute-done.2.refs_2_), channel_id=1, source_target_pairs={{0,224},{32,0},{64,32},{96,64},{128,96},{160,128},{192,160},{224,1... | collective-permute-start | bytes 589832 | tf_op jit(solution)/shard_map/ppermute | solution.py:402
  85.9 2.7 %collective-permute-start.13 = (bf16[1024,256]{1,0:T(8,128)(2,1)}, bf16[1024,256]{1,0:T(8,128)(2,1)}, u32[]{:S(2)}, u32[]{:S(2)}) collective-permute-start(bf16[1024,256]{1,0:T(8,128)(2,1)} %collective-permute-done.4.refs_2_), channel_id=1, source_target_pairs={{0,224},{32,0},{64,32},{96,64},{128,96},{160,128},{192,160},{224,1... | collective-permute-start | bytes 1572872 | tf_op jit(solution)/shard_map/ppermute | solution.py:402
  88.6 0.4 collective-permute-done.6.refs_3_
  89.0 2.7 %collective-permute-start.8 = (bf16[6,128,128]{2,1,0:T(8,128)(2,1)S(1)}, bf16[6,128,128]{2,1,0:T(8,128)(2,1)S(1)}, u32[]{:S(2)}, u32[]{:S(2)}) collective-permute-start(bf16[6,128,128]{2,1,0:T(8,128)(2,1)S(1)} %collective-permute-done.5.refs_4_.refs_0_), channel_id=1, source_target_pairs={{0,224},{32,0},{64,32},{96,64},{128,96},{160,128},{192,160},{224,1... | collective-permute-start | bytes 589832 | tf_op jit(solution)/shard_map/ppermute | solution.py:402
  91.7 1.0 pad_maximum_fusion.query
  92.7 5.5 %collective-permute-start.11 = (bf16[2048,128]{1,0:T(8,128)(2,1)S(1)}, bf16[2048,128]{1,0:T(8,128)(2,1)}, u32[]{:S(2)}, u32[]{:S(2)}) collective-permute-start(bf16[2048,128]{1,0:T(8,128)(2,1)S(1)} %pad_maximum_fusion.query), channel_id=1, source_target_pairs={{0,8},{8,0},{1,9},{9,1},{2,10},{10,2},{3,11},{11,3},{4,12},{12,4},... | collective-permute-start | bytes 1572872 | tf_op jit(solution)/shard_map/ppermute | solution.py:398
  98.2 9.2 %attend.4 = (f32[2048,256]{1,0:T(8,128)}, f32[2048,128]{1,0:T(8,128)}) custom-call(s32[3]{0:T(128)} %pad_add_fusion.place, bf16[2048,128]{1,0:T(8,128)(2,1)} %copy-done.3, bf16[6,128,128]{2,1,0:T(8,128)(2,1)} %get-tuple-element.30.refs_0_, bf16[6,128,128]{2,1,0:T(8,128)(2,1)} %copy-done.16, bf16[6,128,128]{2,1,0:T(8,128)(2,1)} %copy-done.17, ...), custom_call_target="tpu_custom_call" | custom-call | flops 1879048192 | bytes 3014656 | tf_op jit(solution)/shard_map/attend/pallas_call | solution.py:195
  107.4 6.7 %all-to-all-start = ((bf16[8,512,256]{2,1,0:T(8,128)(2,1)}), bf16[8,512,256]{2,1,0:T(8,128)(2,1)S(1)}, u32[]{:S(2)}, u32[]{:S(2)}) async-start(bf16[8,512,256]{2,1,0:T(8,128)(2,1)} %get-tuple-element.52), calls=%async_computation | async-start | bytes 4194304 | tf_op jit(solution)/shard_map/all_to_all | solution.py:466
  114.4 2.7 %collective-permute-start.15 = (bf16[1024,256]{1,0:T(8,128)(2,1)}, bf16[1024,256]{1,0:T(8,128)(2,1)S(1)}, u32[]{:S(2)}, u32[]{:S(2)}) collective-permute-start(bf16[1024,256]{1,0:T(8,128)(2,1)} %collective-permute-done.13.refs_4_), channel_id=1, source_target_pairs={{0,224},{32,0},{64,32},{96,64},{128,96},{160,128},{192,160},{224,1... | collective-permute-start | bytes 1572872 | tf_op jit(solution)/shard_map/ppermute | solution.py:402
  117.2 2.7 %collective-permute-start.10 = (bf16[3,128,128]{2,1,0:T(8,128)(2,1)S(1)}, bf16[3,128,128]{2,1,0:T(8,128)(2,1)S(1)}, u32[]{:S(2)}, u32[]{:S(2)}) collective-permute-start(bf16[3,128,128]{2,1,0:T(8,128)(2,1)S(1)} %slice.25), channel_id=1, source_target_pairs={{0,224},{32,0},{64,32},{96,64},{128,96},{160,128},{192,160},{224,1... | collective-permute-start | bytes 294920 | tf_op jit(solution)/shard_map/ppermute | solution.py:402
  119.8 9.2 %attend.6 = (f32[2048,256]{1,0:T(8,128)}, f32[2048,128]{1,0:T(8,128)}) custom-call(s32[3]{0:T(128)} %pad_add_fusion.place, bf16[2048,128]{1,0:T(8,128)(2,1)} %collective-permute-done.11.query, bf16[6,128,128]{2,1,0:T(8,128)(2,1)} %get-tuple-element.30.refs_0_, bf16[6,128,128]{2,1,0:T(8,128)(2,1)} %copy-done.16, bf16[6,128,128]{2,1,0:T(8,128)(2,1)} %copy-done.17, ...), custom_call_target="tpu_custom_call" | custom-call | flops 1879048192 | bytes 3014656 | tf_op jit(solution)/shard_map/attend/pallas_call | solution.py:195
  129.1 1.3 collective-permute-done.9.refs_3_
  130.3 0.6 copy-done.19
  131.0 0.6 copy-done.20
  131.6 8.0 %attend.7 = (bf16[2048,128]{1,0:T(8,128)(2,1)}, f32[16,1,128]{2,1,0:T(1,128)}) custom-call(s32[3]{0:T(128)} %pad_add_fusion.place, bf16[2048,128]{1,0:T(8,128)(2,1)} %collective-permute-done.11.query, bf16[6,128,128]{2,1,0:T(8,128)(2,1)} %copy-done.15, bf16[6,128,128]{2,1,0:T(8,128)(2,1)} %copy-done.7, bf16[6,128,128]{2,1,0:T(8,128)(2,1)} %copy-done.8, ...), custom_call_target="tpu_custom_call" | custom-call | flops 1342177280 | bytes 2752512 | tf_op jit(solution)/shard_map/attend/pallas_call | solution.py:195
  139.6 1.9 collective-permute-start.16
  141.6 2.7 %collective-permute-start.19 = (bf16[512,256]{1,0:T(8,128)(2,1)S(1)}, bf16[512,256]{1,0:T(8,128)(2,1)S(1)}, u32[]{:S(2)}, u32[]{:S(2)}) collective-permute-start(bf16[512,256]{1,0:T(8,128)(2,1)S(1)} %slice.29), channel_id=1, source_target_pairs={{0,224},{32,0},{64,32},{96,64},{128,96},{160,128},{192,160},{224,1... | collective-permute-start | bytes 786440 | tf_op jit(solution)/shard_map/ppermute | solution.py:402
  144.3 0.6 collective-permute-start.17
  144.9 8.0 %attend.5 = (bf16[2048,128]{1,0:T(8,128)(2,1)}, f32[16,1,128]{2,1,0:T(1,128)}) custom-call(s32[3]{0:T(128)} %pad_add_fusion.place, bf16[2048,128]{1,0:T(8,128)(2,1)} %copy-done.3, bf16[6,128,128]{2,1,0:T(8,128)(2,1)} %copy-done.15, bf16[6,128,128]{2,1,0:T(8,128)(2,1)} %copy-done.7, bf16[6,128,128]{2,1,0:T(8,128)(2,1)} %copy-done.8, ...), custom_call_target="tpu_custom_call" | custom-call | flops 1342177280 | bytes 2752512 | tf_op jit(solution)/shard_map/attend/pallas_call | solution.py:195
  153.0 0.5 copy-done.9
  153.5 0.4 copy-done.4
  153.9 2.4 merge.1
  156.3 0.4 collective-permute-start.20
  156.7 1.1 collective-permute-start.21
  157.8 12.5 %collective-permute-done.21.other_lse = f32[16,1,128]{2,1,0:T(1,128)S(1)} collective-permute-done((f32[16,1,128]{2,1,0:T(1,128)}, f32[16,1,128]{2,1,0:T(1,128)S(1)}, u32[]{:S(2)}, u32[]{:S(2)}) %collective-permute-start.21) | collective-permute-done | bytes 8224 | tf_op jit(solution)/shard_map/ppermute | solution.py:398
  170.3 0.6 copy-done.10
  170.8 1.0 copy-done.2
  171.8 2.4 merge_last.1.near
  174.2 0.8 collective-permute-start.22
  175.0 2.5 %collective-permute-done.22.far = bf16[2,128,1024]{2,1,0:T(8,128)(2,1)S(1)} collective-permute-done((bf16[2,128,1024]{2,1,0:T(8,128)(2,1)}, bf16[2,128,1024]{2,1,0:T(8,128)(2,1)S(1)}, u32[]{:S(2)}, u32[]{:S(2)}) %collective-permute-start.22) | collective-permute-done | bytes 524320 | tf_op jit(solution)/shard_map/ppermute | solution.py:398
  177.4 0.8 copy-done.12
  178.2 6.2 %project.1 = bf16[4,8,128,256]{3,2,1,0:T(8,128)(2,1)} custom-call(s32[3]{0:T(128)} %pad_add_fusion.place, bf16[2,128,1024]{2,1,0:T(8,128)(2,1)} %merge_last.1.near, bf16[2,128,1024]{2,1,0:T(8,128)(2,1)} %copy-done.12, bf16[1024,256]{1,0:T(8,128)(2,1)} %refs_0_.1, bf16[1024,256]{1,0:T(8,128)(2,1)} %copy-done.11, ...), custom_call_target="tpu_custom_call" | custom-call | flops 2147483648 | bytes 4000000 | tf_op jit(solution)/shard_map/project/pallas_call | solution.py:297
  184.4 7.5 %all-to-all-start.1 = ((bf16[32,128,256]{2,1,0:T(8,128)(2,1)}), bf16[32,128,256]{2,1,0:T(8,128)(2,1)}, u32[]{:S(2)}, u32[]{:S(2)}) async-start(bf16[32,128,256]{2,1,0:T(8,128)(2,1)} %bitcast.17), calls=%async_computation.1 | async-start | bytes 4194304 | tf_op jit(solution)/shard_map/all_to_all | solution.py:482
  191.9 29.8 %all-to-all-done.1 = bf16[32,128,256]{2,1,0:T(8,128)(2,1)} async-done(((bf16[32,128,256]{2,1,0:T(8,128)(2,1)}), bf16[32,128,256]{2,1,0:T(8,128)(2,1)}, u32[]{:S(2)}, u32[]{:S(2)}) %all-to-all-start.1) | async-done | bytes 2097184 | tf_op jit(solution)/shard_map/all_to_all | solution.py:482
  221.7 4.9 %third.1 = (bf16[128,1024]{1,0:T(8,128)(2,1)}, bf16[8,144,256]{2,1,0:T(8,128)(2,1)}) custom-call(s32[3]{0:T(128)} %pad_add_fusion.place, bf16[4,8,128,256]{3,2,1,0:T(8,128)(2,1)} %bitcast.9.received, bf16[128,1024]{1,0:T(8,128)(2,1)} %hidden.1, f32[1,1024]{1,0:T(1,128)} %bitcast.20, bf16[8,512,256]{2,1,0:T(8,128)(2,1)} %copy-done, ...), custom_call_target="tpu_custom_call" | custom-call | tf_op jit(solution)/shard_map/third/pallas_call | solution.py:350
  226.7 3.5 %all-to-all-start.2 = ((bf16[8,144,256]{2,1,0:T(8,128)(2,1)}), bf16[8,144,256]{2,1,0:T(8,128)(2,1)S(1)}, u32[]{:S(2)}, u32[]{:S(2)}) async-start(bf16[8,144,256]{2,1,0:T(8,128)(2,1)} %get-tuple-element.55), calls=%async_computation.2 | async-start | bytes 1179648 | tf_op jit(solution)/shard_map/all_to_all | solution.py:488
  230.9 10.3 %all-to-all-done.2.partial = bf16[8,144,256]{2,1,0:T(8,128)(2,1)S(1)} async-done(((bf16[8,144,256]{2,1,0:T(8,128)(2,1)}), bf16[8,144,256]{2,1,0:T(8,128)(2,1)S(1)}, u32[]{:S(2)}, u32[]{:S(2)}) %all-to-all-start.2) | async-done | bytes 589856 | tf_op jit(solution)/shard_map/all_to_all | solution.py:488
  241.2 0.8 copy-done.1
  242.0 2.1 final.1
  (71 shorter events, 1.2 us)
Async XLA Ops:
  0.6 82.5 %collective-permute-start.3 = (bf16[1024,256]{1,0:T(8,128)(2,1)}, bf16[1024,256]{1,0:T(8,128)(2,1)S(1)}, u32[]{:S(2)}, u32[]{:S(2)}) collective-permute-start(bf16[1024,256]{1,0:T(8,128)(2,1)} %refs_0_.1), channel_id=1, source_target_pairs={{0,32},{32,64},{64,96},{96,128},{128,160},{160,192},{192,224},{224... | collective-permute-start | bytes 1572872 | tf_op jit(solution)/shard_map/ppermute | solution.py:402
  3.2 80.0 %collective-permute-start.4 = (bf16[1024,256]{1,0:T(8,128)(2,1)}, bf16[1024,256]{1,0:T(8,128)(2,1)}, u32[]{:S(2)}, u32[]{:S(2)}) collective-permute-start(bf16[1024,256]{1,0:T(8,128)(2,1)} %refs_0_.1), channel_id=1, source_target_pairs={{0,224},{32,0},{64,32},{96,64},{128,96},{160,128},{192,160},{224,1... | collective-permute-start | bytes 1572872 | tf_op jit(solution)/shard_map/ppermute | solution.py:402
  76.2 7.0 %collective-permute-start.1 = (bf16[6,128,128]{2,1,0:T(8,128)(2,1)}, bf16[6,128,128]{2,1,0:T(8,128)(2,1)S(1)}, u32[]{:S(2)}, u32[]{:S(2)}) collective-permute-start(bf16[6,128,128]{2,1,0:T(8,128)(2,1)} %get-tuple-element.30.refs_0_), channel_id=1, source_target_pairs={{0,32},{32,64},{64,96},{96,128},{128,160},{160,192},{192,224},{224... | collective-permute-start | bytes 589832 | tf_op jit(solution)/shard_map/ppermute | solution.py:402
  76.3 6.9 %collective-permute-start.2 = (bf16[6,128,128]{2,1,0:T(8,128)(2,1)}, bf16[6,128,128]{2,1,0:T(8,128)(2,1)S(1)}, u32[]{:S(2)}, u32[]{:S(2)}) collective-permute-start(bf16[6,128,128]{2,1,0:T(8,128)(2,1)} %get-tuple-element.30.refs_0_), channel_id=1, source_target_pairs={{0,224},{32,0},{64,32},{96,64},{128,96},{160,128},{192,160},{224,1... | collective-permute-start | bytes 589832 | tf_op jit(solution)/shard_map/ppermute | solution.py:402
  78.9 12.7 %collective-permute-start = (bf16[1024,128]{1,0:T(8,128)(2,1)}, bf16[1024,128]{1,0:T(8,128)(2,1)S(1)}, u32[]{:S(2)}, u32[]{:S(2)}) collective-permute-start(bf16[1024,128]{1,0:T(8,128)(2,1)} %bitcast.18), channel_id=1, source_target_pairs={{0,16},{16,0},{1,17},{17,1},{2,18},{18,2},{3,19},{19,3},{4,20},{20... | collective-permute-start | bytes 786440 | tf_op jit(solution)/shard_map/ppermute | solution.py:398
  83.1 15.0 %copy-start.16 = (bf16[6,128,128]{2,1,0:T(8,128)(2,1)}, bf16[6,128,128]{2,1,0:T(8,128)(2,1)S(1)}, u32[]{:S(2)}) copy-start(bf16[6,128,128]{2,1,0:T(8,128)(2,1)S(1)} %collective-permute-done.1.refs_1_) | copy-start | bytes 589828
  83.1 15.0 %copy-start.17 = (bf16[6,128,128]{2,1,0:T(8,128)(2,1)}, bf16[6,128,128]{2,1,0:T(8,128)(2,1)S(1)}, u32[]{:S(2)}) copy-start(bf16[6,128,128]{2,1,0:T(8,128)(2,1)S(1)} %collective-permute-done.2.refs_2_) | copy-start | bytes 589828
  83.1 24.2 %copy-start.11 = (bf16[1024,256]{1,0:T(8,128)(2,1)}, bf16[1024,256]{1,0:T(8,128)(2,1)S(1)}, u32[]{:S(2)}) copy-start(bf16[1024,256]{1,0:T(8,128)(2,1)S(1)} %collective-permute-done.3.refs_1_) | copy-start | bytes 1572868
  83.2 5.8 %collective-permute-start.6 = (bf16[6,128,128]{2,1,0:T(8,128)(2,1)S(1)}, bf16[6,128,128]{2,1,0:T(8,128)(2,1)S(1)}, u32[]{:S(2)}, u32[]{:S(2)}) collective-permute-start(bf16[6,128,128]{2,1,0:T(8,128)(2,1)S(1)} %collective-permute-done.1.refs_1_), channel_id=1, source_target_pairs={{0,32},{32,64},{64,96},{96,128},{128,160},{160,192},{192,224},{224... | collective-permute-start | bytes 589832 | tf_op jit(solution)/shard_map/ppermute | solution.py:402
  83.3 5.7 %collective-permute-start.5 = (bf16[6,128,128]{2,1,0:T(8,128)(2,1)S(1)}, bf16[6,128,128]{2,1,0:T(8,128)(2,1)S(1)}, u32[]{:S(2)}, u32[]{:S(2)}) collective-permute-start(bf16[6,128,128]{2,1,0:T(8,128)(2,1)S(1)} %collective-permute-done.2.refs_2_), channel_id=1, source_target_pairs={{0,224},{32,0},{64,32},{96,64},{128,96},{160,128},{192,160},{224,1... | collective-permute-start | bytes 589832 | tf_op jit(solution)/shard_map/ppermute | solution.py:402
  85.9 28.2 %collective-permute-start.12 = (bf16[1024,256]{1,0:T(8,128)(2,1)S(1)}, bf16[1024,256]{1,0:T(8,128)(2,1)}, u32[]{:S(2)}, u32[]{:S(2)}) collective-permute-start(bf16[1024,256]{1,0:T(8,128)(2,1)S(1)} %collective-permute-done.3.refs_1_), channel_id=1, source_target_pairs={{0,32},{32,64},{64,96},{96,128},{128,160},{160,192},{192,224},{224... | collective-permute-start | bytes 1572872 | tf_op jit(solution)/shard_map/ppermute | solution.py:402
  85.9 28.2 %collective-permute-start.13 = (bf16[1024,256]{1,0:T(8,128)(2,1)}, bf16[1024,256]{1,0:T(8,128)(2,1)}, u32[]{:S(2)}, u32[]{:S(2)}) collective-permute-start(bf16[1024,256]{1,0:T(8,128)(2,1)} %collective-permute-done.4.refs_2_), channel_id=1, source_target_pairs={{0,224},{32,0},{64,32},{96,64},{128,96},{160,128},{192,160},{224,1... | collective-permute-start | bytes 1572872 | tf_op jit(solution)/shard_map/ppermute | solution.py:402
  89.0 9.2 %copy-start.18 = (bf16[6,128,128]{2,1,0:T(8,128)(2,1)}, bf16[6,128,128]{2,1,0:T(8,128)(2,1)S(1)}, u32[]{:S(2)}) copy-start(bf16[6,128,128]{2,1,0:T(8,128)(2,1)S(1)} %collective-permute-done.6.refs_3_) | copy-start | bytes 589828
  89.0 18.4 %collective-permute-start.7 = (bf16[6,128,128]{2,1,0:T(8,128)(2,1)S(1)}, bf16[6,128,128]{2,1,0:T(8,128)(2,1)S(1)}, u32[]{:S(2)}, u32[]{:S(2)}) collective-permute-start(bf16[6,128,128]{2,1,0:T(8,128)(2,1)S(1)} %collective-permute-done.6.refs_3_), channel_id=1, source_target_pairs={{0,32},{32,64},{64,96},{96,128},{128,160},{160,192},{192,224},{224... | collective-permute-start | bytes 589832 | tf_op jit(solution)/shard_map/ppermute | solution.py:402
  89.0 9.2 %copy-start.15 = (bf16[6,128,128]{2,1,0:T(8,128)(2,1)}, bf16[6,128,128]{2,1,0:T(8,128)(2,1)S(1)}, u32[]{:S(2)}) copy-start(bf16[6,128,128]{2,1,0:T(8,128)(2,1)S(1)} %collective-permute-done.5.refs_4_.refs_0_) | copy-start | bytes 589828
  89.0 18.4 %collective-permute-start.8 = (bf16[6,128,128]{2,1,0:T(8,128)(2,1)S(1)}, bf16[6,128,128]{2,1,0:T(8,128)(2,1)S(1)}, u32[]{:S(2)}, u32[]{:S(2)}) collective-permute-start(bf16[6,128,128]{2,1,0:T(8,128)(2,1)S(1)} %collective-permute-done.5.refs_4_.refs_0_), channel_id=1, source_target_pairs={{0,224},{32,0},{64,32},{96,64},{128,96},{160,128},{192,160},{224,1... | collective-permute-start | bytes 589832 | tf_op jit(solution)/shard_map/ppermute | solution.py:402
  92.7 5.5 %copy-start.3 = (bf16[2048,128]{1,0:T(8,128)(2,1)}, bf16[2048,128]{1,0:T(8,128)(2,1)S(1)}, u32[]{:S(2)}) copy-start(bf16[2048,128]{1,0:T(8,128)(2,1)S(1)} %pad_maximum_fusion.query) | copy-start | bytes 1572868
  92.7 27.2 %collective-permute-start.11 = (bf16[2048,128]{1,0:T(8,128)(2,1)S(1)}, bf16[2048,128]{1,0:T(8,128)(2,1)}, u32[]{:S(2)}, u32[]{:S(2)}) collective-permute-start(bf16[2048,128]{1,0:T(8,128)(2,1)S(1)} %pad_maximum_fusion.query), channel_id=1, source_target_pairs={{0,8},{8,0},{1,9},{9,1},{2,10},{10,2},{3,11},{11,3},{4,12},{12,4},... | collective-permute-start | bytes 1572872 | tf_op jit(solution)/shard_map/ppermute | solution.py:398
  107.4 9.6 %copy-start.7 = (bf16[6,128,128]{2,1,0:T(8,128)(2,1)}, bf16[6,128,128]{2,1,0:T(8,128)(2,1)S(1)}, u32[]{:S(2)}) copy-start(bf16[6,128,128]{2,1,0:T(8,128)(2,1)S(1)} %collective-permute-done.7.refs_1_) | copy-start | bytes 589828
  107.4 9.6 %copy-start.8 = (bf16[6,128,128]{2,1,0:T(8,128)(2,1)}, bf16[6,128,128]{2,1,0:T(8,128)(2,1)S(1)}, u32[]{:S(2)}) copy-start(bf16[6,128,128]{2,1,0:T(8,128)(2,1)S(1)} %collective-permute-done.8.refs_2_) | copy-start | bytes 589828
  107.4 62.8 %all-to-all-start = ((bf16[8,512,256]{2,1,0:T(8,128)(2,1)}), bf16[8,512,256]{2,1,0:T(8,128)(2,1)S(1)}, u32[]{:S(2)}, u32[]{:S(2)}) async-start(bf16[8,512,256]{2,1,0:T(8,128)(2,1)} %get-tuple-element.52), calls=%async_computation | async-start | bytes 4194304 | tf_op jit(solution)/shard_map/all_to_all | solution.py:466
  114.1 14.9 %collective-permute-start.14 = (bf16[1024,256]{1,0:T(8,128)(2,1)}, bf16[1024,256]{1,0:T(8,128)(2,1)S(1)}, u32[]{:S(2)}, u32[]{:S(2)}) collective-permute-start(bf16[1024,256]{1,0:T(8,128)(2,1)} %collective-permute-done.12.refs_3_), channel_id=1, source_target_pairs={{0,32},{32,64},{64,96},{96,128},{128,160},{160,192},{192,224},{224... | collective-permute-start | bytes 1572872 | tf_op jit(solution)/shard_map/ppermute | solution.py:402
  114.4 14.7 %collective-permute-start.15 = (bf16[1024,256]{1,0:T(8,128)(2,1)}, bf16[1024,256]{1,0:T(8,128)(2,1)S(1)}, u32[]{:S(2)}, u32[]{:S(2)}) collective-permute-start(bf16[1024,256]{1,0:T(8,128)(2,1)} %collective-permute-done.13.refs_4_), channel_id=1, source_target_pairs={{0,224},{32,0},{64,32},{96,64},{128,96},{160,128},{192,160},{224,1... | collective-permute-start | bytes 1572872 | tf_op jit(solution)/shard_map/ppermute | solution.py:402
  117.1 13.3 %collective-permute-start.9 = (bf16[3,128,128]{2,1,0:T(8,128)(2,1)S(1)}, bf16[3,128,128]{2,1,0:T(8,128)(2,1)S(1)}, u32[]{:S(2)}, u32[]{:S(2)}) collective-permute-start(bf16[3,128,128]{2,1,0:T(8,128)(2,1)S(1)} %slice.24), channel_id=1, source_target_pairs={{0,32},{32,64},{64,96},{96,128},{128,160},{160,192},{192,224},{224... | collective-permute-start | bytes 294920 | tf_op jit(solution)/shard_map/ppermute | solution.py:402
  117.2 13.2 %collective-permute-start.10 = (bf16[3,128,128]{2,1,0:T(8,128)(2,1)S(1)}, bf16[3,128,128]{2,1,0:T(8,128)(2,1)S(1)}, u32[]{:S(2)}, u32[]{:S(2)}) collective-permute-start(bf16[3,128,128]{2,1,0:T(8,128)(2,1)S(1)} %slice.25), channel_id=1, source_target_pairs={{0,224},{32,0},{64,32},{96,64},{128,96},{160,128},{192,160},{224,1... | collective-permute-start | bytes 294920 | tf_op jit(solution)/shard_map/ppermute | solution.py:402
  129.0 12.4 %copy-start.5 = (bf16[1024,256]{1,0:T(8,128)(2,1)}, bf16[1024,256]{1,0:T(8,128)(2,1)S(1)}, u32[]{:S(2)}) copy-start(bf16[1024,256]{1,0:T(8,128)(2,1)S(1)} %collective-permute-done.14.refs_5_) | copy-start | bytes 1572868
  129.1 12.5 %copy-start.6 = (bf16[1024,256]{1,0:T(8,128)(2,1)}, bf16[1024,256]{1,0:T(8,128)(2,1)S(1)}, u32[]{:S(2)}) copy-start(bf16[1024,256]{1,0:T(8,128)(2,1)S(1)} %collective-permute-done.15.refs_6_) | copy-start | bytes 1572868
  130.3 0.6 copy-start.19
  131.0 0.6 copy-start.20
  139.6 13.4 %collective-permute-start.16 = (bf16[2048,128]{1,0:T(8,128)(2,1)}, bf16[2048,128]{1,0:T(8,128)(2,1)S(1)}, u32[]{:S(2)}, u32[]{:S(2)}) collective-permute-start(bf16[2048,128]{1,0:T(8,128)(2,1)} %get-tuple-element.46), channel_id=1, source_target_pairs={{0,8},{8,0},{1,9},{9,1},{2,10},{10,2},{3,11},{11,3},{4,12},{12,4},... | collective-permute-start | bytes 1572872 | tf_op jit(solution)/shard_map/ppermute | solution.py:398
  141.5 11.4 %collective-permute-start.18 = (bf16[512,256]{1,0:T(8,128)(2,1)S(1)}, bf16[512,256]{1,0:T(8,128)(2,1)S(1)}, u32[]{:S(2)}, u32[]{:S(2)}) collective-permute-start(bf16[512,256]{1,0:T(8,128)(2,1)S(1)} %slice.28), channel_id=1, source_target_pairs={{0,32},{32,64},{64,96},{96,128},{128,160},{160,192},{192,224},{224... | collective-permute-start | bytes 786440 | tf_op jit(solution)/shard_map/ppermute | solution.py:402
  141.6 11.3 %collective-permute-start.19 = (bf16[512,256]{1,0:T(8,128)(2,1)S(1)}, bf16[512,256]{1,0:T(8,128)(2,1)S(1)}, u32[]{:S(2)}, u32[]{:S(2)}) collective-permute-start(bf16[512,256]{1,0:T(8,128)(2,1)S(1)} %slice.29), channel_id=1, source_target_pairs={{0,224},{32,0},{64,32},{96,64},{128,96},{160,128},{192,160},{224,1... | collective-permute-start | bytes 786440 | tf_op jit(solution)/shard_map/ppermute | solution.py:402
  144.3 8.6 %collective-permute-start.17 = (f32[16,1,128]{2,1,0:T(1,128)}, f32[16,1,128]{2,1,0:T(1,128)S(1)}, u32[]{:S(2)}, u32[]{:S(2)}) collective-permute-start(f32[16,1,128]{2,1,0:T(1,128)} %get-tuple-element.47), channel_id=1, source_target_pairs={{0,8},{8,0},{1,9},{9,1},{2,10},{10,2},{3,11},{11,3},{4,12},{12,4},... | collective-permute-start | bytes 24584 | tf_op jit(solution)/shard_map/ppermute | solution.py:398
  152.9 0.6 copy-start.9
  152.9 24.5 %copy-start.13 = (bf16[512,256]{1,0:T(8,128)(2,1)}, bf16[512,256]{1,0:T(8,128)(2,1)S(1)}, u32[]{:S(2)}) copy-start(bf16[512,256]{1,0:T(8,128)(2,1)S(1)} %collective-permute-done.18.refs_7_) | copy-start | bytes 786436
  153.0 24.5 %copy-start.14 = (bf16[512,256]{1,0:T(8,128)(2,1)}, bf16[512,256]{1,0:T(8,128)(2,1)S(1)}, u32[]{:S(2)}) copy-start(bf16[512,256]{1,0:T(8,128)(2,1)S(1)} %collective-permute-done.19.refs_8_) | copy-start | bytes 786436
  153.0 0.9 copy-start.4
  156.3 14.0 %collective-permute-start.20 = (bf16[2048,128]{1,0:T(8,128)(2,1)}, bf16[2048,128]{1,0:T(8,128)(2,1)S(1)}, u32[]{:S(2)}, u32[]{:S(2)}) collective-permute-start(bf16[2048,128]{1,0:T(8,128)(2,1)} %get-tuple-element.49.own), channel_id=1, source_target_pairs={{0,16},{16,0},{1,17},{17,1},{2,18},{18,2},{3,19},{19,3},{4,20},{20... | collective-permute-start | bytes 1572872 | tf_op jit(solution)/shard_map/ppermute | solution.py:398
  156.7 13.5 %collective-permute-start.21 = (f32[16,1,128]{2,1,0:T(1,128)}, f32[16,1,128]{2,1,0:T(1,128)S(1)}, u32[]{:S(2)}, u32[]{:S(2)}) collective-permute-start(f32[16,1,128]{2,1,0:T(1,128)} %get-tuple-element.50.own_lse), channel_id=1, source_target_pairs={{0,16},{16,0},{1,17},{17,1},{2,18},{18,2},{3,19},{19,3},{4,20},{20... | collective-permute-start | bytes 24584 | tf_op jit(solution)/shard_map/ppermute | solution.py:398
  170.2 0.6 copy-start.10
  170.3 14.2 %copy-start = (bf16[8,512,256]{2,1,0:T(8,128)(2,1)}, bf16[8,512,256]{2,1,0:T(8,128)(2,1)S(1)}, u32[]{:S(2)}) copy-start(bf16[8,512,256]{2,1,0:T(8,128)(2,1)S(1)} %all-to-all-done.near) | copy-start | bytes 6291460
  170.8 1.0 copy-start.2
  174.2 3.2 %collective-permute-start.22 = (bf16[2,128,1024]{2,1,0:T(8,128)(2,1)}, bf16[2,128,1024]{2,1,0:T(8,128)(2,1)S(1)}, u32[]{:S(2)}, u32[]{:S(2)}) collective-permute-start(bf16[2,128,1024]{2,1,0:T(8,128)(2,1)} %merge_last.1.near), channel_id=1, source_target_pairs={{0,8},{8,0},{1,9},{9,1},{2,10},{10,2},{3,11},{11,3},{4,12},{12,4},... | collective-permute-start | bytes 1572872 | tf_op jit(solution)/shard_map/ppermute | solution.py:398
  175.0 17.0 %collective-permute-start.23 = (bf16[8,512,256]{2,1,0:T(8,128)(2,1)S(1)}, bf16[8,512,256]{2,1,0:T(8,128)(2,1)}, u32[]{:S(2)}, u32[]{:S(2)}) collective-permute-start(bf16[8,512,256]{2,1,0:T(8,128)(2,1)S(1)} %all-to-all-done.near), channel_id=1, source_target_pairs={{0,8},{8,0},{1,9},{9,1},{2,10},{10,2},{3,11},{11,3},{4,12},{12,4},... | collective-permute-start | bytes 6291464 | tf_op jit(solution)/shard_map/ppermute | solution.py:398
  177.4 0.8 copy-start.12
  184.4 37.3 %all-to-all-start.1 = ((bf16[32,128,256]{2,1,0:T(8,128)(2,1)}), bf16[32,128,256]{2,1,0:T(8,128)(2,1)}, u32[]{:S(2)}, u32[]{:S(2)}) async-start(bf16[32,128,256]{2,1,0:T(8,128)(2,1)} %bitcast.17), calls=%async_computation.1 | async-start | bytes 4194304 | tf_op jit(solution)/shard_map/all_to_all | solution.py:482
  226.7 14.5 %all-to-all-start.2 = ((bf16[8,144,256]{2,1,0:T(8,128)(2,1)}), bf16[8,144,256]{2,1,0:T(8,128)(2,1)S(1)}, u32[]{:S(2)}, u32[]{:S(2)}) async-start(bf16[8,144,256]{2,1,0:T(8,128)(2,1)} %get-tuple-element.55), calls=%async_computation.2 | async-start | bytes 1179648 | tf_op jit(solution)/shard_map/all_to_all | solution.py:488
  241.2 0.8 copy-start.1

commit v4 on v3

--- a/solution.py
+++ b/solution.py
@@ -21,7 +21,6 @@
 VMEM = 56 * 1024 * 1024
 CHUNK = 512
 BLOCKS = 3
-DISTANCES = (0, -1, 1, -2, 2, -3, 3, 4)
 
 
 def params(**more):
@@ -78,7 +77,7 @@
         in_specs=[pl.BlockSpec(memory_space=pltpu.SMEM)]
         + [vmem] * 5
         + [pl.BlockSpec(memory_space=pl.ANY)],
-        out_specs=(vmem, vmem, pl.BlockSpec(memory_space=pl.ANY)),
+        out_specs=(vmem, vmem, vmem),
         out_shape=(
             jax.ShapeDtypeStruct((GROUP, ROWS, HEAD), jnp.bfloat16),
             jax.ShapeDtypeStruct((2 * BLOCKS, ROWS, HEAD), jnp.bfloat16),
@@ -114,21 +113,18 @@
     z, yl, c = place[0], place[1], place[2]
     steps = len(cached) + len(fresh)
 
-    def value_block(ref, k):
-        return ref[BLOCKS + k] if ref.shape[0] == 2 * BLOCKS else ref[k]
-
     @pl.when(step == 0)
     def _():
         at = 0
         for kp, vp in cached:
             for k in range(2):
                 keys[:, at : at + ROWS] = pieces[kp][k]
-                values[at : at + ROWS, :HEAD] = value_block(pieces[vp], k)
+                values[at : at + ROWS, :HEAD] = pieces[vp][BLOCKS + k]
                 at += ROWS
         for pair in fresh:
             for kp, vp, _ in pair:
                 keys[:, at : at + ROWS] = pieces[kp][BLOCKS - 1]
-                values[at : at + ROWS, :HEAD] = value_block(pieces[vp], BLOCKS - 1)
+                values[at : at + ROWS, :HEAD] = pieces[vp][2 * BLOCKS - 1]
                 at += ROWS
         values[:, HEAD:] = jnp.ones((steps * 2 * ROWS, HEAD), jnp.bfloat16)
 
@@ -271,42 +267,34 @@
     )(own, own_lse, other, other_lse)
 
 
-def project_kernel(place, near, far, *refs):
-    weights, top, bottom, out = refs[:7], refs[7], refs[8], refs[9]
-    z, yl, c = place[0], place[1], place[2]
-    width = GROUP * HEAD
+def project_kernel(place, near, far, weights, out):
+    yl, c = place[1], place[2]
     for rc, rows in ((0, near), (1, far)):
-        lhs = rows[...].reshape(2 * ROWS, width)
-        for i, distance in enumerate(DISTANCES):
-            if i < 7:
-                product = jnp.dot(lhs, weights[i][...], preferred_element_type=jnp.float32)
-            else:
-                product = jnp.dot(
-                    lhs[:, : width // 2], top[...], preferred_element_type=jnp.float32
-                ) + jnp.dot(lhs[:, width // 2 :], bottom[...], preferred_element_type=jnp.float32)
+        lhs = rows[...].reshape(2 * ROWS, GROUP * HEAD)
+        for target in range(Z):
+            product = jnp.dot(lhs, weights[target], preferred_element_type=jnp.float32)
             product = product.astype(jnp.bfloat16)
-            target = lax.rem(z + distance + Z, Z)
             for ryl in range(2):
                 q = (yl ^ ryl) * 2 + (c ^ rc)
                 out[q, target] = product[ryl * ROWS : (ryl + 1) * ROWS, :]
 
 
-def project(place, near, far, pieces):
+def project(place, near, far, weights):
     vmem = pl.BlockSpec(memory_space=pltpu.VMEM)
-    columns = pieces[0].shape[1]
+    columns = weights.shape[2]
     return pl.pallas_call(
         project_kernel,
-        in_specs=[pl.BlockSpec(memory_space=pltpu.SMEM)] + [vmem] * 11,
+        in_specs=[pl.BlockSpec(memory_space=pltpu.SMEM)] + [vmem] * 3,
         out_specs=vmem,
         out_shape=jax.ShapeDtypeStruct((4, Z, ROWS, columns), jnp.bfloat16),
         compiler_params=params(),
         name="project",
         cost_estimate=pl.CostEstimate(
             flops=2 * 4 * ROWS * GROUP * HEAD * Z * columns,
-            bytes_accessed=4_000_000,
+            bytes_accessed=7_000_000,
             transcendentals=0,
         ),
-    )(place, near, far, *pieces)
+    )(place, near, far, weights)
 
 
 PAD = 16
@@ -410,11 +398,6 @@
     return [along_z(pair[0], 1), along_z(pair[1], -1)]
 
 
-def last_step(pair):
-    half = pair[0].shape[0] // 2
-    return [along_z(pair[0][:half], 1), along_z(pair[1][half:], -1)]
-
-
 def local(
     hidden,
     query,
@@ -441,36 +424,29 @@
         sine,
         layer3_key_value_weight.reshape(Z, 2, MODEL_WIDTH // Z // 2, 2 * HEAD),
     )
-    weights_1 = step([out_weight, out_weight])
-    kv_1 = list(after(step([kv, kv]), *weights_1))
-    kv_2 = step(kv_1)
-    weights_2 = step(weights_1)
-    kv_3 = step(kv_2)
-    weights_2 = list(after(weights_2, *kv_3))
-    weights_3 = step(weights_2)
-    weights_4 = last_step(weights_3)
-    weights = [out_weight, *weights_1, *weights_2, *weights_3, *weights_4]
     rotated_query = rotated_query.reshape(GROUP * ROWS, HEAD)
     near_query = jnp.concatenate([rotated_query, swap(rotated_query, "yl")], axis=0)
     far_query = swap(near_query, "c")
+    weights = lax.all_gather(out_weight, "z")
+    kv_1 = list(after(step([kv, kv]), near_query))
+    kv_2 = step(kv_1)
+    kv_3 = step(kv_2)
     early = [kv, *kv_1, *kv_2]
     early_cached = [(i, i) for i in range(5)]
     early_fresh = [[(0, 0, 0), (1, 1, -1)], [(2, 2, 1), (3, 3, -2)]]
-    late_cached = [(1, 1), (2, 2), (3, 4)]
-    late_fresh = [[(0, 0, 2), (1, 1, -3)], [(2, 2, 3), (3, 4, 4)]]
+    late_cached = [(1, 1), (2, 2), (3, 3)]
+    late_fresh = [[(0, 0, 2), (1, 1, -3)], [(2, 2, 3), (3, 3, 4)]]
     near_state = attend(place, 0, near_query, early, early_cached, early_fresh)
     kv_3 = list(after(kv_3, near_state))
-    late = [kv_2[1], *kv_3, *last_step(kv_3)]
-    far_query = after(far_query, near_state, *weights_2)
+    late = [kv_2[1], *kv_3, along_z(kv_3[0], 1)]
+    far_query = after(far_query, near_state)
     third_rows = after(third_rows, *kv_3)
     third_near = lax.all_to_all(third_rows, HEAD_AXES, 0, 0, tiled=True)
     third_far = swap(third_near, "c")
     far_state = attend(place, 1, far_query, early, early_cached, early_fresh)
-    far_state = after(far_state, *weights_3)
     send, send_lse = attend(place, 1, far_query, late, late_cached, late_fresh, far_state, True)
     got, got_lse = swap(send, "c"), swap(send_lse, "c")
     own, own_lse = attend(place, 0, near_query, late, late_cached, late_fresh, near_state, True)
-    got_lse = after(got_lse, *weights_4)
     own, own_lse = merge(own, own_lse, got, got_lse)
     got, got_lse = swap(own, "yl"), swap(own_lse, "yl")
     got_lse = after(got_lse, third_near)

time: 245 us -> 193 us (0.79)
  Pallas kernels: 119 us -> 56.5 us
  starting transfers between devices: 55.1 us -> 41.3 us
  between operations: 1.62 us -> 14.9 us
  waiting for transfers between devices: 59.6 us -> 69 us
    pallas_call x1, Pallas kernels: 66.5 us -> 4.17 us  [prepare(): pl.pallas_call(prepare_kernel, in_specs=[pl.BlockSpec(memory_space=pltpu....]
    ppermute x16 -> x7, starting transfers between devices: 25.9 us -> 11.8 us  [along_z(): return lax.ppermute(x, 'z', [(i, (i + distance) % Z) for i in range(Z)])]
    ppermute x16 -> x7, waiting for transfers between devices: 4.58 us -> 13.7 us  [along_z(): return lax.ppermute(x, 'z', [(i, (i + distance) % Z) for i in range(Z)])]
    unnamed x42 -> x34, local copies, waits for them, and re-layouts: 5.44 us -> 6.79 us
  transfers between devices with their start and end apart: 27 -> 19, of which waited for: 7 -> 7; matrix products, arithmetic and copies ran while one was open for 1% -> 2% of each run, Pallas kernels for 45% -> 26%
where the time goes in v4:
time: 193 us; the launch traced here: 192 us
  waiting for transfers between devices  69 us (36%)
  Pallas kernels  56.5 us (29%)
  starting transfers between devices  41.3 us (21%)
  between operations  14.9 us (8%)
  local copies, waits for them, and re-layouts  6.79 us (4%)
  other arithmetic  3.36 us (2%)
    pallas_call x4, Pallas kernels, attend(): pl.pallas_call(functools.partial(attend_kernel, cached, fresh, state is N...  34.4 us
    all_to_all x1, waiting for transfers between devices, local(): lax.all_to_all(products, ('yl', 'c', 'x', 'yh'), 0, 0, tiled=True)  29.8 us
    ppermute x8, waiting for transfers between devices, swap(): return lax.ppermute(x, axis, [(0, 1), (1, 0)])  14.5 us
    ppermute x7, waiting for transfers between devices, along_z(): return lax.ppermute(x, 'z', [(i, (i + distance) % Z) for i in range(Z)])  13.7 us
    ppermute x8, starting transfers between devices, swap(): return lax.ppermute(x, axis, [(0, 1), (1, 0)])  12.2 us
    ppermute x7, starting transfers between devices, along_z(): return lax.ppermute(x, 'z', [(i, (i + distance) % Z) for i in range(Z)])  11.8 us
    all_to_all x1, waiting for transfers between devices, local(): partial = lax.all_to_all(partial, HEAD_AXES, 0, 0, tiled=True)  10.3 us
    all_to_all x1, starting transfers between devices, local(): lax.all_to_all(products, ('yl', 'c', 'x', 'yh'), 0, 0, tiled=True)  7.44 us
  transfers between devices with their start and end apart: 19, of which 7 were waited for; matrix products, arithmetic and copies ran while one was open for 2% of the time, Pallas kernels for 26%

profile of v4, /device:TPU:1, one launch (start us, length us, event | category | flops | bytes accessed | tf_op | source)
XLA Modules:
  0.0 191.9 jit_solution(6492211631412285612)
XLA Ops:
  7.2 0.7 all-gather.3.cloned.1.call-update
  7.9 0.7 convert_element_type.36
  8.6 0.6 pad_add_fusion.place
  9.2 0.3 fusion.2
  9.5 0.8 pad_maximum_fusion.1
  10.3 4.2 %prepare.1 = (bf16[8,128,128]{2,1,0:T(8,128)(2,1)}, bf16[6,128,128]{2,1,0:T(8,128)(2,1)}, bf16[8,512,256]{2,1,0:T(8,128)(2,1)}) custom-call(s32[3]{0:T(128)} %pad_add_fusion.place, bf16[128,1024]{1,0:T(8,128)(2,1)} %query.1, bf16[2,128,128]{2,1,0:T(8,128)(2,1)} %fresh.1, bf16[2,256,128]{2,1,0:T(8,128)(2,1)} %cached.1, f32[128,128]{1,0:T(8,128)} %get-tuple-element.52.cosine, ...), custom_call_target="tpu_custom_call" | custom-call | flops 2000000 | bytes 5500000 | tf_op jit(solution)/shard_map/prepare/pallas_call | solution.py:75
  14.5 2.2 %collective-permute-start = (bf16[1024,128]{1,0:T(8,128)(2,1)}, bf16[1024,128]{1,0:T(8,128)(2,1)S(1)}, u32[]{:S(2)}, u32[]{:S(2)}) collective-permute-start(bf16[1024,128]{1,0:T(8,128)(2,1)} %bitcast.19), channel_id=1, source_target_pairs={{0,16},{16,0},{1,17},{17,1},{2,18},{18,2},{3,19},{19,3},{4,20},{20... | collective-permute-start | bytes 786440 | tf_op jit(solution)/shard_map/ppermute | solution.py:386
  16.7 1.6 collective-permute-start.1
  18.3 3.9 %collective-permute-start.2 = (bf16[6,128,128]{2,1,0:T(8,128)(2,1)}, bf16[6,128,128]{2,1,0:T(8,128)(2,1)S(1)}, u32[]{:S(2)}, u32[]{:S(2)}) collective-permute-start(bf16[6,128,128]{2,1,0:T(8,128)(2,1)} %get-tuple-element.25.refs_0_), channel_id=1, source_target_pairs={{0,224},{32,0},{64,32},{96,64},{128,96},{160,128},{192,160},{224,1... | collective-permute-start | bytes 589832 | tf_op jit(solution)/shard_map/ppermute | solution.py:390
  22.3 1.0 pad_maximum_fusion.query
  23.3 3.5 %collective-permute-done.1.refs_1_ = bf16[6,128,128]{2,1,0:T(8,128)(2,1)S(1)} collective-permute-done((bf16[6,128,128]{2,1,0:T(8,128)(2,1)}, bf16[6,128,128]{2,1,0:T(8,128)(2,1)S(1)}, u32[]{:S(2)}, u32[]{:S(2)}) %collective-permute-start.1) | collective-permute-done | bytes 196640 | tf_op jit(solution)/shard_map/ppermute | solution.py:390
  26.8 0.1 collective-permute-start.4
  26.9 3.1 %collective-permute-start.3 = (bf16[6,128,128]{2,1,0:T(8,128)(2,1)S(1)}, bf16[6,128,128]{2,1,0:T(8,128)(2,1)S(1)}, u32[]{:S(2)}, u32[]{:S(2)}) collective-permute-start(bf16[6,128,128]{2,1,0:T(8,128)(2,1)S(1)} %collective-permute-done.2.refs_2_), channel_id=1, source_target_pairs={{0,224},{32,0},{64,32},{96,64},{128,96},{160,128},{192,160},{224,1... | collective-permute-start | bytes 589832 | tf_op jit(solution)/shard_map/ppermute | solution.py:390
  30.0 8.1 %collective-permute-done.4.refs_3_ = bf16[6,128,128]{2,1,0:T(8,128)(2,1)S(1)} collective-permute-done((bf16[6,128,128]{2,1,0:T(8,128)(2,1)S(1)}, bf16[6,128,128]{2,1,0:T(8,128)(2,1)S(1)}, u32[]{:S(2)}, u32[]{:S(2)}) %collective-permute-start.4) | collective-permute-done | bytes 196640 | tf_op jit(solution)/shard_map/ppermute | solution.py:390
  38.1 2.7 %collective-permute-start.6 = (bf16[6,128,128]{2,1,0:T(8,128)(2,1)S(1)}, bf16[6,128,128]{2,1,0:T(8,128)(2,1)S(1)}, u32[]{:S(2)}, u32[]{:S(2)}) collective-permute-start(bf16[6,128,128]{2,1,0:T(8,128)(2,1)S(1)} %collective-permute-done.3.refs_4_.refs_0_), channel_id=1, source_target_pairs={{0,224},{32,0},{64,32},{96,64},{128,96},{160,128},{192,160},{224,1... | collective-permute-start | bytes 589832 | tf_op jit(solution)/shard_map/ppermute | solution.py:390
  40.8 6.1 %collective-permute-start.8 = (bf16[2048,128]{1,0:T(8,128)(2,1)S(1)}, bf16[2048,128]{1,0:T(8,128)(2,1)S(1)}, u32[]{:S(2)}, u32[]{:S(2)}) collective-permute-start(bf16[2048,128]{1,0:T(8,128)(2,1)S(1)} %pad_maximum_fusion.query), channel_id=1, source_target_pairs={{0,8},{8,0},{1,9},{9,1},{2,10},{10,2},{3,11},{11,3},{4,12},{12,4},... | collective-permute-start | bytes 1572872 | tf_op jit(solution)/shard_map/ppermute | solution.py:386
  47.0 9.2 %attend.4 = (f32[2048,256]{1,0:T(8,128)}, f32[2048,128]{1,0:T(8,128)}) custom-call(s32[3]{0:T(128)} %pad_add_fusion.place, bf16[2048,128]{1,0:T(8,128)(2,1)} %copy-done.3, bf16[6,128,128]{2,1,0:T(8,128)(2,1)} %get-tuple-element.25.refs_0_, bf16[6,128,128]{2,1,0:T(8,128)(2,1)} %copy-done.10, bf16[6,128,128]{2,1,0:T(8,128)(2,1)} %copy-done.11, ...), custom_call_target="tpu_custom_call" | custom-call | flops 1879048192 | bytes 3014656 | tf_op jit(solution)/shard_map/attend/pallas_call | solution.py:191
  56.2 0.7 copy-done.12
  56.9 0.7 copy-done.14
  57.6 6.4 %all-to-all-start = ((bf16[8,512,256]{2,1,0:T(8,128)(2,1)}), bf16[8,512,256]{2,1,0:T(8,128)(2,1)S(1)}, u32[]{:S(2)}, u32[]{:S(2)}) async-start(bf16[8,512,256]{2,1,0:T(8,128)(2,1)} %get-tuple-element.42), calls=%async_computation | async-start | bytes 4194304 | tf_op jit(solution)/shard_map/all_to_all | solution.py:444
  64.0 0.3 collective-permute-start.7
  64.3 0.8 copy-done.7
  65.1 9.2 %attend.6 = (f32[2048,256]{1,0:T(8,128)}, f32[2048,128]{1,0:T(8,128)}) custom-call(s32[3]{0:T(128)} %pad_add_fusion.place, bf16[2048,128]{1,0:T(8,128)(2,1)} %copy-done.7, bf16[6,128,128]{2,1,0:T(8,128)(2,1)} %get-tuple-element.25.refs_0_, bf16[6,128,128]{2,1,0:T(8,128)(2,1)} %copy-done.10, bf16[6,128,128]{2,1,0:T(8,128)(2,1)} %copy-done.11, ...), custom_call_target="tpu_custom_call" | custom-call | flops 1879048192 | bytes 3014656 | tf_op jit(solution)/shard_map/attend/pallas_call | solution.py:191
  74.3 2.1 %collective-permute-done.7.refs_3_ = bf16[6,128,128]{2,1,0:T(8,128)(2,1)S(1)} collective-permute-done((bf16[6,128,128]{2,1,0:T(8,128)(2,1)S(1)}, bf16[6,128,128]{2,1,0:T(8,128)(2,1)S(1)}, u32[]{:S(2)}, u32[]{:S(2)}) %collective-permute-start.7) | collective-permute-done | bytes 196640 | tf_op jit(solution)/shard_map/ppermute | solution.py:390
  76.4 0.7 copy-done.16
  77.1 8.0 %attend.7 = (bf16[2048,128]{1,0:T(8,128)(2,1)}, f32[16,1,128]{2,1,0:T(1,128)}) custom-call(s32[3]{0:T(128)} %pad_add_fusion.place, bf16[2048,128]{1,0:T(8,128)(2,1)} %copy-done.7, bf16[6,128,128]{2,1,0:T(8,128)(2,1)} %copy-done.9, bf16[6,128,128]{2,1,0:T(8,128)(2,1)} %copy-done.12, bf16[6,128,128]{2,1,0:T(8,128)(2,1)} %copy-done.14, ...), custom_call_target="tpu_custom_call" | custom-call | flops 1342177280 | bytes 2752512 | tf_op jit(solution)/shard_map/attend/pallas_call | solution.py:191
  85.1 1.0 collective-permute-start.9
  86.1 0.1 collective-permute-start.10
  86.2 8.0 %attend.5 = (bf16[2048,128]{1,0:T(8,128)(2,1)}, f32[16,1,128]{2,1,0:T(1,128)}) custom-call(s32[3]{0:T(128)} %pad_add_fusion.place, bf16[2048,128]{1,0:T(8,128)(2,1)} %copy-done.3, bf16[6,128,128]{2,1,0:T(8,128)(2,1)} %copy-done.9, bf16[6,128,128]{2,1,0:T(8,128)(2,1)} %copy-done.12, bf16[6,128,128]{2,1,0:T(8,128)(2,1)} %copy-done.14, ...), custom_call_target="tpu_custom_call" | custom-call | flops 1342177280 | bytes 2752512 | tf_op jit(solution)/shard_map/attend/pallas_call | solution.py:191
  94.2 0.6 copy-done.5
  94.8 0.2 copy-done.4
  95.0 2.4 %merge.1 = (bf16[2048,128]{1,0:T(8,128)(2,1)}, f32[16,1,128]{2,1,0:T(1,128)}) custom-call(bf16[2048,128]{1,0:T(8,128)(2,1)} %get-tuple-element.32.own, f32[16,1,128]{2,1,0:T(1,128)} %get-tuple-element.33.own_lse, bf16[2048,128]{1,0:T(8,128)(2,1)} %copy-done.4, f32[16,1,128]{2,1,0:T(1,128)} %copy-done.5), custom_call_target="tpu_custom_call" | custom-call | flops 2000000 | bytes 1600000 | tf_op jit(solution)/shard_map/merge/pallas_call | solution.py:248
  97.4 1.5 collective-permute-start.12
  98.9 12.0 %collective-permute-done.12.other_lse = f32[16,1,128]{2,1,0:T(1,128)S(1)} collective-permute-done((f32[16,1,128]{2,1,0:T(1,128)}, f32[16,1,128]{2,1,0:T(1,128)S(1)}, u32[]{:S(2)}, u32[]{:S(2)}) %collective-permute-start.12) | collective-permute-done | bytes 8224 | tf_op jit(solution)/shard_map/ppermute | solution.py:386
  110.9 0.6 copy-done.6
  111.5 0.9 copy-done.2
  112.4 2.4 %merge_last.1.near = bf16[2,128,1024]{2,1,0:T(8,128)(2,1)} custom-call(bf16[2048,128]{1,0:T(8,128)(2,1)} %get-tuple-element.39.own, f32[16,1,128]{2,1,0:T(1,128)} %get-tuple-element.40.own_lse, bf16[2048,128]{1,0:T(8,128)(2,1)} %copy-done.2, f32[16,1,128]{2,1,0:T(1,128)} %copy-done.6), custom_call_target="tpu_custom_call" | custom-call | flops 2000000 | bytes 1600000 | tf_op jit(solution)/shard_map/merge_last/pallas_call | solution.py:261
  114.7 1.3 collective-permute-start.13
  116.0 2.5 %collective-permute-done.13.far = bf16[2,128,1024]{2,1,0:T(8,128)(2,1)S(1)} collective-permute-done((bf16[2,128,1024]{2,1,0:T(8,128)(2,1)}, bf16[2,128,1024]{2,1,0:T(8,128)(2,1)S(1)}, u32[]{:S(2)}, u32[]{:S(2)}) %collective-permute-start.13) | collective-permute-done | bytes 524320 | tf_op jit(solution)/shard_map/ppermute | solution.py:386
  118.5 0.8 copy-done.8
  119.3 6.2 %project.1 = bf16[4,8,128,256]{3,2,1,0:T(8,128)(2,1)} custom-call(s32[3]{0:T(128)} %pad_add_fusion.place, bf16[2,128,1024]{2,1,0:T(8,128)(2,1)} %merge_last.1.near, bf16[2,128,1024]{2,1,0:T(8,128)(2,1)} %copy-done.8, bf16[8,1024,256]{2,1,0:T(8,128)(2,1)} %bitcast.24), custom_call_target="tpu_custom_call" | custom-call | flops 2147483648 | bytes 7000000 | tf_op jit(solution)/shard_map/project/pallas_call | solution.py:285
  125.4 7.4 %all-to-all-start.1 = ((bf16[32,128,256]{2,1,0:T(8,128)(2,1)}), bf16[32,128,256]{2,1,0:T(8,128)(2,1)}, u32[]{:S(2)}, u32[]{:S(2)}) async-start(bf16[32,128,256]{2,1,0:T(8,128)(2,1)} %bitcast.18), calls=%async_computation.1 | async-start | bytes 4194304 | tf_op jit(solution)/shard_map/all_to_all | solution.py:458
  132.9 29.8 %all-to-all-done.1 = bf16[32,128,256]{2,1,0:T(8,128)(2,1)} async-done(((bf16[32,128,256]{2,1,0:T(8,128)(2,1)}), bf16[32,128,256]{2,1,0:T(8,128)(2,1)}, u32[]{:S(2)}, u32[]{:S(2)}) %all-to-all-start.1) | async-done | bytes 2097184 | tf_op jit(solution)/shard_map/all_to_all | solution.py:458
  162.7 4.9 %third.1 = (bf16[128,1024]{1,0:T(8,128)(2,1)}, bf16[8,144,256]{2,1,0:T(8,128)(2,1)}) custom-call(s32[3]{0:T(128)} %pad_add_fusion.place, bf16[4,8,128,256]{3,2,1,0:T(8,128)(2,1)} %bitcast.10.received, bf16[128,1024]{1,0:T(8,128)(2,1)} %hidden.1, f32[1,1024]{1,0:T(1,128)} %bitcast.21, bf16[8,512,256]{2,1,0:T(8,128)(2,1)} %copy-done, ...), custom_call_target="tpu_custom_call" | custom-call | tf_op jit(solution)/shard_map/third/pallas_call | solution.py:338
  167.6 3.5 %all-to-all-start.2 = ((bf16[8,144,256]{2,1,0:T(8,128)(2,1)}), bf16[8,144,256]{2,1,0:T(8,128)(2,1)S(1)}, u32[]{:S(2)}, u32[]{:S(2)}) async-start(bf16[8,144,256]{2,1,0:T(8,128)(2,1)} %get-tuple-element.45), calls=%async_computation.2 | async-start | bytes 1179648 | tf_op jit(solution)/shard_map/all_to_all | solution.py:464
  171.8 10.3 %all-to-all-done.2.partial = bf16[8,144,256]{2,1,0:T(8,128)(2,1)S(1)} async-done(((bf16[8,144,256]{2,1,0:T(8,128)(2,1)}), bf16[8,144,256]{2,1,0:T(8,128)(2,1)S(1)}, u32[]{:S(2)}, u32[]{:S(2)}) %all-to-all-start.2) | async-done | bytes 589856 | tf_op jit(solution)/shard_map/all_to_all | solution.py:464
  182.1 0.8 copy-done.1
  183.0 2.1 %final.1 = bf16[128,256]{1,0:T(8,128)(2,1)} custom-call(s32[1]{0:T(128)S(6)} %copy.13.count, bf16[8,144,256]{2,1,0:T(8,128)(2,1)} %copy-done.1, f32[1,256]{1,0:T(1,128)} %bitcast.22, f32[128,128]{1,0:T(8,128)} %get-tuple-element.52.cosine, f32[128,128]{1,0:T(8,128)} %get-tuple-element.53.sine, s32[1,128]{1,0:T(1,128)} %bitcast.23), custom_call_target="tpu_custom_call" | custom-call | tf_op jit(solution)/shard_map/final/pallas_call | solution.py:375
  (44 shorter events, 0.2 us)
Async XLA Ops:
  7.2 111.3 %all-gather.3.cloned.1.call-start = ((), (), s32[]{:S(2)}) async-start(), calls=%async_computation.3 | async-start | bytes 4718592 | tf_op jit(solution)/shard_map/all_gather | solution.py:430
  14.5 7.8 %collective-permute-start = (bf16[1024,128]{1,0:T(8,128)(2,1)}, bf16[1024,128]{1,0:T(8,128)(2,1)S(1)}, u32[]{:S(2)}, u32[]{:S(2)}) collective-permute-start(bf16[1024,128]{1,0:T(8,128)(2,1)} %bitcast.19), channel_id=1, source_target_pairs={{0,16},{16,0},{1,17},{17,1},{2,18},{18,2},{3,19},{19,3},{4,20},{20... | collective-permute-start | bytes 786440 | tf_op jit(solution)/shard_map/ppermute | solution.py:386
  16.7 10.1 %collective-permute-start.1 = (bf16[6,128,128]{2,1,0:T(8,128)(2,1)}, bf16[6,128,128]{2,1,0:T(8,128)(2,1)S(1)}, u32[]{:S(2)}, u32[]{:S(2)}) collective-permute-start(bf16[6,128,128]{2,1,0:T(8,128)(2,1)} %get-tuple-element.25.refs_0_), channel_id=1, source_target_pairs={{0,32},{32,64},{64,96},{96,128},{128,160},{160,192},{192,224},{224... | collective-permute-start | bytes 589832 | tf_op jit(solution)/shard_map/ppermute | solution.py:390
  18.3 8.5 %collective-permute-start.2 = (bf16[6,128,128]{2,1,0:T(8,128)(2,1)}, bf16[6,128,128]{2,1,0:T(8,128)(2,1)S(1)}, u32[]{:S(2)}, u32[]{:S(2)}) collective-permute-start(bf16[6,128,128]{2,1,0:T(8,128)(2,1)} %get-tuple-element.25.refs_0_), channel_id=1, source_target_pairs={{0,224},{32,0},{64,32},{96,64},{128,96},{160,128},{192,160},{224,1... | collective-permute-start | bytes 589832 | tf_op jit(solution)/shard_map/ppermute | solution.py:390
  23.3 23.7 %copy-start.3 = (bf16[2048,128]{1,0:T(8,128)(2,1)}, bf16[2048,128]{1,0:T(8,128)(2,1)S(1)}, u32[]{:S(2)}) copy-start(bf16[2048,128]{1,0:T(8,128)(2,1)S(1)} %pad_maximum_fusion.query) | copy-start | bytes 1572868
  26.8 20.2 %copy-start.10 = (bf16[6,128,128]{2,1,0:T(8,128)(2,1)}, bf16[6,128,128]{2,1,0:T(8,128)(2,1)S(1)}, u32[]{:S(2)}) copy-start(bf16[6,128,128]{2,1,0:T(8,128)(2,1)S(1)} %collective-permute-done.1.refs_1_) | copy-start | bytes 589828
  26.8 20.2 %copy-start.11 = (bf16[6,128,128]{2,1,0:T(8,128)(2,1)}, bf16[6,128,128]{2,1,0:T(8,128)(2,1)S(1)}, u32[]{:S(2)}) copy-start(bf16[6,128,128]{2,1,0:T(8,128)(2,1)S(1)} %collective-permute-done.2.refs_2_) | copy-start | bytes 589828
  26.8 11.3 %collective-permute-start.4 = (bf16[6,128,128]{2,1,0:T(8,128)(2,1)S(1)}, bf16[6,128,128]{2,1,0:T(8,128)(2,1)S(1)}, u32[]{:S(2)}, u32[]{:S(2)}) collective-permute-start(bf16[6,128,128]{2,1,0:T(8,128)(2,1)S(1)} %collective-permute-done.1.refs_1_), channel_id=1, source_target_pairs={{0,32},{32,64},{64,96},{96,128},{128,160},{160,192},{192,224},{224... | collective-permute-start | bytes 589832 | tf_op jit(solution)/shard_map/ppermute | solution.py:390
  26.9 11.2 %collective-permute-start.3 = (bf16[6,128,128]{2,1,0:T(8,128)(2,1)S(1)}, bf16[6,128,128]{2,1,0:T(8,128)(2,1)S(1)}, u32[]{:S(2)}, u32[]{:S(2)}) collective-permute-start(bf16[6,128,128]{2,1,0:T(8,128)(2,1)S(1)} %collective-permute-done.2.refs_2_), channel_id=1, source_target_pairs={{0,224},{32,0},{64,32},{96,64},{128,96},{160,128},{192,160},{224,1... | collective-permute-start | bytes 589832 | tf_op jit(solution)/shard_map/ppermute | solution.py:390
  38.1 8.9 %copy-start.15 = (bf16[6,128,128]{2,1,0:T(8,128)(2,1)}, bf16[6,128,128]{2,1,0:T(8,128)(2,1)S(1)}, u32[]{:S(2)}) copy-start(bf16[6,128,128]{2,1,0:T(8,128)(2,1)S(1)} %collective-permute-done.4.refs_3_) | copy-start | bytes 589828
  38.1 18.1 %collective-permute-start.5 = (bf16[6,128,128]{2,1,0:T(8,128)(2,1)S(1)}, bf16[6,128,128]{2,1,0:T(8,128)(2,1)S(1)}, u32[]{:S(2)}, u32[]{:S(2)}) collective-permute-start(bf16[6,128,128]{2,1,0:T(8,128)(2,1)S(1)} %collective-permute-done.4.refs_3_), channel_id=1, source_target_pairs={{0,32},{32,64},{64,96},{96,128},{128,160},{160,192},{192,224},{224... | collective-permute-start | bytes 589832 | tf_op jit(solution)/shard_map/ppermute | solution.py:390
  38.1 8.9 %copy-start.9 = (bf16[6,128,128]{2,1,0:T(8,128)(2,1)}, bf16[6,128,128]{2,1,0:T(8,128)(2,1)S(1)}, u32[]{:S(2)}) copy-start(bf16[6,128,128]{2,1,0:T(8,128)(2,1)S(1)} %collective-permute-done.3.refs_4_.refs_0_) | copy-start | bytes 589828
  38.1 18.1 %collective-permute-start.6 = (bf16[6,128,128]{2,1,0:T(8,128)(2,1)S(1)}, bf16[6,128,128]{2,1,0:T(8,128)(2,1)S(1)}, u32[]{:S(2)}, u32[]{:S(2)}) collective-permute-start(bf16[6,128,128]{2,1,0:T(8,128)(2,1)S(1)} %collective-permute-done.3.refs_4_.refs_0_), channel_id=1, source_target_pairs={{0,224},{32,0},{64,32},{96,64},{128,96},{160,128},{192,160},{224,1... | collective-permute-start | bytes 589832 | tf_op jit(solution)/shard_map/ppermute | solution.py:390
  40.8 23.4 %collective-permute-start.8 = (bf16[2048,128]{1,0:T(8,128)(2,1)S(1)}, bf16[2048,128]{1,0:T(8,128)(2,1)S(1)}, u32[]{:S(2)}, u32[]{:S(2)}) collective-permute-start(bf16[2048,128]{1,0:T(8,128)(2,1)S(1)} %pad_maximum_fusion.query), channel_id=1, source_target_pairs={{0,8},{8,0},{1,9},{9,1},{2,10},{10,2},{3,11},{11,3},{4,12},{12,4},... | collective-permute-start | bytes 1572872 | tf_op jit(solution)/shard_map/ppermute | solution.py:386
  56.2 0.7 copy-start.12
  56.9 0.7 copy-start.14
  57.6 6.4 %copy-start.13 = (bf16[6,128,128]{2,1,0:T(8,128)(2,1)S(1)}, bf16[6,128,128]{2,1,0:T(8,128)(2,1)}, u32[]{:S(2)}) copy-start(bf16[6,128,128]{2,1,0:T(8,128)(2,1)} %copy-done.12) | copy-start | bytes 589828
  57.6 53.3 %all-to-all-start = ((bf16[8,512,256]{2,1,0:T(8,128)(2,1)}), bf16[8,512,256]{2,1,0:T(8,128)(2,1)S(1)}, u32[]{:S(2)}, u32[]{:S(2)}) async-start(bf16[8,512,256]{2,1,0:T(8,128)(2,1)} %get-tuple-element.42), calls=%async_computation | async-start | bytes 4194304 | tf_op jit(solution)/shard_map/all_to_all | solution.py:444
  64.0 12.4 %collective-permute-start.7 = (bf16[6,128,128]{2,1,0:T(8,128)(2,1)S(1)}, bf16[6,128,128]{2,1,0:T(8,128)(2,1)S(1)}, u32[]{:S(2)}, u32[]{:S(2)}) collective-permute-start(bf16[6,128,128]{2,1,0:T(8,128)(2,1)S(1)} %copy-done.13), channel_id=1, source_target_pairs={{0,32},{32,64},{64,96},{96,128},{128,160},{160,192},{192,224},{224... | collective-permute-start | bytes 589832 | tf_op jit(solution)/shard_map/ppermute | solution.py:390
  64.3 0.8 copy-start.7
  76.4 0.7 copy-start.16
  85.1 9.1 %collective-permute-start.9 = (bf16[2048,128]{1,0:T(8,128)(2,1)}, bf16[2048,128]{1,0:T(8,128)(2,1)S(1)}, u32[]{:S(2)}, u32[]{:S(2)}) collective-permute-start(bf16[2048,128]{1,0:T(8,128)(2,1)} %get-tuple-element.37), channel_id=1, source_target_pairs={{0,8},{8,0},{1,9},{9,1},{2,10},{10,2},{3,11},{11,3},{4,12},{12,4},... | collective-permute-start | bytes 1572872 | tf_op jit(solution)/shard_map/ppermute | solution.py:386
  86.1 8.1 %collective-permute-start.10 = (f32[16,1,128]{2,1,0:T(1,128)}, f32[16,1,128]{2,1,0:T(1,128)S(1)}, u32[]{:S(2)}, u32[]{:S(2)}) collective-permute-start(f32[16,1,128]{2,1,0:T(1,128)} %get-tuple-element.38), channel_id=1, source_target_pairs={{0,8},{8,0},{1,9},{9,1},{2,10},{10,2},{3,11},{11,3},{4,12},{12,4},... | collective-permute-start | bytes 24584 | tf_op jit(solution)/shard_map/ppermute | solution.py:386
  94.2 0.6 copy-start.5
  94.2 0.8 copy-start.4
  97.4 13.5 %collective-permute-start.11 = (bf16[2048,128]{1,0:T(8,128)(2,1)}, bf16[2048,128]{1,0:T(8,128)(2,1)S(1)}, u32[]{:S(2)}, u32[]{:S(2)}) collective-permute-start(bf16[2048,128]{1,0:T(8,128)(2,1)} %get-tuple-element.39.own), channel_id=1, source_target_pairs={{0,16},{16,0},{1,17},{17,1},{2,18},{18,2},{3,19},{19,3},{4,20},{20... | collective-permute-start | bytes 1572872 | tf_op jit(solution)/shard_map/ppermute | solution.py:386
  97.4 13.5 %collective-permute-start.12 = (f32[16,1,128]{2,1,0:T(1,128)}, f32[16,1,128]{2,1,0:T(1,128)S(1)}, u32[]{:S(2)}, u32[]{:S(2)}) collective-permute-start(f32[16,1,128]{2,1,0:T(1,128)} %get-tuple-element.40.own_lse), channel_id=1, source_target_pairs={{0,16},{16,0},{1,17},{17,1},{2,18},{18,2},{3,19},{19,3},{4,20},{20... | collective-permute-start | bytes 24584 | tf_op jit(solution)/shard_map/ppermute | solution.py:386
  110.9 0.6 copy-start.6
  110.9 14.6 %copy-start = (bf16[8,512,256]{2,1,0:T(8,128)(2,1)}, bf16[8,512,256]{2,1,0:T(8,128)(2,1)S(1)}, u32[]{:S(2)}) copy-start(bf16[8,512,256]{2,1,0:T(8,128)(2,1)S(1)} %all-to-all-done.near) | copy-start | bytes 6291460
  111.5 0.9 copy-start.2
  114.7 3.7 %collective-permute-start.13 = (bf16[2,128,1024]{2,1,0:T(8,128)(2,1)}, bf16[2,128,1024]{2,1,0:T(8,128)(2,1)S(1)}, u32[]{:S(2)}, u32[]{:S(2)}) collective-permute-start(bf16[2,128,1024]{2,1,0:T(8,128)(2,1)} %merge_last.1.near), channel_id=1, source_target_pairs={{0,8},{8,0},{1,9},{9,1},{2,10},{10,2},{3,11},{11,3},{4,12},{12,4},... | collective-permute-start | bytes 1572872 | tf_op jit(solution)/shard_map/ppermute | solution.py:386
  116.0 16.9 %collective-permute-start.14 = (bf16[8,512,256]{2,1,0:T(8,128)(2,1)S(1)}, bf16[8,512,256]{2,1,0:T(8,128)(2,1)}, u32[]{:S(2)}, u32[]{:S(2)}) collective-permute-start(bf16[8,512,256]{2,1,0:T(8,128)(2,1)S(1)} %all-to-all-done.near), channel_id=1, source_target_pairs={{0,8},{8,0},{1,9},{9,1},{2,10},{10,2},{3,11},{11,3},{4,12},{12,4},... | collective-permute-start | bytes 6291464 | tf_op jit(solution)/shard_map/ppermute | solution.py:386
  118.5 0.8 copy-start.8
  125.4 37.2 %all-to-all-start.1 = ((bf16[32,128,256]{2,1,0:T(8,128)(2,1)}), bf16[32,128,256]{2,1,0:T(8,128)(2,1)}, u32[]{:S(2)}, u32[]{:S(2)}) async-start(bf16[32,128,256]{2,1,0:T(8,128)(2,1)} %bitcast.18), calls=%async_computation.1 | async-start | bytes 4194304 | tf_op jit(solution)/shard_map/all_to_all | solution.py:458
  167.6 14.5 %all-to-all-start.2 = ((bf16[8,144,256]{2,1,0:T(8,128)(2,1)}), bf16[8,144,256]{2,1,0:T(8,128)(2,1)S(1)}, u32[]{:S(2)}, u32[]{:S(2)}) async-start(bf16[8,144,256]{2,1,0:T(8,128)(2,1)} %get-tuple-element.45), calls=%async_computation.2 | async-start | bytes 1179648 | tf_op jit(solution)/shard_map/all_to_all | solution.py:464
  182.1 0.8 copy-start.1
Sparse Core Ops, SparseCore 0:
  9.8 71.2 all-gather.2

commit v5 on v4

--- a/solution.py
+++ b/solution.py
@@ -20,6 +20,7 @@
 HEAD_AXES = ("x", "yh")
 VMEM = 56 * 1024 * 1024
 CHUNK = 512
+DISTANCES = (0, -1, 1, -2, 2, -3, 3, 4)
 BLOCKS = 3
 
 
@@ -98,8 +99,9 @@
     return jnp.transpose(column)[0:1, :]
 
 
-def attend_kernel(cached, fresh, first, last, rc, place, query, *refs):
+def attend_kernel(cached, fresh, n_queries, first, last, first_rc, place, *refs):
     n_in = 1 + max([max(k, v) for k, v in cached] + [max(p[0], p[1]) for pair in fresh for p in pair])
+    queries, refs = refs[:n_queries], refs[n_queries:]
     pieces, rest = refs[:n_in], list(refs[n_in:])
     if not first:
         acc_in, m_in = rest[:2]
@@ -108,8 +110,17 @@
         out, lse_out = rest[:2]
     else:
         acc_out, m_out = rest[:2]
-    keys, values = rest[2:]
+    keys, values, query = rest[2:]
     step = pl.program_id(0)
+    each = pl.num_programs(0) // n_queries
+    for k, ref in enumerate(queries):
+
+        @pl.when(step // each == k)
+        def _():
+            query[...] = ref[...]
+
+    which = step // each
+    rc, ryl = first_rc + which // 2, lax.rem(which, 2)
     z, yl, c = place[0], place[1], place[2]
     steps = len(cached) + len(fresh)
 
@@ -128,8 +139,6 @@
                 at += ROWS
         values[:, HEAD:] = jnp.ones((steps * 2 * ROWS, HEAD), jnp.bfloat16)
 
-    per_block = GROUP * ROWS // CHUNK
-    ryl = step // per_block
     block = z * 4 + (yl ^ ryl) * 2 + (c ^ rc)
     inside = lax.broadcasted_iota(jnp.int32, (CHUNK, 1), 0) & (ROWS - 1)
     query_token = block * ROWS + inside
@@ -166,15 +175,26 @@
         lse_out[step * (CHUNK // ROWS) + k] = row_of(lse[k * ROWS : (k + 1) * ROWS, :])
 
 
-def attend(place, rc, query, pieces, cached, fresh, state=None, last=False):
-    rows = query.shape[0]
+def attend(place, queries, first_rc, pieces, cached, fresh, state=None, offset=0, last=False):
+    each = queries[0].shape[0] // CHUNK
+    rows = each * len(queries) * CHUNK
     total = 2 * ROWS * (len(cached) + len(fresh))
+    first_block = offset // CHUNK
+
+    def query_spec(k):
+        return pl.BlockSpec(
+            (CHUNK, HEAD), lambda i, s: (jnp.clip(i - k * each, 0, each - 1), 0)
+        )
+
     row_spec = pl.BlockSpec((CHUNK, HEAD), lambda i, s: (i, 0))
-    wide_spec = pl.BlockSpec((CHUNK, 2 * HEAD), lambda i, s: (i, 0))
-    in_specs = [row_spec] + [pl.BlockSpec(p.shape, lambda i, s: (0, 0, 0)) for p in pieces]
-    args = [query, *pieces]
+    in_specs = [query_spec(k) for k in range(len(queries))]
+    in_specs += [pl.BlockSpec(p.shape, lambda i, s: (0, 0, 0)) for p in pieces]
+    args = [*queries, *pieces]
     if state is not None:
-        in_specs += [wide_spec, row_spec]
+        in_specs += [
+            pl.BlockSpec((CHUNK, 2 * HEAD), lambda i, s: (i + first_block, 0)),
+            pl.BlockSpec((CHUNK, HEAD), lambda i, s: (i + first_block, 0)),
+        ]
         args += list(state)
     if last:
         out_specs = [row_spec, pl.BlockSpec((rows // ROWS, 1, ROWS), lambda i, s: (0, 0, 0))]
@@ -183,13 +203,15 @@
             jax.ShapeDtypeStruct((rows // ROWS, 1, ROWS), jnp.float32),
         )
     else:
-        out_specs = [wide_spec, row_spec]
+        out_specs = [pl.BlockSpec((CHUNK, 2 * HEAD), lambda i, s: (i, 0)), row_spec]
         out_shape = (
             jax.ShapeDtypeStruct((rows, 2 * HEAD), jnp.float32),
             jax.ShapeDtypeStruct((rows, HEAD), jnp.float32),
         )
     return pl.pallas_call(
-        functools.partial(attend_kernel, cached, fresh, state is None, last, rc),
+        functools.partial(
+            attend_kernel, cached, fresh, len(queries), state is None, last, first_rc
+        ),
         grid_spec=pltpu.PrefetchScalarGridSpec(
             num_scalar_prefetch=1,
             grid=(rows // CHUNK,),
@@ -198,6 +220,7 @@
             scratch_shapes=[
                 pltpu.VMEM((HEAD, total), jnp.bfloat16),
                 pltpu.VMEM((total, 2 * HEAD), jnp.bfloat16),
+                pltpu.VMEM((CHUNK, HEAD), jnp.bfloat16),
             ],
         ),
         out_shape=out_shape,
@@ -267,26 +290,31 @@
     )(own, own_lse, other, other_lse)
 
 
-def project_kernel(place, near, far, weights, out):
-    yl, c = place[1], place[2]
-    for rc, rows in ((0, near), (1, far)):
-        lhs = rows[...].reshape(2 * ROWS, GROUP * HEAD)
-        for target in range(Z):
-            product = jnp.dot(lhs, weights[target], preferred_element_type=jnp.float32)
-            product = product.astype(jnp.bfloat16)
-            for ryl in range(2):
-                q = (yl ^ ryl) * 2 + (c ^ rc)
-                out[q, target] = product[ryl * ROWS : (ryl + 1) * ROWS, :]
+def project_kernel(place, near, far, *refs):
+    weights, out, rows = refs[:Z], refs[Z], refs[Z + 1]
+    z, yl, c = place[0], place[1], place[2]
+    for ryl in range(2):
+        rows[ryl * ROWS : (ryl + 1) * ROWS, :] = near[ryl]
+        rows[(2 + ryl) * ROWS : (3 + ryl) * ROWS, :] = far[ryl]
+    lhs = rows[...]
+    for weight, distance in zip(weights, DISTANCES):
+        product = jnp.dot(lhs, weight[...], preferred_element_type=jnp.float32)
+        product = product.astype(jnp.bfloat16)
+        target = lax.rem(z + distance + Z, Z)
+        for k in range(4):
+            q = (yl ^ (k % 2)) * 2 + (c ^ (k // 2))
+            out[q, target] = product[k * ROWS : (k + 1) * ROWS, :]
 
 
 def project(place, near, far, weights):
     vmem = pl.BlockSpec(memory_space=pltpu.VMEM)
-    columns = weights.shape[2]
+    columns = weights[0].shape[1]
     return pl.pallas_call(
         project_kernel,
-        in_specs=[pl.BlockSpec(memory_space=pltpu.SMEM)] + [vmem] * 3,
+        in_specs=[pl.BlockSpec(memory_space=pltpu.SMEM)] + [vmem] * (2 + Z),
         out_specs=vmem,
         out_shape=jax.ShapeDtypeStruct((4, Z, ROWS, columns), jnp.bfloat16),
+        scratch_shapes=[pltpu.VMEM((4 * ROWS, GROUP * HEAD), jnp.bfloat16)],
         compiler_params=params(),
         name="project",
         cost_estimate=pl.CostEstimate(
@@ -294,7 +322,7 @@
             bytes_accessed=7_000_000,
             transcendentals=0,
         ),
-    )(place, near, far, weights)
+    )(place, near, far, *weights)
 
 
 PAD = 16
@@ -425,33 +453,60 @@
         layer3_key_value_weight.reshape(Z, 2, MODEL_WIDTH // Z // 2, 2 * HEAD),
     )
     rotated_query = rotated_query.reshape(GROUP * ROWS, HEAD)
-    near_query = jnp.concatenate([rotated_query, swap(rotated_query, "yl")], axis=0)
-    far_query = swap(near_query, "c")
-    weights = lax.all_gather(out_weight, "z")
-    kv_1 = list(after(step([kv, kv]), near_query))
-    kv_2 = step(kv_1)
+    across = swap(rotated_query, "yl")
+    other_core = swap(rotated_query, "c")
+    kv_1, across = lax.optimization_barrier((step([kv, kv]), across))
+    near_query, far_query = [rotated_query, across], [other_core, swap(across, "c")]
+    own_weight = after(out_weight, *kv_1)
+    weights_1 = step([own_weight, own_weight])
+    state = attend(
+        place,
+        near_query + far_query,
+        0,
+        [kv, *kv_1],
+        [(0, 0), (1, 1), (2, 2)],
+        [[(0, 0, 0), (1, 1, -1)]],
+    )
+    kv_2 = list(after(step(kv_1), state))
     kv_3 = step(kv_2)
-    early = [kv, *kv_1, *kv_2]
-    early_cached = [(i, i) for i in range(5)]
-    early_fresh = [[(0, 0, 0), (1, 1, -1)], [(2, 2, 1), (3, 3, -2)]]
+    near_query, far_query, kv_3, state, weights_1 = lax.optimization_barrier(
+        (near_query, far_query, kv_3, state, weights_1)
+    )
+    weights_2 = step(weights_1)
+    third_rows = after(third_rows, *kv_2)
+    third_near = lax.all_to_all(third_rows, HEAD_AXES, 0, 0, tiled=True)
+    third_far = swap(third_near, "c")
+    kv_4 = along_z(kv_3[0], 1)
+    state = attend(
+        place,
+        near_query + far_query,
+        0,
+        [kv_1[1], *kv_2],
+        [(1, 1), (2, 2)],
+        [[(0, 0, 1), (1, 1, -2)]],
+        state,
+    )
+    kv_4, state = lax.optimization_barrier((kv_4, state))
+    late = [kv_2[1], *kv_3, kv_4]
     late_cached = [(1, 1), (2, 2), (3, 3)]
     late_fresh = [[(0, 0, 2), (1, 1, -3)], [(2, 2, 3), (3, 3, 4)]]
-    near_state = attend(place, 0, near_query, early, early_cached, early_fresh)
-    kv_3 = list(after(kv_3, near_state))
-    late = [kv_2[1], *kv_3, along_z(kv_3[0], 1)]
-    far_query = after(far_query, near_state)
-    third_rows = after(third_rows, *kv_3)
-    third_near = lax.all_to_all(third_rows, HEAD_AXES, 0, 0, tiled=True)
-    third_far = swap(third_near, "c")
-    far_state = attend(place, 1, far_query, early, early_cached, early_fresh)
-    send, send_lse = attend(place, 1, far_query, late, late_cached, late_fresh, far_state, True)
+    state = after(state, *weights_2)
+    weights_3 = step(weights_2)
+    send, send_lse = attend(
+        place, far_query, 1, late, late_cached, late_fresh, state, 2 * GROUP * ROWS, True
+    )
     got, got_lse = swap(send, "c"), swap(send_lse, "c")
-    own, own_lse = attend(place, 0, near_query, late, late_cached, late_fresh, near_state, True)
+    own, own_lse = attend(
+        place, near_query, 0, late, late_cached, late_fresh, state, 0, True
+    )
+    got_lse = after(got_lse, *weights_3)
     own, own_lse = merge(own, own_lse, got, got_lse)
     got, got_lse = swap(own, "yl"), swap(own_lse, "yl")
+    weights_4 = along_z(weights_3[0], 1)
     got_lse = after(got_lse, third_near)
     near = merge_last(own, own_lse, got, got_lse)
     far = swap(near, "c")
+    weights = [out_weight, *weights_1, *weights_2, *weights_3, weights_4]
 
     products = project(place, near, far, weights)
     products = products.reshape(4 * Z, *products.shape[2:])

time: 193 us -> 183 us (0.948)
  between operations: 14.9 us -> 1.58 us
  starting transfers between devices: 41.3 us -> 48.1 us
  Pallas kernels: 56.5 us -> 61.8 us
  waiting for transfers between devices: 69 us -> 63.9 us
  local copies, waits for them, and re-layouts: 6.79 us -> 4.71 us
    ppermute x7 -> x14, starting transfers between devices: 11.8 us -> 19.2 us  [along_z(): return lax.ppermute(x, 'z', [(i, (i + distance) % Z) for i in range(Z)])]
    pallas_call x4, Pallas kernels: 34.4 us -> 39.7 us  [attend(): pl.pallas_call(functools.partial(attend_kernel, cached, fresh, len(querie...]
    ppermute x7 -> x14, waiting for transfers between devices: 13.7 us -> 9.36 us  [along_z(): return lax.ppermute(x, 'z', [(i, (i + distance) % Z) for i in range(Z)])]
    unnamed x34 -> x42, local copies, waits for them, and re-layouts: 6.79 us -> 4.7 us
    ppermute x8 -> x9, starting transfers between devices: 12.2 us -> 11.5 us  [swap(): return lax.ppermute(x, axis, [(0, 1), (1, 0)])]
    ppermute x8 -> x9, waiting for transfers between devices: 14.5 us -> 14.5 us  [swap(): return lax.ppermute(x, axis, [(0, 1), (1, 0)])]
  transfers between devices with their start and end apart: 19 -> 26, of which waited for: 7 -> 7; matrix products, arithmetic and copies ran while one was open for 2% -> 0% of each run, Pallas kernels for 26% -> 28%
where the time goes in v5:
time: 183 us
  waiting for transfers between devices  63.9 us (35%)
  Pallas kernels  61.8 us (34%)
  starting transfers between devices  48.1 us (26%)
  local copies, waits for them, and re-layouts  4.71 us (3%)
  other arithmetic  2.48 us (1%)
    pallas_call x4, Pallas kernels, attend(): pl.pallas_call(functools.partial(attend_kernel, cached, fresh, len(querie...  39.7 us
    all_to_all x1, waiting for transfers between devices, local(): lax.all_to_all(products, ('yl', 'c', 'x', 'yh'), 0, 0, tiled=True)  29.8 us
    ppermute x14, starting transfers between devices, along_z(): return lax.ppermute(x, 'z', [(i, (i + distance) % Z) for i in range(Z)])  19.2 us
    ppermute x9, waiting for transfers between devices, swap(): return lax.ppermute(x, axis, [(0, 1), (1, 0)])  14.5 us
    ppermute x9, starting transfers between devices, swap(): return lax.ppermute(x, axis, [(0, 1), (1, 0)])  11.5 us
    all_to_all x1, waiting for transfers between devices, local(): partial = lax.all_to_all(partial, HEAD_AXES, 0, 0, tiled=True)  10.3 us
    ppermute x14, waiting for transfers between devices, along_z(): return lax.ppermute(x, 'z', [(i, (i + distance) % Z) for i in range(Z)])  9.36 us
    all_to_all x1, starting transfers between devices, local(): lax.all_to_all(products, ('yl', 'c', 'x', 'yh'), 0, 0, tiled=True)  7.5 us
  transfers between devices with their start and end apart: 26, of which 7 were waited for; matrix products, arithmetic and copies ran while one was open for 0% of the time, Pallas kernels for 28%

profile of v5, /device:TPU:1, one launch (start us, length us, event | category | flops | bytes accessed | tf_op | source)
XLA Modules:
  0.0 182.7 jit_solution(16505834131613205216)
XLA Ops:
  0.7 0.7 convert_element_type.36
  1.4 0.3 fusion.2
  1.7 0.8 pad_maximum_fusion
  2.5 0.7 pad_add_fusion.place
  3.1 4.1 %prepare.1 = (bf16[8,128,128]{2,1,0:T(8,128)(2,1)}, bf16[6,128,128]{2,1,0:T(8,128)(2,1)}, bf16[8,512,256]{2,1,0:T(8,128)(2,1)}) custom-call(s32[3]{0:T(128)} %pad_add_fusion.place, bf16[128,1024]{1,0:T(8,128)(2,1)} %query.1, bf16[2,128,128]{2,1,0:T(8,128)(2,1)} %fresh.1, bf16[2,256,128]{2,1,0:T(8,128)(2,1)} %cached.1, f32[128,128]{1,0:T(8,128)} %get-tuple-element.86.cosine, ...), custom_call_target="tpu_custom_call" | custom-call | flops 2000000 | bytes 5500000 | tf_op jit(solution)/shard_map/prepare/pallas_call | solution.py:76
  7.3 2.2 %collective-permute-start.2 = (bf16[1024,128]{1,0:T(8,128)(2,1)}, bf16[1024,128]{1,0:T(8,128)(2,1)S(1)}, u32[]{:S(2)}, u32[]{:S(2)}) collective-permute-start(bf16[1024,128]{1,0:T(8,128)(2,1)} %bitcast.18), channel_id=1, source_target_pairs={{0,16},{16,0},{1,17},{17,1},{2,18},{18,2},{3,19},{19,3},{4,20},{20... | collective-permute-start | bytes 786440 | tf_op jit(solution)/shard_map/ppermute | solution.py:414
  9.5 1.6 collective-permute-start
  11.1 3.9 %collective-permute-start.1 = (bf16[6,128,128]{2,1,0:T(8,128)(2,1)}, bf16[6,128,128]{2,1,0:T(8,128)(2,1)S(1)}, u32[]{:S(2)}, u32[]{:S(2)}) collective-permute-start(bf16[6,128,128]{2,1,0:T(8,128)(2,1)} %get-tuple-element.42.refs_4_), channel_id=1, source_target_pairs={{0,224},{32,0},{64,32},{96,64},{128,96},{160,128},{192,160},{224,1... | collective-permute-start | bytes 589832 | tf_op jit(solution)/shard_map/ppermute | solution.py:418
  15.1 1.2 collective-permute-start.3
  16.3 3.3 %collective-permute-done.refs_5_ = bf16[6,128,128]{2,1,0:T(8,128)(2,1)S(1)} collective-permute-done((bf16[6,128,128]{2,1,0:T(8,128)(2,1)}, bf16[6,128,128]{2,1,0:T(8,128)(2,1)S(1)}, u32[]{:S(2)}, u32[]{:S(2)}) %collective-permute-start) | collective-permute-done | bytes 196640 | tf_op jit(solution)/shard_map/ppermute | solution.py:418
  19.6 1.6 collective-permute-start.4
  21.3 2.7 %collective-permute-start.10 = (bf16[1024,256]{1,0:T(8,128)(2,1)}, bf16[1024,256]{1,0:T(8,128)(2,1)}, u32[]{:S(2)}, u32[]{:S(2)}) collective-permute-start(bf16[1024,256]{1,0:T(8,128)(2,1)} %refs_0_.1), channel_id=1, source_target_pairs={{0,224},{32,0},{64,32},{96,64},{128,96},{160,128},{192,160},{224,1... | collective-permute-start | bytes 1572872 | tf_op jit(solution)/shard_map/ppermute | solution.py:418
  23.9 2.7 %collective-permute-start.6 = (bf16[6,128,128]{2,1,0:T(8,128)(2,1)S(1)}, bf16[6,128,128]{2,1,0:T(8,128)(2,1)S(1)}, u32[]{:S(2)}, u32[]{:S(2)}) collective-permute-start(bf16[6,128,128]{2,1,0:T(8,128)(2,1)S(1)} %collective-permute-done.1.refs_6_.refs_4_), channel_id=1, source_target_pairs={{0,224},{32,0},{64,32},{96,64},{128,96},{160,128},{192,160},{224,1... | collective-permute-start | bytes 589832 | tf_op jit(solution)/shard_map/ppermute | solution.py:418
  26.7 0.7 copy-done.5
  27.4 11.9 %attend.4 = (f32[4096,256]{1,0:T(8,128)}, f32[4096,128]{1,0:T(8,128)}) custom-call(s32[3]{0:T(128)} %pad_add_fusion.place, bf16[1024,128]{1,0:T(8,128)(2,1)} %bitcast.20, bf16[1024,128]{1,0:T(8,128)(2,1)} %copy-done.3, bf16[1024,128]{1,0:T(8,128)(2,1)} %copy-done.4, bf16[1024,128]{1,0:T(8,128)(2,1)} %copy-done.5, ...), custom_call_target="tpu_custom_call" | custom-call | flops 2147483648 | bytes 4718592 | tf_op jit(solution)/shard_map/attend/pallas_call | solution.py:211
  39.3 3.4 %collective-permute-done.5.refs_5_ = bf16[6,128,128]{2,1,0:T(8,128)(2,1)S(1)} collective-permute-done((bf16[6,128,128]{2,1,0:T(8,128)(2,1)S(1)}, bf16[6,128,128]{2,1,0:T(8,128)(2,1)S(1)}, u32[]{:S(2)}, u32[]{:S(2)}) %collective-permute-start.5) | collective-permute-done | bytes 196640 | tf_op jit(solution)/shard_map/ppermute | solution.py:418
  42.7 0.1 collective-permute-start.7
  42.8 2.7 %collective-permute-start.8 = (bf16[6,128,128]{2,1,0:T(8,128)(2,1)S(1)}, bf16[6,128,128]{2,1,0:T(8,128)(2,1)S(1)}, u32[]{:S(2)}, u32[]{:S(2)}) collective-permute-start(bf16[6,128,128]{2,1,0:T(8,128)(2,1)S(1)} %collective-permute-done.6.refs_6_.refs_2_), channel_id=1, source_target_pairs={{0,224},{32,0},{64,32},{96,64},{128,96},{160,128},{192,160},{224,1... | collective-permute-start | bytes 589832 | tf_op jit(solution)/shard_map/ppermute | solution.py:418
  45.5 6.4 %all-to-all-start = ((bf16[8,512,256]{2,1,0:T(8,128)(2,1)}), bf16[8,512,256]{2,1,0:T(8,128)(2,1)S(1)}, u32[]{:S(2)}, u32[]{:S(2)}) async-start(bf16[8,512,256]{2,1,0:T(8,128)(2,1)} %get-tuple-element.76), calls=%async_computation | async-start | bytes 4194304 | tf_op jit(solution)/shard_map/all_to_all | solution.py:477
  51.9 0.1 collective-permute-start.12
  52.0 2.7 %collective-permute-start.13 = (bf16[1024,256]{1,0:T(8,128)(2,1)}, bf16[1024,256]{1,0:T(8,128)(2,1)S(1)}, u32[]{:S(2)}, u32[]{:S(2)}) collective-permute-start(bf16[1024,256]{1,0:T(8,128)(2,1)} %collective-permute-done.10.refs_2_), channel_id=1, source_target_pairs={{0,224},{32,0},{64,32},{96,64},{128,96},{160,128},{192,160},{224,1... | collective-permute-start | bytes 1572872 | tf_op jit(solution)/shard_map/ppermute | solution.py:418
  54.6 11.7 %attend.5 = (f32[4096,256]{1,0:T(8,128)}, f32[4096,128]{1,0:T(8,128)}) custom-call(s32[3]{0:T(128)} %pad_add_fusion.place, bf16[1024,128]{1,0:T(8,128)(2,1)} %bitcast.21, bf16[1024,128]{1,0:T(8,128)(2,1)} %copy-done.3, bf16[1024,128]{1,0:T(8,128)(2,1)} %copy-done.4, bf16[1024,128]{1,0:T(8,128)(2,1)} %copy-done.5, bf16[6,128,128]{2,1,0:T(8,128)(2,1)} %copy-done.11, ...), custom_call_target="tpu_custom_call" | custom-call | flops 1610612736 | bytes 4587520 | tf_op jit(solution)/shard_map/attend/pallas_call | solution.py:211
  66.3 2.7 %collective-permute-done.11.refs_5_ = bf16[6,128,128]{2,1,0:T(8,128)(2,1)S(1)} collective-permute-done((bf16[6,128,128]{2,1,0:T(8,128)(2,1)S(1)}, bf16[6,128,128]{2,1,0:T(8,128)(2,1)S(1)}, u32[]{:S(2)}, u32[]{:S(2)}) %collective-permute-start.11) | collective-permute-done | bytes 196640 | tf_op jit(solution)/shard_map/ppermute | solution.py:418
  69.0 0.1 collective-permute-start.16
  69.1 2.7 %collective-permute-start.17 = (bf16[1024,256]{1,0:T(8,128)(2,1)S(1)}, bf16[1024,256]{1,0:T(8,128)(2,1)S(1)}, u32[]{:S(2)}, u32[]{:S(2)}) collective-permute-start(bf16[1024,256]{1,0:T(8,128)(2,1)S(1)} %collective-permute-done.13.refs_4_), channel_id=1, source_target_pairs={{0,224},{32,0},{64,32},{96,64},{128,96},{160,128},{192,160},{224,1... | collective-permute-start | bytes 1572872 | tf_op jit(solution)/shard_map/ppermute | solution.py:418
  71.8 8.1 %attend.7 = (bf16[2048,128]{1,0:T(8,128)(2,1)}, f32[16,1,128]{2,1,0:T(1,128)}) custom-call(s32[3]{0:T(128)} %pad_add_fusion.place, bf16[1024,128]{1,0:T(8,128)(2,1)} %copy-done.4, bf16[1024,128]{1,0:T(8,128)(2,1)} %copy-done.5, bf16[6,128,128]{2,1,0:T(8,128)(2,1)} %copy-done.2, bf16[6,128,128]{2,1,0:T(8,128)(2,1)} %copy-done.6, ...), custom_call_target="tpu_custom_call" | custom-call | flops 1342177280 | bytes 2752512 | tf_op jit(solution)/shard_map/attend/pallas_call | solution.py:211
  79.8 3.6 %collective-permute-start.14 = (bf16[2048,128]{1,0:T(8,128)(2,1)}, bf16[2048,128]{1,0:T(8,128)(2,1)S(1)}, u32[]{:S(2)}, u32[]{:S(2)}) collective-permute-start(bf16[2048,128]{1,0:T(8,128)(2,1)} %get-tuple-element.70), channel_id=1, source_target_pairs={{0,8},{8,0},{1,9},{9,1},{2,10},{10,2},{3,11},{11,3},{4,12},{12,4},... | collective-permute-start | bytes 1572872 | tf_op jit(solution)/shard_map/ppermute | solution.py:414
  83.4 0.1 collective-permute-start.15
  83.5 8.0 %attend.6 = (bf16[2048,128]{1,0:T(8,128)(2,1)}, f32[16,1,128]{2,1,0:T(1,128)}) custom-call(s32[3]{0:T(128)} %pad_add_fusion.place, bf16[1024,128]{1,0:T(8,128)(2,1)} %bitcast.22, bf16[1024,128]{1,0:T(8,128)(2,1)} %copy-done.3, bf16[6,128,128]{2,1,0:T(8,128)(2,1)} %copy-done.2, bf16[6,128,128]{2,1,0:T(8,128)(2,1)} %copy-done.6, ...), custom_call_target="tpu_custom_call" | custom-call | flops 1342177280 | bytes 2752512 | tf_op jit(solution)/shard_map/attend/pallas_call | solution.py:211
  91.6 0.5 copy-done.13
  92.2 0.3 copy-done.10
  92.5 2.4 %merge.1 = (bf16[2048,128]{1,0:T(8,128)(2,1)}, f32[16,1,128]{2,1,0:T(1,128)}) custom-call(bf16[2048,128]{1,0:T(8,128)(2,1)} %get-tuple-element.68.own, f32[16,1,128]{2,1,0:T(1,128)} %get-tuple-element.69.own_lse, bf16[2048,128]{1,0:T(8,128)(2,1)} %copy-done.10, f32[16,1,128]{2,1,0:T(1,128)} %copy-done.13), custom_call_target="tpu_custom_call" | custom-call | flops 2000000 | bytes 1600000 | tf_op jit(solution)/shard_map/merge/pallas_call | solution.py:271
  94.9 1.5 collective-permute-start.19
  96.3 12.0 %collective-permute-done.19.other_lse = f32[16,1,128]{2,1,0:T(1,128)S(1)} collective-permute-done((f32[16,1,128]{2,1,0:T(1,128)}, f32[16,1,128]{2,1,0:T(1,128)S(1)}, u32[]{:S(2)}, u32[]{:S(2)}) %collective-permute-start.19) | collective-permute-done | bytes 8224 | tf_op jit(solution)/shard_map/ppermute | solution.py:414
  108.3 0.6 copy-done.14
  108.9 0.9 copy-done.9
  109.8 2.4 %merge_last.1.near = bf16[2,128,1024]{2,1,0:T(8,128)(2,1)} custom-call(bf16[2048,128]{1,0:T(8,128)(2,1)} %get-tuple-element.73.own, f32[16,1,128]{2,1,0:T(1,128)} %get-tuple-element.74.own_lse, bf16[2048,128]{1,0:T(8,128)(2,1)} %copy-done.9, f32[16,1,128]{2,1,0:T(1,128)} %copy-done.14), custom_call_target="tpu_custom_call" | custom-call | flops 2000000 | bytes 1600000 | tf_op jit(solution)/shard_map/merge_last/pallas_call | solution.py:284
  112.2 1.3 collective-permute-start.20
  113.5 2.5 %collective-permute-done.20.far = bf16[2,128,1024]{2,1,0:T(8,128)(2,1)S(1)} collective-permute-done((bf16[2,128,1024]{2,1,0:T(8,128)(2,1)}, bf16[2,128,1024]{2,1,0:T(8,128)(2,1)S(1)}, u32[]{:S(2)}, u32[]{:S(2)}) %collective-permute-start.20) | collective-permute-done | bytes 524320 | tf_op jit(solution)/shard_map/ppermute | solution.py:414
  115.9 0.8 copy-done.19
  116.7 6.3 %project.1 = bf16[4,8,128,256]{3,2,1,0:T(8,128)(2,1)} custom-call(s32[3]{0:T(128)} %pad_add_fusion.place, bf16[2,128,1024]{2,1,0:T(8,128)(2,1)} %merge_last.1.near, bf16[2,128,1024]{2,1,0:T(8,128)(2,1)} %copy-done.19, bf16[1024,256]{1,0:T(8,128)(2,1)} %refs_0_.1, bf16[1024,256]{1,0:T(8,128)(2,1)} %collective-permute-done.9.refs_1_, ...), custom_call_target="tpu_custom_call" | custom-call | flops 2147483648 | bytes 7000000 | tf_op jit(solution)/shard_map/project/pallas_call | solution.py:312
  123.0 7.5 %all-to-all-start.1 = ((bf16[32,128,256]{2,1,0:T(8,128)(2,1)}), bf16[32,128,256]{2,1,0:T(8,128)(2,1)}, u32[]{:S(2)}, u32[]{:S(2)}) async-start(bf16[32,128,256]{2,1,0:T(8,128)(2,1)} %bitcast.17), calls=%async_computation.1 | async-start | bytes 4194304 | tf_op jit(solution)/shard_map/all_to_all | solution.py:513
  130.5 29.8 %all-to-all-done.1 = bf16[32,128,256]{2,1,0:T(8,128)(2,1)} async-done(((bf16[32,128,256]{2,1,0:T(8,128)(2,1)}), bf16[32,128,256]{2,1,0:T(8,128)(2,1)}, u32[]{:S(2)}, u32[]{:S(2)}) %all-to-all-start.1) | async-done | bytes 2097184 | tf_op jit(solution)/shard_map/all_to_all | solution.py:513
  160.3 4.9 %third.1 = (bf16[128,1024]{1,0:T(8,128)(2,1)}, bf16[8,144,256]{2,1,0:T(8,128)(2,1)}) custom-call(s32[3]{0:T(128)} %pad_add_fusion.place, bf16[4,8,128,256]{3,2,1,0:T(8,128)(2,1)} %bitcast.9.received, bf16[128,1024]{1,0:T(8,128)(2,1)} %hidden.1, f32[1,1024]{1,0:T(1,128)} %bitcast.23, bf16[8,512,256]{2,1,0:T(8,128)(2,1)} %copy-done, ...), custom_call_target="tpu_custom_call" | custom-call | tf_op jit(solution)/shard_map/third/pallas_call | solution.py:366
  165.2 3.5 %all-to-all-start.2 = ((bf16[8,144,256]{2,1,0:T(8,128)(2,1)}), bf16[8,144,256]{2,1,0:T(8,128)(2,1)S(1)}, u32[]{:S(2)}, u32[]{:S(2)}) async-start(bf16[8,144,256]{2,1,0:T(8,128)(2,1)} %get-tuple-element.79), calls=%async_computation.2 | async-start | bytes 1179648 | tf_op jit(solution)/shard_map/all_to_all | solution.py:519
  169.4 10.3 %all-to-all-done.2.partial = bf16[8,144,256]{2,1,0:T(8,128)(2,1)S(1)} async-done(((bf16[8,144,256]{2,1,0:T(8,128)(2,1)}), bf16[8,144,256]{2,1,0:T(8,128)(2,1)S(1)}, u32[]{:S(2)}, u32[]{:S(2)}) %all-to-all-start.2) | async-done | bytes 589856 | tf_op jit(solution)/shard_map/all_to_all | solution.py:519
  179.7 0.8 copy-done.1
  180.6 2.1 %final.1 = bf16[128,256]{1,0:T(8,128)(2,1)} custom-call(s32[1]{0:T(128)S(6)} %copy.13.count, bf16[8,144,256]{2,1,0:T(8,128)(2,1)} %copy-done.1, f32[1,256]{1,0:T(1,128)} %bitcast.24, f32[128,128]{1,0:T(8,128)} %get-tuple-element.86.cosine, f32[128,128]{1,0:T(8,128)} %get-tuple-element.87.sine, s32[1,128]{1,0:T(1,128)} %bitcast.25), custom_call_target="tpu_custom_call" | custom-call | tf_op jit(solution)/shard_map/final/pallas_call | solution.py:403
  (64 shorter events, 0.2 us)
Async XLA Ops:
  7.3 12.3 %collective-permute-start.2 = (bf16[1024,128]{1,0:T(8,128)(2,1)}, bf16[1024,128]{1,0:T(8,128)(2,1)S(1)}, u32[]{:S(2)}, u32[]{:S(2)}) collective-permute-start(bf16[1024,128]{1,0:T(8,128)(2,1)} %bitcast.18), channel_id=1, source_target_pairs={{0,16},{16,0},{1,17},{17,1},{2,18},{18,2},{3,19},{19,3},{4,20},{20... | collective-permute-start | bytes 786440 | tf_op jit(solution)/shard_map/ppermute | solution.py:414
  9.5 10.1 %collective-permute-start = (bf16[6,128,128]{2,1,0:T(8,128)(2,1)}, bf16[6,128,128]{2,1,0:T(8,128)(2,1)S(1)}, u32[]{:S(2)}, u32[]{:S(2)}) collective-permute-start(bf16[6,128,128]{2,1,0:T(8,128)(2,1)} %get-tuple-element.42.refs_4_), channel_id=1, source_target_pairs={{0,32},{32,64},{64,96},{96,128},{128,160},{160,192},{192,224},{224... | collective-permute-start | bytes 589832 | tf_op jit(solution)/shard_map/ppermute | solution.py:418
  11.1 8.5 %collective-permute-start.1 = (bf16[6,128,128]{2,1,0:T(8,128)(2,1)}, bf16[6,128,128]{2,1,0:T(8,128)(2,1)S(1)}, u32[]{:S(2)}, u32[]{:S(2)}) collective-permute-start(bf16[6,128,128]{2,1,0:T(8,128)(2,1)} %get-tuple-element.42.refs_4_), channel_id=1, source_target_pairs={{0,224},{32,0},{64,32},{96,64},{128,96},{160,128},{192,160},{224,1... | collective-permute-start | bytes 589832 | tf_op jit(solution)/shard_map/ppermute | solution.py:418
  15.1 8.9 %collective-permute-start.3 = (bf16[1024,128]{1,0:T(8,128)(2,1)}, bf16[1024,128]{1,0:T(8,128)(2,1)S(1)}, u32[]{:S(2)}, u32[]{:S(2)}) collective-permute-start(bf16[1024,128]{1,0:T(8,128)(2,1)} %bitcast.19), channel_id=1, source_target_pairs={{0,8},{8,0},{1,9},{9,1},{2,10},{10,2},{3,11},{11,3},{4,12},{12,4},... | collective-permute-start | bytes 786440 | tf_op jit(solution)/shard_map/ppermute | solution.py:414
  19.6 7.1 %copy-start.20 = (bf16[6,128,128]{2,1,0:T(8,128)(2,1)}, bf16[6,128,128]{2,1,0:T(8,128)(2,1)S(1)}, u32[]{:S(2)}) copy-start(bf16[6,128,128]{2,1,0:T(8,128)(2,1)S(1)} %collective-permute-done.refs_5_) | copy-start | bytes 589828
  19.6 7.1 %copy-start.11 = (bf16[6,128,128]{2,1,0:T(8,128)(2,1)}, bf16[6,128,128]{2,1,0:T(8,128)(2,1)S(1)}, u32[]{:S(2)}) copy-start(bf16[6,128,128]{2,1,0:T(8,128)(2,1)S(1)} %collective-permute-done.1.refs_6_.refs_4_) | copy-start | bytes 589828
  19.6 7.1 %copy-start.3 = (bf16[1024,128]{1,0:T(8,128)(2,1)}, bf16[1024,128]{1,0:T(8,128)(2,1)S(1)}, u32[]{:S(2)}) copy-start(bf16[1024,128]{1,0:T(8,128)(2,1)S(1)} %collective-permute-done.2.refs_1_) | copy-start | bytes 786436
  19.6 7.1 %collective-permute-start.4 = (bf16[1024,128]{1,0:T(8,128)(2,1)S(1)}, bf16[1024,128]{1,0:T(8,128)(2,1)S(1)}, u32[]{:S(2)}, u32[]{:S(2)}) collective-permute-start(bf16[1024,128]{1,0:T(8,128)(2,1)S(1)} %collective-permute-done.2.refs_1_), channel_id=1, source_target_pairs={{0,8},{8,0},{1,9},{9,1},{2,10},{10,2},{3,11},{11,3},{4,12},{12,4},... | collective-permute-start | bytes 786440 | tf_op jit(solution)/shard_map/ppermute | solution.py:414
  21.3 30.6 %collective-permute-start.10 = (bf16[1024,256]{1,0:T(8,128)(2,1)}, bf16[1024,256]{1,0:T(8,128)(2,1)}, u32[]{:S(2)}, u32[]{:S(2)}) collective-permute-start(bf16[1024,256]{1,0:T(8,128)(2,1)} %refs_0_.1), channel_id=1, source_target_pairs={{0,224},{32,0},{64,32},{96,64},{128,96},{160,128},{192,160},{224,1... | collective-permute-start | bytes 1572872 | tf_op jit(solution)/shard_map/ppermute | solution.py:418
  23.9 28.0 %collective-permute-start.9 = (bf16[1024,256]{1,0:T(8,128)(2,1)}, bf16[1024,256]{1,0:T(8,128)(2,1)}, u32[]{:S(2)}, u32[]{:S(2)}) collective-permute-start(bf16[1024,256]{1,0:T(8,128)(2,1)} %refs_0_.1), channel_id=1, source_target_pairs={{0,32},{32,64},{64,96},{96,128},{128,160},{160,192},{192,224},{224... | collective-permute-start | bytes 1572872 | tf_op jit(solution)/shard_map/ppermute | solution.py:418
  23.9 18.8 %collective-permute-start.5 = (bf16[6,128,128]{2,1,0:T(8,128)(2,1)S(1)}, bf16[6,128,128]{2,1,0:T(8,128)(2,1)S(1)}, u32[]{:S(2)}, u32[]{:S(2)}) collective-permute-start(bf16[6,128,128]{2,1,0:T(8,128)(2,1)S(1)} %collective-permute-done.refs_5_), channel_id=1, source_target_pairs={{0,32},{32,64},{64,96},{96,128},{128,160},{160,192},{192,224},{224... | collective-permute-start | bytes 589832 | tf_op jit(solution)/shard_map/ppermute | solution.py:418
  23.9 2.8 %copy-start.4 = (bf16[1024,128]{1,0:T(8,128)(2,1)}, bf16[1024,128]{1,0:T(8,128)(2,1)S(1)}, u32[]{:S(2)}) copy-start(bf16[1024,128]{1,0:T(8,128)(2,1)S(1)} %collective-permute-done.3.refs_2_.refs_0_) | copy-start | bytes 786436
  23.9 18.8 %collective-permute-start.6 = (bf16[6,128,128]{2,1,0:T(8,128)(2,1)S(1)}, bf16[6,128,128]{2,1,0:T(8,128)(2,1)S(1)}, u32[]{:S(2)}, u32[]{:S(2)}) collective-permute-start(bf16[6,128,128]{2,1,0:T(8,128)(2,1)S(1)} %collective-permute-done.1.refs_6_.refs_4_), channel_id=1, source_target_pairs={{0,224},{32,0},{64,32},{96,64},{128,96},{160,128},{192,160},{224,1... | collective-permute-start | bytes 589832 | tf_op jit(solution)/shard_map/ppermute | solution.py:418
  26.7 0.7 copy-start.5
  42.7 2.8 %copy-start.12 = (bf16[6,128,128]{2,1,0:T(8,128)(2,1)}, bf16[6,128,128]{2,1,0:T(8,128)(2,1)S(1)}, u32[]{:S(2)}) copy-start(bf16[6,128,128]{2,1,0:T(8,128)(2,1)S(1)} %collective-permute-done.5.refs_5_) | copy-start | bytes 589828
  42.7 2.8 %copy-start.2 = (bf16[6,128,128]{2,1,0:T(8,128)(2,1)}, bf16[6,128,128]{2,1,0:T(8,128)(2,1)S(1)}, u32[]{:S(2)}) copy-start(bf16[6,128,128]{2,1,0:T(8,128)(2,1)S(1)} %collective-permute-done.6.refs_6_.refs_2_) | copy-start | bytes 589828
  42.7 9.1 %collective-permute-start.7 = (bf16[6,128,128]{2,1,0:T(8,128)(2,1)S(1)}, bf16[6,128,128]{2,1,0:T(8,128)(2,1)S(1)}, u32[]{:S(2)}, u32[]{:S(2)}) collective-permute-start(bf16[6,128,128]{2,1,0:T(8,128)(2,1)S(1)} %collective-permute-done.5.refs_5_), channel_id=1, source_target_pairs={{0,32},{32,64},{64,96},{96,128},{128,160},{160,192},{192,224},{224... | collective-permute-start | bytes 589832 | tf_op jit(solution)/shard_map/ppermute | solution.py:418
  42.8 9.0 %collective-permute-start.8 = (bf16[6,128,128]{2,1,0:T(8,128)(2,1)S(1)}, bf16[6,128,128]{2,1,0:T(8,128)(2,1)S(1)}, u32[]{:S(2)}, u32[]{:S(2)}) collective-permute-start(bf16[6,128,128]{2,1,0:T(8,128)(2,1)S(1)} %collective-permute-done.6.refs_6_.refs_2_), channel_id=1, source_target_pairs={{0,224},{32,0},{64,32},{96,64},{128,96},{160,128},{192,160},{224,1... | collective-permute-start | bytes 589832 | tf_op jit(solution)/shard_map/ppermute | solution.py:418
  45.5 62.9 %all-to-all-start = ((bf16[8,512,256]{2,1,0:T(8,128)(2,1)}), bf16[8,512,256]{2,1,0:T(8,128)(2,1)S(1)}, u32[]{:S(2)}, u32[]{:S(2)}) async-start(bf16[8,512,256]{2,1,0:T(8,128)(2,1)} %get-tuple-element.76), calls=%async_computation | async-start | bytes 4194304 | tf_op jit(solution)/shard_map/all_to_all | solution.py:477
  51.8 14.5 %copy-start.6 = (bf16[6,128,128]{2,1,0:T(8,128)(2,1)}, bf16[6,128,128]{2,1,0:T(8,128)(2,1)S(1)}, u32[]{:S(2)}) copy-start(bf16[6,128,128]{2,1,0:T(8,128)(2,1)S(1)} %collective-permute-done.7.refs_3_) | copy-start | bytes 589828
  51.9 14.5 %copy-start.7 = (bf16[6,128,128]{2,1,0:T(8,128)(2,1)}, bf16[6,128,128]{2,1,0:T(8,128)(2,1)S(1)}, u32[]{:S(2)}) copy-start(bf16[6,128,128]{2,1,0:T(8,128)(2,1)S(1)} %collective-permute-done.8.refs_4_) | copy-start | bytes 589828
  51.9 17.1 %collective-permute-start.12 = (bf16[1024,256]{1,0:T(8,128)(2,1)}, bf16[1024,256]{1,0:T(8,128)(2,1)S(1)}, u32[]{:S(2)}, u32[]{:S(2)}) collective-permute-start(bf16[1024,256]{1,0:T(8,128)(2,1)} %collective-permute-done.9.refs_1_), channel_id=1, source_target_pairs={{0,32},{32,64},{64,96},{96,128},{128,160},{160,192},{192,224},{224... | collective-permute-start | bytes 1572872 | tf_op jit(solution)/shard_map/ppermute | solution.py:418
  52.0 17.0 %collective-permute-start.13 = (bf16[1024,256]{1,0:T(8,128)(2,1)}, bf16[1024,256]{1,0:T(8,128)(2,1)S(1)}, u32[]{:S(2)}, u32[]{:S(2)}) collective-permute-start(bf16[1024,256]{1,0:T(8,128)(2,1)} %collective-permute-done.10.refs_2_), channel_id=1, source_target_pairs={{0,224},{32,0},{64,32},{96,64},{128,96},{160,128},{192,160},{224,1... | collective-permute-start | bytes 1572872 | tf_op jit(solution)/shard_map/ppermute | solution.py:418
  54.6 14.3 %collective-permute-start.11 = (bf16[6,128,128]{2,1,0:T(8,128)(2,1)S(1)}, bf16[6,128,128]{2,1,0:T(8,128)(2,1)S(1)}, u32[]{:S(2)}, u32[]{:S(2)}) collective-permute-start(bf16[6,128,128]{2,1,0:T(8,128)(2,1)S(1)} %collective-permute-done.7.refs_3_), channel_id=1, source_target_pairs={{0,32},{32,64},{64,96},{96,128},{128,160},{160,192},{192,224},{224... | collective-permute-start | bytes 589832 | tf_op jit(solution)/shard_map/ppermute | solution.py:418
  69.0 2.8 %copy-start.8 = (bf16[6,128,128]{2,1,0:T(8,128)(2,1)}, bf16[6,128,128]{2,1,0:T(8,128)(2,1)S(1)}, u32[]{:S(2)}) copy-start(bf16[6,128,128]{2,1,0:T(8,128)(2,1)S(1)} %collective-permute-done.11.refs_5_) | copy-start | bytes 589828
  69.0 10.8 %copy-start.15 = (bf16[1024,256]{1,0:T(8,128)(2,1)}, bf16[1024,256]{1,0:T(8,128)(2,1)S(1)}, u32[]{:S(2)}) copy-start(bf16[1024,256]{1,0:T(8,128)(2,1)S(1)} %collective-permute-done.12.refs_3_) | copy-start | bytes 1572868
  69.0 10.8 %copy-start.16 = (bf16[1024,256]{1,0:T(8,128)(2,1)}, bf16[1024,256]{1,0:T(8,128)(2,1)S(1)}, u32[]{:S(2)}) copy-start(bf16[1024,256]{1,0:T(8,128)(2,1)S(1)} %collective-permute-done.13.refs_4_) | copy-start | bytes 1572868
  69.0 22.6 %collective-permute-start.16 = (bf16[1024,256]{1,0:T(8,128)(2,1)S(1)}, bf16[1024,256]{1,0:T(8,128)(2,1)}, u32[]{:S(2)}, u32[]{:S(2)}) collective-permute-start(bf16[1024,256]{1,0:T(8,128)(2,1)S(1)} %collective-permute-done.12.refs_3_), channel_id=1, source_target_pairs={{0,32},{32,64},{64,96},{96,128},{128,160},{160,192},{192,224},{224... | collective-permute-start | bytes 1572872 | tf_op jit(solution)/shard_map/ppermute | solution.py:418
  69.1 22.5 %collective-permute-start.17 = (bf16[1024,256]{1,0:T(8,128)(2,1)S(1)}, bf16[1024,256]{1,0:T(8,128)(2,1)S(1)}, u32[]{:S(2)}, u32[]{:S(2)}) collective-permute-start(bf16[1024,256]{1,0:T(8,128)(2,1)S(1)} %collective-permute-done.13.refs_4_), channel_id=1, source_target_pairs={{0,224},{32,0},{64,32},{96,64},{128,96},{160,128},{192,160},{224,1... | collective-permute-start | bytes 1572872 | tf_op jit(solution)/shard_map/ppermute | solution.py:418
  79.8 11.8 %collective-permute-start.14 = (bf16[2048,128]{1,0:T(8,128)(2,1)}, bf16[2048,128]{1,0:T(8,128)(2,1)S(1)}, u32[]{:S(2)}, u32[]{:S(2)}) collective-permute-start(bf16[2048,128]{1,0:T(8,128)(2,1)} %get-tuple-element.70), channel_id=1, source_target_pairs={{0,8},{8,0},{1,9},{9,1},{2,10},{10,2},{3,11},{11,3},{4,12},{12,4},... | collective-permute-start | bytes 1572872 | tf_op jit(solution)/shard_map/ppermute | solution.py:414
  83.4 8.1 %collective-permute-start.15 = (f32[16,1,128]{2,1,0:T(1,128)}, f32[16,1,128]{2,1,0:T(1,128)S(1)}, u32[]{:S(2)}, u32[]{:S(2)}) collective-permute-start(f32[16,1,128]{2,1,0:T(1,128)} %get-tuple-element.71), channel_id=1, source_target_pairs={{0,8},{8,0},{1,9},{9,1},{2,10},{10,2},{3,11},{11,3},{4,12},{12,4},... | collective-permute-start | bytes 24584 | tf_op jit(solution)/shard_map/ppermute | solution.py:414
  91.6 0.6 copy-start.13
  91.6 4.7 %copy-start.17 = (bf16[1024,256]{1,0:T(8,128)(2,1)}, bf16[1024,256]{1,0:T(8,128)(2,1)S(1)}, u32[]{:S(2)}) copy-start(bf16[1024,256]{1,0:T(8,128)(2,1)S(1)} %collective-permute-done.17.refs_6_) | copy-start | bytes 1572868
  91.6 0.8 copy-start.10
  94.9 13.5 %collective-permute-start.18 = (bf16[2048,128]{1,0:T(8,128)(2,1)}, bf16[2048,128]{1,0:T(8,128)(2,1)S(1)}, u32[]{:S(2)}, u32[]{:S(2)}) collective-permute-start(bf16[2048,128]{1,0:T(8,128)(2,1)} %get-tuple-element.73.own), channel_id=1, source_target_pairs={{0,16},{16,0},{1,17},{17,1},{2,18},{18,2},{3,19},{19,3},{4,20},{20... | collective-permute-start | bytes 1572872 | tf_op jit(solution)/shard_map/ppermute | solution.py:414
  94.9 13.5 %collective-permute-start.19 = (f32[16,1,128]{2,1,0:T(1,128)}, f32[16,1,128]{2,1,0:T(1,128)S(1)}, u32[]{:S(2)}, u32[]{:S(2)}) collective-permute-start(f32[16,1,128]{2,1,0:T(1,128)} %get-tuple-element.74.own_lse), channel_id=1, source_target_pairs={{0,16},{16,0},{1,17},{17,1},{2,18},{18,2},{3,19},{19,3},{4,20},{20... | collective-permute-start | bytes 24584 | tf_op jit(solution)/shard_map/ppermute | solution.py:414
  96.3 17.1 %collective-permute-start.21 = (bf16[1024,256]{1,0:T(8,128)(2,1)}, bf16[1024,256]{1,0:T(8,128)(2,1)S(1)}, u32[]{:S(2)}, u32[]{:S(2)}) collective-permute-start(bf16[1024,256]{1,0:T(8,128)(2,1)} %collective-permute-done.16.refs_5_), channel_id=1, source_target_pairs={{0,32},{32,64},{64,96},{96,128},{128,160},{160,192},{192,224},{224... | collective-permute-start | bytes 1572872 | tf_op jit(solution)/shard_map/ppermute | solution.py:418
  108.3 0.6 copy-start.14
  108.3 14.7 %copy-start = (bf16[8,512,256]{2,1,0:T(8,128)(2,1)}, bf16[8,512,256]{2,1,0:T(8,128)(2,1)S(1)}, u32[]{:S(2)}) copy-start(bf16[8,512,256]{2,1,0:T(8,128)(2,1)S(1)} %all-to-all-done.near) | copy-start | bytes 6291460
  108.9 0.9 copy-start.9
  112.2 3.7 %collective-permute-start.20 = (bf16[2,128,1024]{2,1,0:T(8,128)(2,1)}, bf16[2,128,1024]{2,1,0:T(8,128)(2,1)S(1)}, u32[]{:S(2)}, u32[]{:S(2)}) collective-permute-start(bf16[2,128,1024]{2,1,0:T(8,128)(2,1)} %merge_last.1.near), channel_id=1, source_target_pairs={{0,8},{8,0},{1,9},{9,1},{2,10},{10,2},{3,11},{11,3},{4,12},{12,4},... | collective-permute-start | bytes 1572872 | tf_op jit(solution)/shard_map/ppermute | solution.py:414
  113.5 17.0 %collective-permute-start.22 = (bf16[8,512,256]{2,1,0:T(8,128)(2,1)S(1)}, bf16[8,512,256]{2,1,0:T(8,128)(2,1)}, u32[]{:S(2)}, u32[]{:S(2)}) collective-permute-start(bf16[8,512,256]{2,1,0:T(8,128)(2,1)S(1)} %all-to-all-done.near), channel_id=1, source_target_pairs={{0,8},{8,0},{1,9},{9,1},{2,10},{10,2},{3,11},{11,3},{4,12},{12,4},... | collective-permute-start | bytes 6291464 | tf_op jit(solution)/shard_map/ppermute | solution.py:414
  113.5 2.5 %copy-start.18 = (bf16[1024,256]{1,0:T(8,128)(2,1)}, bf16[1024,256]{1,0:T(8,128)(2,1)S(1)}, u32[]{:S(2)}) copy-start(bf16[1024,256]{1,0:T(8,128)(2,1)S(1)} %collective-permute-done.21.refs_7_) | copy-start | bytes 1572868
  115.9 0.8 copy-start.19
  123.0 37.3 %all-to-all-start.1 = ((bf16[32,128,256]{2,1,0:T(8,128)(2,1)}), bf16[32,128,256]{2,1,0:T(8,128)(2,1)}, u32[]{:S(2)}, u32[]{:S(2)}) async-start(bf16[32,128,256]{2,1,0:T(8,128)(2,1)} %bitcast.17), calls=%async_computation.1 | async-start | bytes 4194304 | tf_op jit(solution)/shard_map/all_to_all | solution.py:513
  165.2 14.5 %all-to-all-start.2 = ((bf16[8,144,256]{2,1,0:T(8,128)(2,1)}), bf16[8,144,256]{2,1,0:T(8,128)(2,1)S(1)}, u32[]{:S(2)}, u32[]{:S(2)}) async-start(bf16[8,144,256]{2,1,0:T(8,128)(2,1)} %get-tuple-element.79), calls=%async_computation.2 | async-start | bytes 1179648 | tf_op jit(solution)/shard_map/all_to_all | solution.py:519
  179.7 0.8 copy-start.1

commit v6 on v5

--- a/solution.py
+++ b/solution.py
@@ -19,7 +19,6 @@
 CTX_AXES = ("z", "yl", "c")
 HEAD_AXES = ("x", "yh")
 VMEM = 56 * 1024 * 1024
-CHUNK = 512
 DISTANCES = (0, -1, 1, -2, 2, -3, 3, 4)
 BLOCKS = 3
 
@@ -53,11 +52,7 @@
     return x * cosine + pltpu.roll(x, HEAD // 2, 1) * sine
 
 
-def prepare_kernel(
-    place, query, fresh, cached, cosine, sine, weight, query_out, kv_out, weight_out, sem
-):
-    copy = pltpu.make_async_copy(weight.at[:, place[2]], weight_out, sem)
-    copy.start()
+def prepare_kernel(query, fresh, cached, cosine, sine, query_out, kv_out):
     cos, sin = cosine[...], sine[...]
     for g in range(GROUP):
         piece = query[:, g * HEAD : (g + 1) * HEAD].astype(jnp.float32)
@@ -68,27 +63,40 @@
     new_key = rotated(fresh[0].astype(jnp.float32), cos, sin).astype(jnp.bfloat16)
     kv_out[BLOCKS - 1] = jnp.transpose(new_key)
     kv_out[2 * BLOCKS - 1] = fresh[1]
-    copy.wait()
-
-
-def prepare(place, query, fresh, cached, cosine, sine, weight):
-    vmem = pl.BlockSpec(memory_space=pltpu.VMEM)
+
+
+def prepare(query, fresh, cached, cosine, sine):
     return pl.pallas_call(
         prepare_kernel,
-        in_specs=[pl.BlockSpec(memory_space=pltpu.SMEM)]
-        + [vmem] * 5
-        + [pl.BlockSpec(memory_space=pl.ANY)],
-        out_specs=(vmem, vmem, vmem),
         out_shape=(
             jax.ShapeDtypeStruct((GROUP, ROWS, HEAD), jnp.bfloat16),
             jax.ShapeDtypeStruct((2 * BLOCKS, ROWS, HEAD), jnp.bfloat16),
-            jax.ShapeDtypeStruct((Z, *weight.shape[2:]), jnp.bfloat16),
-        ),
-        scratch_shapes=[pltpu.SemaphoreType.DMA],
+        ),
         compiler_params=params(),
         name="prepare",
-        cost_estimate=pl.CostEstimate(flops=2_000_000, bytes_accessed=5_500_000, transcendentals=0),
-    )(place, query, fresh, cached, cosine, sine, weight)
+        cost_estimate=pl.CostEstimate(flops=2_000_000, bytes_accessed=1_500_000, transcendentals=0),
+    )(query, fresh, cached, cosine, sine)
+
+
+def half_kernel(place, weight, out):
+    out[...] = weight[:, 0]
+
+
+def weight_half(place, weight):
+    rows, columns = weight.shape[2:]
+    return pl.pallas_call(
+        half_kernel,
+        grid_spec=pltpu.PrefetchScalarGridSpec(
+            num_scalar_prefetch=1,
+            grid=(Z // 2,),
+            in_specs=[pl.BlockSpec((2, 1, rows, columns), lambda i, s: (i, s[2], 0, 0))],
+            out_specs=pl.BlockSpec((2, rows, columns), lambda i, s: (i, 0, 0)),
+        ),
+        out_shape=jax.ShapeDtypeStruct((Z, rows, columns), jnp.bfloat16),
+        compiler_params=params(),
+        name="half",
+        cost_estimate=pl.CostEstimate(flops=0, bytes_accessed=8_000_000, transcendentals=0),
+    )(place, weight)
 
 
 def column_of(row):
@@ -99,7 +107,7 @@
     return jnp.transpose(column)[0:1, :]
 
 
-def attend_kernel(cached, fresh, n_queries, first, last, first_rc, place, *refs):
+def attend_kernel(chunk, cached, fresh, n_queries, first, last, first_rc, place, *refs):
     n_in = 1 + max([max(k, v) for k, v in cached] + [max(p[0], p[1]) for pair in fresh for p in pair])
     queries, refs = refs[:n_queries], refs[n_queries:]
     pieces, rest = refs[:n_in], list(refs[n_in:])
@@ -140,13 +148,13 @@
         values[:, HEAD:] = jnp.ones((steps * 2 * ROWS, HEAD), jnp.bfloat16)
 
     block = z * 4 + (yl ^ ryl) * 2 + (c ^ rc)
-    inside = lax.broadcasted_iota(jnp.int32, (CHUNK, 1), 0) & (ROWS - 1)
+    inside = lax.broadcasted_iota(jnp.int32, (chunk, 1), 0) & (ROWS - 1)
     query_token = block * ROWS + inside
     lane = lax.broadcasted_iota(jnp.int32, (1, 2 * ROWS), 1)
     q = query[...]
     if first:
-        m = jnp.full((CHUNK, 1), -1e30, jnp.float32)
-        acc = jnp.zeros((CHUNK, 2 * HEAD), jnp.float32)
+        m = jnp.full((chunk, 1), -1e30, jnp.float32)
+        acc = jnp.zeros((chunk, 2 * HEAD), jnp.float32)
     else:
         m = jnp.max(m_in[...], axis=1, keepdims=True)
         acc = acc_in[...]
@@ -166,34 +174,34 @@
         m = raised
     if not last:
         acc_out[...] = acc
-        m_out[...] = jnp.broadcast_to(m, (CHUNK, HEAD))
+        m_out[...] = jnp.broadcast_to(m, (chunk, HEAD))
         return
     totals = acc[:, HEAD:]
     out[...] = (acc[:, :HEAD] / totals).astype(jnp.bfloat16)
     lse = m * SCALE + jnp.log2(totals)
-    for k in range(CHUNK // ROWS):
-        lse_out[step * (CHUNK // ROWS) + k] = row_of(lse[k * ROWS : (k + 1) * ROWS, :])
-
-
-def attend(place, queries, first_rc, pieces, cached, fresh, state=None, offset=0, last=False):
-    each = queries[0].shape[0] // CHUNK
-    rows = each * len(queries) * CHUNK
+    for k in range(chunk // ROWS):
+        lse_out[step * (chunk // ROWS) + k] = row_of(lse[k * ROWS : (k + 1) * ROWS, :])
+
+
+def attend(chunk, place, queries, first_rc, pieces, cached, fresh, state=None, offset=0, last=False):
+    each = queries[0].shape[0] // chunk
+    rows = each * len(queries) * chunk
     total = 2 * ROWS * (len(cached) + len(fresh))
-    first_block = offset // CHUNK
+    first_block = offset // chunk
 
     def query_spec(k):
         return pl.BlockSpec(
-            (CHUNK, HEAD), lambda i, s: (jnp.clip(i - k * each, 0, each - 1), 0)
+            (chunk, HEAD), lambda i, s: (jnp.clip(i - k * each, 0, each - 1), 0)
         )
 
-    row_spec = pl.BlockSpec((CHUNK, HEAD), lambda i, s: (i, 0))
+    row_spec = pl.BlockSpec((chunk, HEAD), lambda i, s: (i, 0))
     in_specs = [query_spec(k) for k in range(len(queries))]
     in_specs += [pl.BlockSpec(p.shape, lambda i, s: (0, 0, 0)) for p in pieces]
     args = [*queries, *pieces]
     if state is not None:
         in_specs += [
-            pl.BlockSpec((CHUNK, 2 * HEAD), lambda i, s: (i + first_block, 0)),
-            pl.BlockSpec((CHUNK, HEAD), lambda i, s: (i + first_block, 0)),
+            pl.BlockSpec((chunk, 2 * HEAD), lambda i, s: (i + first_block, 0)),
+            pl.BlockSpec((chunk, HEAD), lambda i, s: (i + first_block, 0)),
         ]
         args += list(state)
     if last:
@@ -203,24 +211,24 @@
             jax.ShapeDtypeStruct((rows // ROWS, 1, ROWS), jnp.float32),
         )
     else:
-        out_specs = [pl.BlockSpec((CHUNK, 2 * HEAD), lambda i, s: (i, 0)), row_spec]
+        out_specs = [pl.BlockSpec((chunk, 2 * HEAD), lambda i, s: (i, 0)), row_spec]
         out_shape = (
             jax.ShapeDtypeStruct((rows, 2 * HEAD), jnp.float32),
             jax.ShapeDtypeStruct((rows, HEAD), jnp.float32),
         )
     return pl.pallas_call(
         functools.partial(
-            attend_kernel, cached, fresh, len(queries), state is None, last, first_rc
+            attend_kernel, chunk, cached, fresh, len(queries), state is None, last, first_rc
         ),
         grid_spec=pltpu.PrefetchScalarGridSpec(
             num_scalar_prefetch=1,
-            grid=(rows // CHUNK,),
+            grid=(rows // chunk,),
             in_specs=in_specs,
             out_specs=out_specs,
             scratch_shapes=[
                 pltpu.VMEM((HEAD, total), jnp.bfloat16),
                 pltpu.VMEM((total, 2 * HEAD), jnp.bfloat16),
-                pltpu.VMEM((CHUNK, HEAD), jnp.bfloat16),
+                pltpu.VMEM((chunk, HEAD), jnp.bfloat16),
             ],
         ),
         out_shape=out_shape,
@@ -291,36 +299,56 @@
 
 
 def project_kernel(place, near, far, *refs):
-    weights, out, rows = refs[:Z], refs[Z], refs[Z + 1]
+    weights, out, rows, held, products, in_sem, out_sem = refs[: Z + 1], *refs[Z + 1 :]
     z, yl, c = place[0], place[1], place[2]
+    half = held.shape[1] // 2
+    targets = [held.at[i] for i in range(Z - 1)]
+    targets += [held.at[Z - 1, pl.ds(0, half)], held.at[Z - 1, pl.ds(half, half)]]
+    copies = [
+        pltpu.make_async_copy(weights[i], targets[i], in_sem.at[i]) for i in range(Z + 1)
+    ]
+    for copy in copies:
+        copy.start()
     for ryl in range(2):
         rows[ryl * ROWS : (ryl + 1) * ROWS, :] = near[ryl]
         rows[(2 + ryl) * ROWS : (3 + ryl) * ROWS, :] = far[ryl]
-    lhs = rows[...]
-    for weight, distance in zip(weights, DISTANCES):
-        product = jnp.dot(lhs, weight[...], preferred_element_type=jnp.float32)
+    sent = []
+    for i, distance in enumerate(DISTANCES):
+        for copy in copies[i : i + 1 if i < Z - 1 else Z + 1]:
+            copy.wait()
+        product = jnp.dot(rows[...], held[i], preferred_element_type=jnp.float32)
         product = product.astype(jnp.bfloat16)
-        target = lax.rem(z + distance + Z, Z)
         for k in range(4):
             q = (yl ^ (k % 2)) * 2 + (c ^ (k // 2))
-            out[q, target] = product[k * ROWS : (k + 1) * ROWS, :]
+            products[i, q] = product[k * ROWS : (k + 1) * ROWS, :]
+        target = lax.rem(z + distance + Z, Z)
+        copy = pltpu.make_async_copy(products.at[i], out.at[:, target], out_sem.at[i])
+        copy.start()
+        sent.append(copy)
+    for copy in sent:
+        copy.wait()
 
 
 def project(place, near, far, weights):
     vmem = pl.BlockSpec(memory_space=pltpu.VMEM)
-    columns = weights[0].shape[1]
+    anywhere = pl.BlockSpec(memory_space=pl.ANY)
+    depth, columns = weights[0].shape
     return pl.pallas_call(
         project_kernel,
-        in_specs=[pl.BlockSpec(memory_space=pltpu.SMEM)] + [vmem] * (2 + Z),
-        out_specs=vmem,
+        in_specs=[pl.BlockSpec(memory_space=pltpu.SMEM), vmem, vmem] + [anywhere] * (Z + 1),
+        out_specs=anywhere,
         out_shape=jax.ShapeDtypeStruct((4, Z, ROWS, columns), jnp.bfloat16),
-        scratch_shapes=[pltpu.VMEM((4 * ROWS, GROUP * HEAD), jnp.bfloat16)],
+        scratch_shapes=[
+            pltpu.VMEM((4 * ROWS, depth), jnp.bfloat16),
+            pltpu.VMEM((Z, depth, columns), jnp.bfloat16),
+            pltpu.VMEM((Z, 4, ROWS, columns), jnp.bfloat16),
+            pltpu.SemaphoreType.DMA((Z + 1,)),
+            pltpu.SemaphoreType.DMA((Z,)),
+        ],
         compiler_params=params(),
         name="project",
         cost_estimate=pl.CostEstimate(
-            flops=2 * 4 * ROWS * GROUP * HEAD * Z * columns,
-            bytes_accessed=7_000_000,
-            transcendentals=0,
+            flops=2 * 4 * ROWS * depth * Z * columns, bytes_accessed=7_000_000, transcendentals=0
         ),
     )(place, near, far, *weights)
 
@@ -443,23 +471,19 @@
     place = jnp.stack([z, yl, c]).astype(jnp.int32)
 
     cosine, sine = tables(positions, HEAD)
-    rotated_query, kv, third_rows = prepare(
-        place,
-        query,
-        fresh_key_value,
-        cached_key_value,
-        cosine,
-        sine,
-        layer3_key_value_weight.reshape(Z, 2, MODEL_WIDTH // Z // 2, 2 * HEAD),
+    rotated_query, kv = prepare(query, fresh_key_value, cached_key_value, cosine, sine)
+    third_rows = weight_half(
+        place, layer3_key_value_weight.reshape(Z, 2, MODEL_WIDTH // Z // 2, 2 * HEAD)
     )
     rotated_query = rotated_query.reshape(GROUP * ROWS, HEAD)
     across = swap(rotated_query, "yl")
     other_core = swap(rotated_query, "c")
-    kv_1, across = lax.optimization_barrier((step([kv, kv]), across))
+    kv_1, across, third_rows = lax.optimization_barrier((step([kv, kv]), across, third_rows))
     near_query, far_query = [rotated_query, across], [other_core, swap(across, "c")]
     own_weight = after(out_weight, *kv_1)
     weights_1 = step([own_weight, own_weight])
     state = attend(
+        1024,
         place,
         near_query + far_query,
         0,
@@ -468,45 +492,33 @@
         [[(0, 0, 0), (1, 1, -1)]],
     )
     kv_2 = list(after(step(kv_1), state))
-    kv_3 = step(kv_2)
-    near_query, far_query, kv_3, state, weights_1 = lax.optimization_barrier(
-        (near_query, far_query, kv_3, state, weights_1)
-    )
-    weights_2 = step(weights_1)
-    third_rows = after(third_rows, *kv_2)
+    kv_3, weights_1, state = lax.optimization_barrier((step(kv_2), weights_1, state))
     third_near = lax.all_to_all(third_rows, HEAD_AXES, 0, 0, tiled=True)
     third_far = swap(third_near, "c")
+    weights_2 = step(weights_1)
     kv_4 = along_z(kv_3[0], 1)
-    state = attend(
-        place,
-        near_query + far_query,
-        0,
-        [kv_1[1], *kv_2],
-        [(1, 1), (2, 2)],
-        [[(0, 0, 1), (1, 1, -2)]],
-        state,
-    )
     kv_4, state = lax.optimization_barrier((kv_4, state))
-    late = [kv_2[1], *kv_3, kv_4]
-    late_cached = [(1, 1), (2, 2), (3, 3)]
-    late_fresh = [[(0, 0, 2), (1, 1, -3)], [(2, 2, 3), (3, 3, 4)]]
-    state = after(state, *weights_2)
+    late = [kv_1[1], *kv_2, *kv_3, kv_4]
+    late_cached = [(i, i) for i in range(1, 6)]
+    late_fresh = [[(0, 0, 1), (1, 1, -2)], [(2, 2, 2), (3, 3, -3)], [(4, 4, 3), (5, 5, 4)]]
+    offset = 2 * GROUP * ROWS
+    send, send_lse = attend(
+        512, place, far_query, 1, late, late_cached, late_fresh, state, offset, True
+    )
+    got, got_lse = swap(send, "c"), swap(send_lse, "c")
+    near_query, _, weights_2 = lax.optimization_barrier((near_query, send_lse, weights_2))
     weights_3 = step(weights_2)
-    send, send_lse = attend(
-        place, far_query, 1, late, late_cached, late_fresh, state, 2 * GROUP * ROWS, True
-    )
-    got, got_lse = swap(send, "c"), swap(send_lse, "c")
     own, own_lse = attend(
-        place, near_query, 0, late, late_cached, late_fresh, state, 0, True
-    )
-    got_lse = after(got_lse, *weights_3)
+        512, place, near_query, 0, late, late_cached, late_fresh, state, 0, True
+    )
     own, own_lse = merge(own, own_lse, got, got_lse)
     got, got_lse = swap(own, "yl"), swap(own_lse, "yl")
-    weights_4 = along_z(weights_3[0], 1)
-    got_lse = after(got_lse, third_near)
+    depth = out_weight.shape[0] // 2
+    weights_4 = [along_z(weights_3[0][:depth], 1), along_z(weights_3[1][depth:], -1)]
+    got_lse = after(got_lse, third_near, *weights_4)
     near = merge_last(own, own_lse, got, got_lse)
     far = swap(near, "c")
-    weights = [out_weight, *weights_1, *weights_2, *weights_3, weights_4]
+    weights = [out_weight, *weights_1, *weights_2, *weights_3, *weights_4]
 
     products = project(place, near, far, weights)
     products = products.reshape(4 * Z, *products.shape[2:])

time: 183 us -> 178 us (0.973)
  waiting for transfers between devices: 63.9 us -> 58.2 us
  Pallas kernels: 61.8 us -> 58.1 us
  starting transfers between devices: 48.1 us -> 51.8 us
    pallas_call x5, Pallas kernels: 43.8 us -> 37.5 us  [the longest x3 31 us: attend(): pl.pallas_call(functools.partial(attend_kernel, chunk, cached, fresh, len...]
    ppermute x14 -> x15, starting transfers between devices: 19.2 us -> 22.9 us  [along_z(): return lax.ppermute(x, 'z', [(i, (i + distance) % Z) for i in range(Z)])]
    ppermute x14 -> x15, waiting for transfers between devices: 9.36 us -> 6.01 us  [along_z(): return lax.ppermute(x, 'z', [(i, (i + distance) % Z) for i in range(Z)])]
    ppermute x9, waiting for transfers between devices: 14.5 us -> 12.1 us  [swap(): return lax.ppermute(x, axis, [(0, 1), (1, 0)])]
    pallas_call x1, Pallas kernels: 6.27 us -> 8.67 us  [project(): pl.pallas_call(project_kernel, in_specs=[pl.BlockSpec(memory_space=pltpu....]
    unnamed x42 -> x44, local copies, waits for them, and re-layouts: 4.7 us -> 5.46 us
  transfers between devices with their start and end apart: 26 -> 27, of which waited for: 7 -> 7; matrix products, arithmetic and copies ran while one was open for 0% -> 0% of each run, Pallas kernels for 28% -> 26%
where the time goes in v6:
time: 178 us
  waiting for transfers between devices  58.2 us (33%)
  Pallas kernels  58.1 us (33%)
  starting transfers between devices  51.8 us (29%)
  local copies, waits for them, and re-layouts  5.5 us (3%)
  other arithmetic  2.47 us (1%)
    pallas_call x3, Pallas kernels, attend(): pl.pallas_call(functools.partial(attend_kernel, chunk, cached, fresh, len...  31 us
    all_to_all x1, waiting for transfers between devices, local(): lax.all_to_all(products, ('yl', 'c', 'x', 'yh'), 0, 0, tiled=True)  29.8 us
    ppermute x15, starting transfers between devices, along_z(): return lax.ppermute(x, 'z', [(i, (i + distance) % Z) for i in range(Z)])  22.9 us
    ppermute x9, waiting for transfers between devices, swap(): return lax.ppermute(x, axis, [(0, 1), (1, 0)])  12.1 us
    ppermute x9, starting transfers between devices, swap(): return lax.ppermute(x, axis, [(0, 1), (1, 0)])  11.5 us
    all_to_all x1, waiting for transfers between devices, local(): partial = lax.all_to_all(partial, HEAD_AXES, 0, 0, tiled=True)  10.3 us
    pallas_call x1, Pallas kernels, project(): pl.pallas_call(project_kernel, in_specs=[pl.BlockSpec(memory_space=pltpu....  8.67 us
    all_to_all x1, starting transfers between devices, local(): lax.all_to_all(products, ('yl', 'c', 'x', 'yh'), 0, 0, tiled=True)  7.51 us
  transfers between devices with their start and end apart: 27, of which 7 were waited for; matrix products, arithmetic and copies ran while one was open for 0% of the time, Pallas kernels for 26%

profile of v6, /device:TPU:1, one launch (start us, length us, event | category | flops | bytes accessed | tf_op | source)
XLA Modules:
  0.0 177.7 jit_solution(12784734508458859088)
XLA Ops:
  0.7 0.7 convert_element_type.36
  1.4 0.3 fusion.2
  1.7 0.8 pad_maximum_fusion
  2.5 2.0 %prepare.1 = (bf16[8,128,128]{2,1,0:T(8,128)(2,1)}, bf16[6,128,128]{2,1,0:T(8,128)(2,1)}) custom-call(bf16[128,1024]{1,0:T(8,128)(2,1)} %query.1, bf16[2,128,128]{2,1,0:T(8,128)(2,1)} %fresh.1, bf16[2,256,128]{2,1,0:T(8,128)(2,1)} %cached.1, f32[128,128]{1,0:T(8,128)} %get-tuple-element.74.cosine, f32[128,128]{1,0:T(8,128)} %get-tuple-element.75.sine), custom_call_target="tpu_custom_call" | custom-call | flops 2000000 | bytes 1500000 | tf_op jit(solution)/shard_map/prepare/pallas_call | solution.py:69
  4.5 2.1 %collective-permute-start.2 = (bf16[1024,128]{1,0:T(8,128)(2,1)}, bf16[1024,128]{1,0:T(8,128)(2,1)S(1)}, u32[]{:S(2)}, u32[]{:S(2)}) collective-permute-start(bf16[1024,128]{1,0:T(8,128)(2,1)} %bitcast.18), channel_id=1, source_target_pairs={{0,16},{16,0},{1,17},{17,1},{2,18},{18,2},{3,19},{19,3},{4,20},{20... | collective-permute-start | bytes 786440 | tf_op jit(solution)/shard_map/ppermute | solution.py:442
  6.6 1.6 collective-permute-start
  8.2 3.9 %collective-permute-start.1 = (bf16[6,128,128]{2,1,0:T(8,128)(2,1)}, bf16[6,128,128]{2,1,0:T(8,128)(2,1)S(1)}, u32[]{:S(2)}, u32[]{:S(2)}) collective-permute-start(bf16[6,128,128]{2,1,0:T(8,128)(2,1)} %get-tuple-element.36.refs_4_), channel_id=1, source_target_pairs={{0,224},{32,0},{64,32},{96,64},{128,96},{160,128},{192,160},{224,1... | collective-permute-start | bytes 589832 | tf_op jit(solution)/shard_map/ppermute | solution.py:446
  12.2 1.2 collective-permute-start.3
  13.4 0.7 pad_add_fusion.place
  14.1 4.5 %half.1 = bf16[8,512,256]{2,1,0:T(8,128)(2,1)} custom-call(s32[3]{0:T(128)} %pad_add_fusion.place, bf16[8,2,512,256]{3,2,1,0:T(8,128)(2,1)} %bitcast.16), custom_call_target="tpu_custom_call" | custom-call | bytes 8000000 | tf_op jit(solution)/shard_map/half/pallas_call | solution.py:87
  18.7 2.3 %collective-permute-start.10 = (bf16[1024,256]{1,0:T(8,128)(2,1)}, bf16[1024,256]{1,0:T(8,128)(2,1)}, u32[]{:S(2)}, u32[]{:S(2)}) collective-permute-start(bf16[1024,256]{1,0:T(8,128)(2,1)} %refs_0_.1), channel_id=1, source_target_pairs={{0,224},{32,0},{64,32},{96,64},{128,96},{160,128},{192,160},{224,1... | collective-permute-start | bytes 1572872 | tf_op jit(solution)/shard_map/ppermute | solution.py:446
  21.0 6.4 %all-to-all-start = ((bf16[8,512,256]{2,1,0:T(8,128)(2,1)}), bf16[8,512,256]{2,1,0:T(8,128)(2,1)S(1)}, u32[]{:S(2)}, u32[]{:S(2)}) async-start(bf16[8,512,256]{2,1,0:T(8,128)(2,1)} %half.1), calls=%async_computation | async-start | bytes 4194304 | tf_op jit(solution)/shard_map/all_to_all | solution.py:496
  27.4 2.8 %collective-permute-start.6 = (bf16[6,128,128]{2,1,0:T(8,128)(2,1)S(1)}, bf16[6,128,128]{2,1,0:T(8,128)(2,1)S(1)}, u32[]{:S(2)}, u32[]{:S(2)}) collective-permute-start(bf16[6,128,128]{2,1,0:T(8,128)(2,1)S(1)} %collective-permute-done.1.refs_6_.refs_2_), channel_id=1, source_target_pairs={{0,224},{32,0},{64,32},{96,64},{128,96},{160,128},{192,160},{224,1... | collective-permute-start | bytes 589832 | tf_op jit(solution)/shard_map/ppermute | solution.py:446
  30.2 0.7 copy-done.12
  30.9 10.3 %attend.3 = (f32[4096,256]{1,0:T(8,128)}, f32[4096,128]{1,0:T(8,128)}) custom-call(s32[3]{0:T(128)} %pad_add_fusion.place, bf16[1024,128]{1,0:T(8,128)(2,1)} %bitcast.20, bf16[1024,128]{1,0:T(8,128)(2,1)} %copy-done.10, bf16[1024,128]{1,0:T(8,128)(2,1)} %copy-done.11, bf16[1024,128]{1,0:T(8,128)(2,1)} %copy-done.12, ...), custom_call_target="tpu_custom_call" | custom-call | flops 2147483648 | bytes 4718592 | tf_op jit(solution)/shard_map/attend/pallas_call | solution.py:219
  41.4 2.6 %collective-permute-start.8 = (bf16[6,128,128]{2,1,0:T(8,128)(2,1)S(1)}, bf16[6,128,128]{2,1,0:T(8,128)(2,1)S(1)}, u32[]{:S(2)}, u32[]{:S(2)}) collective-permute-start(bf16[6,128,128]{2,1,0:T(8,128)(2,1)S(1)} %collective-permute-done.6.refs_4_), channel_id=1, source_target_pairs={{0,224},{32,0},{64,32},{96,64},{128,96},{160,128},{192,160},{224,1... | collective-permute-start | bytes 589832 | tf_op jit(solution)/shard_map/ppermute | solution.py:446
  44.0 3.7 %collective-permute-done.7.refs_5_ = bf16[6,128,128]{2,1,0:T(8,128)(2,1)S(1)} collective-permute-done((bf16[6,128,128]{2,1,0:T(8,128)(2,1)S(1)}, bf16[6,128,128]{2,1,0:T(8,128)(2,1)S(1)}, u32[]{:S(2)}, u32[]{:S(2)}) %collective-permute-start.7) | collective-permute-done | bytes 196640 | tf_op jit(solution)/shard_map/ppermute | solution.py:446
  47.9 1.3 collective-permute-start.11
  49.1 0.8 collective-permute-start.12
  49.9 1.9 %collective-permute-start.13 = (bf16[1024,256]{1,0:T(8,128)(2,1)}, bf16[1024,256]{1,0:T(8,128)(2,1)S(1)}, u32[]{:S(2)}, u32[]{:S(2)}) collective-permute-start(bf16[1024,256]{1,0:T(8,128)(2,1)} %collective-permute-done.10.refs_2_), channel_id=1, source_target_pairs={{0,224},{32,0},{64,32},{96,64},{128,96},{160,128},{192,160},{224,1... | collective-permute-start | bytes 1572872 | tf_op jit(solution)/shard_map/ppermute | solution.py:446
  51.8 2.2 %collective-permute-done.11.refs_7_ = bf16[6,128,128]{2,1,0:T(8,128)(2,1)S(1)} collective-permute-done((bf16[6,128,128]{2,1,0:T(8,128)(2,1)S(1)}, bf16[6,128,128]{2,1,0:T(8,128)(2,1)S(1)}, u32[]{:S(2)}, u32[]{:S(2)}) %collective-permute-start.11) | collective-permute-done | bytes 196640 | tf_op jit(solution)/shard_map/ppermute | solution.py:446
  54.0 0.7 copy-done.7
  54.7 10.4 %attend.4 = (bf16[2048,128]{1,0:T(8,128)(2,1)}, f32[16,1,128]{2,1,0:T(1,128)}) custom-call(s32[3]{0:T(128)} %pad_add_fusion.place, bf16[1024,128]{1,0:T(8,128)(2,1)} %copy-done.11, bf16[1024,128]{1,0:T(8,128)(2,1)} %copy-done.12, bf16[6,128,128]{2,1,0:T(8,128)(2,1)} %copy-done.2, bf16[6,128,128]{2,1,0:T(8,128)(2,1)} %copy-done.3, ...), custom_call_target="tpu_custom_call" | custom-call | flops 2147483648 | bytes 3145728 | tf_op jit(solution)/shard_map/attend/pallas_call | solution.py:219
  65.0 5.2 %collective-permute-start.14 = (bf16[2048,128]{1,0:T(8,128)(2,1)}, bf16[2048,128]{1,0:T(8,128)(2,1)S(1)}, u32[]{:S(2)}, u32[]{:S(2)}) collective-permute-start(bf16[2048,128]{1,0:T(8,128)(2,1)} %get-tuple-element.59), channel_id=1, source_target_pairs={{0,8},{8,0},{1,9},{9,1},{2,10},{10,2},{3,11},{11,3},{4,12},{12,4},... | collective-permute-start | bytes 1572872 | tf_op jit(solution)/shard_map/ppermute | solution.py:442
  70.3 0.3 collective-permute-start.18
  70.6 2.4 %collective-permute-start.20 = (bf16[1024,256]{1,0:T(8,128)(2,1)S(1)}, bf16[1024,256]{1,0:T(8,128)(2,1)S(1)}, u32[]{:S(2)}, u32[]{:S(2)}) collective-permute-start(bf16[1024,256]{1,0:T(8,128)(2,1)S(1)} %collective-permute-done.13.refs_4_), channel_id=1, source_target_pairs={{0,224},{32,0},{64,32},{96,64},{128,96},{160,128},{192,160},{224,1... | collective-permute-start | bytes 1572872 | tf_op jit(solution)/shard_map/ppermute | solution.py:446
  73.0 0.6 collective-permute-start.15
  73.6 10.3 %attend.5 = (bf16[2048,128]{1,0:T(8,128)(2,1)}, f32[16,1,128]{2,1,0:T(1,128)}) custom-call(s32[3]{0:T(128)} %pad_add_fusion.place, bf16[1024,128]{1,0:T(8,128)(2,1)} %bitcast.21, bf16[1024,128]{1,0:T(8,128)(2,1)} %copy-done.10, bf16[6,128,128]{2,1,0:T(8,128)(2,1)} %copy-done.2, bf16[6,128,128]{2,1,0:T(8,128)(2,1)} %copy-done.3, ...), custom_call_target="tpu_custom_call" | custom-call | flops 2147483648 | bytes 3145728 | tf_op jit(solution)/shard_map/attend/pallas_call | solution.py:219
  84.0 0.6 copy-done.15
  84.6 0.2 copy-done.9
  84.8 2.4 %merge.1 = (bf16[2048,128]{1,0:T(8,128)(2,1)}, f32[16,1,128]{2,1,0:T(1,128)}) custom-call(bf16[2048,128]{1,0:T(8,128)(2,1)} %get-tuple-element.57.own, f32[16,1,128]{2,1,0:T(1,128)} %get-tuple-element.58.own_lse, bf16[2048,128]{1,0:T(8,128)(2,1)} %copy-done.9, f32[16,1,128]{2,1,0:T(1,128)} %copy-done.15), custom_call_target="tpu_custom_call" | custom-call | flops 2000000 | bytes 1600000 | tf_op jit(solution)/shard_map/merge/pallas_call | solution.py:279
  87.4 2.7 %collective-permute-start.21 = (bf16[512,256]{1,0:T(8,128)(2,1)S(1)}, bf16[512,256]{1,0:T(8,128)(2,1)}, u32[]{:S(2)}, u32[]{:S(2)}) collective-permute-start(bf16[512,256]{1,0:T(8,128)(2,1)S(1)} %slice.21), channel_id=1, source_target_pairs={{0,224},{32,0},{64,32},{96,64},{128,96},{160,128},{192,160},{224,1... | collective-permute-start | bytes 786440 | tf_op jit(solution)/shard_map/ppermute | solution.py:446
  90.1 1.4 collective-permute-start.17
  91.6 9.6 %collective-permute-done.17.other_lse = f32[16,1,128]{2,1,0:T(1,128)S(1)} collective-permute-done((f32[16,1,128]{2,1,0:T(1,128)}, f32[16,1,128]{2,1,0:T(1,128)S(1)}, u32[]{:S(2)}, u32[]{:S(2)}) %collective-permute-start.17) | collective-permute-done | bytes 8224 | tf_op jit(solution)/shard_map/ppermute | solution.py:442
  101.2 0.5 copy-done.16
  101.8 1.0 copy-done.8
  102.8 2.4 %merge_last.1.near = bf16[2,128,1024]{2,1,0:T(8,128)(2,1)} custom-call(bf16[2048,128]{1,0:T(8,128)(2,1)} %get-tuple-element.60.own, f32[16,1,128]{2,1,0:T(1,128)} %get-tuple-element.61.own_lse, bf16[2048,128]{1,0:T(8,128)(2,1)} %copy-done.8, f32[16,1,128]{2,1,0:T(1,128)} %copy-done.16), custom_call_target="tpu_custom_call" | custom-call | flops 2000000 | bytes 1600000 | tf_op jit(solution)/shard_map/merge_last/pallas_call | solution.py:292
  105.2 0.8 collective-permute-start.22
  106.0 2.5 %collective-permute-done.22.far = bf16[2,128,1024]{2,1,0:T(8,128)(2,1)S(1)} collective-permute-done((bf16[2,128,1024]{2,1,0:T(8,128)(2,1)}, bf16[2,128,1024]{2,1,0:T(8,128)(2,1)S(1)}, u32[]{:S(2)}, u32[]{:S(2)}) %collective-permute-start.22) | collective-permute-done | bytes 524320 | tf_op jit(solution)/shard_map/ppermute | solution.py:442
  108.5 0.9 copy-done.19
  109.3 8.7 %project.1 = bf16[4,8,128,256]{3,2,1,0:T(8,128)(2,1)} custom-call(s32[3]{0:T(128)} %pad_add_fusion.place, bf16[2,128,1024]{2,1,0:T(8,128)(2,1)} %merge_last.1.near, bf16[2,128,1024]{2,1,0:T(8,128)(2,1)} %copy-done.19, bf16[1024,256]{1,0:T(8,128)(2,1)} %refs_0_.1, bf16[1024,256]{1,0:T(8,128)(2,1)} %collective-permute-done.9.refs_1_, ...), custom_call_target="tpu_custom_call" | custom-call | flops 2147483648 | bytes 7000000 | tf_op jit(solution)/shard_map/project/pallas_call | solution.py:336
  118.0 7.5 %all-to-all-start.1 = ((bf16[32,128,256]{2,1,0:T(8,128)(2,1)}), bf16[32,128,256]{2,1,0:T(8,128)(2,1)}, u32[]{:S(2)}, u32[]{:S(2)}) async-start(bf16[32,128,256]{2,1,0:T(8,128)(2,1)} %bitcast.17), calls=%async_computation.1 | async-start | bytes 4194304 | tf_op jit(solution)/shard_map/all_to_all | solution.py:525
  125.5 29.8 %all-to-all-done.1 = bf16[32,128,256]{2,1,0:T(8,128)(2,1)} async-done(((bf16[32,128,256]{2,1,0:T(8,128)(2,1)}), bf16[32,128,256]{2,1,0:T(8,128)(2,1)}, u32[]{:S(2)}, u32[]{:S(2)}) %all-to-all-start.1) | async-done | bytes 2097184 | tf_op jit(solution)/shard_map/all_to_all | solution.py:525
  155.3 4.9 %third.1 = (bf16[128,1024]{1,0:T(8,128)(2,1)}, bf16[8,144,256]{2,1,0:T(8,128)(2,1)}) custom-call(s32[3]{0:T(128)} %pad_add_fusion.place, bf16[4,8,128,256]{3,2,1,0:T(8,128)(2,1)} %bitcast.9.received, bf16[128,1024]{1,0:T(8,128)(2,1)} %hidden.1, f32[1,1024]{1,0:T(1,128)} %bitcast.22, bf16[8,512,256]{2,1,0:T(8,128)(2,1)} %copy-done, ...), custom_call_target="tpu_custom_call" | custom-call | tf_op jit(solution)/shard_map/third/pallas_call | solution.py:394
  160.3 3.5 %all-to-all-start.2 = ((bf16[8,144,256]{2,1,0:T(8,128)(2,1)}), bf16[8,144,256]{2,1,0:T(8,128)(2,1)S(1)}, u32[]{:S(2)}, u32[]{:S(2)}) async-start(bf16[8,144,256]{2,1,0:T(8,128)(2,1)} %get-tuple-element.67), calls=%async_computation.2 | async-start | bytes 1179648 | tf_op jit(solution)/shard_map/all_to_all | solution.py:531
  164.5 10.3 %all-to-all-done.2.partial = bf16[8,144,256]{2,1,0:T(8,128)(2,1)S(1)} async-done(((bf16[8,144,256]{2,1,0:T(8,128)(2,1)}), bf16[8,144,256]{2,1,0:T(8,128)(2,1)S(1)}, u32[]{:S(2)}, u32[]{:S(2)}) %all-to-all-start.2) | async-done | bytes 589856 | tf_op jit(solution)/shard_map/all_to_all | solution.py:531
  174.8 0.8 copy-done.1
  175.6 2.1 %final.1 = bf16[128,256]{1,0:T(8,128)(2,1)} custom-call(s32[1]{0:T(128)S(6)} %copy.13.count, bf16[8,144,256]{2,1,0:T(8,128)(2,1)} %copy-done.1, f32[1,256]{1,0:T(1,128)} %bitcast.23, f32[128,128]{1,0:T(8,128)} %get-tuple-element.74.cosine, f32[128,128]{1,0:T(8,128)} %get-tuple-element.75.sine, s32[1,128]{1,0:T(1,128)} %bitcast.24), custom_call_target="tpu_custom_call" | custom-call | tf_op jit(solution)/shard_map/final/pallas_call | solution.py:431
  (70 shorter events, 0.6 us)
Async XLA Ops:
  4.5 14.1 %collective-permute-start.2 = (bf16[1024,128]{1,0:T(8,128)(2,1)}, bf16[1024,128]{1,0:T(8,128)(2,1)S(1)}, u32[]{:S(2)}, u32[]{:S(2)}) collective-permute-start(bf16[1024,128]{1,0:T(8,128)(2,1)} %bitcast.18), channel_id=1, source_target_pairs={{0,16},{16,0},{1,17},{17,1},{2,18},{18,2},{3,19},{19,3},{4,20},{20... | collective-permute-start | bytes 786440 | tf_op jit(solution)/shard_map/ppermute | solution.py:442
  6.6 12.0 %collective-permute-start = (bf16[6,128,128]{2,1,0:T(8,128)(2,1)}, bf16[6,128,128]{2,1,0:T(8,128)(2,1)S(1)}, u32[]{:S(2)}, u32[]{:S(2)}) collective-permute-start(bf16[6,128,128]{2,1,0:T(8,128)(2,1)} %get-tuple-element.36.refs_4_), channel_id=1, source_target_pairs={{0,32},{32,64},{64,96},{96,128},{128,160},{160,192},{192,224},{224... | collective-permute-start | bytes 589832 | tf_op jit(solution)/shard_map/ppermute | solution.py:446
  8.2 10.3 %collective-permute-start.1 = (bf16[6,128,128]{2,1,0:T(8,128)(2,1)}, bf16[6,128,128]{2,1,0:T(8,128)(2,1)S(1)}, u32[]{:S(2)}, u32[]{:S(2)}) collective-permute-start(bf16[6,128,128]{2,1,0:T(8,128)(2,1)} %get-tuple-element.36.refs_4_), channel_id=1, source_target_pairs={{0,224},{32,0},{64,32},{96,64},{128,96},{160,128},{192,160},{224,1... | collective-permute-start | bytes 589832 | tf_op jit(solution)/shard_map/ppermute | solution.py:446
  12.2 15.2 %collective-permute-start.3 = (bf16[1024,128]{1,0:T(8,128)(2,1)}, bf16[1024,128]{1,0:T(8,128)(2,1)S(1)}, u32[]{:S(2)}, u32[]{:S(2)}) collective-permute-start(bf16[1024,128]{1,0:T(8,128)(2,1)} %bitcast.19), channel_id=1, source_target_pairs={{0,8},{8,0},{1,9},{9,1},{2,10},{10,2},{3,11},{11,3},{4,12},{12,4},... | collective-permute-start | bytes 786440 | tf_op jit(solution)/shard_map/ppermute | solution.py:442
  18.6 2.5 %copy-start.21 = (bf16[6,128,128]{2,1,0:T(8,128)(2,1)}, bf16[6,128,128]{2,1,0:T(8,128)(2,1)S(1)}, u32[]{:S(2)}) copy-start(bf16[6,128,128]{2,1,0:T(8,128)(2,1)S(1)} %collective-permute-done.refs_5_) | copy-start | bytes 589828
  18.6 8.9 %copy-start.2 = (bf16[6,128,128]{2,1,0:T(8,128)(2,1)}, bf16[6,128,128]{2,1,0:T(8,128)(2,1)S(1)}, u32[]{:S(2)}) copy-start(bf16[6,128,128]{2,1,0:T(8,128)(2,1)S(1)} %collective-permute-done.1.refs_6_.refs_2_) | copy-start | bytes 589828
  18.6 2.5 %copy-start.10 = (bf16[1024,128]{1,0:T(8,128)(2,1)}, bf16[1024,128]{1,0:T(8,128)(2,1)S(1)}, u32[]{:S(2)}) copy-start(bf16[1024,128]{1,0:T(8,128)(2,1)S(1)} %collective-permute-done.2.refs_1_) | copy-start | bytes 786436
  18.6 11.6 %collective-permute-start.4 = (bf16[1024,128]{1,0:T(8,128)(2,1)S(1)}, bf16[1024,128]{1,0:T(8,128)(2,1)S(1)}, u32[]{:S(2)}, u32[]{:S(2)}) collective-permute-start(bf16[1024,128]{1,0:T(8,128)(2,1)S(1)} %collective-permute-done.2.refs_1_), channel_id=1, source_target_pairs={{0,8},{8,0},{1,9},{9,1},{2,10},{10,2},{3,11},{11,3},{4,12},{12,4},... | collective-permute-start | bytes 786440 | tf_op jit(solution)/shard_map/ppermute | solution.py:442
  18.7 29.2 %collective-permute-start.10 = (bf16[1024,256]{1,0:T(8,128)(2,1)}, bf16[1024,256]{1,0:T(8,128)(2,1)}, u32[]{:S(2)}, u32[]{:S(2)}) collective-permute-start(bf16[1024,256]{1,0:T(8,128)(2,1)} %refs_0_.1), channel_id=1, source_target_pairs={{0,224},{32,0},{64,32},{96,64},{128,96},{160,128},{192,160},{224,1... | collective-permute-start | bytes 1572872 | tf_op jit(solution)/shard_map/ppermute | solution.py:446
  21.0 26.8 %collective-permute-start.9 = (bf16[1024,256]{1,0:T(8,128)(2,1)}, bf16[1024,256]{1,0:T(8,128)(2,1)}, u32[]{:S(2)}, u32[]{:S(2)}) collective-permute-start(bf16[1024,256]{1,0:T(8,128)(2,1)} %refs_0_.1), channel_id=1, source_target_pairs={{0,32},{32,64},{64,96},{96,128},{128,160},{160,192},{192,224},{224... | collective-permute-start | bytes 1572872 | tf_op jit(solution)/shard_map/ppermute | solution.py:446
  21.0 20.2 %collective-permute-start.5 = (bf16[6,128,128]{2,1,0:T(8,128)(2,1)S(1)}, bf16[6,128,128]{2,1,0:T(8,128)(2,1)S(1)}, u32[]{:S(2)}, u32[]{:S(2)}) collective-permute-start(bf16[6,128,128]{2,1,0:T(8,128)(2,1)S(1)} %collective-permute-done.refs_5_), channel_id=1, source_target_pairs={{0,32},{32,64},{64,96},{96,128},{128,160},{160,192},{192,224},{224... | collective-permute-start | bytes 589832 | tf_op jit(solution)/shard_map/ppermute | solution.py:446
  21.0 80.2 %all-to-all-start = ((bf16[8,512,256]{2,1,0:T(8,128)(2,1)}), bf16[8,512,256]{2,1,0:T(8,128)(2,1)S(1)}, u32[]{:S(2)}, u32[]{:S(2)}) async-start(bf16[8,512,256]{2,1,0:T(8,128)(2,1)} %half.1), calls=%async_computation | async-start | bytes 4194304 | tf_op jit(solution)/shard_map/all_to_all | solution.py:496
  27.4 2.8 %copy-start.11 = (bf16[1024,128]{1,0:T(8,128)(2,1)}, bf16[1024,128]{1,0:T(8,128)(2,1)S(1)}, u32[]{:S(2)}) copy-start(bf16[1024,128]{1,0:T(8,128)(2,1)S(1)} %collective-permute-done.3.refs_2_.refs_0_) | copy-start | bytes 786436
  27.4 13.8 %collective-permute-start.6 = (bf16[6,128,128]{2,1,0:T(8,128)(2,1)S(1)}, bf16[6,128,128]{2,1,0:T(8,128)(2,1)S(1)}, u32[]{:S(2)}, u32[]{:S(2)}) collective-permute-start(bf16[6,128,128]{2,1,0:T(8,128)(2,1)S(1)} %collective-permute-done.1.refs_6_.refs_2_), channel_id=1, source_target_pairs={{0,224},{32,0},{64,32},{96,64},{128,96},{160,128},{192,160},{224,1... | collective-permute-start | bytes 589832 | tf_op jit(solution)/shard_map/ppermute | solution.py:446
  30.2 0.7 copy-start.12
  41.2 12.7 %copy-start.3 = (bf16[6,128,128]{2,1,0:T(8,128)(2,1)}, bf16[6,128,128]{2,1,0:T(8,128)(2,1)S(1)}, u32[]{:S(2)}) copy-start(bf16[6,128,128]{2,1,0:T(8,128)(2,1)S(1)} %collective-permute-done.5.refs_3_) | copy-start | bytes 589828
  41.3 12.7 %copy-start.4 = (bf16[6,128,128]{2,1,0:T(8,128)(2,1)}, bf16[6,128,128]{2,1,0:T(8,128)(2,1)S(1)}, u32[]{:S(2)}) copy-start(bf16[6,128,128]{2,1,0:T(8,128)(2,1)S(1)} %collective-permute-done.6.refs_4_) | copy-start | bytes 589828
  41.3 6.5 %collective-permute-start.7 = (bf16[6,128,128]{2,1,0:T(8,128)(2,1)S(1)}, bf16[6,128,128]{2,1,0:T(8,128)(2,1)S(1)}, u32[]{:S(2)}, u32[]{:S(2)}) collective-permute-start(bf16[6,128,128]{2,1,0:T(8,128)(2,1)S(1)} %collective-permute-done.5.refs_3_), channel_id=1, source_target_pairs={{0,32},{32,64},{64,96},{96,128},{128,160},{160,192},{192,224},{224... | collective-permute-start | bytes 589832 | tf_op jit(solution)/shard_map/ppermute | solution.py:446
  41.4 6.4 %collective-permute-start.8 = (bf16[6,128,128]{2,1,0:T(8,128)(2,1)S(1)}, bf16[6,128,128]{2,1,0:T(8,128)(2,1)S(1)}, u32[]{:S(2)}, u32[]{:S(2)}) collective-permute-start(bf16[6,128,128]{2,1,0:T(8,128)(2,1)S(1)} %collective-permute-done.6.refs_4_), channel_id=1, source_target_pairs={{0,224},{32,0},{64,32},{96,64},{128,96},{160,128},{192,160},{224,1... | collective-permute-start | bytes 589832 | tf_op jit(solution)/shard_map/ppermute | solution.py:446
  47.8 6.2 %copy-start.5 = (bf16[6,128,128]{2,1,0:T(8,128)(2,1)}, bf16[6,128,128]{2,1,0:T(8,128)(2,1)S(1)}, u32[]{:S(2)}) copy-start(bf16[6,128,128]{2,1,0:T(8,128)(2,1)S(1)} %collective-permute-done.7.refs_5_) | copy-start | bytes 589828
  47.8 6.1 %copy-start.6 = (bf16[6,128,128]{2,1,0:T(8,128)(2,1)}, bf16[6,128,128]{2,1,0:T(8,128)(2,1)S(1)}, u32[]{:S(2)}) copy-start(bf16[6,128,128]{2,1,0:T(8,128)(2,1)S(1)} %collective-permute-done.8.refs_6_) | copy-start | bytes 589828
  47.9 6.1 %collective-permute-start.11 = (bf16[6,128,128]{2,1,0:T(8,128)(2,1)S(1)}, bf16[6,128,128]{2,1,0:T(8,128)(2,1)S(1)}, u32[]{:S(2)}, u32[]{:S(2)}) collective-permute-start(bf16[6,128,128]{2,1,0:T(8,128)(2,1)S(1)} %collective-permute-done.7.refs_5_), channel_id=1, source_target_pairs={{0,32},{32,64},{64,96},{96,128},{128,160},{160,192},{192,224},{224... | collective-permute-start | bytes 589832 | tf_op jit(solution)/shard_map/ppermute | solution.py:446
  49.1 21.1 %collective-permute-start.12 = (bf16[1024,256]{1,0:T(8,128)(2,1)}, bf16[1024,256]{1,0:T(8,128)(2,1)S(1)}, u32[]{:S(2)}, u32[]{:S(2)}) collective-permute-start(bf16[1024,256]{1,0:T(8,128)(2,1)} %collective-permute-done.9.refs_1_), channel_id=1, source_target_pairs={{0,32},{32,64},{64,96},{96,128},{128,160},{160,192},{192,224},{224... | collective-permute-start | bytes 1572872 | tf_op jit(solution)/shard_map/ppermute | solution.py:446
  49.9 20.4 %collective-permute-start.13 = (bf16[1024,256]{1,0:T(8,128)(2,1)}, bf16[1024,256]{1,0:T(8,128)(2,1)S(1)}, u32[]{:S(2)}, u32[]{:S(2)}) collective-permute-start(bf16[1024,256]{1,0:T(8,128)(2,1)} %collective-permute-done.10.refs_2_), channel_id=1, source_target_pairs={{0,224},{32,0},{64,32},{96,64},{128,96},{160,128},{192,160},{224,1... | collective-permute-start | bytes 1572872 | tf_op jit(solution)/shard_map/ppermute | solution.py:446
  54.0 0.7 copy-start.7
  65.0 19.0 %collective-permute-start.14 = (bf16[2048,128]{1,0:T(8,128)(2,1)}, bf16[2048,128]{1,0:T(8,128)(2,1)S(1)}, u32[]{:S(2)}, u32[]{:S(2)}) collective-permute-start(bf16[2048,128]{1,0:T(8,128)(2,1)} %get-tuple-element.59), channel_id=1, source_target_pairs={{0,8},{8,0},{1,9},{9,1},{2,10},{10,2},{3,11},{11,3},{4,12},{12,4},... | collective-permute-start | bytes 1572872 | tf_op jit(solution)/shard_map/ppermute | solution.py:442
  70.3 13.7 %copy-start.17 = (bf16[1024,256]{1,0:T(8,128)(2,1)}, bf16[1024,256]{1,0:T(8,128)(2,1)S(1)}, u32[]{:S(2)}) copy-start(bf16[1024,256]{1,0:T(8,128)(2,1)S(1)} %collective-permute-done.12.refs_3_) | copy-start | bytes 1572868
  70.3 13.7 %copy-start.18 = (bf16[1024,256]{1,0:T(8,128)(2,1)}, bf16[1024,256]{1,0:T(8,128)(2,1)S(1)}, u32[]{:S(2)}) copy-start(bf16[1024,256]{1,0:T(8,128)(2,1)S(1)} %collective-permute-done.13.refs_4_) | copy-start | bytes 1572868
  70.3 17.0 %collective-permute-start.18 = (bf16[1024,256]{1,0:T(8,128)(2,1)S(1)}, bf16[1024,256]{1,0:T(8,128)(2,1)S(1)}, u32[]{:S(2)}, u32[]{:S(2)}) collective-permute-start(bf16[1024,256]{1,0:T(8,128)(2,1)S(1)} %collective-permute-done.12.refs_3_), channel_id=1, source_target_pairs={{0,32},{32,64},{64,96},{96,128},{128,160},{160,192},{192,224},{224... | collective-permute-start | bytes 1572872 | tf_op jit(solution)/shard_map/ppermute | solution.py:446
  70.6 16.8 %collective-permute-start.20 = (bf16[1024,256]{1,0:T(8,128)(2,1)S(1)}, bf16[1024,256]{1,0:T(8,128)(2,1)S(1)}, u32[]{:S(2)}, u32[]{:S(2)}) collective-permute-start(bf16[1024,256]{1,0:T(8,128)(2,1)S(1)} %collective-permute-done.13.refs_4_), channel_id=1, source_target_pairs={{0,224},{32,0},{64,32},{96,64},{128,96},{160,128},{192,160},{224,1... | collective-permute-start | bytes 1572872 | tf_op jit(solution)/shard_map/ppermute | solution.py:446
  73.0 10.9 %collective-permute-start.15 = (f32[16,1,128]{2,1,0:T(1,128)}, f32[16,1,128]{2,1,0:T(1,128)S(1)}, u32[]{:S(2)}, u32[]{:S(2)}) collective-permute-start(f32[16,1,128]{2,1,0:T(1,128)} %get-tuple-element.52), channel_id=1, source_target_pairs={{0,8},{8,0},{1,9},{9,1},{2,10},{10,2},{3,11},{11,3},{4,12},{12,4},... | collective-permute-start | bytes 24584 | tf_op jit(solution)/shard_map/ppermute | solution.py:442
  84.0 0.6 copy-start.15
  84.0 0.8 copy-start.9
  87.2 14.0 %collective-permute-start.16 = (bf16[2048,128]{1,0:T(8,128)(2,1)}, bf16[2048,128]{1,0:T(8,128)(2,1)S(1)}, u32[]{:S(2)}, u32[]{:S(2)}) collective-permute-start(bf16[2048,128]{1,0:T(8,128)(2,1)} %get-tuple-element.60.own), channel_id=1, source_target_pairs={{0,16},{16,0},{1,17},{17,1},{2,18},{18,2},{3,19},{19,3},{4,20},{20... | collective-permute-start | bytes 1572872 | tf_op jit(solution)/shard_map/ppermute | solution.py:442
  87.2 21.2 %copy-start.13 = (bf16[1024,256]{1,0:T(8,128)(2,1)}, bf16[1024,256]{1,0:T(8,128)(2,1)S(1)}, u32[]{:S(2)}) copy-start(bf16[1024,256]{1,0:T(8,128)(2,1)S(1)} %collective-permute-done.18.refs_5_) | copy-start | bytes 1572868
  87.3 13.9 %collective-permute-start.19 = (bf16[512,256]{1,0:T(8,128)(2,1)S(1)}, bf16[512,256]{1,0:T(8,128)(2,1)S(1)}, u32[]{:S(2)}, u32[]{:S(2)}) collective-permute-start(bf16[512,256]{1,0:T(8,128)(2,1)S(1)} %slice.20), channel_id=1, source_target_pairs={{0,32},{32,64},{64,96},{96,128},{128,160},{160,192},{192,224},{224... | collective-permute-start | bytes 786440 | tf_op jit(solution)/shard_map/ppermute | solution.py:446
  87.4 13.8 %copy-start.14 = (bf16[1024,256]{1,0:T(8,128)(2,1)}, bf16[1024,256]{1,0:T(8,128)(2,1)S(1)}, u32[]{:S(2)}) copy-start(bf16[1024,256]{1,0:T(8,128)(2,1)S(1)} %collective-permute-done.20.refs_6_) | copy-start | bytes 1572868
  87.4 13.8 %collective-permute-start.21 = (bf16[512,256]{1,0:T(8,128)(2,1)S(1)}, bf16[512,256]{1,0:T(8,128)(2,1)}, u32[]{:S(2)}, u32[]{:S(2)}) collective-permute-start(bf16[512,256]{1,0:T(8,128)(2,1)S(1)} %slice.21), channel_id=1, source_target_pairs={{0,224},{32,0},{64,32},{96,64},{128,96},{160,128},{192,160},{224,1... | collective-permute-start | bytes 786440 | tf_op jit(solution)/shard_map/ppermute | solution.py:446
  90.1 11.0 %collective-permute-start.17 = (f32[16,1,128]{2,1,0:T(1,128)}, f32[16,1,128]{2,1,0:T(1,128)S(1)}, u32[]{:S(2)}, u32[]{:S(2)}) collective-permute-start(f32[16,1,128]{2,1,0:T(1,128)} %get-tuple-element.61.own_lse), channel_id=1, source_target_pairs={{0,16},{16,0},{1,17},{17,1},{2,18},{18,2},{3,19},{19,3},{4,20},{20... | collective-permute-start | bytes 24584 | tf_op jit(solution)/shard_map/ppermute | solution.py:442
  101.2 7.3 %copy-start.20 = (bf16[512,256]{1,0:T(8,128)(2,1)}, bf16[512,256]{1,0:T(8,128)(2,1)S(1)}, u32[]{:S(2)}) copy-start(bf16[512,256]{1,0:T(8,128)(2,1)S(1)} %collective-permute-done.19.refs_7_) | copy-start | bytes 786436
  101.2 16.8 %copy-start = (bf16[8,512,256]{2,1,0:T(8,128)(2,1)}, bf16[8,512,256]{2,1,0:T(8,128)(2,1)S(1)}, u32[]{:S(2)}) copy-start(bf16[8,512,256]{2,1,0:T(8,128)(2,1)S(1)} %all-to-all-done.near) | copy-start | bytes 6291460
  101.8 1.0 copy-start.8
  105.2 3.2 %collective-permute-start.22 = (bf16[2,128,1024]{2,1,0:T(8,128)(2,1)}, bf16[2,128,1024]{2,1,0:T(8,128)(2,1)S(1)}, u32[]{:S(2)}, u32[]{:S(2)}) collective-permute-start(bf16[2,128,1024]{2,1,0:T(8,128)(2,1)} %merge_last.1.near), channel_id=1, source_target_pairs={{0,8},{8,0},{1,9},{9,1},{2,10},{10,2},{3,11},{11,3},{4,12},{12,4},... | collective-permute-start | bytes 1572872 | tf_op jit(solution)/shard_map/ppermute | solution.py:442
  106.0 19.5 %collective-permute-start.23 = (bf16[8,512,256]{2,1,0:T(8,128)(2,1)S(1)}, bf16[8,512,256]{2,1,0:T(8,128)(2,1)}, u32[]{:S(2)}, u32[]{:S(2)}) collective-permute-start(bf16[8,512,256]{2,1,0:T(8,128)(2,1)S(1)} %all-to-all-done.near), channel_id=1, source_target_pairs={{0,8},{8,0},{1,9},{9,1},{2,10},{10,2},{3,11},{11,3},{4,12},{12,4},... | collective-permute-start | bytes 6291464 | tf_op jit(solution)/shard_map/ppermute | solution.py:442
  108.5 0.9 copy-start.19
  118.0 37.3 %all-to-all-start.1 = ((bf16[32,128,256]{2,1,0:T(8,128)(2,1)}), bf16[32,128,256]{2,1,0:T(8,128)(2,1)}, u32[]{:S(2)}, u32[]{:S(2)}) async-start(bf16[32,128,256]{2,1,0:T(8,128)(2,1)} %bitcast.17), calls=%async_computation.1 | async-start | bytes 4194304 | tf_op jit(solution)/shard_map/all_to_all | solution.py:525
  160.3 14.5 %all-to-all-start.2 = ((bf16[8,144,256]{2,1,0:T(8,128)(2,1)}), bf16[8,144,256]{2,1,0:T(8,128)(2,1)S(1)}, u32[]{:S(2)}, u32[]{:S(2)}) async-start(bf16[8,144,256]{2,1,0:T(8,128)(2,1)} %get-tuple-element.67), calls=%async_computation.2 | async-start | bytes 1179648 | tf_op jit(solution)/shard_map/all_to_all | solution.py:531
  174.8 0.8 copy-start.1
  (1 other events, 0.6 us)

commit v7 on v6

--- a/solution.py
+++ b/solution.py
@@ -299,52 +299,35 @@
 
 
 def project_kernel(place, near, far, *refs):
-    weights, out, rows, held, products, in_sem, out_sem = refs[: Z + 1], *refs[Z + 1 :]
+    weights, top, bottom, out, rows = refs[: Z - 1], *refs[Z - 1 :]
     z, yl, c = place[0], place[1], place[2]
-    half = held.shape[1] // 2
-    targets = [held.at[i] for i in range(Z - 1)]
-    targets += [held.at[Z - 1, pl.ds(0, half)], held.at[Z - 1, pl.ds(half, half)]]
-    copies = [
-        pltpu.make_async_copy(weights[i], targets[i], in_sem.at[i]) for i in range(Z + 1)
-    ]
-    for copy in copies:
-        copy.start()
     for ryl in range(2):
         rows[ryl * ROWS : (ryl + 1) * ROWS, :] = near[ryl]
         rows[(2 + ryl) * ROWS : (3 + ryl) * ROWS, :] = far[ryl]
-    sent = []
+    lhs = rows[...]
+    half = GROUP * HEAD // 2
     for i, distance in enumerate(DISTANCES):
-        for copy in copies[i : i + 1 if i < Z - 1 else Z + 1]:
-            copy.wait()
-        product = jnp.dot(rows[...], held[i], preferred_element_type=jnp.float32)
+        if i < Z - 1:
+            product = jnp.dot(lhs, weights[i][...], preferred_element_type=jnp.float32)
+        else:
+            product = jnp.dot(lhs[:, :half], top[...], preferred_element_type=jnp.float32)
+            product += jnp.dot(lhs[:, half:], bottom[...], preferred_element_type=jnp.float32)
         product = product.astype(jnp.bfloat16)
+        target = lax.rem(z + distance + Z, Z)
         for k in range(4):
             q = (yl ^ (k % 2)) * 2 + (c ^ (k // 2))
-            products[i, q] = product[k * ROWS : (k + 1) * ROWS, :]
-        target = lax.rem(z + distance + Z, Z)
-        copy = pltpu.make_async_copy(products.at[i], out.at[:, target], out_sem.at[i])
-        copy.start()
-        sent.append(copy)
-    for copy in sent:
-        copy.wait()
+            out[q, target] = product[k * ROWS : (k + 1) * ROWS, :]
 
 
 def project(place, near, far, weights):
     vmem = pl.BlockSpec(memory_space=pltpu.VMEM)
-    anywhere = pl.BlockSpec(memory_space=pl.ANY)
     depth, columns = weights[0].shape
     return pl.pallas_call(
         project_kernel,
-        in_specs=[pl.BlockSpec(memory_space=pltpu.SMEM), vmem, vmem] + [anywhere] * (Z + 1),
-        out_specs=anywhere,
+        in_specs=[pl.BlockSpec(memory_space=pltpu.SMEM)] + [vmem] * (3 + Z),
+        out_specs=vmem,
         out_shape=jax.ShapeDtypeStruct((4, Z, ROWS, columns), jnp.bfloat16),
-        scratch_shapes=[
-            pltpu.VMEM((4 * ROWS, depth), jnp.bfloat16),
-            pltpu.VMEM((Z, depth, columns), jnp.bfloat16),
-            pltpu.VMEM((Z, 4, ROWS, columns), jnp.bfloat16),
-            pltpu.SemaphoreType.DMA((Z + 1,)),
-            pltpu.SemaphoreType.DMA((Z,)),
-        ],
+        scratch_shapes=[pltpu.VMEM((4 * ROWS, depth), jnp.bfloat16)],
         compiler_params=params(),
         name="project",
         cost_estimate=pl.CostEstimate(

time: 178 us -> 176 us (0.989)
  Pallas kernels: 58.1 us -> 55.6 us
    pallas_call x1, Pallas kernels: 8.67 us -> 6.26 us  [project(): pl.pallas_call(project_kernel, in_specs=[pl.BlockSpec(memory_space=pltpu....]
  transfers between devices with their start and end apart: 27 -> 27, of which waited for: 7 -> 7; matrix products, arithmetic and copies ran while one was open for 0% -> 0% of each run, Pallas kernels for 26% -> 25%
where the time goes in v7:
time: 176 us; the launch traced here: 175 us
  waiting for transfers between devices  58.2 us (33%)
  Pallas kernels  55.6 us (32%)
  starting transfers between devices  51.8 us (29%)
  local copies, waits for them, and re-layouts  5.5 us (3%)
  other arithmetic  2.47 us (1%)
    pallas_call x3, Pallas kernels, attend(): pl.pallas_call(functools.partial(attend_kernel, chunk, cached, fresh, len...  31 us
    all_to_all x1, waiting for transfers between devices, local(): lax.all_to_all(products, ('yl', 'c', 'x', 'yh'), 0, 0, tiled=True)  29.8 us
    ppermute x15, starting transfers between devices, along_z(): return lax.ppermute(x, 'z', [(i, (i + distance) % Z) for i in range(Z)])  22.9 us
    ppermute x9, waiting for transfers between devices, swap(): return lax.ppermute(x, axis, [(0, 1), (1, 0)])  12.1 us
    ppermute x9, starting transfers between devices, swap(): return lax.ppermute(x, axis, [(0, 1), (1, 0)])  11.5 us
    all_to_all x1, waiting for transfers between devices, local(): partial = lax.all_to_all(partial, HEAD_AXES, 0, 0, tiled=True)  10.3 us
    all_to_all x1, starting transfers between devices, local(): lax.all_to_all(products, ('yl', 'c', 'x', 'yh'), 0, 0, tiled=True)  7.49 us
    all_to_all x1, starting transfers between devices, local(): third_near = lax.all_to_all(third_rows, HEAD_AXES, 0, 0, tiled=True)  6.37 us
  transfers between devices with their start and end apart: 27, of which 7 were waited for; matrix products, arithmetic and copies ran while one was open for 0% of the time, Pallas kernels for 25%

profile of v7, /device:TPU:1, one launch (start us, length us, event | category | flops | bytes accessed | tf_op | source)
XLA Modules:
  0.0 175.2 jit_solution(17974489520851984507)
XLA Ops:
  0.7 0.7 convert_element_type.36
  1.4 0.3 fusion.2
  1.7 0.8 pad_maximum_fusion
  2.5 2.0 %prepare.1 = (bf16[8,128,128]{2,1,0:T(8,128)(2,1)}, bf16[6,128,128]{2,1,0:T(8,128)(2,1)}) custom-call(bf16[128,1024]{1,0:T(8,128)(2,1)} %query.1, bf16[2,128,128]{2,1,0:T(8,128)(2,1)} %fresh.1, bf16[2,256,128]{2,1,0:T(8,128)(2,1)} %cached.1, f32[128,128]{1,0:T(8,128)} %get-tuple-element.74.cosine, f32[128,128]{1,0:T(8,128)} %get-tuple-element.75.sine), custom_call_target="tpu_custom_call" | custom-call | flops 2000000 | bytes 1500000 | tf_op jit(solution)/shard_map/prepare/pallas_call | solution.py:69
  4.5 2.1 %collective-permute-start.2 = (bf16[1024,128]{1,0:T(8,128)(2,1)}, bf16[1024,128]{1,0:T(8,128)(2,1)S(1)}, u32[]{:S(2)}, u32[]{:S(2)}) collective-permute-start(bf16[1024,128]{1,0:T(8,128)(2,1)} %bitcast.18), channel_id=1, source_target_pairs={{0,16},{16,0},{1,17},{17,1},{2,18},{18,2},{3,19},{19,3},{4,20},{20... | collective-permute-start | bytes 786440 | tf_op jit(solution)/shard_map/ppermute | solution.py:425
  6.6 1.6 collective-permute-start
  8.2 3.9 %collective-permute-start.1 = (bf16[6,128,128]{2,1,0:T(8,128)(2,1)}, bf16[6,128,128]{2,1,0:T(8,128)(2,1)S(1)}, u32[]{:S(2)}, u32[]{:S(2)}) collective-permute-start(bf16[6,128,128]{2,1,0:T(8,128)(2,1)} %get-tuple-element.36.refs_4_), channel_id=1, source_target_pairs={{0,224},{32,0},{64,32},{96,64},{128,96},{160,128},{192,160},{224,1... | collective-permute-start | bytes 589832 | tf_op jit(solution)/shard_map/ppermute | solution.py:429
  12.2 1.2 collective-permute-start.3
  13.4 0.7 pad_add_fusion.place
  14.1 4.5 %half.1 = bf16[8,512,256]{2,1,0:T(8,128)(2,1)} custom-call(s32[3]{0:T(128)} %pad_add_fusion.place, bf16[8,2,512,256]{3,2,1,0:T(8,128)(2,1)} %bitcast.16), custom_call_target="tpu_custom_call" | custom-call | bytes 8000000 | tf_op jit(solution)/shard_map/half/pallas_call | solution.py:87
  18.7 2.3 %collective-permute-start.10 = (bf16[1024,256]{1,0:T(8,128)(2,1)}, bf16[1024,256]{1,0:T(8,128)(2,1)}, u32[]{:S(2)}, u32[]{:S(2)}) collective-permute-start(bf16[1024,256]{1,0:T(8,128)(2,1)} %refs_0_.1), channel_id=1, source_target_pairs={{0,224},{32,0},{64,32},{96,64},{128,96},{160,128},{192,160},{224,1... | collective-permute-start | bytes 1572872 | tf_op jit(solution)/shard_map/ppermute | solution.py:429
  21.0 6.4 %all-to-all-start = ((bf16[8,512,256]{2,1,0:T(8,128)(2,1)}), bf16[8,512,256]{2,1,0:T(8,128)(2,1)S(1)}, u32[]{:S(2)}, u32[]{:S(2)}) async-start(bf16[8,512,256]{2,1,0:T(8,128)(2,1)} %half.1), calls=%async_computation | async-start | bytes 4194304 | tf_op jit(solution)/shard_map/all_to_all | solution.py:479
  27.4 2.8 %collective-permute-start.6 = (bf16[6,128,128]{2,1,0:T(8,128)(2,1)S(1)}, bf16[6,128,128]{2,1,0:T(8,128)(2,1)S(1)}, u32[]{:S(2)}, u32[]{:S(2)}) collective-permute-start(bf16[6,128,128]{2,1,0:T(8,128)(2,1)S(1)} %collective-permute-done.1.refs_6_.refs_2_), channel_id=1, source_target_pairs={{0,224},{32,0},{64,32},{96,64},{128,96},{160,128},{192,160},{224,1... | collective-permute-start | bytes 589832 | tf_op jit(solution)/shard_map/ppermute | solution.py:429
  30.2 0.7 copy-done.12
  30.9 10.3 %attend.3 = (f32[4096,256]{1,0:T(8,128)}, f32[4096,128]{1,0:T(8,128)}) custom-call(s32[3]{0:T(128)} %pad_add_fusion.place, bf16[1024,128]{1,0:T(8,128)(2,1)} %bitcast.20, bf16[1024,128]{1,0:T(8,128)(2,1)} %copy-done.10, bf16[1024,128]{1,0:T(8,128)(2,1)} %copy-done.11, bf16[1024,128]{1,0:T(8,128)(2,1)} %copy-done.12, ...), custom_call_target="tpu_custom_call" | custom-call | flops 2147483648 | bytes 4718592 | tf_op jit(solution)/shard_map/attend/pallas_call | solution.py:219
  41.4 2.6 %collective-permute-start.8 = (bf16[6,128,128]{2,1,0:T(8,128)(2,1)S(1)}, bf16[6,128,128]{2,1,0:T(8,128)(2,1)S(1)}, u32[]{:S(2)}, u32[]{:S(2)}) collective-permute-start(bf16[6,128,128]{2,1,0:T(8,128)(2,1)S(1)} %collective-permute-done.6.refs_4_), channel_id=1, source_target_pairs={{0,224},{32,0},{64,32},{96,64},{128,96},{160,128},{192,160},{224,1... | collective-permute-start | bytes 589832 | tf_op jit(solution)/shard_map/ppermute | solution.py:429
  44.0 3.7 %collective-permute-done.7.refs_5_ = bf16[6,128,128]{2,1,0:T(8,128)(2,1)S(1)} collective-permute-done((bf16[6,128,128]{2,1,0:T(8,128)(2,1)S(1)}, bf16[6,128,128]{2,1,0:T(8,128)(2,1)S(1)}, u32[]{:S(2)}, u32[]{:S(2)}) %collective-permute-start.7) | collective-permute-done | bytes 196640 | tf_op jit(solution)/shard_map/ppermute | solution.py:429
  47.9 1.3 collective-permute-start.11
  49.1 0.8 collective-permute-start.12
  49.9 1.9 %collective-permute-start.13 = (bf16[1024,256]{1,0:T(8,128)(2,1)}, bf16[1024,256]{1,0:T(8,128)(2,1)S(1)}, u32[]{:S(2)}, u32[]{:S(2)}) collective-permute-start(bf16[1024,256]{1,0:T(8,128)(2,1)} %collective-permute-done.10.refs_2_), channel_id=1, source_target_pairs={{0,224},{32,0},{64,32},{96,64},{128,96},{160,128},{192,160},{224,1... | collective-permute-start | bytes 1572872 | tf_op jit(solution)/shard_map/ppermute | solution.py:429
  51.8 2.2 %collective-permute-done.11.refs_7_ = bf16[6,128,128]{2,1,0:T(8,128)(2,1)S(1)} collective-permute-done((bf16[6,128,128]{2,1,0:T(8,128)(2,1)S(1)}, bf16[6,128,128]{2,1,0:T(8,128)(2,1)S(1)}, u32[]{:S(2)}, u32[]{:S(2)}) %collective-permute-start.11) | collective-permute-done | bytes 196640 | tf_op jit(solution)/shard_map/ppermute | solution.py:429
  54.0 0.7 copy-done.7
  54.7 10.4 %attend.4 = (bf16[2048,128]{1,0:T(8,128)(2,1)}, f32[16,1,128]{2,1,0:T(1,128)}) custom-call(s32[3]{0:T(128)} %pad_add_fusion.place, bf16[1024,128]{1,0:T(8,128)(2,1)} %copy-done.11, bf16[1024,128]{1,0:T(8,128)(2,1)} %copy-done.12, bf16[6,128,128]{2,1,0:T(8,128)(2,1)} %copy-done.2, bf16[6,128,128]{2,1,0:T(8,128)(2,1)} %copy-done.3, ...), custom_call_target="tpu_custom_call" | custom-call | flops 2147483648 | bytes 3145728 | tf_op jit(solution)/shard_map/attend/pallas_call | solution.py:219
  65.0 5.2 %collective-permute-start.14 = (bf16[2048,128]{1,0:T(8,128)(2,1)}, bf16[2048,128]{1,0:T(8,128)(2,1)S(1)}, u32[]{:S(2)}, u32[]{:S(2)}) collective-permute-start(bf16[2048,128]{1,0:T(8,128)(2,1)} %get-tuple-element.59), channel_id=1, source_target_pairs={{0,8},{8,0},{1,9},{9,1},{2,10},{10,2},{3,11},{11,3},{4,12},{12,4},... | collective-permute-start | bytes 1572872 | tf_op jit(solution)/shard_map/ppermute | solution.py:425
  70.3 0.3 collective-permute-start.18
  70.6 2.4 %collective-permute-start.20 = (bf16[1024,256]{1,0:T(8,128)(2,1)S(1)}, bf16[1024,256]{1,0:T(8,128)(2,1)S(1)}, u32[]{:S(2)}, u32[]{:S(2)}) collective-permute-start(bf16[1024,256]{1,0:T(8,128)(2,1)S(1)} %collective-permute-done.13.refs_4_), channel_id=1, source_target_pairs={{0,224},{32,0},{64,32},{96,64},{128,96},{160,128},{192,160},{224,1... | collective-permute-start | bytes 1572872 | tf_op jit(solution)/shard_map/ppermute | solution.py:429
  73.0 0.6 collective-permute-start.15
  73.6 10.3 %attend.5 = (bf16[2048,128]{1,0:T(8,128)(2,1)}, f32[16,1,128]{2,1,0:T(1,128)}) custom-call(s32[3]{0:T(128)} %pad_add_fusion.place, bf16[1024,128]{1,0:T(8,128)(2,1)} %bitcast.21, bf16[1024,128]{1,0:T(8,128)(2,1)} %copy-done.10, bf16[6,128,128]{2,1,0:T(8,128)(2,1)} %copy-done.2, bf16[6,128,128]{2,1,0:T(8,128)(2,1)} %copy-done.3, ...), custom_call_target="tpu_custom_call" | custom-call | flops 2147483648 | bytes 3145728 | tf_op jit(solution)/shard_map/attend/pallas_call | solution.py:219
  84.0 0.6 copy-done.15
  84.6 0.2 copy-done.9
  84.8 2.4 %merge.1 = (bf16[2048,128]{1,0:T(8,128)(2,1)}, f32[16,1,128]{2,1,0:T(1,128)}) custom-call(bf16[2048,128]{1,0:T(8,128)(2,1)} %get-tuple-element.57.own, f32[16,1,128]{2,1,0:T(1,128)} %get-tuple-element.58.own_lse, bf16[2048,128]{1,0:T(8,128)(2,1)} %copy-done.9, f32[16,1,128]{2,1,0:T(1,128)} %copy-done.15), custom_call_target="tpu_custom_call" | custom-call | flops 2000000 | bytes 1600000 | tf_op jit(solution)/shard_map/merge/pallas_call | solution.py:279
  87.4 2.7 %collective-permute-start.21 = (bf16[512,256]{1,0:T(8,128)(2,1)S(1)}, bf16[512,256]{1,0:T(8,128)(2,1)}, u32[]{:S(2)}, u32[]{:S(2)}) collective-permute-start(bf16[512,256]{1,0:T(8,128)(2,1)S(1)} %slice.21), channel_id=1, source_target_pairs={{0,224},{32,0},{64,32},{96,64},{128,96},{160,128},{192,160},{224,1... | collective-permute-start | bytes 786440 | tf_op jit(solution)/shard_map/ppermute | solution.py:429
  90.1 1.4 collective-permute-start.17
  91.6 9.6 %collective-permute-done.17.other_lse = f32[16,1,128]{2,1,0:T(1,128)S(1)} collective-permute-done((f32[16,1,128]{2,1,0:T(1,128)}, f32[16,1,128]{2,1,0:T(1,128)S(1)}, u32[]{:S(2)}, u32[]{:S(2)}) %collective-permute-start.17) | collective-permute-done | bytes 8224 | tf_op jit(solution)/shard_map/ppermute | solution.py:425
  101.2 0.5 copy-done.16
  101.8 1.0 copy-done.8
  102.8 2.4 %merge_last.1.near = bf16[2,128,1024]{2,1,0:T(8,128)(2,1)} custom-call(bf16[2048,128]{1,0:T(8,128)(2,1)} %get-tuple-element.60.own, f32[16,1,128]{2,1,0:T(1,128)} %get-tuple-element.61.own_lse, bf16[2048,128]{1,0:T(8,128)(2,1)} %copy-done.8, f32[16,1,128]{2,1,0:T(1,128)} %copy-done.16), custom_call_target="tpu_custom_call" | custom-call | flops 2000000 | bytes 1600000 | tf_op jit(solution)/shard_map/merge_last/pallas_call | solution.py:292
  105.2 0.8 collective-permute-start.22
  106.0 2.5 %collective-permute-done.22.far = bf16[2,128,1024]{2,1,0:T(8,128)(2,1)S(1)} collective-permute-done((bf16[2,128,1024]{2,1,0:T(8,128)(2,1)}, bf16[2,128,1024]{2,1,0:T(8,128)(2,1)S(1)}, u32[]{:S(2)}, u32[]{:S(2)}) %collective-permute-start.22) | collective-permute-done | bytes 524320 | tf_op jit(solution)/shard_map/ppermute | solution.py:425
  108.5 0.9 copy-done.19
  109.3 6.3 %project.1 = bf16[4,8,128,256]{3,2,1,0:T(8,128)(2,1)} custom-call(s32[3]{0:T(128)} %pad_add_fusion.place, bf16[2,128,1024]{2,1,0:T(8,128)(2,1)} %merge_last.1.near, bf16[2,128,1024]{2,1,0:T(8,128)(2,1)} %copy-done.19, bf16[1024,256]{1,0:T(8,128)(2,1)} %refs_0_.1, bf16[1024,256]{1,0:T(8,128)(2,1)} %collective-permute-done.9.refs_1_, ...), custom_call_target="tpu_custom_call" | custom-call | flops 2147483648 | bytes 7000000 | tf_op jit(solution)/shard_map/project/pallas_call | solution.py:325
  115.6 7.5 %all-to-all-start.1 = ((bf16[32,128,256]{2,1,0:T(8,128)(2,1)}), bf16[32,128,256]{2,1,0:T(8,128)(2,1)}, u32[]{:S(2)}, u32[]{:S(2)}) async-start(bf16[32,128,256]{2,1,0:T(8,128)(2,1)} %bitcast.17), calls=%async_computation.1 | async-start | bytes 4194304 | tf_op jit(solution)/shard_map/all_to_all | solution.py:508
  123.1 29.8 %all-to-all-done.1 = bf16[32,128,256]{2,1,0:T(8,128)(2,1)} async-done(((bf16[32,128,256]{2,1,0:T(8,128)(2,1)}), bf16[32,128,256]{2,1,0:T(8,128)(2,1)}, u32[]{:S(2)}, u32[]{:S(2)}) %all-to-all-start.1) | async-done | bytes 2097184 | tf_op jit(solution)/shard_map/all_to_all | solution.py:508
  152.9 4.9 %third.1 = (bf16[128,1024]{1,0:T(8,128)(2,1)}, bf16[8,144,256]{2,1,0:T(8,128)(2,1)}) custom-call(s32[3]{0:T(128)} %pad_add_fusion.place, bf16[4,8,128,256]{3,2,1,0:T(8,128)(2,1)} %bitcast.9.received, bf16[128,1024]{1,0:T(8,128)(2,1)} %hidden.1, f32[1,1024]{1,0:T(1,128)} %bitcast.22, bf16[8,512,256]{2,1,0:T(8,128)(2,1)} %copy-done, ...), custom_call_target="tpu_custom_call" | custom-call | tf_op jit(solution)/shard_map/third/pallas_call | solution.py:377
  157.8 3.5 %all-to-all-start.2 = ((bf16[8,144,256]{2,1,0:T(8,128)(2,1)}), bf16[8,144,256]{2,1,0:T(8,128)(2,1)S(1)}, u32[]{:S(2)}, u32[]{:S(2)}) async-start(bf16[8,144,256]{2,1,0:T(8,128)(2,1)} %get-tuple-element.67), calls=%async_computation.2 | async-start | bytes 1179648 | tf_op jit(solution)/shard_map/all_to_all | solution.py:514
  162.0 10.3 %all-to-all-done.2.partial = bf16[8,144,256]{2,1,0:T(8,128)(2,1)S(1)} async-done(((bf16[8,144,256]{2,1,0:T(8,128)(2,1)}), bf16[8,144,256]{2,1,0:T(8,128)(2,1)S(1)}, u32[]{:S(2)}, u32[]{:S(2)}) %all-to-all-start.2) | async-done | bytes 589856 | tf_op jit(solution)/shard_map/all_to_all | solution.py:514
  172.3 0.8 copy-done.1
  173.2 2.1 %final.1 = bf16[128,256]{1,0:T(8,128)(2,1)} custom-call(s32[1]{0:T(128)S(6)} %copy.13.count, bf16[8,144,256]{2,1,0:T(8,128)(2,1)} %copy-done.1, f32[1,256]{1,0:T(1,128)} %bitcast.23, f32[128,128]{1,0:T(8,128)} %get-tuple-element.74.cosine, f32[128,128]{1,0:T(8,128)} %get-tuple-element.75.sine, s32[1,128]{1,0:T(1,128)} %bitcast.24), custom_call_target="tpu_custom_call" | custom-call | tf_op jit(solution)/shard_map/final/pallas_call | solution.py:414
  (70 shorter events, 0.6 us)
Async XLA Ops:
  4.5 14.1 %collective-permute-start.2 = (bf16[1024,128]{1,0:T(8,128)(2,1)}, bf16[1024,128]{1,0:T(8,128)(2,1)S(1)}, u32[]{:S(2)}, u32[]{:S(2)}) collective-permute-start(bf16[1024,128]{1,0:T(8,128)(2,1)} %bitcast.18), channel_id=1, source_target_pairs={{0,16},{16,0},{1,17},{17,1},{2,18},{18,2},{3,19},{19,3},{4,20},{20... | collective-permute-start | bytes 786440 | tf_op jit(solution)/shard_map/ppermute | solution.py:425
  6.6 12.0 %collective-permute-start = (bf16[6,128,128]{2,1,0:T(8,128)(2,1)}, bf16[6,128,128]{2,1,0:T(8,128)(2,1)S(1)}, u32[]{:S(2)}, u32[]{:S(2)}) collective-permute-start(bf16[6,128,128]{2,1,0:T(8,128)(2,1)} %get-tuple-element.36.refs_4_), channel_id=1, source_target_pairs={{0,32},{32,64},{64,96},{96,128},{128,160},{160,192},{192,224},{224... | collective-permute-start | bytes 589832 | tf_op jit(solution)/shard_map/ppermute | solution.py:429
  8.2 10.3 %collective-permute-start.1 = (bf16[6,128,128]{2,1,0:T(8,128)(2,1)}, bf16[6,128,128]{2,1,0:T(8,128)(2,1)S(1)}, u32[]{:S(2)}, u32[]{:S(2)}) collective-permute-start(bf16[6,128,128]{2,1,0:T(8,128)(2,1)} %get-tuple-element.36.refs_4_), channel_id=1, source_target_pairs={{0,224},{32,0},{64,32},{96,64},{128,96},{160,128},{192,160},{224,1... | collective-permute-start | bytes 589832 | tf_op jit(solution)/shard_map/ppermute | solution.py:429
  12.2 15.2 %collective-permute-start.3 = (bf16[1024,128]{1,0:T(8,128)(2,1)}, bf16[1024,128]{1,0:T(8,128)(2,1)S(1)}, u32[]{:S(2)}, u32[]{:S(2)}) collective-permute-start(bf16[1024,128]{1,0:T(8,128)(2,1)} %bitcast.19), channel_id=1, source_target_pairs={{0,8},{8,0},{1,9},{9,1},{2,10},{10,2},{3,11},{11,3},{4,12},{12,4},... | collective-permute-start | bytes 786440 | tf_op jit(solution)/shard_map/ppermute | solution.py:425
  18.6 2.5 %copy-start.21 = (bf16[6,128,128]{2,1,0:T(8,128)(2,1)}, bf16[6,128,128]{2,1,0:T(8,128)(2,1)S(1)}, u32[]{:S(2)}) copy-start(bf16[6,128,128]{2,1,0:T(8,128)(2,1)S(1)} %collective-permute-done.refs_5_) | copy-start | bytes 589828
  18.6 8.9 %copy-start.2 = (bf16[6,128,128]{2,1,0:T(8,128)(2,1)}, bf16[6,128,128]{2,1,0:T(8,128)(2,1)S(1)}, u32[]{:S(2)}) copy-start(bf16[6,128,128]{2,1,0:T(8,128)(2,1)S(1)} %collective-permute-done.1.refs_6_.refs_2_) | copy-start | bytes 589828
  18.6 2.5 %copy-start.10 = (bf16[1024,128]{1,0:T(8,128)(2,1)}, bf16[1024,128]{1,0:T(8,128)(2,1)S(1)}, u32[]{:S(2)}) copy-start(bf16[1024,128]{1,0:T(8,128)(2,1)S(1)} %collective-permute-done.2.refs_1_) | copy-start | bytes 786436
  18.6 11.6 %collective-permute-start.4 = (bf16[1024,128]{1,0:T(8,128)(2,1)S(1)}, bf16[1024,128]{1,0:T(8,128)(2,1)S(1)}, u32[]{:S(2)}, u32[]{:S(2)}) collective-permute-start(bf16[1024,128]{1,0:T(8,128)(2,1)S(1)} %collective-permute-done.2.refs_1_), channel_id=1, source_target_pairs={{0,8},{8,0},{1,9},{9,1},{2,10},{10,2},{3,11},{11,3},{4,12},{12,4},... | collective-permute-start | bytes 786440 | tf_op jit(solution)/shard_map/ppermute | solution.py:425
  18.7 29.2 %collective-permute-start.10 = (bf16[1024,256]{1,0:T(8,128)(2,1)}, bf16[1024,256]{1,0:T(8,128)(2,1)}, u32[]{:S(2)}, u32[]{:S(2)}) collective-permute-start(bf16[1024,256]{1,0:T(8,128)(2,1)} %refs_0_.1), channel_id=1, source_target_pairs={{0,224},{32,0},{64,32},{96,64},{128,96},{160,128},{192,160},{224,1... | collective-permute-start | bytes 1572872 | tf_op jit(solution)/shard_map/ppermute | solution.py:429
  21.0 26.8 %collective-permute-start.9 = (bf16[1024,256]{1,0:T(8,128)(2,1)}, bf16[1024,256]{1,0:T(8,128)(2,1)}, u32[]{:S(2)}, u32[]{:S(2)}) collective-permute-start(bf16[1024,256]{1,0:T(8,128)(2,1)} %refs_0_.1), channel_id=1, source_target_pairs={{0,32},{32,64},{64,96},{96,128},{128,160},{160,192},{192,224},{224... | collective-permute-start | bytes 1572872 | tf_op jit(solution)/shard_map/ppermute | solution.py:429
  21.0 20.2 %collective-permute-start.5 = (bf16[6,128,128]{2,1,0:T(8,128)(2,1)S(1)}, bf16[6,128,128]{2,1,0:T(8,128)(2,1)S(1)}, u32[]{:S(2)}, u32[]{:S(2)}) collective-permute-start(bf16[6,128,128]{2,1,0:T(8,128)(2,1)S(1)} %collective-permute-done.refs_5_), channel_id=1, source_target_pairs={{0,32},{32,64},{64,96},{96,128},{128,160},{160,192},{192,224},{224... | collective-permute-start | bytes 589832 | tf_op jit(solution)/shard_map/ppermute | solution.py:429
  21.0 80.2 %all-to-all-start = ((bf16[8,512,256]{2,1,0:T(8,128)(2,1)}), bf16[8,512,256]{2,1,0:T(8,128)(2,1)S(1)}, u32[]{:S(2)}, u32[]{:S(2)}) async-start(bf16[8,512,256]{2,1,0:T(8,128)(2,1)} %half.1), calls=%async_computation | async-start | bytes 4194304 | tf_op jit(solution)/shard_map/all_to_all | solution.py:479
  27.4 2.8 %copy-start.11 = (bf16[1024,128]{1,0:T(8,128)(2,1)}, bf16[1024,128]{1,0:T(8,128)(2,1)S(1)}, u32[]{:S(2)}) copy-start(bf16[1024,128]{1,0:T(8,128)(2,1)S(1)} %collective-permute-done.3.refs_2_.refs_0_) | copy-start | bytes 786436
  27.4 13.8 %collective-permute-start.6 = (bf16[6,128,128]{2,1,0:T(8,128)(2,1)S(1)}, bf16[6,128,128]{2,1,0:T(8,128)(2,1)S(1)}, u32[]{:S(2)}, u32[]{:S(2)}) collective-permute-start(bf16[6,128,128]{2,1,0:T(8,128)(2,1)S(1)} %collective-permute-done.1.refs_6_.refs_2_), channel_id=1, source_target_pairs={{0,224},{32,0},{64,32},{96,64},{128,96},{160,128},{192,160},{224,1... | collective-permute-start | bytes 589832 | tf_op jit(solution)/shard_map/ppermute | solution.py:429
  30.2 0.7 copy-start.12
  41.2 12.7 %copy-start.3 = (bf16[6,128,128]{2,1,0:T(8,128)(2,1)}, bf16[6,128,128]{2,1,0:T(8,128)(2,1)S(1)}, u32[]{:S(2)}) copy-start(bf16[6,128,128]{2,1,0:T(8,128)(2,1)S(1)} %collective-permute-done.5.refs_3_) | copy-start | bytes 589828
  41.3 12.7 %copy-start.4 = (bf16[6,128,128]{2,1,0:T(8,128)(2,1)}, bf16[6,128,128]{2,1,0:T(8,128)(2,1)S(1)}, u32[]{:S(2)}) copy-start(bf16[6,128,128]{2,1,0:T(8,128)(2,1)S(1)} %collective-permute-done.6.refs_4_) | copy-start | bytes 589828
  41.3 6.5 %collective-permute-start.7 = (bf16[6,128,128]{2,1,0:T(8,128)(2,1)S(1)}, bf16[6,128,128]{2,1,0:T(8,128)(2,1)S(1)}, u32[]{:S(2)}, u32[]{:S(2)}) collective-permute-start(bf16[6,128,128]{2,1,0:T(8,128)(2,1)S(1)} %collective-permute-done.5.refs_3_), channel_id=1, source_target_pairs={{0,32},{32,64},{64,96},{96,128},{128,160},{160,192},{192,224},{224... | collective-permute-start | bytes 589832 | tf_op jit(solution)/shard_map/ppermute | solution.py:429
  41.4 6.4 %collective-permute-start.8 = (bf16[6,128,128]{2,1,0:T(8,128)(2,1)S(1)}, bf16[6,128,128]{2,1,0:T(8,128)(2,1)S(1)}, u32[]{:S(2)}, u32[]{:S(2)}) collective-permute-start(bf16[6,128,128]{2,1,0:T(8,128)(2,1)S(1)} %collective-permute-done.6.refs_4_), channel_id=1, source_target_pairs={{0,224},{32,0},{64,32},{96,64},{128,96},{160,128},{192,160},{224,1... | collective-permute-start | bytes 589832 | tf_op jit(solution)/shard_map/ppermute | solution.py:429
  47.8 6.2 %copy-start.5 = (bf16[6,128,128]{2,1,0:T(8,128)(2,1)}, bf16[6,128,128]{2,1,0:T(8,128)(2,1)S(1)}, u32[]{:S(2)}) copy-start(bf16[6,128,128]{2,1,0:T(8,128)(2,1)S(1)} %collective-permute-done.7.refs_5_) | copy-start | bytes 589828
  47.8 6.1 %copy-start.6 = (bf16[6,128,128]{2,1,0:T(8,128)(2,1)}, bf16[6,128,128]{2,1,0:T(8,128)(2,1)S(1)}, u32[]{:S(2)}) copy-start(bf16[6,128,128]{2,1,0:T(8,128)(2,1)S(1)} %collective-permute-done.8.refs_6_) | copy-start | bytes 589828
  47.9 6.1 %collective-permute-start.11 = (bf16[6,128,128]{2,1,0:T(8,128)(2,1)S(1)}, bf16[6,128,128]{2,1,0:T(8,128)(2,1)S(1)}, u32[]{:S(2)}, u32[]{:S(2)}) collective-permute-start(bf16[6,128,128]{2,1,0:T(8,128)(2,1)S(1)} %collective-permute-done.7.refs_5_), channel_id=1, source_target_pairs={{0,32},{32,64},{64,96},{96,128},{128,160},{160,192},{192,224},{224... | collective-permute-start | bytes 589832 | tf_op jit(solution)/shard_map/ppermute | solution.py:429
  49.1 21.1 %collective-permute-start.12 = (bf16[1024,256]{1,0:T(8,128)(2,1)}, bf16[1024,256]{1,0:T(8,128)(2,1)S(1)}, u32[]{:S(2)}, u32[]{:S(2)}) collective-permute-start(bf16[1024,256]{1,0:T(8,128)(2,1)} %collective-permute-done.9.refs_1_), channel_id=1, source_target_pairs={{0,32},{32,64},{64,96},{96,128},{128,160},{160,192},{192,224},{224... | collective-permute-start | bytes 1572872 | tf_op jit(solution)/shard_map/ppermute | solution.py:429
  49.9 20.4 %collective-permute-start.13 = (bf16[1024,256]{1,0:T(8,128)(2,1)}, bf16[1024,256]{1,0:T(8,128)(2,1)S(1)}, u32[]{:S(2)}, u32[]{:S(2)}) collective-permute-start(bf16[1024,256]{1,0:T(8,128)(2,1)} %collective-permute-done.10.refs_2_), channel_id=1, source_target_pairs={{0,224},{32,0},{64,32},{96,64},{128,96},{160,128},{192,160},{224,1... | collective-permute-start | bytes 1572872 | tf_op jit(solution)/shard_map/ppermute | solution.py:429
  54.0 0.7 copy-start.7
  65.0 19.0 %collective-permute-start.14 = (bf16[2048,128]{1,0:T(8,128)(2,1)}, bf16[2048,128]{1,0:T(8,128)(2,1)S(1)}, u32[]{:S(2)}, u32[]{:S(2)}) collective-permute-start(bf16[2048,128]{1,0:T(8,128)(2,1)} %get-tuple-element.59), channel_id=1, source_target_pairs={{0,8},{8,0},{1,9},{9,1},{2,10},{10,2},{3,11},{11,3},{4,12},{12,4},... | collective-permute-start | bytes 1572872 | tf_op jit(solution)/shard_map/ppermute | solution.py:425
  70.3 13.7 %copy-start.17 = (bf16[1024,256]{1,0:T(8,128)(2,1)}, bf16[1024,256]{1,0:T(8,128)(2,1)S(1)}, u32[]{:S(2)}) copy-start(bf16[1024,256]{1,0:T(8,128)(2,1)S(1)} %collective-permute-done.12.refs_3_) | copy-start | bytes 1572868
  70.3 13.7 %copy-start.18 = (bf16[1024,256]{1,0:T(8,128)(2,1)}, bf16[1024,256]{1,0:T(8,128)(2,1)S(1)}, u32[]{:S(2)}) copy-start(bf16[1024,256]{1,0:T(8,128)(2,1)S(1)} %collective-permute-done.13.refs_4_) | copy-start | bytes 1572868
  70.3 17.0 %collective-permute-start.18 = (bf16[1024,256]{1,0:T(8,128)(2,1)S(1)}, bf16[1024,256]{1,0:T(8,128)(2,1)S(1)}, u32[]{:S(2)}, u32[]{:S(2)}) collective-permute-start(bf16[1024,256]{1,0:T(8,128)(2,1)S(1)} %collective-permute-done.12.refs_3_), channel_id=1, source_target_pairs={{0,32},{32,64},{64,96},{96,128},{128,160},{160,192},{192,224},{224... | collective-permute-start | bytes 1572872 | tf_op jit(solution)/shard_map/ppermute | solution.py:429
  70.6 16.8 %collective-permute-start.20 = (bf16[1024,256]{1,0:T(8,128)(2,1)S(1)}, bf16[1024,256]{1,0:T(8,128)(2,1)S(1)}, u32[]{:S(2)}, u32[]{:S(2)}) collective-permute-start(bf16[1024,256]{1,0:T(8,128)(2,1)S(1)} %collective-permute-done.13.refs_4_), channel_id=1, source_target_pairs={{0,224},{32,0},{64,32},{96,64},{128,96},{160,128},{192,160},{224,1... | collective-permute-start | bytes 1572872 | tf_op jit(solution)/shard_map/ppermute | solution.py:429
  73.0 10.9 %collective-permute-start.15 = (f32[16,1,128]{2,1,0:T(1,128)}, f32[16,1,128]{2,1,0:T(1,128)S(1)}, u32[]{:S(2)}, u32[]{:S(2)}) collective-permute-start(f32[16,1,128]{2,1,0:T(1,128)} %get-tuple-element.52), channel_id=1, source_target_pairs={{0,8},{8,0},{1,9},{9,1},{2,10},{10,2},{3,11},{11,3},{4,12},{12,4},... | collective-permute-start | bytes 24584 | tf_op jit(solution)/shard_map/ppermute | solution.py:425
  84.0 0.6 copy-start.15
  84.0 0.8 copy-start.9
  87.2 14.0 %collective-permute-start.16 = (bf16[2048,128]{1,0:T(8,128)(2,1)}, bf16[2048,128]{1,0:T(8,128)(2,1)S(1)}, u32[]{:S(2)}, u32[]{:S(2)}) collective-permute-start(bf16[2048,128]{1,0:T(8,128)(2,1)} %get-tuple-element.60.own), channel_id=1, source_target_pairs={{0,16},{16,0},{1,17},{17,1},{2,18},{18,2},{3,19},{19,3},{4,20},{20... | collective-permute-start | bytes 1572872 | tf_op jit(solution)/shard_map/ppermute | solution.py:425
  87.2 21.2 %copy-start.13 = (bf16[1024,256]{1,0:T(8,128)(2,1)}, bf16[1024,256]{1,0:T(8,128)(2,1)S(1)}, u32[]{:S(2)}) copy-start(bf16[1024,256]{1,0:T(8,128)(2,1)S(1)} %collective-permute-done.18.refs_5_) | copy-start | bytes 1572868
  87.3 13.9 %collective-permute-start.19 = (bf16[512,256]{1,0:T(8,128)(2,1)S(1)}, bf16[512,256]{1,0:T(8,128)(2,1)S(1)}, u32[]{:S(2)}, u32[]{:S(2)}) collective-permute-start(bf16[512,256]{1,0:T(8,128)(2,1)S(1)} %slice.20), channel_id=1, source_target_pairs={{0,32},{32,64},{64,96},{96,128},{128,160},{160,192},{192,224},{224... | collective-permute-start | bytes 786440 | tf_op jit(solution)/shard_map/ppermute | solution.py:429
  87.4 13.8 %copy-start.14 = (bf16[1024,256]{1,0:T(8,128)(2,1)}, bf16[1024,256]{1,0:T(8,128)(2,1)S(1)}, u32[]{:S(2)}) copy-start(bf16[1024,256]{1,0:T(8,128)(2,1)S(1)} %collective-permute-done.20.refs_6_) | copy-start | bytes 1572868
  87.4 13.8 %collective-permute-start.21 = (bf16[512,256]{1,0:T(8,128)(2,1)S(1)}, bf16[512,256]{1,0:T(8,128)(2,1)}, u32[]{:S(2)}, u32[]{:S(2)}) collective-permute-start(bf16[512,256]{1,0:T(8,128)(2,1)S(1)} %slice.21), channel_id=1, source_target_pairs={{0,224},{32,0},{64,32},{96,64},{128,96},{160,128},{192,160},{224,1... | collective-permute-start | bytes 786440 | tf_op jit(solution)/shard_map/ppermute | solution.py:429
  90.1 11.0 %collective-permute-start.17 = (f32[16,1,128]{2,1,0:T(1,128)}, f32[16,1,128]{2,1,0:T(1,128)S(1)}, u32[]{:S(2)}, u32[]{:S(2)}) collective-permute-start(f32[16,1,128]{2,1,0:T(1,128)} %get-tuple-element.61.own_lse), channel_id=1, source_target_pairs={{0,16},{16,0},{1,17},{17,1},{2,18},{18,2},{3,19},{19,3},{4,20},{20... | collective-permute-start | bytes 24584 | tf_op jit(solution)/shard_map/ppermute | solution.py:425
  101.2 7.3 %copy-start.20 = (bf16[512,256]{1,0:T(8,128)(2,1)}, bf16[512,256]{1,0:T(8,128)(2,1)S(1)}, u32[]{:S(2)}) copy-start(bf16[512,256]{1,0:T(8,128)(2,1)S(1)} %collective-permute-done.19.refs_7_) | copy-start | bytes 786436
  101.2 14.4 %copy-start = (bf16[8,512,256]{2,1,0:T(8,128)(2,1)}, bf16[8,512,256]{2,1,0:T(8,128)(2,1)S(1)}, u32[]{:S(2)}) copy-start(bf16[8,512,256]{2,1,0:T(8,128)(2,1)S(1)} %all-to-all-done.near) | copy-start | bytes 6291460
  101.8 1.0 copy-start.8
  105.2 3.2 %collective-permute-start.22 = (bf16[2,128,1024]{2,1,0:T(8,128)(2,1)}, bf16[2,128,1024]{2,1,0:T(8,128)(2,1)S(1)}, u32[]{:S(2)}, u32[]{:S(2)}) collective-permute-start(bf16[2,128,1024]{2,1,0:T(8,128)(2,1)} %merge_last.1.near), channel_id=1, source_target_pairs={{0,8},{8,0},{1,9},{9,1},{2,10},{10,2},{3,11},{11,3},{4,12},{12,4},... | collective-permute-start | bytes 1572872 | tf_op jit(solution)/shard_map/ppermute | solution.py:425
  106.0 17.1 %collective-permute-start.23 = (bf16[8,512,256]{2,1,0:T(8,128)(2,1)S(1)}, bf16[8,512,256]{2,1,0:T(8,128)(2,1)}, u32[]{:S(2)}, u32[]{:S(2)}) collective-permute-start(bf16[8,512,256]{2,1,0:T(8,128)(2,1)S(1)} %all-to-all-done.near), channel_id=1, source_target_pairs={{0,8},{8,0},{1,9},{9,1},{2,10},{10,2},{3,11},{11,3},{4,12},{12,4},... | collective-permute-start | bytes 6291464 | tf_op jit(solution)/shard_map/ppermute | solution.py:425
  108.5 0.9 copy-start.19
  115.6 37.3 %all-to-all-start.1 = ((bf16[32,128,256]{2,1,0:T(8,128)(2,1)}), bf16[32,128,256]{2,1,0:T(8,128)(2,1)}, u32[]{:S(2)}, u32[]{:S(2)}) async-start(bf16[32,128,256]{2,1,0:T(8,128)(2,1)} %bitcast.17), calls=%async_computation.1 | async-start | bytes 4194304 | tf_op jit(solution)/shard_map/all_to_all | solution.py:508
  157.8 14.5 %all-to-all-start.2 = ((bf16[8,144,256]{2,1,0:T(8,128)(2,1)}), bf16[8,144,256]{2,1,0:T(8,128)(2,1)S(1)}, u32[]{:S(2)}, u32[]{:S(2)}) async-start(bf16[8,144,256]{2,1,0:T(8,128)(2,1)} %get-tuple-element.67), calls=%async_computation.2 | async-start | bytes 1179648 | tf_op jit(solution)/shard_map/all_to_all | solution.py:514
  172.3 0.8 copy-start.1
  (1 other events, 0.6 us)

commit v8 on v7

--- a/solution.py
+++ b/solution.py
@@ -339,50 +339,78 @@
 PAD = 16
 
 
-def third_kernel(place, received, hidden, gain, near, far, out, partial, scaled):
-    c = place[2]
+def third_kernel(
+    place, received, hidden, gain, near, far, out, partial, scaled, squares, held, sem
+):
+    c, q = place[2], pl.program_id(0)
+    copies = [pltpu.make_async_copy(ref, held.at[k], sem.at[k]) for k, ref in ((0, near), (1, far))]
+
+    @pl.when(q == 0)
+    def _():
+        for copy in copies:
+            copy.start()
+        squares[...] = jnp.zeros_like(squares)
+
+    total = received[0, 0].astype(jnp.float32)
+    for h in range(1, Z):
+        total = total + received[0, h].astype(jnp.float32)
+    result = (hidden[...].astype(jnp.float32) + total).astype(jnp.bfloat16)
+    out[...] = result
+    wide = result.astype(jnp.float32)
+    squares[...] += wide * wide
+    scaled[q] = (wide * gain[...]).astype(jnp.bfloat16)
+
+    @pl.when(q == pl.num_programs(0) - 1)
+    def _():
+        row = row_of(
+            jnp.broadcast_to(jnp.sum(squares[...], axis=1, keepdims=True), (ROWS, ROWS))
+        )
+        high = row.astype(jnp.bfloat16)
+        low = (row - high.astype(jnp.float32)).astype(jnp.bfloat16)
+        tail = jnp.broadcast_to(
+            jnp.concatenate([high, low], axis=1).astype(jnp.float32), (PAD, 2 * ROWS)
+        ).astype(jnp.bfloat16)
+        for copy in copies:
+            copy.wait()
+        near_rows = jnp.concatenate([scaled[2 * c], scaled[2 * c + 1]], axis=1)
+        far_rows = jnp.concatenate([scaled[2 - 2 * c], scaled[3 - 2 * c]], axis=1)
+        for h in range(Z):
+            product = jnp.dot(near_rows, held[0, h], preferred_element_type=jnp.float32)
+            product += jnp.dot(far_rows, held[1, h], preferred_element_type=jnp.float32)
+            partial[h, :ROWS, :] = product.astype(jnp.bfloat16)
+            partial[h, ROWS:, :] = tail
+
+
+def third_partials(place, received, hidden, gain, near, far):
     columns = received.shape[3]
-    squares = jnp.zeros((ROWS, columns), jnp.float32)
-    for q in range(4):
-        at = slice(q * columns, (q + 1) * columns)
-        total = received[q, 0].astype(jnp.float32)
-        for h in range(1, Z):
-            total = total + received[q, h].astype(jnp.float32)
-        result = (hidden[:, at].astype(jnp.float32) + total).astype(jnp.bfloat16)
-        out[:, at] = result
-        wide = result.astype(jnp.float32)
-        squares = squares + wide * wide
-        scaled[q // 2, :, (q % 2) * columns : (q % 2 + 1) * columns] = (
-            wide * gain[:, at]
-        ).astype(jnp.bfloat16)
-    squares = jnp.sum(squares, axis=1, keepdims=True)
-    row = row_of(jnp.broadcast_to(squares, (ROWS, ROWS)))
-    high = row.astype(jnp.bfloat16)
-    low = (row - high.astype(jnp.float32)).astype(jnp.bfloat16)
-    tail = jnp.broadcast_to(
-        jnp.concatenate([high, low], axis=1).astype(jnp.float32), (PAD, 2 * ROWS)
-    ).astype(jnp.bfloat16)
-    near_rows, far_rows = scaled[c], scaled[1 - c]
-    for h in range(Z):
-        product = jnp.dot(near_rows, near[h], preferred_element_type=jnp.float32) + jnp.dot(
-            far_rows, far[h], preferred_element_type=jnp.float32
-        )
-        partial[h, :ROWS, :] = product.astype(jnp.bfloat16)
-        partial[h, ROWS:, :] = tail
-
-
-def third_partials(place, received, hidden, gain, near, far):
-    vmem = pl.BlockSpec(memory_space=pltpu.VMEM)
-    width = hidden.shape[1]
+    anywhere = pl.BlockSpec(memory_space=pl.ANY)
     return pl.pallas_call(
         third_kernel,
-        in_specs=[pl.BlockSpec(memory_space=pltpu.SMEM)] + [vmem] * 5,
-        out_specs=(vmem, vmem),
+        grid_spec=pltpu.PrefetchScalarGridSpec(
+            num_scalar_prefetch=1,
+            grid=(4,),
+            in_specs=[
+                pl.BlockSpec((1, Z, ROWS, columns), lambda i, s: (i, 0, 0, 0)),
+                pl.BlockSpec((ROWS, columns), lambda i, s: (0, i)),
+                pl.BlockSpec((1, columns), lambda i, s: (0, i)),
+                anywhere,
+                anywhere,
+            ],
+            out_specs=[
+                pl.BlockSpec((ROWS, columns), lambda i, s: (0, i)),
+                pl.BlockSpec((Z, ROWS + PAD, 2 * HEAD), lambda i, s: (0, 0, 0)),
+            ],
+            scratch_shapes=[
+                pltpu.VMEM((4, ROWS, columns), jnp.bfloat16),
+                pltpu.VMEM((ROWS, columns), jnp.float32),
+                pltpu.VMEM((2, *near.shape), jnp.bfloat16),
+                pltpu.SemaphoreType.DMA((2,)),
+            ],
+        ),
         out_shape=(
             jax.ShapeDtypeStruct(hidden.shape, jnp.bfloat16),
             jax.ShapeDtypeStruct((Z, ROWS + PAD, 2 * HEAD), jnp.bfloat16),
         ),
-        scratch_shapes=[pltpu.VMEM((2, ROWS, width // 2), jnp.bfloat16)],
         compiler_params=params(),
         name="third",
     )(place, received, hidden, gain, near, far)

time: 176 us -> 177 us (level)
  no operation moved by 1% of the time
where the time goes in v8:
time: 177 us
  waiting for transfers between devices  58.2 us (33%)
  Pallas kernels  57 us (32%)
  starting transfers between devices  51.8 us (29%)
  local copies, waits for them, and re-layouts  5.5 us (3%)
  other arithmetic  2.47 us (1%)
    pallas_call x3, Pallas kernels, attend(): pl.pallas_call(functools.partial(attend_kernel, chunk, cached, fresh, len...  31 us
    all_to_all x1, waiting for transfers between devices, local(): lax.all_to_all(products, ('yl', 'c', 'x', 'yh'), 0, 0, tiled=True)  29.8 us
    ppermute x15, starting transfers between devices, along_z(): return lax.ppermute(x, 'z', [(i, (i + distance) % Z) for i in range(Z)])  22.9 us
    ppermute x9, waiting for transfers between devices, swap(): return lax.ppermute(x, axis, [(0, 1), (1, 0)])  12.1 us
    ppermute x9, starting transfers between devices, swap(): return lax.ppermute(x, axis, [(0, 1), (1, 0)])  11.5 us
    all_to_all x1, waiting for transfers between devices, local(): partial = lax.all_to_all(partial, HEAD_AXES, 0, 0, tiled=True)  10.3 us
    all_to_all x1, starting transfers between devices, local(): lax.all_to_all(products, ('yl', 'c', 'x', 'yh'), 0, 0, tiled=True)  7.49 us
    all_to_all x1, starting transfers between devices, local(): third_near = lax.all_to_all(third_rows, HEAD_AXES, 0, 0, tiled=True)  6.37 us
  transfers between devices with their start and end apart: 27, of which 7 were waited for; matrix products, arithmetic and copies ran while one was open for 0% of the time, Pallas kernels for 25%

profile of v8, /device:TPU:1, one launch (start us, length us, event | category | flops | bytes accessed | tf_op | source)
XLA Modules:
  0.0 176.6 jit_solution(1134307958627274463)
XLA Ops:
  0.7 0.7 convert_element_type.36
  1.4 0.3 fusion.2
  1.7 0.8 pad_maximum_fusion
  2.5 2.0 %prepare.1 = (bf16[8,128,128]{2,1,0:T(8,128)(2,1)}, bf16[6,128,128]{2,1,0:T(8,128)(2,1)}) custom-call(bf16[128,1024]{1,0:T(8,128)(2,1)} %query.1, bf16[2,128,128]{2,1,0:T(8,128)(2,1)} %fresh.1, bf16[2,256,128]{2,1,0:T(8,128)(2,1)} %cached.1, f32[128,128]{1,0:T(8,128)} %get-tuple-element.74.cosine, f32[128,128]{1,0:T(8,128)} %get-tuple-element.75.sine), custom_call_target="tpu_custom_call" | custom-call | flops 2000000 | bytes 1500000 | tf_op jit(solution)/shard_map/prepare/pallas_call | solution.py:69
  4.5 2.1 %collective-permute-start.2 = (bf16[1024,128]{1,0:T(8,128)(2,1)}, bf16[1024,128]{1,0:T(8,128)(2,1)S(1)}, u32[]{:S(2)}, u32[]{:S(2)}) collective-permute-start(bf16[1024,128]{1,0:T(8,128)(2,1)} %bitcast.18), channel_id=1, source_target_pairs={{0,16},{16,0},{1,17},{17,1},{2,18},{18,2},{3,19},{19,3},{4,20},{20... | collective-permute-start | bytes 786440 | tf_op jit(solution)/shard_map/ppermute | solution.py:453
  6.6 1.6 collective-permute-start
  8.2 3.9 %collective-permute-start.1 = (bf16[6,128,128]{2,1,0:T(8,128)(2,1)}, bf16[6,128,128]{2,1,0:T(8,128)(2,1)S(1)}, u32[]{:S(2)}, u32[]{:S(2)}) collective-permute-start(bf16[6,128,128]{2,1,0:T(8,128)(2,1)} %get-tuple-element.36.refs_4_), channel_id=1, source_target_pairs={{0,224},{32,0},{64,32},{96,64},{128,96},{160,128},{192,160},{224,1... | collective-permute-start | bytes 589832 | tf_op jit(solution)/shard_map/ppermute | solution.py:457
  12.2 1.2 collective-permute-start.3
  13.4 0.7 pad_add_fusion.place
  14.1 4.5 %half.1 = bf16[8,512,256]{2,1,0:T(8,128)(2,1)} custom-call(s32[3]{0:T(128)} %pad_add_fusion.place, bf16[8,2,512,256]{3,2,1,0:T(8,128)(2,1)} %bitcast.16), custom_call_target="tpu_custom_call" | custom-call | bytes 8000000 | tf_op jit(solution)/shard_map/half/pallas_call | solution.py:87
  18.7 2.3 %collective-permute-start.10 = (bf16[1024,256]{1,0:T(8,128)(2,1)}, bf16[1024,256]{1,0:T(8,128)(2,1)}, u32[]{:S(2)}, u32[]{:S(2)}) collective-permute-start(bf16[1024,256]{1,0:T(8,128)(2,1)} %refs_0_.1), channel_id=1, source_target_pairs={{0,224},{32,0},{64,32},{96,64},{128,96},{160,128},{192,160},{224,1... | collective-permute-start | bytes 1572872 | tf_op jit(solution)/shard_map/ppermute | solution.py:457
  21.0 6.4 %all-to-all-start = ((bf16[8,512,256]{2,1,0:T(8,128)(2,1)}), bf16[8,512,256]{2,1,0:T(8,128)(2,1)S(1)}, u32[]{:S(2)}, u32[]{:S(2)}) async-start(bf16[8,512,256]{2,1,0:T(8,128)(2,1)} %half.1), calls=%async_computation | async-start | bytes 4194304 | tf_op jit(solution)/shard_map/all_to_all | solution.py:507
  27.4 2.8 %collective-permute-start.6 = (bf16[6,128,128]{2,1,0:T(8,128)(2,1)S(1)}, bf16[6,128,128]{2,1,0:T(8,128)(2,1)S(1)}, u32[]{:S(2)}, u32[]{:S(2)}) collective-permute-start(bf16[6,128,128]{2,1,0:T(8,128)(2,1)S(1)} %collective-permute-done.1.refs_6_.refs_2_), channel_id=1, source_target_pairs={{0,224},{32,0},{64,32},{96,64},{128,96},{160,128},{192,160},{224,1... | collective-permute-start | bytes 589832 | tf_op jit(solution)/shard_map/ppermute | solution.py:457
  30.2 0.7 copy-done.12
  30.9 10.3 %attend.3 = (f32[4096,256]{1,0:T(8,128)}, f32[4096,128]{1,0:T(8,128)}) custom-call(s32[3]{0:T(128)} %pad_add_fusion.place, bf16[1024,128]{1,0:T(8,128)(2,1)} %bitcast.20, bf16[1024,128]{1,0:T(8,128)(2,1)} %copy-done.10, bf16[1024,128]{1,0:T(8,128)(2,1)} %copy-done.11, bf16[1024,128]{1,0:T(8,128)(2,1)} %copy-done.12, ...), custom_call_target="tpu_custom_call" | custom-call | flops 2147483648 | bytes 4718592 | tf_op jit(solution)/shard_map/attend/pallas_call | solution.py:219
  41.4 2.6 %collective-permute-start.8 = (bf16[6,128,128]{2,1,0:T(8,128)(2,1)S(1)}, bf16[6,128,128]{2,1,0:T(8,128)(2,1)S(1)}, u32[]{:S(2)}, u32[]{:S(2)}) collective-permute-start(bf16[6,128,128]{2,1,0:T(8,128)(2,1)S(1)} %collective-permute-done.6.refs_4_), channel_id=1, source_target_pairs={{0,224},{32,0},{64,32},{96,64},{128,96},{160,128},{192,160},{224,1... | collective-permute-start | bytes 589832 | tf_op jit(solution)/shard_map/ppermute | solution.py:457
  44.0 3.7 %collective-permute-done.7.refs_5_ = bf16[6,128,128]{2,1,0:T(8,128)(2,1)S(1)} collective-permute-done((bf16[6,128,128]{2,1,0:T(8,128)(2,1)S(1)}, bf16[6,128,128]{2,1,0:T(8,128)(2,1)S(1)}, u32[]{:S(2)}, u32[]{:S(2)}) %collective-permute-start.7) | collective-permute-done | bytes 196640 | tf_op jit(solution)/shard_map/ppermute | solution.py:457
  47.9 1.3 collective-permute-start.11
  49.1 0.8 collective-permute-start.12
  49.9 1.9 %collective-permute-start.13 = (bf16[1024,256]{1,0:T(8,128)(2,1)}, bf16[1024,256]{1,0:T(8,128)(2,1)S(1)}, u32[]{:S(2)}, u32[]{:S(2)}) collective-permute-start(bf16[1024,256]{1,0:T(8,128)(2,1)} %collective-permute-done.10.refs_2_), channel_id=1, source_target_pairs={{0,224},{32,0},{64,32},{96,64},{128,96},{160,128},{192,160},{224,1... | collective-permute-start | bytes 1572872 | tf_op jit(solution)/shard_map/ppermute | solution.py:457
  51.8 2.2 %collective-permute-done.11.refs_7_ = bf16[6,128,128]{2,1,0:T(8,128)(2,1)S(1)} collective-permute-done((bf16[6,128,128]{2,1,0:T(8,128)(2,1)S(1)}, bf16[6,128,128]{2,1,0:T(8,128)(2,1)S(1)}, u32[]{:S(2)}, u32[]{:S(2)}) %collective-permute-start.11) | collective-permute-done | bytes 196640 | tf_op jit(solution)/shard_map/ppermute | solution.py:457
  54.0 0.7 copy-done.7
  54.7 10.4 %attend.4 = (bf16[2048,128]{1,0:T(8,128)(2,1)}, f32[16,1,128]{2,1,0:T(1,128)}) custom-call(s32[3]{0:T(128)} %pad_add_fusion.place, bf16[1024,128]{1,0:T(8,128)(2,1)} %copy-done.11, bf16[1024,128]{1,0:T(8,128)(2,1)} %copy-done.12, bf16[6,128,128]{2,1,0:T(8,128)(2,1)} %copy-done.2, bf16[6,128,128]{2,1,0:T(8,128)(2,1)} %copy-done.3, ...), custom_call_target="tpu_custom_call" | custom-call | flops 2147483648 | bytes 3145728 | tf_op jit(solution)/shard_map/attend/pallas_call | solution.py:219
  65.0 5.2 %collective-permute-start.14 = (bf16[2048,128]{1,0:T(8,128)(2,1)}, bf16[2048,128]{1,0:T(8,128)(2,1)S(1)}, u32[]{:S(2)}, u32[]{:S(2)}) collective-permute-start(bf16[2048,128]{1,0:T(8,128)(2,1)} %get-tuple-element.59), channel_id=1, source_target_pairs={{0,8},{8,0},{1,9},{9,1},{2,10},{10,2},{3,11},{11,3},{4,12},{12,4},... | collective-permute-start | bytes 1572872 | tf_op jit(solution)/shard_map/ppermute | solution.py:453
  70.3 0.3 collective-permute-start.18
  70.6 2.4 %collective-permute-start.20 = (bf16[1024,256]{1,0:T(8,128)(2,1)S(1)}, bf16[1024,256]{1,0:T(8,128)(2,1)S(1)}, u32[]{:S(2)}, u32[]{:S(2)}) collective-permute-start(bf16[1024,256]{1,0:T(8,128)(2,1)S(1)} %collective-permute-done.13.refs_4_), channel_id=1, source_target_pairs={{0,224},{32,0},{64,32},{96,64},{128,96},{160,128},{192,160},{224,1... | collective-permute-start | bytes 1572872 | tf_op jit(solution)/shard_map/ppermute | solution.py:457
  73.0 0.6 collective-permute-start.15
  73.6 10.3 %attend.5 = (bf16[2048,128]{1,0:T(8,128)(2,1)}, f32[16,1,128]{2,1,0:T(1,128)}) custom-call(s32[3]{0:T(128)} %pad_add_fusion.place, bf16[1024,128]{1,0:T(8,128)(2,1)} %bitcast.21, bf16[1024,128]{1,0:T(8,128)(2,1)} %copy-done.10, bf16[6,128,128]{2,1,0:T(8,128)(2,1)} %copy-done.2, bf16[6,128,128]{2,1,0:T(8,128)(2,1)} %copy-done.3, ...), custom_call_target="tpu_custom_call" | custom-call | flops 2147483648 | bytes 3145728 | tf_op jit(solution)/shard_map/attend/pallas_call | solution.py:219
  84.0 0.6 copy-done.15
  84.6 0.2 copy-done.9
  84.8 2.4 %merge.1 = (bf16[2048,128]{1,0:T(8,128)(2,1)}, f32[16,1,128]{2,1,0:T(1,128)}) custom-call(bf16[2048,128]{1,0:T(8,128)(2,1)} %get-tuple-element.57.own, f32[16,1,128]{2,1,0:T(1,128)} %get-tuple-element.58.own_lse, bf16[2048,128]{1,0:T(8,128)(2,1)} %copy-done.9, f32[16,1,128]{2,1,0:T(1,128)} %copy-done.15), custom_call_target="tpu_custom_call" | custom-call | flops 2000000 | bytes 1600000 | tf_op jit(solution)/shard_map/merge/pallas_call | solution.py:279
  87.4 2.7 %collective-permute-start.21 = (bf16[512,256]{1,0:T(8,128)(2,1)S(1)}, bf16[512,256]{1,0:T(8,128)(2,1)}, u32[]{:S(2)}, u32[]{:S(2)}) collective-permute-start(bf16[512,256]{1,0:T(8,128)(2,1)S(1)} %slice.21), channel_id=1, source_target_pairs={{0,224},{32,0},{64,32},{96,64},{128,96},{160,128},{192,160},{224,1... | collective-permute-start | bytes 786440 | tf_op jit(solution)/shard_map/ppermute | solution.py:457
  90.1 1.4 collective-permute-start.17
  91.6 9.6 %collective-permute-done.17.other_lse = f32[16,1,128]{2,1,0:T(1,128)S(1)} collective-permute-done((f32[16,1,128]{2,1,0:T(1,128)}, f32[16,1,128]{2,1,0:T(1,128)S(1)}, u32[]{:S(2)}, u32[]{:S(2)}) %collective-permute-start.17) | collective-permute-done | bytes 8224 | tf_op jit(solution)/shard_map/ppermute | solution.py:453
  101.2 0.5 copy-done.16
  101.8 1.0 copy-done.8
  102.8 2.4 %merge_last.1.near = bf16[2,128,1024]{2,1,0:T(8,128)(2,1)} custom-call(bf16[2048,128]{1,0:T(8,128)(2,1)} %get-tuple-element.60.own, f32[16,1,128]{2,1,0:T(1,128)} %get-tuple-element.61.own_lse, bf16[2048,128]{1,0:T(8,128)(2,1)} %copy-done.8, f32[16,1,128]{2,1,0:T(1,128)} %copy-done.16), custom_call_target="tpu_custom_call" | custom-call | flops 2000000 | bytes 1600000 | tf_op jit(solution)/shard_map/merge_last/pallas_call | solution.py:292
  105.2 0.8 collective-permute-start.22
  106.0 2.5 %collective-permute-done.22.far = bf16[2,128,1024]{2,1,0:T(8,128)(2,1)S(1)} collective-permute-done((bf16[2,128,1024]{2,1,0:T(8,128)(2,1)}, bf16[2,128,1024]{2,1,0:T(8,128)(2,1)S(1)}, u32[]{:S(2)}, u32[]{:S(2)}) %collective-permute-start.22) | collective-permute-done | bytes 524320 | tf_op jit(solution)/shard_map/ppermute | solution.py:453
  108.5 0.9 copy-done.19
  109.3 6.3 %project.1 = bf16[4,8,128,256]{3,2,1,0:T(8,128)(2,1)} custom-call(s32[3]{0:T(128)} %pad_add_fusion.place, bf16[2,128,1024]{2,1,0:T(8,128)(2,1)} %merge_last.1.near, bf16[2,128,1024]{2,1,0:T(8,128)(2,1)} %copy-done.19, bf16[1024,256]{1,0:T(8,128)(2,1)} %refs_0_.1, bf16[1024,256]{1,0:T(8,128)(2,1)} %collective-permute-done.9.refs_1_, ...), custom_call_target="tpu_custom_call" | custom-call | flops 2147483648 | bytes 7000000 | tf_op jit(solution)/shard_map/project/pallas_call | solution.py:325
  115.6 7.5 %all-to-all-start.1 = ((bf16[32,128,256]{2,1,0:T(8,128)(2,1)}), bf16[32,128,256]{2,1,0:T(8,128)(2,1)}, u32[]{:S(2)}, u32[]{:S(2)}) async-start(bf16[32,128,256]{2,1,0:T(8,128)(2,1)} %bitcast.17), calls=%async_computation.1 | async-start | bytes 4194304 | tf_op jit(solution)/shard_map/all_to_all | solution.py:536
  123.1 29.8 %all-to-all-done.1 = bf16[32,128,256]{2,1,0:T(8,128)(2,1)} async-done(((bf16[32,128,256]{2,1,0:T(8,128)(2,1)}), bf16[32,128,256]{2,1,0:T(8,128)(2,1)}, u32[]{:S(2)}, u32[]{:S(2)}) %all-to-all-start.1) | async-done | bytes 2097184 | tf_op jit(solution)/shard_map/all_to_all | solution.py:536
  152.9 6.3 %third.1 = (bf16[128,1024]{1,0:T(8,128)(2,1)}, bf16[8,144,256]{2,1,0:T(8,128)(2,1)}) custom-call(s32[3]{0:T(128)} %pad_add_fusion.place, bf16[4,8,128,256]{3,2,1,0:T(8,128)(2,1)} %bitcast.9.received, bf16[128,1024]{1,0:T(8,128)(2,1)} %hidden.1, f32[1,1024]{1,0:T(1,128)} %bitcast.22, bf16[8,512,256]{2,1,0:T(8,128)(2,1)} %copy-done, ...), custom_call_target="tpu_custom_call" | custom-call | tf_op jit(solution)/shard_map/third/pallas_call | solution.py:387
  159.2 3.5 %all-to-all-start.2 = ((bf16[8,144,256]{2,1,0:T(8,128)(2,1)}), bf16[8,144,256]{2,1,0:T(8,128)(2,1)S(1)}, u32[]{:S(2)}, u32[]{:S(2)}) async-start(bf16[8,144,256]{2,1,0:T(8,128)(2,1)} %get-tuple-element.67), calls=%async_computation.2 | async-start | bytes 1179648 | tf_op jit(solution)/shard_map/all_to_all | solution.py:542
  163.4 10.3 %all-to-all-done.2.partial = bf16[8,144,256]{2,1,0:T(8,128)(2,1)S(1)} async-done(((bf16[8,144,256]{2,1,0:T(8,128)(2,1)}), bf16[8,144,256]{2,1,0:T(8,128)(2,1)S(1)}, u32[]{:S(2)}, u32[]{:S(2)}) %all-to-all-start.2) | async-done | bytes 589856 | tf_op jit(solution)/shard_map/all_to_all | solution.py:542
  173.7 0.8 copy-done.1
  174.6 2.1 %final.1 = bf16[128,256]{1,0:T(8,128)(2,1)} custom-call(s32[1]{0:T(128)S(6)} %copy.13.count, bf16[8,144,256]{2,1,0:T(8,128)(2,1)} %copy-done.1, f32[1,256]{1,0:T(1,128)} %bitcast.23, f32[128,128]{1,0:T(8,128)} %get-tuple-element.74.cosine, f32[128,128]{1,0:T(8,128)} %get-tuple-element.75.sine, s32[1,128]{1,0:T(1,128)} %bitcast.24), custom_call_target="tpu_custom_call" | custom-call | tf_op jit(solution)/shard_map/final/pallas_call | solution.py:442
  (70 shorter events, 0.6 us)
Async XLA Ops:
  4.5 14.1 %collective-permute-start.2 = (bf16[1024,128]{1,0:T(8,128)(2,1)}, bf16[1024,128]{1,0:T(8,128)(2,1)S(1)}, u32[]{:S(2)}, u32[]{:S(2)}) collective-permute-start(bf16[1024,128]{1,0:T(8,128)(2,1)} %bitcast.18), channel_id=1, source_target_pairs={{0,16},{16,0},{1,17},{17,1},{2,18},{18,2},{3,19},{19,3},{4,20},{20... | collective-permute-start | bytes 786440 | tf_op jit(solution)/shard_map/ppermute | solution.py:453
  6.6 12.0 %collective-permute-start = (bf16[6,128,128]{2,1,0:T(8,128)(2,1)}, bf16[6,128,128]{2,1,0:T(8,128)(2,1)S(1)}, u32[]{:S(2)}, u32[]{:S(2)}) collective-permute-start(bf16[6,128,128]{2,1,0:T(8,128)(2,1)} %get-tuple-element.36.refs_4_), channel_id=1, source_target_pairs={{0,32},{32,64},{64,96},{96,128},{128,160},{160,192},{192,224},{224... | collective-permute-start | bytes 589832 | tf_op jit(solution)/shard_map/ppermute | solution.py:457
  8.2 10.3 %collective-permute-start.1 = (bf16[6,128,128]{2,1,0:T(8,128)(2,1)}, bf16[6,128,128]{2,1,0:T(8,128)(2,1)S(1)}, u32[]{:S(2)}, u32[]{:S(2)}) collective-permute-start(bf16[6,128,128]{2,1,0:T(8,128)(2,1)} %get-tuple-element.36.refs_4_), channel_id=1, source_target_pairs={{0,224},{32,0},{64,32},{96,64},{128,96},{160,128},{192,160},{224,1... | collective-permute-start | bytes 589832 | tf_op jit(solution)/shard_map/ppermute | solution.py:457
  12.2 15.2 %collective-permute-start.3 = (bf16[1024,128]{1,0:T(8,128)(2,1)}, bf16[1024,128]{1,0:T(8,128)(2,1)S(1)}, u32[]{:S(2)}, u32[]{:S(2)}) collective-permute-start(bf16[1024,128]{1,0:T(8,128)(2,1)} %bitcast.19), channel_id=1, source_target_pairs={{0,8},{8,0},{1,9},{9,1},{2,10},{10,2},{3,11},{11,3},{4,12},{12,4},... | collective-permute-start | bytes 786440 | tf_op jit(solution)/shard_map/ppermute | solution.py:453
  18.6 2.5 %copy-start.21 = (bf16[6,128,128]{2,1,0:T(8,128)(2,1)}, bf16[6,128,128]{2,1,0:T(8,128)(2,1)S(1)}, u32[]{:S(2)}) copy-start(bf16[6,128,128]{2,1,0:T(8,128)(2,1)S(1)} %collective-permute-done.refs_5_) | copy-start | bytes 589828
  18.6 8.9 %copy-start.2 = (bf16[6,128,128]{2,1,0:T(8,128)(2,1)}, bf16[6,128,128]{2,1,0:T(8,128)(2,1)S(1)}, u32[]{:S(2)}) copy-start(bf16[6,128,128]{2,1,0:T(8,128)(2,1)S(1)} %collective-permute-done.1.refs_6_.refs_2_) | copy-start | bytes 589828
  18.6 2.5 %copy-start.10 = (bf16[1024,128]{1,0:T(8,128)(2,1)}, bf16[1024,128]{1,0:T(8,128)(2,1)S(1)}, u32[]{:S(2)}) copy-start(bf16[1024,128]{1,0:T(8,128)(2,1)S(1)} %collective-permute-done.2.refs_1_) | copy-start | bytes 786436
  18.6 11.6 %collective-permute-start.4 = (bf16[1024,128]{1,0:T(8,128)(2,1)S(1)}, bf16[1024,128]{1,0:T(8,128)(2,1)S(1)}, u32[]{:S(2)}, u32[]{:S(2)}) collective-permute-start(bf16[1024,128]{1,0:T(8,128)(2,1)S(1)} %collective-permute-done.2.refs_1_), channel_id=1, source_target_pairs={{0,8},{8,0},{1,9},{9,1},{2,10},{10,2},{3,11},{11,3},{4,12},{12,4},... | collective-permute-start | bytes 786440 | tf_op jit(solution)/shard_map/ppermute | solution.py:453
  18.7 29.2 %collective-permute-start.10 = (bf16[1024,256]{1,0:T(8,128)(2,1)}, bf16[1024,256]{1,0:T(8,128)(2,1)}, u32[]{:S(2)}, u32[]{:S(2)}) collective-permute-start(bf16[1024,256]{1,0:T(8,128)(2,1)} %refs_0_.1), channel_id=1, source_target_pairs={{0,224},{32,0},{64,32},{96,64},{128,96},{160,128},{192,160},{224,1... | collective-permute-start | bytes 1572872 | tf_op jit(solution)/shard_map/ppermute | solution.py:457
  21.0 26.8 %collective-permute-start.9 = (bf16[1024,256]{1,0:T(8,128)(2,1)}, bf16[1024,256]{1,0:T(8,128)(2,1)}, u32[]{:S(2)}, u32[]{:S(2)}) collective-permute-start(bf16[1024,256]{1,0:T(8,128)(2,1)} %refs_0_.1), channel_id=1, source_target_pairs={{0,32},{32,64},{64,96},{96,128},{128,160},{160,192},{192,224},{224... | collective-permute-start | bytes 1572872 | tf_op jit(solution)/shard_map/ppermute | solution.py:457
  21.0 20.2 %collective-permute-start.5 = (bf16[6,128,128]{2,1,0:T(8,128)(2,1)S(1)}, bf16[6,128,128]{2,1,0:T(8,128)(2,1)S(1)}, u32[]{:S(2)}, u32[]{:S(2)}) collective-permute-start(bf16[6,128,128]{2,1,0:T(8,128)(2,1)S(1)} %collective-permute-done.refs_5_), channel_id=1, source_target_pairs={{0,32},{32,64},{64,96},{96,128},{128,160},{160,192},{192,224},{224... | collective-permute-start | bytes 589832 | tf_op jit(solution)/shard_map/ppermute | solution.py:457
  21.0 80.2 %all-to-all-start = ((bf16[8,512,256]{2,1,0:T(8,128)(2,1)}), bf16[8,512,256]{2,1,0:T(8,128)(2,1)S(1)}, u32[]{:S(2)}, u32[]{:S(2)}) async-start(bf16[8,512,256]{2,1,0:T(8,128)(2,1)} %half.1), calls=%async_computation | async-start | bytes 4194304 | tf_op jit(solution)/shard_map/all_to_all | solution.py:507
  27.4 2.8 %copy-start.11 = (bf16[1024,128]{1,0:T(8,128)(2,1)}, bf16[1024,128]{1,0:T(8,128)(2,1)S(1)}, u32[]{:S(2)}) copy-start(bf16[1024,128]{1,0:T(8,128)(2,1)S(1)} %collective-permute-done.3.refs_2_.refs_0_) | copy-start | bytes 786436
  27.4 13.8 %collective-permute-start.6 = (bf16[6,128,128]{2,1,0:T(8,128)(2,1)S(1)}, bf16[6,128,128]{2,1,0:T(8,128)(2,1)S(1)}, u32[]{:S(2)}, u32[]{:S(2)}) collective-permute-start(bf16[6,128,128]{2,1,0:T(8,128)(2,1)S(1)} %collective-permute-done.1.refs_6_.refs_2_), channel_id=1, source_target_pairs={{0,224},{32,0},{64,32},{96,64},{128,96},{160,128},{192,160},{224,1... | collective-permute-start | bytes 589832 | tf_op jit(solution)/shard_map/ppermute | solution.py:457
  30.2 0.7 copy-start.12
  41.2 12.7 %copy-start.3 = (bf16[6,128,128]{2,1,0:T(8,128)(2,1)}, bf16[6,128,128]{2,1,0:T(8,128)(2,1)S(1)}, u32[]{:S(2)}) copy-start(bf16[6,128,128]{2,1,0:T(8,128)(2,1)S(1)} %collective-permute-done.5.refs_3_) | copy-start | bytes 589828
  41.3 12.7 %copy-start.4 = (bf16[6,128,128]{2,1,0:T(8,128)(2,1)}, bf16[6,128,128]{2,1,0:T(8,128)(2,1)S(1)}, u32[]{:S(2)}) copy-start(bf16[6,128,128]{2,1,0:T(8,128)(2,1)S(1)} %collective-permute-done.6.refs_4_) | copy-start | bytes 589828
  41.3 6.5 %collective-permute-start.7 = (bf16[6,128,128]{2,1,0:T(8,128)(2,1)S(1)}, bf16[6,128,128]{2,1,0:T(8,128)(2,1)S(1)}, u32[]{:S(2)}, u32[]{:S(2)}) collective-permute-start(bf16[6,128,128]{2,1,0:T(8,128)(2,1)S(1)} %collective-permute-done.5.refs_3_), channel_id=1, source_target_pairs={{0,32},{32,64},{64,96},{96,128},{128,160},{160,192},{192,224},{224... | collective-permute-start | bytes 589832 | tf_op jit(solution)/shard_map/ppermute | solution.py:457
  41.4 6.4 %collective-permute-start.8 = (bf16[6,128,128]{2,1,0:T(8,128)(2,1)S(1)}, bf16[6,128,128]{2,1,0:T(8,128)(2,1)S(1)}, u32[]{:S(2)}, u32[]{:S(2)}) collective-permute-start(bf16[6,128,128]{2,1,0:T(8,128)(2,1)S(1)} %collective-permute-done.6.refs_4_), channel_id=1, source_target_pairs={{0,224},{32,0},{64,32},{96,64},{128,96},{160,128},{192,160},{224,1... | collective-permute-start | bytes 589832 | tf_op jit(solution)/shard_map/ppermute | solution.py:457
  47.8 6.2 %copy-start.5 = (bf16[6,128,128]{2,1,0:T(8,128)(2,1)}, bf16[6,128,128]{2,1,0:T(8,128)(2,1)S(1)}, u32[]{:S(2)}) copy-start(bf16[6,128,128]{2,1,0:T(8,128)(2,1)S(1)} %collective-permute-done.7.refs_5_) | copy-start | bytes 589828
  47.8 6.1 %copy-start.6 = (bf16[6,128,128]{2,1,0:T(8,128)(2,1)}, bf16[6,128,128]{2,1,0:T(8,128)(2,1)S(1)}, u32[]{:S(2)}) copy-start(bf16[6,128,128]{2,1,0:T(8,128)(2,1)S(1)} %collective-permute-done.8.refs_6_) | copy-start | bytes 589828
  47.9 6.1 %collective-permute-start.11 = (bf16[6,128,128]{2,1,0:T(8,128)(2,1)S(1)}, bf16[6,128,128]{2,1,0:T(8,128)(2,1)S(1)}, u32[]{:S(2)}, u32[]{:S(2)}) collective-permute-start(bf16[6,128,128]{2,1,0:T(8,128)(2,1)S(1)} %collective-permute-done.7.refs_5_), channel_id=1, source_target_pairs={{0,32},{32,64},{64,96},{96,128},{128,160},{160,192},{192,224},{224... | collective-permute-start | bytes 589832 | tf_op jit(solution)/shard_map/ppermute | solution.py:457
  49.1 21.1 %collective-permute-start.12 = (bf16[1024,256]{1,0:T(8,128)(2,1)}, bf16[1024,256]{1,0:T(8,128)(2,1)S(1)}, u32[]{:S(2)}, u32[]{:S(2)}) collective-permute-start(bf16[1024,256]{1,0:T(8,128)(2,1)} %collective-permute-done.9.refs_1_), channel_id=1, source_target_pairs={{0,32},{32,64},{64,96},{96,128},{128,160},{160,192},{192,224},{224... | collective-permute-start | bytes 1572872 | tf_op jit(solution)/shard_map/ppermute | solution.py:457
  49.9 20.4 %collective-permute-start.13 = (bf16[1024,256]{1,0:T(8,128)(2,1)}, bf16[1024,256]{1,0:T(8,128)(2,1)S(1)}, u32[]{:S(2)}, u32[]{:S(2)}) collective-permute-start(bf16[1024,256]{1,0:T(8,128)(2,1)} %collective-permute-done.10.refs_2_), channel_id=1, source_target_pairs={{0,224},{32,0},{64,32},{96,64},{128,96},{160,128},{192,160},{224,1... | collective-permute-start | bytes 1572872 | tf_op jit(solution)/shard_map/ppermute | solution.py:457
  54.0 0.7 copy-start.7
  65.0 19.0 %collective-permute-start.14 = (bf16[2048,128]{1,0:T(8,128)(2,1)}, bf16[2048,128]{1,0:T(8,128)(2,1)S(1)}, u32[]{:S(2)}, u32[]{:S(2)}) collective-permute-start(bf16[2048,128]{1,0:T(8,128)(2,1)} %get-tuple-element.59), channel_id=1, source_target_pairs={{0,8},{8,0},{1,9},{9,1},{2,10},{10,2},{3,11},{11,3},{4,12},{12,4},... | collective-permute-start | bytes 1572872 | tf_op jit(solution)/shard_map/ppermute | solution.py:453
  70.3 13.7 %copy-start.17 = (bf16[1024,256]{1,0:T(8,128)(2,1)}, bf16[1024,256]{1,0:T(8,128)(2,1)S(1)}, u32[]{:S(2)}) copy-start(bf16[1024,256]{1,0:T(8,128)(2,1)S(1)} %collective-permute-done.12.refs_3_) | copy-start | bytes 1572868
  70.3 13.7 %copy-start.18 = (bf16[1024,256]{1,0:T(8,128)(2,1)}, bf16[1024,256]{1,0:T(8,128)(2,1)S(1)}, u32[]{:S(2)}) copy-start(bf16[1024,256]{1,0:T(8,128)(2,1)S(1)} %collective-permute-done.13.refs_4_) | copy-start | bytes 1572868
  70.3 17.0 %collective-permute-start.18 = (bf16[1024,256]{1,0:T(8,128)(2,1)S(1)}, bf16[1024,256]{1,0:T(8,128)(2,1)S(1)}, u32[]{:S(2)}, u32[]{:S(2)}) collective-permute-start(bf16[1024,256]{1,0:T(8,128)(2,1)S(1)} %collective-permute-done.12.refs_3_), channel_id=1, source_target_pairs={{0,32},{32,64},{64,96},{96,128},{128,160},{160,192},{192,224},{224... | collective-permute-start | bytes 1572872 | tf_op jit(solution)/shard_map/ppermute | solution.py:457
  70.6 16.8 %collective-permute-start.20 = (bf16[1024,256]{1,0:T(8,128)(2,1)S(1)}, bf16[1024,256]{1,0:T(8,128)(2,1)S(1)}, u32[]{:S(2)}, u32[]{:S(2)}) collective-permute-start(bf16[1024,256]{1,0:T(8,128)(2,1)S(1)} %collective-permute-done.13.refs_4_), channel_id=1, source_target_pairs={{0,224},{32,0},{64,32},{96,64},{128,96},{160,128},{192,160},{224,1... | collective-permute-start | bytes 1572872 | tf_op jit(solution)/shard_map/ppermute | solution.py:457
  73.0 10.9 %collective-permute-start.15 = (f32[16,1,128]{2,1,0:T(1,128)}, f32[16,1,128]{2,1,0:T(1,128)S(1)}, u32[]{:S(2)}, u32[]{:S(2)}) collective-permute-start(f32[16,1,128]{2,1,0:T(1,128)} %get-tuple-element.52), channel_id=1, source_target_pairs={{0,8},{8,0},{1,9},{9,1},{2,10},{10,2},{3,11},{11,3},{4,12},{12,4},... | collective-permute-start | bytes 24584 | tf_op jit(solution)/shard_map/ppermute | solution.py:453
  84.0 0.6 copy-start.15
  84.0 0.8 copy-start.9
  87.2 14.0 %collective-permute-start.16 = (bf16[2048,128]{1,0:T(8,128)(2,1)}, bf16[2048,128]{1,0:T(8,128)(2,1)S(1)}, u32[]{:S(2)}, u32[]{:S(2)}) collective-permute-start(bf16[2048,128]{1,0:T(8,128)(2,1)} %get-tuple-element.60.own), channel_id=1, source_target_pairs={{0,16},{16,0},{1,17},{17,1},{2,18},{18,2},{3,19},{19,3},{4,20},{20... | collective-permute-start | bytes 1572872 | tf_op jit(solution)/shard_map/ppermute | solution.py:453
  87.2 21.2 %copy-start.13 = (bf16[1024,256]{1,0:T(8,128)(2,1)}, bf16[1024,256]{1,0:T(8,128)(2,1)S(1)}, u32[]{:S(2)}) copy-start(bf16[1024,256]{1,0:T(8,128)(2,1)S(1)} %collective-permute-done.18.refs_5_) | copy-start | bytes 1572868
  87.3 13.9 %collective-permute-start.19 = (bf16[512,256]{1,0:T(8,128)(2,1)S(1)}, bf16[512,256]{1,0:T(8,128)(2,1)S(1)}, u32[]{:S(2)}, u32[]{:S(2)}) collective-permute-start(bf16[512,256]{1,0:T(8,128)(2,1)S(1)} %slice.20), channel_id=1, source_target_pairs={{0,32},{32,64},{64,96},{96,128},{128,160},{160,192},{192,224},{224... | collective-permute-start | bytes 786440 | tf_op jit(solution)/shard_map/ppermute | solution.py:457
  87.4 13.8 %copy-start.14 = (bf16[1024,256]{1,0:T(8,128)(2,1)}, bf16[1024,256]{1,0:T(8,128)(2,1)S(1)}, u32[]{:S(2)}) copy-start(bf16[1024,256]{1,0:T(8,128)(2,1)S(1)} %collective-permute-done.20.refs_6_) | copy-start | bytes 1572868
  87.4 13.8 %collective-permute-start.21 = (bf16[512,256]{1,0:T(8,128)(2,1)S(1)}, bf16[512,256]{1,0:T(8,128)(2,1)}, u32[]{:S(2)}, u32[]{:S(2)}) collective-permute-start(bf16[512,256]{1,0:T(8,128)(2,1)S(1)} %slice.21), channel_id=1, source_target_pairs={{0,224},{32,0},{64,32},{96,64},{128,96},{160,128},{192,160},{224,1... | collective-permute-start | bytes 786440 | tf_op jit(solution)/shard_map/ppermute | solution.py:457
  90.1 11.0 %collective-permute-start.17 = (f32[16,1,128]{2,1,0:T(1,128)}, f32[16,1,128]{2,1,0:T(1,128)S(1)}, u32[]{:S(2)}, u32[]{:S(2)}) collective-permute-start(f32[16,1,128]{2,1,0:T(1,128)} %get-tuple-element.61.own_lse), channel_id=1, source_target_pairs={{0,16},{16,0},{1,17},{17,1},{2,18},{18,2},{3,19},{19,3},{4,20},{20... | collective-permute-start | bytes 24584 | tf_op jit(solution)/shard_map/ppermute | solution.py:453
  101.2 7.3 %copy-start.20 = (bf16[512,256]{1,0:T(8,128)(2,1)}, bf16[512,256]{1,0:T(8,128)(2,1)S(1)}, u32[]{:S(2)}) copy-start(bf16[512,256]{1,0:T(8,128)(2,1)S(1)} %collective-permute-done.19.refs_7_) | copy-start | bytes 786436
  101.2 14.4 %copy-start = (bf16[8,512,256]{2,1,0:T(8,128)(2,1)}, bf16[8,512,256]{2,1,0:T(8,128)(2,1)S(1)}, u32[]{:S(2)}) copy-start(bf16[8,512,256]{2,1,0:T(8,128)(2,1)S(1)} %all-to-all-done.near) | copy-start | bytes 6291460
  101.8 1.0 copy-start.8
  105.2 3.2 %collective-permute-start.22 = (bf16[2,128,1024]{2,1,0:T(8,128)(2,1)}, bf16[2,128,1024]{2,1,0:T(8,128)(2,1)S(1)}, u32[]{:S(2)}, u32[]{:S(2)}) collective-permute-start(bf16[2,128,1024]{2,1,0:T(8,128)(2,1)} %merge_last.1.near), channel_id=1, source_target_pairs={{0,8},{8,0},{1,9},{9,1},{2,10},{10,2},{3,11},{11,3},{4,12},{12,4},... | collective-permute-start | bytes 1572872 | tf_op jit(solution)/shard_map/ppermute | solution.py:453
  106.0 17.1 %collective-permute-start.23 = (bf16[8,512,256]{2,1,0:T(8,128)(2,1)S(1)}, bf16[8,512,256]{2,1,0:T(8,128)(2,1)}, u32[]{:S(2)}, u32[]{:S(2)}) collective-permute-start(bf16[8,512,256]{2,1,0:T(8,128)(2,1)S(1)} %all-to-all-done.near), channel_id=1, source_target_pairs={{0,8},{8,0},{1,9},{9,1},{2,10},{10,2},{3,11},{11,3},{4,12},{12,4},... | collective-permute-start | bytes 6291464 | tf_op jit(solution)/shard_map/ppermute | solution.py:453
  108.5 0.9 copy-start.19
  115.6 37.3 %all-to-all-start.1 = ((bf16[32,128,256]{2,1,0:T(8,128)(2,1)}), bf16[32,128,256]{2,1,0:T(8,128)(2,1)}, u32[]{:S(2)}, u32[]{:S(2)}) async-start(bf16[32,128,256]{2,1,0:T(8,128)(2,1)} %bitcast.17), calls=%async_computation.1 | async-start | bytes 4194304 | tf_op jit(solution)/shard_map/all_to_all | solution.py:536
  159.2 14.5 %all-to-all-start.2 = ((bf16[8,144,256]{2,1,0:T(8,128)(2,1)}), bf16[8,144,256]{2,1,0:T(8,128)(2,1)S(1)}, u32[]{:S(2)}, u32[]{:S(2)}) async-start(bf16[8,144,256]{2,1,0:T(8,128)(2,1)} %get-tuple-element.67), calls=%async_computation.2 | async-start | bytes 1179648 | tf_op jit(solution)/shard_map/all_to_all | solution.py:542
  173.7 0.8 copy-start.1
  (1 other events, 0.6 us)

commit v9 on v7

--- a/solution.py
+++ b/solution.py
@@ -492,7 +492,7 @@
     near_query, _, weights_2 = lax.optimization_barrier((near_query, send_lse, weights_2))
     weights_3 = step(weights_2)
     own, own_lse = attend(
-        512, place, near_query, 0, late, late_cached, late_fresh, state, 0, True
+        1024, place, near_query, 0, late, late_cached, late_fresh, state, 0, True
     )
     own, own_lse = merge(own, own_lse, got, got_lse)
     got, got_lse = swap(own, "yl"), swap(own_lse, "yl")

time: 176 us -> 175 us (level)
  no operation moved by 1% of the time
where the time goes in v9:
time: 175 us
  waiting for transfers between devices  58.2 us (33%)
  Pallas kernels  55.3 us (32%)
  starting transfers between devices  51.8 us (30%)
  local copies, waits for them, and re-layouts  5.5 us (3%)
  other arithmetic  2.47 us (1%)
    pallas_call x3, Pallas kernels, attend(): pl.pallas_call(functools.partial(attend_kernel, chunk, cached, fresh, len...  30.6 us
    all_to_all x1, waiting for transfers between devices, local(): lax.all_to_all(products, ('yl', 'c', 'x', 'yh'), 0, 0, tiled=True)  29.8 us
    ppermute x15, starting transfers between devices, along_z(): return lax.ppermute(x, 'z', [(i, (i + distance) % Z) for i in range(Z)])  22.9 us
    ppermute x9, waiting for transfers between devices, swap(): return lax.ppermute(x, axis, [(0, 1), (1, 0)])  12.1 us
    ppermute x9, starting transfers between devices, swap(): return lax.ppermute(x, axis, [(0, 1), (1, 0)])  11.5 us
    all_to_all x1, waiting for transfers between devices, local(): partial = lax.all_to_all(partial, HEAD_AXES, 0, 0, tiled=True)  10.3 us
    all_to_all x1, starting transfers between devices, local(): lax.all_to_all(products, ('yl', 'c', 'x', 'yh'), 0, 0, tiled=True)  7.5 us
    all_to_all x1, starting transfers between devices, local(): third_near = lax.all_to_all(third_rows, HEAD_AXES, 0, 0, tiled=True)  6.37 us
  transfers between devices with their start and end apart: 27, of which 7 were waited for; matrix products, arithmetic and copies ran while one was open for 0% of the time, Pallas kernels for 25%

profile of v9, /device:TPU:1, one launch (start us, length us, event | category | flops | bytes accessed | tf_op | source)
XLA Modules:
  0.0 174.9 jit_solution(3813783749172734646)
XLA Ops:
  0.7 0.7 convert_element_type.36
  1.4 0.3 fusion.2
  1.7 0.8 pad_maximum_fusion
  2.5 2.0 %prepare.1 = (bf16[8,128,128]{2,1,0:T(8,128)(2,1)}, bf16[6,128,128]{2,1,0:T(8,128)(2,1)}) custom-call(bf16[128,1024]{1,0:T(8,128)(2,1)} %query.1, bf16[2,128,128]{2,1,0:T(8,128)(2,1)} %fresh.1, bf16[2,256,128]{2,1,0:T(8,128)(2,1)} %cached.1, f32[128,128]{1,0:T(8,128)} %get-tuple-element.74.cosine, f32[128,128]{1,0:T(8,128)} %get-tuple-element.75.sine), custom_call_target="tpu_custom_call" | custom-call | flops 2000000 | bytes 1500000 | tf_op jit(solution)/shard_map/prepare/pallas_call | solution.py:69
  4.5 2.1 %collective-permute-start.2 = (bf16[1024,128]{1,0:T(8,128)(2,1)}, bf16[1024,128]{1,0:T(8,128)(2,1)S(1)}, u32[]{:S(2)}, u32[]{:S(2)}) collective-permute-start(bf16[1024,128]{1,0:T(8,128)(2,1)} %bitcast.18), channel_id=1, source_target_pairs={{0,16},{16,0},{1,17},{17,1},{2,18},{18,2},{3,19},{19,3},{4,20},{20... | collective-permute-start | bytes 786440 | tf_op jit(solution)/shard_map/ppermute | solution.py:425
  6.6 1.6 collective-permute-start
  8.2 3.9 %collective-permute-start.1 = (bf16[6,128,128]{2,1,0:T(8,128)(2,1)}, bf16[6,128,128]{2,1,0:T(8,128)(2,1)S(1)}, u32[]{:S(2)}, u32[]{:S(2)}) collective-permute-start(bf16[6,128,128]{2,1,0:T(8,128)(2,1)} %get-tuple-element.36.refs_4_), channel_id=1, source_target_pairs={{0,224},{32,0},{64,32},{96,64},{128,96},{160,128},{192,160},{224,1... | collective-permute-start | bytes 589832 | tf_op jit(solution)/shard_map/ppermute | solution.py:429
  12.2 1.2 collective-permute-start.3
  13.4 0.7 pad_add_fusion.place
  14.1 4.5 %half.1 = bf16[8,512,256]{2,1,0:T(8,128)(2,1)} custom-call(s32[3]{0:T(128)} %pad_add_fusion.place, bf16[8,2,512,256]{3,2,1,0:T(8,128)(2,1)} %bitcast.16), custom_call_target="tpu_custom_call" | custom-call | bytes 8000000 | tf_op jit(solution)/shard_map/half/pallas_call | solution.py:87
  18.7 2.3 %collective-permute-start.10 = (bf16[1024,256]{1,0:T(8,128)(2,1)}, bf16[1024,256]{1,0:T(8,128)(2,1)}, u32[]{:S(2)}, u32[]{:S(2)}) collective-permute-start(bf16[1024,256]{1,0:T(8,128)(2,1)} %refs_0_.1), channel_id=1, source_target_pairs={{0,224},{32,0},{64,32},{96,64},{128,96},{160,128},{192,160},{224,1... | collective-permute-start | bytes 1572872 | tf_op jit(solution)/shard_map/ppermute | solution.py:429
  21.0 6.4 %all-to-all-start = ((bf16[8,512,256]{2,1,0:T(8,128)(2,1)}), bf16[8,512,256]{2,1,0:T(8,128)(2,1)S(1)}, u32[]{:S(2)}, u32[]{:S(2)}) async-start(bf16[8,512,256]{2,1,0:T(8,128)(2,1)} %half.1), calls=%async_computation | async-start | bytes 4194304 | tf_op jit(solution)/shard_map/all_to_all | solution.py:479
  27.4 2.8 %collective-permute-start.6 = (bf16[6,128,128]{2,1,0:T(8,128)(2,1)S(1)}, bf16[6,128,128]{2,1,0:T(8,128)(2,1)S(1)}, u32[]{:S(2)}, u32[]{:S(2)}) collective-permute-start(bf16[6,128,128]{2,1,0:T(8,128)(2,1)S(1)} %collective-permute-done.1.refs_6_.refs_2_), channel_id=1, source_target_pairs={{0,224},{32,0},{64,32},{96,64},{128,96},{160,128},{192,160},{224,1... | collective-permute-start | bytes 589832 | tf_op jit(solution)/shard_map/ppermute | solution.py:429
  30.2 0.7 copy-done.12
  30.9 10.3 %attend.3 = (f32[4096,256]{1,0:T(8,128)}, f32[4096,128]{1,0:T(8,128)}) custom-call(s32[3]{0:T(128)} %pad_add_fusion.place, bf16[1024,128]{1,0:T(8,128)(2,1)} %bitcast.20, bf16[1024,128]{1,0:T(8,128)(2,1)} %copy-done.10, bf16[1024,128]{1,0:T(8,128)(2,1)} %copy-done.11, bf16[1024,128]{1,0:T(8,128)(2,1)} %copy-done.12, ...), custom_call_target="tpu_custom_call" | custom-call | flops 2147483648 | bytes 4718592 | tf_op jit(solution)/shard_map/attend/pallas_call | solution.py:219
  41.4 2.6 %collective-permute-start.8 = (bf16[6,128,128]{2,1,0:T(8,128)(2,1)S(1)}, bf16[6,128,128]{2,1,0:T(8,128)(2,1)S(1)}, u32[]{:S(2)}, u32[]{:S(2)}) collective-permute-start(bf16[6,128,128]{2,1,0:T(8,128)(2,1)S(1)} %collective-permute-done.6.refs_4_), channel_id=1, source_target_pairs={{0,224},{32,0},{64,32},{96,64},{128,96},{160,128},{192,160},{224,1... | collective-permute-start | bytes 589832 | tf_op jit(solution)/shard_map/ppermute | solution.py:429
  44.0 3.7 %collective-permute-done.7.refs_5_ = bf16[6,128,128]{2,1,0:T(8,128)(2,1)S(1)} collective-permute-done((bf16[6,128,128]{2,1,0:T(8,128)(2,1)S(1)}, bf16[6,128,128]{2,1,0:T(8,128)(2,1)S(1)}, u32[]{:S(2)}, u32[]{:S(2)}) %collective-permute-start.7) | collective-permute-done | bytes 196640 | tf_op jit(solution)/shard_map/ppermute | solution.py:429
  47.9 1.3 collective-permute-start.11
  49.1 0.8 collective-permute-start.12
  49.9 1.9 %collective-permute-start.13 = (bf16[1024,256]{1,0:T(8,128)(2,1)}, bf16[1024,256]{1,0:T(8,128)(2,1)S(1)}, u32[]{:S(2)}, u32[]{:S(2)}) collective-permute-start(bf16[1024,256]{1,0:T(8,128)(2,1)} %collective-permute-done.10.refs_2_), channel_id=1, source_target_pairs={{0,224},{32,0},{64,32},{96,64},{128,96},{160,128},{192,160},{224,1... | collective-permute-start | bytes 1572872 | tf_op jit(solution)/shard_map/ppermute | solution.py:429
  51.8 2.2 %collective-permute-done.11.refs_7_ = bf16[6,128,128]{2,1,0:T(8,128)(2,1)S(1)} collective-permute-done((bf16[6,128,128]{2,1,0:T(8,128)(2,1)S(1)}, bf16[6,128,128]{2,1,0:T(8,128)(2,1)S(1)}, u32[]{:S(2)}, u32[]{:S(2)}) %collective-permute-start.11) | collective-permute-done | bytes 196640 | tf_op jit(solution)/shard_map/ppermute | solution.py:429
  54.0 0.7 copy-done.7
  54.7 10.4 %attend.4 = (bf16[2048,128]{1,0:T(8,128)(2,1)}, f32[16,1,128]{2,1,0:T(1,128)}) custom-call(s32[3]{0:T(128)} %pad_add_fusion.place, bf16[1024,128]{1,0:T(8,128)(2,1)} %copy-done.11, bf16[1024,128]{1,0:T(8,128)(2,1)} %copy-done.12, bf16[6,128,128]{2,1,0:T(8,128)(2,1)} %copy-done.2, bf16[6,128,128]{2,1,0:T(8,128)(2,1)} %copy-done.3, ...), custom_call_target="tpu_custom_call" | custom-call | flops 2147483648 | bytes 3145728 | tf_op jit(solution)/shard_map/attend/pallas_call | solution.py:219
  65.0 5.2 %collective-permute-start.14 = (bf16[2048,128]{1,0:T(8,128)(2,1)}, bf16[2048,128]{1,0:T(8,128)(2,1)S(1)}, u32[]{:S(2)}, u32[]{:S(2)}) collective-permute-start(bf16[2048,128]{1,0:T(8,128)(2,1)} %get-tuple-element.59), channel_id=1, source_target_pairs={{0,8},{8,0},{1,9},{9,1},{2,10},{10,2},{3,11},{11,3},{4,12},{12,4},... | collective-permute-start | bytes 1572872 | tf_op jit(solution)/shard_map/ppermute | solution.py:425
  70.3 0.3 collective-permute-start.18
  70.6 2.4 %collective-permute-start.20 = (bf16[1024,256]{1,0:T(8,128)(2,1)S(1)}, bf16[1024,256]{1,0:T(8,128)(2,1)S(1)}, u32[]{:S(2)}, u32[]{:S(2)}) collective-permute-start(bf16[1024,256]{1,0:T(8,128)(2,1)S(1)} %collective-permute-done.13.refs_4_), channel_id=1, source_target_pairs={{0,224},{32,0},{64,32},{96,64},{128,96},{160,128},{192,160},{224,1... | collective-permute-start | bytes 1572872 | tf_op jit(solution)/shard_map/ppermute | solution.py:429
  73.0 0.6 collective-permute-start.15
  73.6 9.9 %attend.5 = (bf16[2048,128]{1,0:T(8,128)(2,1)}, f32[16,1,128]{2,1,0:T(1,128)}) custom-call(s32[3]{0:T(128)} %pad_add_fusion.place, bf16[1024,128]{1,0:T(8,128)(2,1)} %bitcast.21, bf16[1024,128]{1,0:T(8,128)(2,1)} %copy-done.10, bf16[6,128,128]{2,1,0:T(8,128)(2,1)} %copy-done.2, bf16[6,128,128]{2,1,0:T(8,128)(2,1)} %copy-done.3, ...), custom_call_target="tpu_custom_call" | custom-call | flops 2147483648 | bytes 3145728 | tf_op jit(solution)/shard_map/attend/pallas_call | solution.py:219
  83.6 0.6 copy-done.15
  84.2 0.2 copy-done.9
  84.4 2.4 %merge.1 = (bf16[2048,128]{1,0:T(8,128)(2,1)}, f32[16,1,128]{2,1,0:T(1,128)}) custom-call(bf16[2048,128]{1,0:T(8,128)(2,1)} %get-tuple-element.57.own, f32[16,1,128]{2,1,0:T(1,128)} %get-tuple-element.58.own_lse, bf16[2048,128]{1,0:T(8,128)(2,1)} %copy-done.9, f32[16,1,128]{2,1,0:T(1,128)} %copy-done.15), custom_call_target="tpu_custom_call" | custom-call | flops 2000000 | bytes 1600000 | tf_op jit(solution)/shard_map/merge/pallas_call | solution.py:279
  87.0 2.7 %collective-permute-start.21 = (bf16[512,256]{1,0:T(8,128)(2,1)S(1)}, bf16[512,256]{1,0:T(8,128)(2,1)}, u32[]{:S(2)}, u32[]{:S(2)}) collective-permute-start(bf16[512,256]{1,0:T(8,128)(2,1)S(1)} %slice.21), channel_id=1, source_target_pairs={{0,224},{32,0},{64,32},{96,64},{128,96},{160,128},{192,160},{224,1... | collective-permute-start | bytes 786440 | tf_op jit(solution)/shard_map/ppermute | solution.py:429
  89.8 1.4 collective-permute-start.17
  91.2 9.6 %collective-permute-done.17.other_lse = f32[16,1,128]{2,1,0:T(1,128)S(1)} collective-permute-done((f32[16,1,128]{2,1,0:T(1,128)}, f32[16,1,128]{2,1,0:T(1,128)S(1)}, u32[]{:S(2)}, u32[]{:S(2)}) %collective-permute-start.17) | collective-permute-done | bytes 8224 | tf_op jit(solution)/shard_map/ppermute | solution.py:425
  100.9 0.5 copy-done.16
  101.4 1.0 copy-done.8
  102.4 2.4 %merge_last.1.near = bf16[2,128,1024]{2,1,0:T(8,128)(2,1)} custom-call(bf16[2048,128]{1,0:T(8,128)(2,1)} %get-tuple-element.60.own, f32[16,1,128]{2,1,0:T(1,128)} %get-tuple-element.61.own_lse, bf16[2048,128]{1,0:T(8,128)(2,1)} %copy-done.8, f32[16,1,128]{2,1,0:T(1,128)} %copy-done.16), custom_call_target="tpu_custom_call" | custom-call | flops 2000000 | bytes 1600000 | tf_op jit(solution)/shard_map/merge_last/pallas_call | solution.py:292
  104.8 0.8 collective-permute-start.22
  105.6 2.5 %collective-permute-done.22.far = bf16[2,128,1024]{2,1,0:T(8,128)(2,1)S(1)} collective-permute-done((bf16[2,128,1024]{2,1,0:T(8,128)(2,1)}, bf16[2,128,1024]{2,1,0:T(8,128)(2,1)S(1)}, u32[]{:S(2)}, u32[]{:S(2)}) %collective-permute-start.22) | collective-permute-done | bytes 524320 | tf_op jit(solution)/shard_map/ppermute | solution.py:425
  108.1 0.9 copy-done.19
  109.0 6.2 %project.1 = bf16[4,8,128,256]{3,2,1,0:T(8,128)(2,1)} custom-call(s32[3]{0:T(128)} %pad_add_fusion.place, bf16[2,128,1024]{2,1,0:T(8,128)(2,1)} %merge_last.1.near, bf16[2,128,1024]{2,1,0:T(8,128)(2,1)} %copy-done.19, bf16[1024,256]{1,0:T(8,128)(2,1)} %refs_0_.1, bf16[1024,256]{1,0:T(8,128)(2,1)} %collective-permute-done.9.refs_1_, ...), custom_call_target="tpu_custom_call" | custom-call | flops 2147483648 | bytes 7000000 | tf_op jit(solution)/shard_map/project/pallas_call | solution.py:325
  115.2 7.5 %all-to-all-start.1 = ((bf16[32,128,256]{2,1,0:T(8,128)(2,1)}), bf16[32,128,256]{2,1,0:T(8,128)(2,1)}, u32[]{:S(2)}, u32[]{:S(2)}) async-start(bf16[32,128,256]{2,1,0:T(8,128)(2,1)} %bitcast.17), calls=%async_computation.1 | async-start | bytes 4194304 | tf_op jit(solution)/shard_map/all_to_all | solution.py:508
  122.7 29.8 %all-to-all-done.1 = bf16[32,128,256]{2,1,0:T(8,128)(2,1)} async-done(((bf16[32,128,256]{2,1,0:T(8,128)(2,1)}), bf16[32,128,256]{2,1,0:T(8,128)(2,1)}, u32[]{:S(2)}, u32[]{:S(2)}) %all-to-all-start.1) | async-done | bytes 2097184 | tf_op jit(solution)/shard_map/all_to_all | solution.py:508
  152.5 4.9 %third.1 = (bf16[128,1024]{1,0:T(8,128)(2,1)}, bf16[8,144,256]{2,1,0:T(8,128)(2,1)}) custom-call(s32[3]{0:T(128)} %pad_add_fusion.place, bf16[4,8,128,256]{3,2,1,0:T(8,128)(2,1)} %bitcast.9.received, bf16[128,1024]{1,0:T(8,128)(2,1)} %hidden.1, f32[1,1024]{1,0:T(1,128)} %bitcast.22, bf16[8,512,256]{2,1,0:T(8,128)(2,1)} %copy-done, ...), custom_call_target="tpu_custom_call" | custom-call | tf_op jit(solution)/shard_map/third/pallas_call | solution.py:377
  157.4 3.5 %all-to-all-start.2 = ((bf16[8,144,256]{2,1,0:T(8,128)(2,1)}), bf16[8,144,256]{2,1,0:T(8,128)(2,1)S(1)}, u32[]{:S(2)}, u32[]{:S(2)}) async-start(bf16[8,144,256]{2,1,0:T(8,128)(2,1)} %get-tuple-element.67), calls=%async_computation.2 | async-start | bytes 1179648 | tf_op jit(solution)/shard_map/all_to_all | solution.py:514
  161.6 10.3 %all-to-all-done.2.partial = bf16[8,144,256]{2,1,0:T(8,128)(2,1)S(1)} async-done(((bf16[8,144,256]{2,1,0:T(8,128)(2,1)}), bf16[8,144,256]{2,1,0:T(8,128)(2,1)S(1)}, u32[]{:S(2)}, u32[]{:S(2)}) %all-to-all-start.2) | async-done | bytes 589856 | tf_op jit(solution)/shard_map/all_to_all | solution.py:514
  172.0 0.8 copy-done.1
  172.8 2.1 %final.1 = bf16[128,256]{1,0:T(8,128)(2,1)} custom-call(s32[1]{0:T(128)S(6)} %copy.13.count, bf16[8,144,256]{2,1,0:T(8,128)(2,1)} %copy-done.1, f32[1,256]{1,0:T(1,128)} %bitcast.23, f32[128,128]{1,0:T(8,128)} %get-tuple-element.74.cosine, f32[128,128]{1,0:T(8,128)} %get-tuple-element.75.sine, s32[1,128]{1,0:T(1,128)} %bitcast.24), custom_call_target="tpu_custom_call" | custom-call | tf_op jit(solution)/shard_map/final/pallas_call | solution.py:414
  (70 shorter events, 0.6 us)
Async XLA Ops:
  4.5 14.1 %collective-permute-start.2 = (bf16[1024,128]{1,0:T(8,128)(2,1)}, bf16[1024,128]{1,0:T(8,128)(2,1)S(1)}, u32[]{:S(2)}, u32[]{:S(2)}) collective-permute-start(bf16[1024,128]{1,0:T(8,128)(2,1)} %bitcast.18), channel_id=1, source_target_pairs={{0,16},{16,0},{1,17},{17,1},{2,18},{18,2},{3,19},{19,3},{4,20},{20... | collective-permute-start | bytes 786440 | tf_op jit(solution)/shard_map/ppermute | solution.py:425
  6.6 12.0 %collective-permute-start = (bf16[6,128,128]{2,1,0:T(8,128)(2,1)}, bf16[6,128,128]{2,1,0:T(8,128)(2,1)S(1)}, u32[]{:S(2)}, u32[]{:S(2)}) collective-permute-start(bf16[6,128,128]{2,1,0:T(8,128)(2,1)} %get-tuple-element.36.refs_4_), channel_id=1, source_target_pairs={{0,32},{32,64},{64,96},{96,128},{128,160},{160,192},{192,224},{224... | collective-permute-start | bytes 589832 | tf_op jit(solution)/shard_map/ppermute | solution.py:429
  8.2 10.3 %collective-permute-start.1 = (bf16[6,128,128]{2,1,0:T(8,128)(2,1)}, bf16[6,128,128]{2,1,0:T(8,128)(2,1)S(1)}, u32[]{:S(2)}, u32[]{:S(2)}) collective-permute-start(bf16[6,128,128]{2,1,0:T(8,128)(2,1)} %get-tuple-element.36.refs_4_), channel_id=1, source_target_pairs={{0,224},{32,0},{64,32},{96,64},{128,96},{160,128},{192,160},{224,1... | collective-permute-start | bytes 589832 | tf_op jit(solution)/shard_map/ppermute | solution.py:429
  12.2 15.2 %collective-permute-start.3 = (bf16[1024,128]{1,0:T(8,128)(2,1)}, bf16[1024,128]{1,0:T(8,128)(2,1)S(1)}, u32[]{:S(2)}, u32[]{:S(2)}) collective-permute-start(bf16[1024,128]{1,0:T(8,128)(2,1)} %bitcast.19), channel_id=1, source_target_pairs={{0,8},{8,0},{1,9},{9,1},{2,10},{10,2},{3,11},{11,3},{4,12},{12,4},... | collective-permute-start | bytes 786440 | tf_op jit(solution)/shard_map/ppermute | solution.py:425
  18.6 2.5 %copy-start.21 = (bf16[6,128,128]{2,1,0:T(8,128)(2,1)}, bf16[6,128,128]{2,1,0:T(8,128)(2,1)S(1)}, u32[]{:S(2)}) copy-start(bf16[6,128,128]{2,1,0:T(8,128)(2,1)S(1)} %collective-permute-done.refs_5_) | copy-start | bytes 589828
  18.6 8.9 %copy-start.2 = (bf16[6,128,128]{2,1,0:T(8,128)(2,1)}, bf16[6,128,128]{2,1,0:T(8,128)(2,1)S(1)}, u32[]{:S(2)}) copy-start(bf16[6,128,128]{2,1,0:T(8,128)(2,1)S(1)} %collective-permute-done.1.refs_6_.refs_2_) | copy-start | bytes 589828
  18.6 2.5 %copy-start.10 = (bf16[1024,128]{1,0:T(8,128)(2,1)}, bf16[1024,128]{1,0:T(8,128)(2,1)S(1)}, u32[]{:S(2)}) copy-start(bf16[1024,128]{1,0:T(8,128)(2,1)S(1)} %collective-permute-done.2.refs_1_) | copy-start | bytes 786436
  18.6 11.6 %collective-permute-start.4 = (bf16[1024,128]{1,0:T(8,128)(2,1)S(1)}, bf16[1024,128]{1,0:T(8,128)(2,1)S(1)}, u32[]{:S(2)}, u32[]{:S(2)}) collective-permute-start(bf16[1024,128]{1,0:T(8,128)(2,1)S(1)} %collective-permute-done.2.refs_1_), channel_id=1, source_target_pairs={{0,8},{8,0},{1,9},{9,1},{2,10},{10,2},{3,11},{11,3},{4,12},{12,4},... | collective-permute-start | bytes 786440 | tf_op jit(solution)/shard_map/ppermute | solution.py:425
  18.7 29.2 %collective-permute-start.10 = (bf16[1024,256]{1,0:T(8,128)(2,1)}, bf16[1024,256]{1,0:T(8,128)(2,1)}, u32[]{:S(2)}, u32[]{:S(2)}) collective-permute-start(bf16[1024,256]{1,0:T(8,128)(2,1)} %refs_0_.1), channel_id=1, source_target_pairs={{0,224},{32,0},{64,32},{96,64},{128,96},{160,128},{192,160},{224,1... | collective-permute-start | bytes 1572872 | tf_op jit(solution)/shard_map/ppermute | solution.py:429
  21.0 26.8 %collective-permute-start.9 = (bf16[1024,256]{1,0:T(8,128)(2,1)}, bf16[1024,256]{1,0:T(8,128)(2,1)}, u32[]{:S(2)}, u32[]{:S(2)}) collective-permute-start(bf16[1024,256]{1,0:T(8,128)(2,1)} %refs_0_.1), channel_id=1, source_target_pairs={{0,32},{32,64},{64,96},{96,128},{128,160},{160,192},{192,224},{224... | collective-permute-start | bytes 1572872 | tf_op jit(solution)/shard_map/ppermute | solution.py:429
  21.0 20.2 %collective-permute-start.5 = (bf16[6,128,128]{2,1,0:T(8,128)(2,1)S(1)}, bf16[6,128,128]{2,1,0:T(8,128)(2,1)S(1)}, u32[]{:S(2)}, u32[]{:S(2)}) collective-permute-start(bf16[6,128,128]{2,1,0:T(8,128)(2,1)S(1)} %collective-permute-done.refs_5_), channel_id=1, source_target_pairs={{0,32},{32,64},{64,96},{96,128},{128,160},{160,192},{192,224},{224... | collective-permute-start | bytes 589832 | tf_op jit(solution)/shard_map/ppermute | solution.py:429
  21.0 79.8 %all-to-all-start = ((bf16[8,512,256]{2,1,0:T(8,128)(2,1)}), bf16[8,512,256]{2,1,0:T(8,128)(2,1)S(1)}, u32[]{:S(2)}, u32[]{:S(2)}) async-start(bf16[8,512,256]{2,1,0:T(8,128)(2,1)} %half.1), calls=%async_computation | async-start | bytes 4194304 | tf_op jit(solution)/shard_map/all_to_all | solution.py:479
  27.4 2.8 %copy-start.11 = (bf16[1024,128]{1,0:T(8,128)(2,1)}, bf16[1024,128]{1,0:T(8,128)(2,1)S(1)}, u32[]{:S(2)}) copy-start(bf16[1024,128]{1,0:T(8,128)(2,1)S(1)} %collective-permute-done.3.refs_2_.refs_0_) | copy-start | bytes 786436
  27.4 13.8 %collective-permute-start.6 = (bf16[6,128,128]{2,1,0:T(8,128)(2,1)S(1)}, bf16[6,128,128]{2,1,0:T(8,128)(2,1)S(1)}, u32[]{:S(2)}, u32[]{:S(2)}) collective-permute-start(bf16[6,128,128]{2,1,0:T(8,128)(2,1)S(1)} %collective-permute-done.1.refs_6_.refs_2_), channel_id=1, source_target_pairs={{0,224},{32,0},{64,32},{96,64},{128,96},{160,128},{192,160},{224,1... | collective-permute-start | bytes 589832 | tf_op jit(solution)/shard_map/ppermute | solution.py:429
  30.2 0.7 copy-start.12
  41.2 12.7 %copy-start.3 = (bf16[6,128,128]{2,1,0:T(8,128)(2,1)}, bf16[6,128,128]{2,1,0:T(8,128)(2,1)S(1)}, u32[]{:S(2)}) copy-start(bf16[6,128,128]{2,1,0:T(8,128)(2,1)S(1)} %collective-permute-done.5.refs_3_) | copy-start | bytes 589828
  41.3 12.7 %copy-start.4 = (bf16[6,128,128]{2,1,0:T(8,128)(2,1)}, bf16[6,128,128]{2,1,0:T(8,128)(2,1)S(1)}, u32[]{:S(2)}) copy-start(bf16[6,128,128]{2,1,0:T(8,128)(2,1)S(1)} %collective-permute-done.6.refs_4_) | copy-start | bytes 589828
  41.3 6.5 %collective-permute-start.7 = (bf16[6,128,128]{2,1,0:T(8,128)(2,1)S(1)}, bf16[6,128,128]{2,1,0:T(8,128)(2,1)S(1)}, u32[]{:S(2)}, u32[]{:S(2)}) collective-permute-start(bf16[6,128,128]{2,1,0:T(8,128)(2,1)S(1)} %collective-permute-done.5.refs_3_), channel_id=1, source_target_pairs={{0,32},{32,64},{64,96},{96,128},{128,160},{160,192},{192,224},{224... | collective-permute-start | bytes 589832 | tf_op jit(solution)/shard_map/ppermute | solution.py:429
  41.4 6.4 %collective-permute-start.8 = (bf16[6,128,128]{2,1,0:T(8,128)(2,1)S(1)}, bf16[6,128,128]{2,1,0:T(8,128)(2,1)S(1)}, u32[]{:S(2)}, u32[]{:S(2)}) collective-permute-start(bf16[6,128,128]{2,1,0:T(8,128)(2,1)S(1)} %collective-permute-done.6.refs_4_), channel_id=1, source_target_pairs={{0,224},{32,0},{64,32},{96,64},{128,96},{160,128},{192,160},{224,1... | collective-permute-start | bytes 589832 | tf_op jit(solution)/shard_map/ppermute | solution.py:429
  47.8 6.2 %copy-start.5 = (bf16[6,128,128]{2,1,0:T(8,128)(2,1)}, bf16[6,128,128]{2,1,0:T(8,128)(2,1)S(1)}, u32[]{:S(2)}) copy-start(bf16[6,128,128]{2,1,0:T(8,128)(2,1)S(1)} %collective-permute-done.7.refs_5_) | copy-start | bytes 589828
  47.8 6.1 %copy-start.6 = (bf16[6,128,128]{2,1,0:T(8,128)(2,1)}, bf16[6,128,128]{2,1,0:T(8,128)(2,1)S(1)}, u32[]{:S(2)}) copy-start(bf16[6,128,128]{2,1,0:T(8,128)(2,1)S(1)} %collective-permute-done.8.refs_6_) | copy-start | bytes 589828
  47.9 6.1 %collective-permute-start.11 = (bf16[6,128,128]{2,1,0:T(8,128)(2,1)S(1)}, bf16[6,128,128]{2,1,0:T(8,128)(2,1)S(1)}, u32[]{:S(2)}, u32[]{:S(2)}) collective-permute-start(bf16[6,128,128]{2,1,0:T(8,128)(2,1)S(1)} %collective-permute-done.7.refs_5_), channel_id=1, source_target_pairs={{0,32},{32,64},{64,96},{96,128},{128,160},{160,192},{192,224},{224... | collective-permute-start | bytes 589832 | tf_op jit(solution)/shard_map/ppermute | solution.py:429
  49.1 21.1 %collective-permute-start.12 = (bf16[1024,256]{1,0:T(8,128)(2,1)}, bf16[1024,256]{1,0:T(8,128)(2,1)S(1)}, u32[]{:S(2)}, u32[]{:S(2)}) collective-permute-start(bf16[1024,256]{1,0:T(8,128)(2,1)} %collective-permute-done.9.refs_1_), channel_id=1, source_target_pairs={{0,32},{32,64},{64,96},{96,128},{128,160},{160,192},{192,224},{224... | collective-permute-start | bytes 1572872 | tf_op jit(solution)/shard_map/ppermute | solution.py:429
  49.9 20.4 %collective-permute-start.13 = (bf16[1024,256]{1,0:T(8,128)(2,1)}, bf16[1024,256]{1,0:T(8,128)(2,1)S(1)}, u32[]{:S(2)}, u32[]{:S(2)}) collective-permute-start(bf16[1024,256]{1,0:T(8,128)(2,1)} %collective-permute-done.10.refs_2_), channel_id=1, source_target_pairs={{0,224},{32,0},{64,32},{96,64},{128,96},{160,128},{192,160},{224,1... | collective-permute-start | bytes 1572872 | tf_op jit(solution)/shard_map/ppermute | solution.py:429
  54.0 0.7 copy-start.7
  65.0 18.6 %collective-permute-start.14 = (bf16[2048,128]{1,0:T(8,128)(2,1)}, bf16[2048,128]{1,0:T(8,128)(2,1)S(1)}, u32[]{:S(2)}, u32[]{:S(2)}) collective-permute-start(bf16[2048,128]{1,0:T(8,128)(2,1)} %get-tuple-element.59), channel_id=1, source_target_pairs={{0,8},{8,0},{1,9},{9,1},{2,10},{10,2},{3,11},{11,3},{4,12},{12,4},... | collective-permute-start | bytes 1572872 | tf_op jit(solution)/shard_map/ppermute | solution.py:425
  70.3 13.3 %copy-start.17 = (bf16[1024,256]{1,0:T(8,128)(2,1)}, bf16[1024,256]{1,0:T(8,128)(2,1)S(1)}, u32[]{:S(2)}) copy-start(bf16[1024,256]{1,0:T(8,128)(2,1)S(1)} %collective-permute-done.12.refs_3_) | copy-start | bytes 1572868
  70.3 13.3 %copy-start.18 = (bf16[1024,256]{1,0:T(8,128)(2,1)}, bf16[1024,256]{1,0:T(8,128)(2,1)S(1)}, u32[]{:S(2)}) copy-start(bf16[1024,256]{1,0:T(8,128)(2,1)S(1)} %collective-permute-done.13.refs_4_) | copy-start | bytes 1572868
  70.3 16.6 %collective-permute-start.18 = (bf16[1024,256]{1,0:T(8,128)(2,1)S(1)}, bf16[1024,256]{1,0:T(8,128)(2,1)S(1)}, u32[]{:S(2)}, u32[]{:S(2)}) collective-permute-start(bf16[1024,256]{1,0:T(8,128)(2,1)S(1)} %collective-permute-done.12.refs_3_), channel_id=1, source_target_pairs={{0,32},{32,64},{64,96},{96,128},{128,160},{160,192},{192,224},{224... | collective-permute-start | bytes 1572872 | tf_op jit(solution)/shard_map/ppermute | solution.py:429
  70.6 16.4 %collective-permute-start.20 = (bf16[1024,256]{1,0:T(8,128)(2,1)S(1)}, bf16[1024,256]{1,0:T(8,128)(2,1)S(1)}, u32[]{:S(2)}, u32[]{:S(2)}) collective-permute-start(bf16[1024,256]{1,0:T(8,128)(2,1)S(1)} %collective-permute-done.13.refs_4_), channel_id=1, source_target_pairs={{0,224},{32,0},{64,32},{96,64},{128,96},{160,128},{192,160},{224,1... | collective-permute-start | bytes 1572872 | tf_op jit(solution)/shard_map/ppermute | solution.py:429
  73.0 10.6 %collective-permute-start.15 = (f32[16,1,128]{2,1,0:T(1,128)}, f32[16,1,128]{2,1,0:T(1,128)S(1)}, u32[]{:S(2)}, u32[]{:S(2)}) collective-permute-start(f32[16,1,128]{2,1,0:T(1,128)} %get-tuple-element.52), channel_id=1, source_target_pairs={{0,8},{8,0},{1,9},{9,1},{2,10},{10,2},{3,11},{11,3},{4,12},{12,4},... | collective-permute-start | bytes 24584 | tf_op jit(solution)/shard_map/ppermute | solution.py:425
  83.6 0.6 copy-start.15
  83.6 0.8 copy-start.9
  86.9 14.0 %collective-permute-start.16 = (bf16[2048,128]{1,0:T(8,128)(2,1)}, bf16[2048,128]{1,0:T(8,128)(2,1)S(1)}, u32[]{:S(2)}, u32[]{:S(2)}) collective-permute-start(bf16[2048,128]{1,0:T(8,128)(2,1)} %get-tuple-element.60.own), channel_id=1, source_target_pairs={{0,16},{16,0},{1,17},{17,1},{2,18},{18,2},{3,19},{19,3},{4,20},{20... | collective-permute-start | bytes 1572872 | tf_op jit(solution)/shard_map/ppermute | solution.py:425
  86.9 21.2 %copy-start.13 = (bf16[1024,256]{1,0:T(8,128)(2,1)}, bf16[1024,256]{1,0:T(8,128)(2,1)S(1)}, u32[]{:S(2)}) copy-start(bf16[1024,256]{1,0:T(8,128)(2,1)S(1)} %collective-permute-done.18.refs_5_) | copy-start | bytes 1572868
  86.9 13.9 %collective-permute-start.19 = (bf16[512,256]{1,0:T(8,128)(2,1)S(1)}, bf16[512,256]{1,0:T(8,128)(2,1)S(1)}, u32[]{:S(2)}, u32[]{:S(2)}) collective-permute-start(bf16[512,256]{1,0:T(8,128)(2,1)S(1)} %slice.20), channel_id=1, source_target_pairs={{0,32},{32,64},{64,96},{96,128},{128,160},{160,192},{192,224},{224... | collective-permute-start | bytes 786440 | tf_op jit(solution)/shard_map/ppermute | solution.py:429
  87.0 13.8 %copy-start.14 = (bf16[1024,256]{1,0:T(8,128)(2,1)}, bf16[1024,256]{1,0:T(8,128)(2,1)S(1)}, u32[]{:S(2)}) copy-start(bf16[1024,256]{1,0:T(8,128)(2,1)S(1)} %collective-permute-done.20.refs_6_) | copy-start | bytes 1572868
  87.0 13.8 %collective-permute-start.21 = (bf16[512,256]{1,0:T(8,128)(2,1)S(1)}, bf16[512,256]{1,0:T(8,128)(2,1)}, u32[]{:S(2)}, u32[]{:S(2)}) collective-permute-start(bf16[512,256]{1,0:T(8,128)(2,1)S(1)} %slice.21), channel_id=1, source_target_pairs={{0,224},{32,0},{64,32},{96,64},{128,96},{160,128},{192,160},{224,1... | collective-permute-start | bytes 786440 | tf_op jit(solution)/shard_map/ppermute | solution.py:429
  89.8 11.0 %collective-permute-start.17 = (f32[16,1,128]{2,1,0:T(1,128)}, f32[16,1,128]{2,1,0:T(1,128)S(1)}, u32[]{:S(2)}, u32[]{:S(2)}) collective-permute-start(f32[16,1,128]{2,1,0:T(1,128)} %get-tuple-element.61.own_lse), channel_id=1, source_target_pairs={{0,16},{16,0},{1,17},{17,1},{2,18},{18,2},{3,19},{19,3},{4,20},{20... | collective-permute-start | bytes 24584 | tf_op jit(solution)/shard_map/ppermute | solution.py:425
  100.8 7.3 %copy-start.20 = (bf16[512,256]{1,0:T(8,128)(2,1)}, bf16[512,256]{1,0:T(8,128)(2,1)S(1)}, u32[]{:S(2)}) copy-start(bf16[512,256]{1,0:T(8,128)(2,1)S(1)} %collective-permute-done.19.refs_7_) | copy-start | bytes 786436
  100.8 14.4 %copy-start = (bf16[8,512,256]{2,1,0:T(8,128)(2,1)}, bf16[8,512,256]{2,1,0:T(8,128)(2,1)S(1)}, u32[]{:S(2)}) copy-start(bf16[8,512,256]{2,1,0:T(8,128)(2,1)S(1)} %all-to-all-done.near) | copy-start | bytes 6291460
  101.4 1.0 copy-start.8
  104.8 3.2 %collective-permute-start.22 = (bf16[2,128,1024]{2,1,0:T(8,128)(2,1)}, bf16[2,128,1024]{2,1,0:T(8,128)(2,1)S(1)}, u32[]{:S(2)}, u32[]{:S(2)}) collective-permute-start(bf16[2,128,1024]{2,1,0:T(8,128)(2,1)} %merge_last.1.near), channel_id=1, source_target_pairs={{0,8},{8,0},{1,9},{9,1},{2,10},{10,2},{3,11},{11,3},{4,12},{12,4},... | collective-permute-start | bytes 1572872 | tf_op jit(solution)/shard_map/ppermute | solution.py:425
  105.6 17.1 %collective-permute-start.23 = (bf16[8,512,256]{2,1,0:T(8,128)(2,1)S(1)}, bf16[8,512,256]{2,1,0:T(8,128)(2,1)}, u32[]{:S(2)}, u32[]{:S(2)}) collective-permute-start(bf16[8,512,256]{2,1,0:T(8,128)(2,1)S(1)} %all-to-all-done.near), channel_id=1, source_target_pairs={{0,8},{8,0},{1,9},{9,1},{2,10},{10,2},{3,11},{11,3},{4,12},{12,4},... | collective-permute-start | bytes 6291464 | tf_op jit(solution)/shard_map/ppermute | solution.py:425
  108.1 0.9 copy-start.19
  115.2 37.3 %all-to-all-start.1 = ((bf16[32,128,256]{2,1,0:T(8,128)(2,1)}), bf16[32,128,256]{2,1,0:T(8,128)(2,1)}, u32[]{:S(2)}, u32[]{:S(2)}) async-start(bf16[32,128,256]{2,1,0:T(8,128)(2,1)} %bitcast.17), calls=%async_computation.1 | async-start | bytes 4194304 | tf_op jit(solution)/shard_map/all_to_all | solution.py:508
  157.4 14.5 %all-to-all-start.2 = ((bf16[8,144,256]{2,1,0:T(8,128)(2,1)}), bf16[8,144,256]{2,1,0:T(8,128)(2,1)S(1)}, u32[]{:S(2)}, u32[]{:S(2)}) async-start(bf16[8,144,256]{2,1,0:T(8,128)(2,1)} %get-tuple-element.67), calls=%async_computation.2 | async-start | bytes 1179648 | tf_op jit(solution)/shard_map/all_to_all | solution.py:514
  172.0 0.8 copy-start.1
  (1 other events, 0.6 us)
